TPU v7x, 32 devices: a whole 2x2x4 slice. The times are simulated.
32 devices in a mesh: cohort: 4 (over y, core), cell: 8 (over z, x).
Axes of the slice: x: 2, y: 2, z: 4, core: 2. Of those that a mesh axis runs over, the one named last changes fastest.
Arguments:
- cohort_features: bfloat16 [2048, 128], P('cohort'), may hold values from -6 to 6
- cell_features: bfloat16 [4096, 128], P('cell'), may hold values from -6 to 6
- cohort_region: int32 [2048], P('cohort'), may hold values from 0 to 31
- cell_region: int32 [4096], P('cell'), may hold values from 0 to 31
- penalty: float32 [32, 32], replicated, may hold values from 0 to 2
- cohort_mass: float32 [2048], P('cohort'), may hold values from 0.5 to 2
- cell_mass: float32 [4096], P('cell'), may hold values from 0.25 to 1
- cohort_segment: int32 [2048], P('cohort'), may hold values from 0 to 31
- spend_merchant: int32 [2048, 1024], P('cohort', 'cell'), may hold values from 0 to 127
- spend_day: int32 [2048, 1024], P('cohort', 'cell'), may hold values from 0 to 63
- spend_amount: float32 [2048, 1024], P('cohort', 'cell'), may hold values from 0.05 to 0.5
Outputs:
- weights: float32 [2048], P('cohort')
- cell_scale: float32 [4096], P('cell')
- trend: float32 [64, 32, 1024], P('cohort', None, 'cell')
All inputs are finite; a program needn't handle non-finite values.
Results may differ from a plain program's by a relative error of at most 0.0003.
Values sent between devices are 32-bit elements; how exact they have to be, the bound alone decides.
No kernel may reach another device: no remote copies, remote signals or barrier semaphores. Data moves between devices by JAX's collectives and lax.ppermute only.
A program may use at most 64 MiB of HBM per device.

v0:
```python
import math

import jax
import jax.numpy as jnp
import numpy as np
from jax import lax
from jax.sharding import PartitionSpec as P

ITERS = 2
SEG = 32
MERCH_DEV = 128
DAYS = 64


half_span = 11


def filter_table(day_count):
    outer = 13.0
    coeffs = []
    for offset_days in range(-half_span, half_span + 1):
        sq = float(offset_days * offset_days)
        top = (
            315.0
            * ((outer - 1) ** 2 - sq)
            * (outer**2 - sq)
            * ((outer + 1) ** 2 - sq)
            * (3 * outer**2 - 16 - 11 * sq)
        )
        bottom = (
            8
            * outer
            * (outer**2 - 1)
            * (4 * outer**2 - 1)
            * (4 * outer**2 - 9)
            * (4 * outer**2 - 25)
        )
        coeffs.append(top / bottom)
    matrix = np.zeros((day_count, day_count))
    for row_day in range(day_count):
        for offset_days in range(-half_span, half_span + 1):
            col_day = row_day + offset_days
            if 0 <= col_day < day_count:
                matrix[row_day, col_day] = coeffs[offset_days + half_span]
        matrix[row_day] = matrix[row_day] / matrix[row_day].sum()
    return matrix


def penalty_block(row_regions, col_regions, penalty):
    region_count = penalty.shape[0]
    row_onehot = (row_regions[:, None] == jnp.arange(region_count)[None, :]).astype(jnp.float32)
    col_onehot = (jnp.arange(region_count)[:, None] == col_regions[None, :]).astype(jnp.float32)
    rowpen = jnp.dot(row_onehot, penalty, precision=lax.Precision.HIGHEST)
    return jnp.dot(rowpen, col_onehot, precision=lax.Precision.HIGHEST)


def gibbs(row_feats, col_feats, pen_block):
    inv_root = 1.0 / math.sqrt(row_feats.shape[1])
    inner = jnp.dot(row_feats, col_feats.T, preferred_element_type=jnp.float32)
    return jnp.exp(inner * inv_root - pen_block)


def divide(operand, summed):
    return operand / summed


def multiply(operand, summed):
    return operand * summed


def finish_rows(partial_value, operand, combine):
    summed = lax.psum(partial_value, "cell")
    return combine(operand, summed)


def spend_table(weights, segments, merchants, days, amounts):
    cohort_count, record_count = amounts.shape
    group = math.gcd(cohort_count, 64)
    steps_count = cohort_count // group
    day_iota = jnp.arange(DAYS, dtype=jnp.int32)
    merch_iota = jnp.arange(MERCH_DEV, dtype=jnp.int32)
    seg_iota = jnp.arange(SEG, dtype=jnp.int32)

    def one_group(running, item):
        group_weights, group_segments, group_merch, group_days, group_amounts = item
        values = group_weights[:, None] * group_amounts
        day_values = jnp.where(
            group_days[:, :, None] == day_iota[None, None, :], values[:, :, None], 0.0
        )
        merch_hot = (group_merch[:, :, None] == merch_iota[None, None, :]).astype(jnp.float32)
        per_cohort = jnp.einsum(
            "brd,brm->bdm", day_values, merch_hot, precision=lax.Precision.HIGHEST
        )
        seg_hot = (group_segments[:, None] == seg_iota[None, :]).astype(jnp.float32)
        added = jnp.einsum("bs,bdm->dsm", seg_hot, per_cohort, precision=lax.Precision.HIGHEST)
        return (running + added, None)

    start = jnp.zeros((DAYS, SEG, MERCH_DEV), jnp.float32)
    result, _ = lax.scan(
        one_group,
        start,
        (
            weights.reshape(steps_count, group),
            segments.reshape(steps_count, group),
            merchants.reshape(steps_count, group, record_count),
            days.reshape(steps_count, group, record_count),
            amounts.reshape(steps_count, group, record_count),
        ),
    )
    return result


def per_device(
    cohort_features,
    cell_features,
    cohort_region,
    cell_region,
    penalty,
    cohort_mass,
    cell_mass,
    cohort_segment,
    spend_merchant,
    spend_day,
    spend_amount,
):
    pen_block = penalty_block(cohort_region, cell_region, penalty)

    def kernel():
        return gibbs(cohort_features, cell_features, pen_block)

    cell_scale = jnp.ones((cell_features.shape[0],), jnp.float32)
    cohort_scale = cohort_mass
    for iteration in range(ITERS):
        partial_value = jnp.dot(kernel(), cell_scale, precision=lax.Precision.HIGHEST)
        cohort_scale = finish_rows(partial_value, cohort_mass, divide)
        column = jnp.dot(cohort_scale, kernel(), precision=lax.Precision.HIGHEST)
        cell_scale = cell_mass / lax.psum(column, "cohort")
    partial_value = jnp.dot(kernel(), cell_scale, precision=lax.Precision.HIGHEST)
    weights = finish_rows(partial_value, cohort_scale, multiply)
    merch_local = MERCH_DEV
    spend_bins = spend_table(weights, cohort_segment, spend_merchant, spend_day, spend_amount)
    henderson = jnp.asarray(filter_table(DAYS), jnp.float32)
    trend_all = jnp.dot(henderson, spend_bins.reshape(DAYS, -1), precision=lax.Precision.HIGHEST)
    trend = lax.psum_scatter(
        trend_all.reshape(DAYS, SEG, merch_local), "cohort", scatter_dimension=0, tiled=True
    )
    return (weights, cell_scale, trend)


def solution(mesh):
    return jax.shard_map(
        per_device,
        mesh=mesh,
        in_specs=(
            P("cohort", None),
            P("cell", None),
            P("cohort"),
            P("cell"),
            P(),
            P("cohort"),
            P("cell"),
            P("cohort"),
            P("cohort", "cell"),
            P("cohort", "cell"),
            P("cohort", "cell"),
        ),
        out_specs=(P("cohort"), P("cell"), P("cohort", None, "cell")),
        check_vma=False,
    )
```

profile of v0, /device:TPU:1, one launch (start us, length us, event | category | flops | bytes accessed | tf_op | source)
XLA Modules:
  0.0 183.9 jit_solution(2227648336410848604)
XLA Ops:
  7.2 0.0 copy-start
  7.2 0.0 reduce-scatter.2.cloned.1.call-start
  7.2 0.8 reshape.66
  8.0 1.1 fusion.30
  9.1 0.0 copy-start.3
  9.1 1.3 fusion.32
  10.3 0.0 copy-done
  10.3 0.0 copy-start.4
  10.3 1.2 fusion.27
  11.6 1.0 fusion.34
  12.6 18.7 %psum.35 = f32[512]{0:T(512)S(1)} all-reduce(f32[512]{0:T(512)S(1)} %bitcast.74), channel_id=1, replica_groups=mesh['cohort'=4,'cell'=8] {'cell'}, use_global_device_ids=true, to_apply=%region_0.0 | all-reduce | flops 512 | bytes 4096 | tf_op jit(solution)/shard_map/psum | solution.py:72
  31.3 0.0 copy-done.3
  31.3 0.6 fusion.37
  31.9 9.4 %psum.36 = f32[512]{0:T(512)S(1)} all-reduce(f32[512]{0:T(512)S(1)} %bitcast.71), channel_id=1, replica_groups=mesh['cohort'=4,'cell'=8] {'cohort'}, use_global_device_ids=true, to_apply=%region_1.0 | all-reduce | flops 512 | bytes 4096 | tf_op jit(solution)/shard_map/psum | solution.py:137
  41.3 0.0 copy-done.4
  41.3 1.0 fusion.38
  42.3 13.7 %psum.37 = f32[512]{0:T(512)S(1)} all-reduce(f32[512]{0:T(512)S(1)} %bitcast.72), channel_id=1, replica_groups=mesh['cohort'=4,'cell'=8] {'cell'}, use_global_device_ids=true, to_apply=%region_2.0 | all-reduce | flops 512 | bytes 4096 | tf_op jit(solution)/shard_map/psum | solution.py:72
  56.0 0.6 fusion.39
  56.6 9.2 %psum.38 = f32[512]{0:T(512)S(1)} all-reduce(f32[512]{0:T(512)S(1)} %bitcast.75), channel_id=1, replica_groups=mesh['cohort'=4,'cell'=8] {'cohort'}, use_global_device_ids=true, to_apply=%region_3.0 | all-reduce | flops 512 | bytes 4096 | tf_op jit(solution)/shard_map/psum | solution.py:137
  65.8 0.0 copy-start.2
  65.8 1.0 fusion.40
  66.8 15.7 %psum.39 = f32[512]{0:T(512)S(1)} all-reduce(f32[512]{0:T(512)S(1)} %bitcast.73), channel_id=1, replica_groups=mesh['cohort'=4,'cell'=8] {'cell'}, use_global_device_ids=true, to_apply=%region_4.0 | all-reduce | flops 512 | bytes 4096 | tf_op jit(solution)/shard_map/psum | solution.py:72
  82.5 0.0 copy-start.5
  82.5 0.1 reshape.63
  82.6 0.0 copy-done.2
  82.6 0.5 copy-done.5
  83.1 65.2 %while.11 = (s32[]{:T(128)}, f32[64,32,128]{2,1,0:T(8,128)S(1)}, s32[8,64,128]{2,1,0:T(8,128)}, f32[8,64]{1,0:T(8,128)S(1)}, f32[8,64,128]{2,1,0:T(8,128)}, /*in...) while((s32[]{:T(128)}, f32[64,32,128]{2,1,0:T(8,128)S(1)}, ...), condition=%wide.region_6.7_spmd.clone, body=%wide.region_5.6_spmd.clone.sunk | while | flops 1009264640 | bytes 6588031 | solution.py:99
  83.1 0.8 bitcast_multiply_fusion.2
  83.9 0.8 dynamic-slice_bitcast_fusion.3
  84.7 4.0 %fusion.66 = f32[64,64,128]{2,1,0:T(8,128)S(1)} fusion(s32[64,128]{1,0:T(8,128)S(1)} %get-tuple-element.147, f32[64,128]{1,0:T(8,128)S(1)} %bitcast_multiply_fusion.2, s32[64,128]{1,0:T(8,128)S(1)} %get-tuple-element.148), kind=kOutput, calls=%fused_computation.4.clone.1 | convolution fusion | flops 807403520 | bytes 2195456 | tf_op jit(solution)/shard_map/while/body/eval_jaxpr/brd,brm->bdm/dot_general | solution.py:91
  88.7 2.5 %fusion.68 = f32[64,32,128]{2,1,0:T(8,128)S(1)} fusion(f32[64,64,128]{2,1,0:T(8,128)S(1)} %fusion.66, f32[64,32,128]{2,1,0:T(8,128)S(1)} %get-tuple-element.159, pred[]{:T(512)S(6)} %compare.3, s32[64]{0:T(128)S(1)} %fusion.67), kind=kOutput, calls=%fused_computation.11.clone.1 | convolution fusion | flops 201852928 | bytes 4194561 | tf_op jit(solution)/shard_map/while/body/eval_jaxpr/bs,bdm->dsm/dot_general | solution.py:95
  91.2 0.8 bitcast_multiply_fusion.2
  92.1 0.8 dynamic-slice_bitcast_fusion.3
  92.9 4.0 %fusion.66 = f32[64,64,128]{2,1,0:T(8,128)S(1)} fusion(s32[64,128]{1,0:T(8,128)S(1)} %get-tuple-element.147, f32[64,128]{1,0:T(8,128)S(1)} %bitcast_multiply_fusion.2, s32[64,128]{1,0:T(8,128)S(1)} %get-tuple-element.148), kind=kOutput, calls=%fused_computation.4.clone.1 | convolution fusion | flops 807403520 | bytes 2195456 | tf_op jit(solution)/shard_map/while/body/eval_jaxpr/brd,brm->bdm/dot_general | solution.py:91
  96.9 2.5 %fusion.68 = f32[64,32,128]{2,1,0:T(8,128)S(1)} fusion(f32[64,64,128]{2,1,0:T(8,128)S(1)} %fusion.66, f32[64,32,128]{2,1,0:T(8,128)S(1)} %get-tuple-element.159, pred[]{:T(512)S(6)} %compare.3, s32[64]{0:T(128)S(1)} %fusion.67), kind=kOutput, calls=%fused_computation.11.clone.1 | convolution fusion | flops 201852928 | bytes 4194561 | tf_op jit(solution)/shard_map/while/body/eval_jaxpr/bs,bdm->dsm/dot_general | solution.py:95
  99.4 0.8 bitcast_multiply_fusion.2
  100.2 0.8 dynamic-slice_bitcast_fusion.3
  101.0 4.0 %fusion.66 = f32[64,64,128]{2,1,0:T(8,128)S(1)} fusion(s32[64,128]{1,0:T(8,128)S(1)} %get-tuple-element.147, f32[64,128]{1,0:T(8,128)S(1)} %bitcast_multiply_fusion.2, s32[64,128]{1,0:T(8,128)S(1)} %get-tuple-element.148), kind=kOutput, calls=%fused_computation.4.clone.1 | convolution fusion | flops 807403520 | bytes 2195456 | tf_op jit(solution)/shard_map/while/body/eval_jaxpr/brd,brm->bdm/dot_general | solution.py:91
  105.0 2.5 %fusion.68 = f32[64,32,128]{2,1,0:T(8,128)S(1)} fusion(f32[64,64,128]{2,1,0:T(8,128)S(1)} %fusion.66, f32[64,32,128]{2,1,0:T(8,128)S(1)} %get-tuple-element.159, pred[]{:T(512)S(6)} %compare.3, s32[64]{0:T(128)S(1)} %fusion.67), kind=kOutput, calls=%fused_computation.11.clone.1 | convolution fusion | flops 201852928 | bytes 4194561 | tf_op jit(solution)/shard_map/while/body/eval_jaxpr/bs,bdm->dsm/dot_general | solution.py:95
  107.6 0.8 bitcast_multiply_fusion.2
  108.4 0.8 dynamic-slice_bitcast_fusion.3
  109.2 4.0 %fusion.66 = f32[64,64,128]{2,1,0:T(8,128)S(1)} fusion(s32[64,128]{1,0:T(8,128)S(1)} %get-tuple-element.147, f32[64,128]{1,0:T(8,128)S(1)} %bitcast_multiply_fusion.2, s32[64,128]{1,0:T(8,128)S(1)} %get-tuple-element.148), kind=kOutput, calls=%fused_computation.4.clone.1 | convolution fusion | flops 807403520 | bytes 2195456 | tf_op jit(solution)/shard_map/while/body/eval_jaxpr/brd,brm->bdm/dot_general | solution.py:91
  113.2 2.5 %fusion.68 = f32[64,32,128]{2,1,0:T(8,128)S(1)} fusion(f32[64,64,128]{2,1,0:T(8,128)S(1)} %fusion.66, f32[64,32,128]{2,1,0:T(8,128)S(1)} %get-tuple-element.159, pred[]{:T(512)S(6)} %compare.3, s32[64]{0:T(128)S(1)} %fusion.67), kind=kOutput, calls=%fused_computation.11.clone.1 | convolution fusion | flops 201852928 | bytes 4194561 | tf_op jit(solution)/shard_map/while/body/eval_jaxpr/bs,bdm->dsm/dot_general | solution.py:95
  115.7 0.8 bitcast_multiply_fusion.2
  116.5 0.8 dynamic-slice_bitcast_fusion.3
  117.3 4.0 %fusion.66 = f32[64,64,128]{2,1,0:T(8,128)S(1)} fusion(s32[64,128]{1,0:T(8,128)S(1)} %get-tuple-element.147, f32[64,128]{1,0:T(8,128)S(1)} %bitcast_multiply_fusion.2, s32[64,128]{1,0:T(8,128)S(1)} %get-tuple-element.148), kind=kOutput, calls=%fused_computation.4.clone.1 | convolution fusion | flops 807403520 | bytes 2195456 | tf_op jit(solution)/shard_map/while/body/eval_jaxpr/brd,brm->bdm/dot_general | solution.py:91
  121.3 2.5 %fusion.68 = f32[64,32,128]{2,1,0:T(8,128)S(1)} fusion(f32[64,64,128]{2,1,0:T(8,128)S(1)} %fusion.66, f32[64,32,128]{2,1,0:T(8,128)S(1)} %get-tuple-element.159, pred[]{:T(512)S(6)} %compare.3, s32[64]{0:T(128)S(1)} %fusion.67), kind=kOutput, calls=%fused_computation.11.clone.1 | convolution fusion | flops 201852928 | bytes 4194561 | tf_op jit(solution)/shard_map/while/body/eval_jaxpr/bs,bdm->dsm/dot_general | solution.py:95
  123.9 0.8 bitcast_multiply_fusion.2
  124.7 0.8 dynamic-slice_bitcast_fusion.3
  125.5 4.0 %fusion.66 = f32[64,64,128]{2,1,0:T(8,128)S(1)} fusion(s32[64,128]{1,0:T(8,128)S(1)} %get-tuple-element.147, f32[64,128]{1,0:T(8,128)S(1)} %bitcast_multiply_fusion.2, s32[64,128]{1,0:T(8,128)S(1)} %get-tuple-element.148), kind=kOutput, calls=%fused_computation.4.clone.1 | convolution fusion | flops 807403520 | bytes 2195456 | tf_op jit(solution)/shard_map/while/body/eval_jaxpr/brd,brm->bdm/dot_general | solution.py:91
  129.5 2.5 %fusion.68 = f32[64,32,128]{2,1,0:T(8,128)S(1)} fusion(f32[64,64,128]{2,1,0:T(8,128)S(1)} %fusion.66, f32[64,32,128]{2,1,0:T(8,128)S(1)} %get-tuple-element.159, pred[]{:T(512)S(6)} %compare.3, s32[64]{0:T(128)S(1)} %fusion.67), kind=kOutput, calls=%fused_computation.11.clone.1 | convolution fusion | flops 201852928 | bytes 4194561 | tf_op jit(solution)/shard_map/while/body/eval_jaxpr/bs,bdm->dsm/dot_general | solution.py:95
  132.0 0.8 bitcast_multiply_fusion.2
  132.9 0.8 dynamic-slice_bitcast_fusion.3
  133.6 4.0 %fusion.66 = f32[64,64,128]{2,1,0:T(8,128)S(1)} fusion(s32[64,128]{1,0:T(8,128)S(1)} %get-tuple-element.147, f32[64,128]{1,0:T(8,128)S(1)} %bitcast_multiply_fusion.2, s32[64,128]{1,0:T(8,128)S(1)} %get-tuple-element.148), kind=kOutput, calls=%fused_computation.4.clone.1 | convolution fusion | flops 807403520 | bytes 2195456 | tf_op jit(solution)/shard_map/while/body/eval_jaxpr/brd,brm->bdm/dot_general | solution.py:91
  137.7 2.5 %fusion.68 = f32[64,32,128]{2,1,0:T(8,128)S(1)} fusion(f32[64,64,128]{2,1,0:T(8,128)S(1)} %fusion.66, f32[64,32,128]{2,1,0:T(8,128)S(1)} %get-tuple-element.159, pred[]{:T(512)S(6)} %compare.3, s32[64]{0:T(128)S(1)} %fusion.67), kind=kOutput, calls=%fused_computation.11.clone.1 | convolution fusion | flops 201852928 | bytes 4194561 | tf_op jit(solution)/shard_map/while/body/eval_jaxpr/bs,bdm->dsm/dot_general | solution.py:95
  140.2 0.8 bitcast_multiply_fusion.2
  141.0 0.8 dynamic-slice_bitcast_fusion.3
  141.8 4.0 %fusion.66 = f32[64,64,128]{2,1,0:T(8,128)S(1)} fusion(s32[64,128]{1,0:T(8,128)S(1)} %get-tuple-element.147, f32[64,128]{1,0:T(8,128)S(1)} %bitcast_multiply_fusion.2, s32[64,128]{1,0:T(8,128)S(1)} %get-tuple-element.148), kind=kOutput, calls=%fused_computation.4.clone.1 | convolution fusion | flops 807403520 | bytes 2195456 | tf_op jit(solution)/shard_map/while/body/eval_jaxpr/brd,brm->bdm/dot_general | solution.py:91
  145.8 2.5 %fusion.68 = f32[64,32,128]{2,1,0:T(8,128)S(1)} fusion(f32[64,64,128]{2,1,0:T(8,128)S(1)} %fusion.66, f32[64,32,128]{2,1,0:T(8,128)S(1)} %get-tuple-element.159, pred[]{:T(512)S(6)} %compare.3, s32[64]{0:T(128)S(1)} %fusion.67), kind=kOutput, calls=%fused_computation.11.clone.1 | convolution fusion | flops 201852928 | bytes 4194561 | tf_op jit(solution)/shard_map/while/body/eval_jaxpr/bs,bdm->dsm/dot_general | solution.py:95
  148.3 0.0 copy-done.1
  148.3 1.6 convolution_bitcast_fusion
  149.9 1.2 copy.17
  151.1 0.0 reduce-scatter.2.cloned.1.call-update
  151.1 25.9 %reduce-scatter.2.cloned.1.call-done = f32[16,32,128]{2,1,0:T(8,128)} async-done(((f32[64,32,128]{2,1,0:T(8,128)}), f32[16,32,128]{2,1,0:T(8,128)}) %reduce-scatter.2.cloned.1.call-update) | async-done | bytes 262160 | tf_op jit(solution)/shard_map/reduce_scatter | solution.py:144
  (23 shorter events, 0.2 us)
Async XLA Ops:
  7.2 3.2 %copy-start = (bf16[512,128]{1,0:T(8,128)(2,1)S(1)}, bf16[512,128]{1,0:T(8,128)(2,1)}, u32[]{:S(2)}) copy-start(bf16[512,128]{1,0:T(8,128)(2,1)} %param.14) | copy-start | bytes 393220
  7.2 169.9 %reduce-scatter.2.cloned.1.call-start = ((), (), s32[]{:S(2)}) async-start(), calls=%async_computation.1 | async-start | bytes 1310720 | tf_op jit(solution)/shard_map/reduce_scatter | solution.py:144
  9.1 22.2 %copy-start.3 = (f32[512]{0:T(512)S(1)}, f32[512]{0:T(512)}, u32[]{:S(2)}) copy-start(f32[512]{0:T(512)} %param.19) | copy-start | bytes 6148
  10.3 31.0 %copy-start.4 = (f32[512]{0:T(512)S(1)}, f32[512]{0:T(512)}, u32[]{:S(2)}) copy-start(f32[512]{0:T(512)} %param.20) | copy-start | bytes 6148
  65.8 16.8 %copy-start.2 = (f32[512]{0:T(512)}, f32[512]{0:T(512)S(1)}, u32[]{:S(2)}) copy-start(f32[512]{0:T(512)S(1)} %div.15) | copy-start | bytes 6148
  82.5 0.6 copy-start.5
  82.6 65.7 %copy-start.1 = (f32[64,64]{1,0:T(8,128)S(1)}, f32[64,64]{1,0:T(8,128)}, u32[]{:S(2)}) copy-start(f32[64,64]{1,0:T(8,128)} %constant.26.clone) | copy-start | bytes 49156
Sparse Core Ops, SparseCore 0:
  151.2 25.7 reduce-scatter.1
where the time goes:
time: 186 us; the launch traced here: 184 us
  blocking collectives  66.7 us (36%)
  matrix products  61 us (33%)
  waiting for transfers between devices  26 us (14%)
  between operations  14.1 us (8%)
  local copies, waits for them, and re-layouts  8.94 us (5%)
  other arithmetic  6.73 us (4%)
    psum x3, blocking collectives, finish_rows(): summed = lax.psum(partial_value, 'cell')  48.1 us
    dot_general x8, matrix products, one_group(): jnp.einsum('brd,brm->bdm', day_values, merch_hot, precision=lax.Precision...  32 us
    reduce_scatter x1, waiting for transfers between devices, per_device(): lax.psum_scatter(trend_all.reshape(DAYS, SEG, merch_local), 'cohort', sca...  25.9 us
    dot_general x8, matrix products, one_group(): jnp.einsum('bs,bdm->dsm', seg_hot, per_cohort, precision=lax.Precision.HI...  19.7 us
    psum x2, blocking collectives, per_device(): cell_scale = cell_mass / lax.psum(column, 'cohort')  18.6 us
    mul x8, other arithmetic, one_group(): values = group_weights[:, None] * group_amounts  6.69 us
    eq x8, local copies, waits for them, and re-layouts, one_group(): group_merch[:, :, None] == merch_iota[None, None, :]  6.27 us
  transfers between devices with their start and end apart: 1, of which 1 were waited for; matrix products, arithmetic and copies ran while one was open for 0% of the time, Pallas kernels for 0%

commit v1 on v0

v1 whole, which is shorter than its diff:
```python
import functools
import math

import jax
import jax.numpy as jnp
import numpy as np
from jax import lax
from jax.experimental import pallas as pl
from jax.experimental.pallas import tpu as pltpu
from jax.sharding import PartitionSpec as P

ITERS = 2
SEG = 32
MERCH_DEV = 128
DAYS = 64
LANES = 128
GROUP = 16

half_span = 11

f32 = jnp.float32
bf16 = jnp.bfloat16
VMEM = pl.BlockSpec(memory_space=pltpu.VMEM)
ANY = pl.BlockSpec(memory_space=pl.ANY)
PARAMS = pltpu.CompilerParams(vmem_limit_bytes=20 * 2**20)


def filter_table(day_count):
    outer = 13.0
    coeffs = []
    for offset_days in range(-half_span, half_span + 1):
        sq = float(offset_days * offset_days)
        top = (
            315.0
            * ((outer - 1) ** 2 - sq)
            * (outer**2 - sq)
            * ((outer + 1) ** 2 - sq)
            * (3 * outer**2 - 16 - 11 * sq)
        )
        bottom = (
            8
            * outer
            * (outer**2 - 1)
            * (4 * outer**2 - 1)
            * (4 * outer**2 - 9)
            * (4 * outer**2 - 25)
        )
        coeffs.append(top / bottom)
    matrix = np.zeros((day_count, day_count))
    for row_day in range(day_count):
        for offset_days in range(-half_span, half_span + 1):
            col_day = row_day + offset_days
            if 0 <= col_day < day_count:
                matrix[row_day, col_day] = coeffs[offset_days + half_span]
        matrix[row_day] = matrix[row_day] / matrix[row_day].sum()
    return matrix


def split2(x):
    hi = x.astype(bf16)
    return hi, (x - hi.astype(f32)).astype(bf16)


def split_rows(x):
    hi = x.astype(bf16)
    rest = x - hi.astype(f32)
    mid = rest.astype(bf16)
    low = (rest - mid.astype(f32)).astype(bf16)
    return jnp.concatenate([hi, mid, low, jnp.zeros((5, x.shape[1]), bf16)], 0)


def cols_of(u, khi_ref, klo_ref):
    rows = split_rows(u)
    out = jnp.dot(rows, khi_ref[...], preferred_element_type=f32)
    out = out + jnp.dot(rows, klo_ref[...], preferred_element_type=f32)
    return jnp.sum(out, axis=0, keepdims=True)


def rows_of(v, khi_ref, klo_ref):
    rows = split_rows(v)
    dims = (((1,), (1,)), ((), ()))
    out = lax.dot_general(rows, khi_ref[...], dims, preferred_element_type=f32)
    out = out + lax.dot_general(rows, klo_ref[...], dims, preferred_element_type=f32)
    return jnp.sum(out, axis=0, keepdims=True)


def gibbs_body(x_ref, y_ref, rr_ref, cr_ref, pen_ref, khi_ref, klo_ref, r_ref):
    n, m = x_ref.shape[0], y_ref.shape[0]
    regions = pen_ref.shape[0]
    inv_root = 1.0 / math.sqrt(x_ref.shape[1])
    dims = (((1,), (1,)), ((), ()))
    inner = lax.dot_general(x_ref[...], y_ref[...], dims, preferred_element_type=f32)
    row_hot = (lax.broadcasted_iota(jnp.int32, (regions, n), 0) == rr_ref[...]).astype(f32).astype(bf16)
    col_hot = (lax.broadcasted_iota(jnp.int32, (regions, m), 0) == cr_ref[...]).astype(f32).astype(bf16)
    phi, plo = split2(pen_ref[...])
    qhi = jnp.dot(phi, col_hot, preferred_element_type=f32).astype(bf16)
    qlo = jnp.dot(plo, col_hot, preferred_element_type=f32).astype(bf16)
    pen = lax.dot_general(
        jnp.concatenate([row_hot, row_hot], 0),
        jnp.concatenate([qhi, qlo], 0),
        (((0,), (0,)), ((), ())),
        preferred_element_type=f32,
    )
    hi, lo = split2(jnp.exp(inner * inv_root - pen))
    khi_ref[...] = hi
    klo_ref[...] = lo
    r_ref[...] = rows_of(jnp.ones((1, m), f32), khi_ref, klo_ref)


def gibbs_call(x, y, rr, cr, penalty):
    n, m = x.shape[0], y.shape[0]
    return pl.pallas_call(
        gibbs_body,
        in_specs=[VMEM] * 5,
        out_specs=[VMEM] * 3,
        out_shape=[pltpu.VMEM((n, m), bf16), pltpu.VMEM((n, m), bf16), pltpu.VMEM((1, n), f32)],
        compiler_params=PARAMS,
        name="gibbs",
    )(x, y, rr, cr, penalty)


def step_body(apply, parts, mass_ref, khi_ref, klo_ref, *refs):
    part_refs, out_refs = refs[:parts], refs[-2:]
    total = part_refs[0][...]
    for ref in part_refs[1:]:
        total = total + ref[...]
    scale = mass_ref[...] / total
    out_refs[0][...] = scale
    out_refs[1][...] = apply(scale, khi_ref, klo_ref)


def step_call(apply, name, mass, khi, klo, partials, tokens):
    out = khi.shape[1] if apply is cols_of else khi.shape[0]
    return pl.pallas_call(
        functools.partial(step_body, apply, len(partials)),
        in_specs=[VMEM] * (3 + len(partials)) + [ANY] * len(tokens),
        out_specs=[VMEM] * 2,
        out_shape=[pltpu.VMEM(mass.shape, f32), pltpu.VMEM((1, out), f32)],
        compiler_params=PARAMS,
        name=name,
    )(mass, khi, klo, *partials, *tokens)


def table_body(first, count, f_ref, m_ref, d_ref, a_ref, after_ref, hi_ref, lo_ref, tok_ref):
    t_count = f_ref.shape[0]
    filt = f_ref[...]
    merch_iota = lax.broadcasted_iota(jnp.int32, (MERCH_DEV, LANES), 0).astype(f32).astype(bf16)
    one, zero = jnp.ones((MERCH_DEV, LANES), bf16), jnp.zeros((MERCH_DEV, LANES), bf16)

    def group(step, carry):
        start = pl.multiple_of(step * GROUP, GROUP)
        rows_in = pl.ds(first + start, GROUP)
        merch = m_ref[rows_in, :].astype(f32).astype(bf16)
        days = d_ref[rows_in, :]
        amounts = a_ref[rows_in, :]
        tables = []
        for i in range(GROUP):
            day = jnp.broadcast_to(days[i : i + 1, :], (t_count, LANES))
            coef = jnp.take_along_axis(filt, day, axis=1, mode="promise_in_bounds")
            chi, clo = split2(coef * amounts[i : i + 1, :])
            hot = jnp.where(merch_iota == merch[i : i + 1, :], one, zero)
            both = lax.dot_general(
                jnp.concatenate([chi, clo], 0), hot, (((1,), (1,)), ((), ())), preferred_element_type=f32
            )
            tables.append(both[:t_count] + both[t_count:])
        hi, lo = split2(jnp.swapaxes(jnp.stack(tables, 0), 0, 1))
        hi_ref[:, pl.ds(start, GROUP), :] = hi
        lo_ref[:, pl.ds(start, GROUP), :] = lo
        return carry

    lax.fori_loop(0, count // GROUP, group, 0)
    tok_ref[...] = jnp.zeros_like(tok_ref)


def table_call(filt, merchants, days, amounts, first, count, after):
    t_count = filt.shape[0]
    hi, lo, token = pl.pallas_call(
        functools.partial(table_body, first, count),
        in_specs=[VMEM] * 4 + [ANY],
        out_specs=[VMEM] * 3,
        out_shape=[pltpu.VMEM((t_count, count, LANES), bf16)] * 2 + [pltpu.VMEM((8, LANES), f32)],
        compiler_params=PARAMS,
        cost_estimate=pl.CostEstimate(
            flops=4 * count * t_count * 128 * 128, transcendentals=0, bytes_accessed=count * 100000
        ),
        name="tables",
    )(filt, merchants, days, amounts, after)
    return (hi, lo), token


def spread_body(t_first, t_count, counts, parts, seg_ref, u_ref, *refs):
    part_refs = refs[:parts]
    pair_refs = refs[parts : parts + 2 * len(counts)]
    o_ref, w_ref = refs[-2:]
    total = part_refs[0][...]
    for ref in part_refs[1:]:
        total = total + ref[...]
    w = u_ref[...] * total
    w_ref[...] = w
    n = w.shape[1]
    hot = lax.broadcasted_iota(jnp.int32, (SEG, n), 0) == seg_ref[...]
    whi, wlo = split2(jnp.where(hot, w, 0.0))
    both = jnp.concatenate([whi, wlo], 0)
    for t in range(t_first, t_first + t_count, 2):
        hi = jnp.concatenate(
            [jnp.concatenate([pair_refs[2 * k][t + q] for k in range(len(counts))], 0) for q in range(2)], 1
        )
        lo = jnp.concatenate(
            [jnp.concatenate([pair_refs[2 * k + 1][t + q] for k in range(len(counts))], 0) for q in range(2)], 1
        )
        p = jnp.dot(both, hi, preferred_element_type=f32)
        q = jnp.dot(whi, lo, preferred_element_type=f32)
        out = p[:SEG] + p[SEG:] + q
        o_ref[t - t_first] = out[:, :LANES]
        o_ref[t - t_first + 1] = out[:, LANES:]


def spread_call(seg, u, partials, pairs, t_first, t_count, tokens):
    counts = [hi.shape[1] for hi, _ in pairs]
    flat = [ref for pair in pairs for ref in pair]
    return pl.pallas_call(
        functools.partial(spread_body, t_first, t_count, counts, len(partials)),
        in_specs=[VMEM] * (2 + len(partials) + len(flat)) + [ANY] * len(tokens),
        out_specs=[VMEM] * 2,
        out_shape=[
            pltpu.VMEM((t_count, SEG, LANES), f32),
            jax.ShapeDtypeStruct(u.shape, f32),
        ],
        compiler_params=PARAMS,
        name="spread",
    )(seg, u, *partials, *flat, *tokens)


def swap(x, axis, size, mask):
    return lax.ppermute(x, axis, [(i, i ^ mask) for i in range(size)])


def shift(x, axis, size, pair, step):
    blocks = size // pair
    return lax.ppermute(
        x, axis, [(b * pair + r, ((b + step) % blocks) * pair + r) for b in range(blocks) for r in range(pair)]
    )


def per_device(
    n_cohort,
    n_cell,
    cohort_features,
    cell_features,
    cohort_region,
    cell_region,
    penalty,
    cohort_mass,
    cell_mass,
    cohort_segment,
    spend_merchant,
    spend_day,
    spend_amount,
):
    n = cohort_features.shape[0]
    row = lambda x: x.reshape(1, -1)
    t_dev = DAYS // n_cohort
    n_y = n_cohort // 2
    table = np.zeros((n_cohort, DAYS, LANES), np.float32)
    henderson = filter_table(DAYS)
    for me in range(n_cohort):
        y, c = divmod(me, 2)
        rows = []
        for core in (1 - c, c):
            for step in range(1, n_y + 1):
                dest = ((y + step) % n_y) * 2 + core
                rows.extend(range(dest * t_dev, (dest + 1) * t_dev))
        table[me, :, :DAYS] = henderson[rows]
    filt = lax.dynamic_index_in_dim(jnp.asarray(table), lax.axis_index("cohort"), 0, keepdims=False)

    windows = 3 * ITERS + 2
    state = {"first": 0, "left": windows}
    pairs = []

    def fill(after, weight):
        state["left"] -= 1
        first = state["first"]
        count = n - first if state["left"] == 0 else min(n - first, weight * GROUP * n // 512)
        if count <= 0:
            return []
        state["first"] = first + count
        pair, token = table_call(filt, spend_merchant, spend_day, spend_amount, first, count, after)
        pairs.append(pair)
        return [token]

    def over_cell(partial):
        other = swap(partial, "cell", n_cell, 1)
        tokens = fill(partial, 3)
        if tokens:
            partial, other, _ = lax.optimization_barrier((partial, other, tokens[0]))
        partial = partial + other
        others = [shift(partial, "cell", n_cell, 2, k) for k in range(1, n_cell // 2)]
        return [partial] + others, fill(partial, 5)

    def over_cohort(partial):
        others = [shift(partial, "cohort", n_cohort, 1, k) for k in range(1, n_cohort)]
        return [partial] + others, fill(partial, 4)

    khi, klo, partial = gibbs_call(cohort_features, cell_features, row(cohort_region), row(cell_region), penalty)
    for _ in range(ITERS):
        partials, tokens = over_cell(partial)
        cohort_scale, partial = step_call(cols_of, "cols", row(cohort_mass), khi, klo, partials, tokens)
        partials, tokens = over_cohort(partial)
        cell_scale, partial = step_call(rows_of, "rows", row(cell_mass), khi, klo, partials, tokens)
    partials, tokens = over_cell(partial)
    half = DAYS // 2
    seg = row(cohort_segment)
    away, weights = spread_call(seg, cohort_scale, partials, pairs, 0, half, tokens)
    came = swap(away, "cohort", n_cohort, 1)
    mine, _ = spread_call(seg, cohort_scale, partials, pairs, half, half, tokens)
    mine = mine + came
    out = mine[(n_y - 1) * t_dev :]
    for step in range(1, n_y):
        out = out + shift(mine[(step - 1) * t_dev : step * t_dev], "cohort", n_cohort, 2, step)
    return (weights.reshape(-1), cell_scale.reshape(-1), out)


def solution(mesh):
    return jax.shard_map(
        functools.partial(per_device, mesh.shape["cohort"], mesh.shape["cell"]),
        mesh=mesh,
        in_specs=(
            P("cohort", None),
            P("cell", None),
            P("cohort"),
            P("cell"),
            P(),
            P("cohort"),
            P("cell"),
            P("cohort"),
            P("cohort", "cell"),
            P("cohort", "cell"),
            P("cohort", "cell"),
        ),
        out_specs=(P("cohort"), P("cell"), P("cohort", None, "cell")),
        check_vma=False,
    )
```

time: 186 us -> 73.5 us (0.40)
  blocking collectives: 66.7 us -> 0 us
  matrix products: 61 us -> 0 us
  Pallas kernels: 0 us -> 28.9 us
  starting transfers between devices: 0.04 us -> 22.6 us
  waiting for transfers between devices: 26 us -> 8.09 us
  between operations: 14.1 us -> 0.9 us
  other arithmetic: 6.73 us -> 0.83 us
  local copies, waits for them, and re-layouts: 8.94 us -> 11 us
    psum x5 -> x0, blocking collectives: 66.7 us -> none  [the longest x3 48.1 us: finish_rows(): summed = lax.psum(partial_value, 'cell')]
    dot_general x25 -> x0, matrix products: 61 us -> none  [the longest x8 32 us: one_group(): jnp.einsum('brd,brm->bdm', day_values, merch_hot, precision=lax.Precision...]
    pallas_call x0 -> x15, Pallas kernels: none -> 28.9 us  [the longest x8 21.9 us: table_call(): pl.pallas_call(functools.partial(table_body, first, count), in_specs=[VME...]
    reduce_scatter x1 -> x0, waiting for transfers between devices: 25.9 us -> none  [per_device(): lax.psum_scatter(trend_all.reshape(DAYS, SEG, merch_local), 'cohort', sca...]
    ppermute x0 -> x20, starting transfers between devices: none -> 22.6 us  [the longest x16 18.3 us: shift(): lax.ppermute(x, axis, [(b * pair + r, (b + step) % blocks * pair + r) for...]
    unnamed x13 -> x29, local copies, waits for them, and re-layouts: 1.7 us -> 10.2 us
    ppermute x0 -> x20, waiting for transfers between devices: none -> 8.09 us  [the longest x16 8.08 us: shift(): lax.ppermute(x, axis, [(b * pair + r, (b + step) % blocks * pair + r) for...]
    mul x9 -> x0, other arithmetic: 6.7 us -> none  [the longest x8 6.69 us: one_group(): values = group_weights[:, None] * group_amounts]
  transfers between devices with their start and end apart: 1 -> 20, of which waited for: 1 -> 3; matrix products, arithmetic and copies ran while one was open for 0% -> 2% of each run, Pallas kernels for 0% -> 33%
where the time goes in v1:
time: 73.5 us; the launch traced here: 72.3 us
  Pallas kernels  28.9 us (39%)
  starting transfers between devices  22.6 us (31%)
  local copies, waits for them, and re-layouts  11 us (15%)
  waiting for transfers between devices  8.09 us (11%)
  between operations  0.9 us (1%)
  other arithmetic  0.83 us (1%)
    pallas_call x8, Pallas kernels, table_call(): pl.pallas_call(functools.partial(table_body, first, count), in_specs=[VME...  21.9 us
    ppermute x16, starting transfers between devices, shift(): lax.ppermute(x, axis, [(b * pair + r, (b + step) % blocks * pair + r) for...  18.3 us
    unnamed x29, local copies, waits for them, and re-layouts  10.2 us
    ppermute x16, waiting for transfers between devices, shift(): lax.ppermute(x, axis, [(b * pair + r, (b + step) % blocks * pair + r) for...  8.08 us
    ppermute x4, starting transfers between devices, swap(): return lax.ppermute(x, axis, [(i, i ^ mask) for i in range(size)])  4.31 us
    pallas_call x2, Pallas kernels, spread_call(): pl.pallas_call(functools.partial(spread_body, t_first, t_count, counts, l...  4 us
    pallas_call x4, Pallas kernels, step_call(): pl.pallas_call(functools.partial(step_body, apply, len(partials)), in_spe...  1.98 us
  transfers between devices with their start and end apart: 20, of which 3 were waited for; matrix products, arithmetic and copies ran while one was open for 2% of the time, Pallas kernels for 33%

profile of v1, /device:TPU:1, one launch (start us, length us, event | category | flops | bytes accessed | tf_op | source)
XLA Modules:
  0.0 72.3 jit_solution(676852597974292621)
XLA Ops:
  0.7 0.9 %copy-done.6 = bf16[512,128]{1,0:T(8,128)(2,1)S(1)} copy-done((bf16[512,128]{1,0:T(8,128)(2,1)S(1)}, bf16[512,128]{1,0:T(8,128)(2,1)}, u32[]{:S(2)}) %copy-start.6) | copy-done | bytes 131096
  1.6 0.9 %copy-done.7 = bf16[512,128]{1,0:T(8,128)(2,1)S(1)} copy-done((bf16[512,128]{1,0:T(8,128)(2,1)S(1)}, bf16[512,128]{1,0:T(8,128)(2,1)}, u32[]{:S(2)}) %copy-start.7) | copy-done | bytes 131096
  2.5 0.7 copy-done.8
  3.2 0.7 copy-done.12
  3.9 0.7 copy-done.13
  4.5 1.0 %gibbs.1 = (bf16[512,512]{1,0:T(8,128)(2,1)S(1)}, bf16[512,512]{1,0:T(8,128)(2,1)S(1)}, f32[1,512]{1,0:T(1,128)S(1)}) custom-call(bf16[512,128]{1,0:T(8,128)(2,1)S(1)} %copy-done.6, bf16[512,128]{1,0:T(8,128)(2,1)S(1)} %copy-done.7, s32[1,512]{1,0:T(1,128)S(1)} %bitcast.16, s32[1,512]{1,0:T(1,128)S(1)} %bitcast.17, f32[32,32]{1,0:T(8,128)S(1)} %copy-done.8), custom_call_target="tpu_custom_call" | custom-call | tf_op jit(solution)/shard_map/gibbs/pallas_call | solution.py:112
  5.6 2.1 %collective-permute-start = (f32[1,512]{1,0:T(1,128)S(1)}, f32[1,512]{1,0:T(1,128)S(1)}, u32[]{:S(2)}, u32[]{:S(2)}) collective-permute-start(f32[1,512]{1,0:T(1,128)S(1)} %get-tuple-element.45.after_ref), channel_id=1, source_target_pairs={{0,1},{1,0},{2,3},{3,2},{4,5},{5,4},{6,7},{7,6},{8,9},{9,8},{10,11... | collective-permute-start | bytes 6152 | tf_op jit(solution)/shard_map/ppermute | solution.py:235
  7.7 0.8 %dynamic-slice_bitcast_fusion.f_ref = f32[64,128]{1,0:T(8,128)S(1)} fusion(f32[4,64,128]{2,1,0:T(8,128)} %constant.13.clone, s32[]{:T(128)S(6)} %select_n.4), kind=kLoop, calls=%fused_computation.1 | loop fusion | bytes 65540 | tf_op jit(solution)/shard_map/jit(dynamic_index_in_dim)/squeeze | solution.py:274
  8.5 0.9 %copy-done = s32[512,128]{1,0:T(8,128)S(1)} copy-done((s32[512,128]{1,0:T(8,128)S(1)}, s32[512,128]{1,0:T(8,128)}, u32[]{:S(2)}) %copy-start) | copy-done | bytes 262168
  9.4 0.9 %copy-done.2 = s32[512,128]{1,0:T(8,128)S(1)} copy-done((s32[512,128]{1,0:T(8,128)S(1)}, s32[512,128]{1,0:T(8,128)}, u32[]{:S(2)}) %copy-start.2) | copy-done | bytes 262168
  10.4 0.9 %copy-done.4 = f32[512,128]{1,0:T(8,128)S(1)} copy-done((f32[512,128]{1,0:T(8,128)S(1)}, f32[512,128]{1,0:T(8,128)}, u32[]{:S(2)}) %copy-start.4) | copy-done | bytes 262168
  11.3 2.5 %tables.12 = (bf16[64,48,128]{2,1,0:T(8,128)(2,1)S(1)}, bf16[64,48,128]{2,1,0:T(8,128)(2,1)S(1)}, f32[8,128]{1,0:T(8,128)}) custom-call(f32[64,128]{1,0:T(8,128)S(1)} %dynamic-slice_bitcast_fusion.f_ref, s32[512,128]{1,0:T(8,128)S(1)} %copy-done, s32[512,128]{1,0:T(8,128)S(1)} %copy-done.2, f32[512,128]{1,0:T(8,128)S(1)} %copy-done.4, ...), custom_call_target="tpu_custom_call" | custom-call | flops 201326592 | bytes 4800000 | tf_op jit(solution)/shard_map/tables/pallas_call | solution.py:177
  13.8 0.0 collective-permute-done
  13.8 3.4 %collective-permute-start.3 = (f32[1,512]{1,0:T(1,128)S(1)}, f32[1,512]{1,0:T(1,128)S(1)}, u32[]{:S(2)}, u32[]{:S(2)}) collective-permute-start(f32[1,512]{1,0:T(1,128)S(1)} %add.19.after_ref.refs_0_), channel_id=1, source_target_pairs={{0,6},{1,7},{2,0},{3,1},{4,2},{5,3},{6,4},{7,5},{8,14},{9,15},{10,... | collective-permute-start | bytes 6152 | tf_op jit(solution)/shard_map/ppermute | solution.py:240
  17.2 0.0 collective-permute-start.2
  17.2 0.4 collective-permute-start.1
  17.6 0.9 %copy-done.1 = s32[512,128]{1,0:T(8,128)S(1)} copy-done((s32[512,128]{1,0:T(8,128)S(1)}, s32[512,128]{1,0:T(8,128)}, u32[]{:S(2)}) %copy-start.1) | copy-done | bytes 262168
  18.6 0.9 %copy-done.3 = s32[512,128]{1,0:T(8,128)S(1)} copy-done((s32[512,128]{1,0:T(8,128)S(1)}, s32[512,128]{1,0:T(8,128)}, u32[]{:S(2)}) %copy-start.3) | copy-done | bytes 262168
  19.5 0.9 %copy-done.5 = f32[512,128]{1,0:T(8,128)S(1)} copy-done((f32[512,128]{1,0:T(8,128)S(1)}, f32[512,128]{1,0:T(8,128)}, u32[]{:S(2)}) %copy-start.5) | copy-done | bytes 262168
  20.5 3.1 %tables.8 = (bf16[64,80,128]{2,1,0:T(8,128)(2,1)S(1)}, bf16[64,80,128]{2,1,0:T(8,128)(2,1)S(1)}, f32[8,128]{1,0:T(8,128)S(1)}) custom-call(f32[64,128]{1,0:T(8,128)S(1)} %dynamic-slice_bitcast_fusion.f_ref, s32[512,128]{1,0:T(8,128)S(1)} %copy-done.1, s32[512,128]{1,0:T(8,128)S(1)} %copy-done.3, f32[512,128]{1,0:T(8,128)S(1)} %copy-done.5, ...), custom_call_target="tpu_custom_call" | custom-call | flops 335544320 | bytes 8000000 | tf_op jit(solution)/shard_map/tables/pallas_call | solution.py:177
  23.6 0.0 copy-start.10
  23.6 0.0 collective-permute-done.3.refs_3_
  23.6 0.0 collective-permute-done.2.refs_2_
  23.7 0.7 cols.2
  24.3 1.8 %collective-permute-start.6 = (f32[1,512]{1,0:T(1,128)S(1)}, f32[1,512]{1,0:T(1,128)S(1)}, u32[]{:S(2)}, u32[]{:S(2)}) collective-permute-start(f32[1,512]{1,0:T(1,128)S(1)} %get-tuple-element.48.after_ref.refs_0_), channel_id=1, source_target_pairs={{0,24},{8,0},{16,8},{24,16},{1,25},{9,1},{17,9},{25,17},{2,26},{10... | collective-permute-start | bytes 6152 | tf_op jit(solution)/shard_map/ppermute | solution.py:240
  26.1 1.2 %collective-permute-start.5 = (f32[1,512]{1,0:T(1,128)S(1)}, f32[1,512]{1,0:T(1,128)S(1)}, u32[]{:S(2)}, u32[]{:S(2)}) collective-permute-start(f32[1,512]{1,0:T(1,128)S(1)} %get-tuple-element.48.after_ref.refs_0_), channel_id=1, source_target_pairs={{0,16},{8,24},{16,0},{24,8},{1,17},{9,25},{17,1},{25,9},{2,18},{10... | collective-permute-start | bytes 6152 | tf_op jit(solution)/shard_map/ppermute | solution.py:240
  27.4 0.4 collective-permute-start.4
  27.8 2.6 %tables.9 = (bf16[64,64,128]{2,1,0:T(8,128)(2,1)S(1)}, bf16[64,64,128]{2,1,0:T(8,128)(2,1)S(1)}, f32[8,128]{1,0:T(8,128)S(1)}) custom-call(f32[64,128]{1,0:T(8,128)S(1)} %dynamic-slice_bitcast_fusion.f_ref, s32[512,128]{1,0:T(8,128)S(1)} %copy-done.1, s32[512,128]{1,0:T(8,128)S(1)} %copy-done.3, f32[512,128]{1,0:T(8,128)S(1)} %copy-done.5, ...), custom_call_target="tpu_custom_call" | custom-call | flops 268435456 | bytes 6400000 | tf_op jit(solution)/shard_map/tables/pallas_call | solution.py:177
  30.3 0.0 collective-permute-done.6.refs_3_
  30.4 0.0 collective-permute-done.4.refs_1_
  30.4 0.7 rows.2
  31.0 0.3 collective-permute-start.7
  31.3 2.5 %tables.13 = (bf16[64,48,128]{2,1,0:T(8,128)(2,1)S(1)}, bf16[64,48,128]{2,1,0:T(8,128)(2,1)S(1)}, f32[8,128]{1,0:T(8,128)}) custom-call(f32[64,128]{1,0:T(8,128)S(1)} %dynamic-slice_bitcast_fusion.f_ref, s32[512,128]{1,0:T(8,128)S(1)} %copy-done.1, s32[512,128]{1,0:T(8,128)S(1)} %copy-done.3, f32[512,128]{1,0:T(8,128)S(1)} %copy-done.5, ...), custom_call_target="tpu_custom_call" | custom-call | flops 201326592 | bytes 4800000 | tf_op jit(solution)/shard_map/tables/pallas_call | solution.py:177
  33.8 2.7 %collective-permute-start.10 = (f32[1,512]{1,0:T(1,128)S(1)}, f32[1,512]{1,0:T(1,128)S(1)}, u32[]{:S(2)}, u32[]{:S(2)}) collective-permute-start(f32[1,512]{1,0:T(1,128)S(1)} %add.21.after_ref.refs_0_), channel_id=1, source_target_pairs={{0,6},{1,7},{2,0},{3,1},{4,2},{5,3},{6,4},{7,5},{8,14},{9,15},{10,... | collective-permute-start | bytes 6152 | tf_op jit(solution)/shard_map/ppermute | solution.py:240
  36.5 0.7 %collective-permute-start.9 = (f32[1,512]{1,0:T(1,128)S(1)}, f32[1,512]{1,0:T(1,128)S(1)}, u32[]{:S(2)}, u32[]{:S(2)}) collective-permute-start(f32[1,512]{1,0:T(1,128)S(1)} %add.21.after_ref.refs_0_), channel_id=1, source_target_pairs={{0,4},{1,5},{2,6},{3,7},{4,0},{5,1},{6,2},{7,3},{8,12},{9,13},{10,... | collective-permute-start | bytes 6152 | tf_op jit(solution)/shard_map/ppermute | solution.py:240
  37.2 0.0 collective-permute-start.8
  37.2 3.1 %tables.10 = (bf16[64,80,128]{2,1,0:T(8,128)(2,1)S(1)}, bf16[64,80,128]{2,1,0:T(8,128)(2,1)S(1)}, f32[8,128]{1,0:T(8,128)S(1)}) custom-call(f32[64,128]{1,0:T(8,128)S(1)} %dynamic-slice_bitcast_fusion.f_ref, s32[512,128]{1,0:T(8,128)S(1)} %copy-done.1, s32[512,128]{1,0:T(8,128)S(1)} %copy-done.3, f32[512,128]{1,0:T(8,128)S(1)} %copy-done.5, ...), custom_call_target="tpu_custom_call" | custom-call | flops 335544320 | bytes 8000000 | tf_op jit(solution)/shard_map/tables/pallas_call | solution.py:177
  40.3 0.0 collective-permute-done.10.refs_3_
  40.4 1.1 %collective-permute-done.8.refs_1_ = f32[1,512]{1,0:T(1,128)S(1)} collective-permute-done((f32[1,512]{1,0:T(1,128)S(1)}, f32[1,512]{1,0:T(1,128)S(1)}, u32[]{:S(2)}, u32[]{:S(2)}) %collective-permute-start.8) | collective-permute-done | bytes 2080 | tf_op jit(solution)/shard_map/ppermute | solution.py:240
  41.4 0.3 cols.3
  41.7 2.8 %collective-permute-start.13 = (f32[1,512]{1,0:T(1,128)S(1)}, f32[1,512]{1,0:T(1,128)S(1)}, u32[]{:S(2)}, u32[]{:S(2)}) collective-permute-start(f32[1,512]{1,0:T(1,128)S(1)} %get-tuple-element.55.after_ref.refs_0_), channel_id=1, source_target_pairs={{0,24},{8,0},{16,8},{24,16},{1,25},{9,1},{17,9},{25,17},{2,26},{10... | collective-permute-start | bytes 6152 | tf_op jit(solution)/shard_map/ppermute | solution.py:240
  44.5 0.3 collective-permute-start.12
  44.9 1.4 %collective-permute-start.11 = (f32[1,512]{1,0:T(1,128)S(1)}, f32[1,512]{1,0:T(1,128)S(1)}, u32[]{:S(2)}, u32[]{:S(2)}) collective-permute-start(f32[1,512]{1,0:T(1,128)S(1)} %get-tuple-element.55.after_ref.refs_0_), channel_id=1, source_target_pairs={{0,8},{8,16},{16,24},{24,0},{1,9},{9,17},{17,25},{25,1},{2,10},{10... | collective-permute-start | bytes 6152 | tf_op jit(solution)/shard_map/ppermute | solution.py:240
  46.2 2.5 %tables.11 = (bf16[64,64,128]{2,1,0:T(8,128)(2,1)S(1)}, bf16[64,64,128]{2,1,0:T(8,128)(2,1)S(1)}, f32[8,128]{1,0:T(8,128)S(1)}) custom-call(f32[64,128]{1,0:T(8,128)S(1)} %dynamic-slice_bitcast_fusion.f_ref, s32[512,128]{1,0:T(8,128)S(1)} %copy-done.1, s32[512,128]{1,0:T(8,128)S(1)} %copy-done.3, f32[512,128]{1,0:T(8,128)S(1)} %copy-done.5, ...), custom_call_target="tpu_custom_call" | custom-call | flops 268435456 | bytes 6400000 | tf_op jit(solution)/shard_map/tables/pallas_call | solution.py:177
  48.8 0.0 collective-permute-done.13.refs_3_
  48.8 0.0 collective-permute-done.12.refs_2_
  48.8 0.4 rows.3
  49.2 0.0 copy-start.11
  49.2 0.8 %collective-permute-start.14 = (f32[1,512]{1,0:T(1,128)S(1)}, f32[1,512]{1,0:T(1,128)S(1)}, u32[]{:S(2)}, u32[]{:S(2)}) collective-permute-start(f32[1,512]{1,0:T(1,128)S(1)} %get-tuple-element.58.after_ref), channel_id=1, source_target_pairs={{0,1},{1,0},{2,3},{3,2},{4,5},{5,4},{6,7},{7,6},{8,9},{9,8},{10,11... | collective-permute-start | bytes 6152 | tf_op jit(solution)/shard_map/ppermute | solution.py:235
  50.0 2.5 %tables.14 = (bf16[64,48,128]{2,1,0:T(8,128)(2,1)S(1)}, bf16[64,48,128]{2,1,0:T(8,128)(2,1)S(1)}, f32[8,128]{1,0:T(8,128)}) custom-call(f32[64,128]{1,0:T(8,128)S(1)} %dynamic-slice_bitcast_fusion.f_ref, s32[512,128]{1,0:T(8,128)S(1)} %copy-done.1, s32[512,128]{1,0:T(8,128)S(1)} %copy-done.3, f32[512,128]{1,0:T(8,128)S(1)} %copy-done.5, ...), custom_call_target="tpu_custom_call" | custom-call | flops 201326592 | bytes 4800000 | tf_op jit(solution)/shard_map/tables/pallas_call | solution.py:177
  52.4 0.0 collective-permute-done.14
  52.5 1.5 %collective-permute-start.17 = (f32[1,512]{1,0:T(1,128)S(1)}, f32[1,512]{1,0:T(1,128)S(1)}, u32[]{:S(2)}, u32[]{:S(2)}) collective-permute-start(f32[1,512]{1,0:T(1,128)S(1)} %add.22.after_ref.refs_0_), channel_id=1, source_target_pairs={{0,6},{1,7},{2,0},{3,1},{4,2},{5,3},{6,4},{7,5},{8,14},{9,15},{10,... | collective-permute-start | bytes 6152 | tf_op jit(solution)/shard_map/ppermute | solution.py:240
  54.0 0.4 collective-permute-start.15
  54.3 3.1 %tables.15 = (bf16[64,80,128]{2,1,0:T(8,128)(2,1)S(1)}, bf16[64,80,128]{2,1,0:T(8,128)(2,1)S(1)}, f32[8,128]{1,0:T(8,128)S(1)}) custom-call(f32[64,128]{1,0:T(8,128)S(1)} %dynamic-slice_bitcast_fusion.f_ref, s32[512,128]{1,0:T(8,128)S(1)} %copy-done.1, s32[512,128]{1,0:T(8,128)S(1)} %copy-done.3, f32[512,128]{1,0:T(8,128)S(1)} %copy-done.5, ...), custom_call_target="tpu_custom_call" | custom-call | flops 335544320 | bytes 8000000 | tf_op jit(solution)/shard_map/tables/pallas_call | solution.py:177
  57.5 0.7 collective-permute-done.15.refs_1_
  58.2 2.0 %spread.2 = (f32[32,32,128]{2,1,0:T(8,128)S(1)}, f32[1,512]{1,0:T(1,128)}) custom-call(s32[1,512]{1,0:T(1,128)S(1)} %bitcast.14, f32[1,512]{1,0:T(1,128)S(1)} %get-tuple-element.54.u_ref, f32[1,512]{1,0:T(1,128)S(1)} %add.22.after_ref.refs_0_, f32[1,512]{1,0:T(1,128)S(1)} %collective-permute-done.15.refs_1_, f32[1,512]{1,0:T(1,128)S(1)} %collective-permute-done.16.refs_2_, ...), custom_call_target="tpu_custom_call" | custom-call | tf_op jit(solution)/shard_map/spread/pallas_call | solution.py:221
  60.2 1.2 %collective-permute-start.18 = (f32[32,32,128]{2,1,0:T(8,128)S(1)}, f32[32,32,128]{2,1,0:T(8,128)S(1)}, u32[]{:S(2)}, u32[]{:S(2)}) collective-permute-start(f32[32,32,128]{2,1,0:T(8,128)S(1)} %get-tuple-element.80), channel_id=1, source_target_pairs={{0,8},{8,0},{16,24},{24,16},{1,9},{9,1},{17,25},{25,17},{2,10},{10... | collective-permute-start | bytes 1572872 | tf_op jit(solution)/shard_map/ppermute | solution.py:235
  61.4 2.0 %spread.3 = (f32[32,32,128]{2,1,0:T(8,128)S(1)}, f32[1,512]{1,0:T(1,128)}) custom-call(s32[1,512]{1,0:T(1,128)S(1)} %bitcast.15, f32[1,512]{1,0:T(1,128)S(1)} %get-tuple-element.54.u_ref, f32[1,512]{1,0:T(1,128)S(1)} %add.22.after_ref.refs_0_, f32[1,512]{1,0:T(1,128)S(1)} %collective-permute-done.15.refs_1_, f32[1,512]{1,0:T(1,128)S(1)} %collective-permute-done.16.refs_2_, ...), custom_call_target="tpu_custom_call" | custom-call | tf_op jit(solution)/shard_map/spread/pallas_call | solution.py:221
  63.4 0.0 collective-permute-done.18
  63.4 0.1 add.23
  63.5 1.2 %collective-permute-start.19 = (f32[16,32,128]{2,1,0:T(8,128)S(1)}, f32[16,32,128]{2,1,0:T(8,128)S(1)}, u32[]{:S(2)}, u32[]{:S(2)}) collective-permute-start(f32[16,32,128]{2,1,0:T(8,128)S(1)} %slice.9), channel_id=1, source_target_pairs={{0,16},{8,24},{16,0},{24,8},{1,17},{9,25},{17,1},{25,9},{2,18},{10... | collective-permute-start | bytes 786440 | tf_op jit(solution)/shard_map/ppermute | solution.py:240
  64.7 0.6 copy.15
  65.3 6.3 %collective-permute-done.19 = f32[16,32,128]{2,1,0:T(8,128)S(1)} collective-permute-done((f32[16,32,128]{2,1,0:T(8,128)S(1)}, f32[16,32,128]{2,1,0:T(8,128)S(1)}, u32[]{:S(2)}, u32[]{:S(2)}) %collective-permute-start.19) | collective-permute-done | bytes 262176 | tf_op jit(solution)/shard_map/ppermute | solution.py:240
  71.5 0.7 %slice_add_fusion = f32[16,32,128]{2,1,0:T(8,128)} fusion(f32[16,32,128]{2,1,0:T(8,128)S(1)} %collective-permute-done.19, f32[32,32,128]{2,1,0:T(8,128)S(1)} %add.23), kind=kLoop, calls=%fused_computation | loop fusion | flops 65536 | bytes 786432 | tf_op jit(solution)/shard_map/add | solution.py:319
  (27 shorter events, 0.1 us)
Async XLA Ops:
  0.6 23.0 %copy-start.9 = (f32[512]{0:T(512)S(1)}, f32[512]{0:T(512)}, u32[]{:S(2)}) copy-start(f32[512]{0:T(512)} %param.17) | copy-start | bytes 6148
  0.6 0.9 %copy-start.6 = (bf16[512,128]{1,0:T(8,128)(2,1)S(1)}, bf16[512,128]{1,0:T(8,128)(2,1)}, u32[]{:S(2)}) copy-start(bf16[512,128]{1,0:T(8,128)(2,1)} %x_ref.1) | copy-start | bytes 393220
  1.6 0.9 %copy-start.7 = (bf16[512,128]{1,0:T(8,128)(2,1)S(1)}, bf16[512,128]{1,0:T(8,128)(2,1)}, u32[]{:S(2)}) copy-start(bf16[512,128]{1,0:T(8,128)(2,1)} %y_ref.1) | copy-start | bytes 393220
  2.5 0.7 copy-start.8
  3.2 0.7 copy-start.12
  3.9 0.7 copy-start.13
  5.6 8.2 %collective-permute-start = (f32[1,512]{1,0:T(1,128)S(1)}, f32[1,512]{1,0:T(1,128)S(1)}, u32[]{:S(2)}, u32[]{:S(2)}) collective-permute-start(f32[1,512]{1,0:T(1,128)S(1)} %get-tuple-element.45.after_ref), channel_id=1, source_target_pairs={{0,1},{1,0},{2,3},{3,2},{4,5},{5,4},{6,7},{7,6},{8,9},{9,8},{10,11... | collective-permute-start | bytes 6152 | tf_op jit(solution)/shard_map/ppermute | solution.py:235
  8.5 0.9 %copy-start = (s32[512,128]{1,0:T(8,128)S(1)}, s32[512,128]{1,0:T(8,128)}, u32[]{:S(2)}) copy-start(s32[512,128]{1,0:T(8,128)} %m_ref.15) | copy-start | bytes 786436
  9.4 0.9 %copy-start.2 = (s32[512,128]{1,0:T(8,128)S(1)}, s32[512,128]{1,0:T(8,128)}, u32[]{:S(2)}) copy-start(s32[512,128]{1,0:T(8,128)} %d_ref.15) | copy-start | bytes 786436
  10.4 0.9 %copy-start.4 = (f32[512,128]{1,0:T(8,128)S(1)}, f32[512,128]{1,0:T(8,128)}, u32[]{:S(2)}) copy-start(f32[512,128]{1,0:T(8,128)} %a_ref.15) | copy-start | bytes 786436
  13.8 9.8 %collective-permute-start.3 = (f32[1,512]{1,0:T(1,128)S(1)}, f32[1,512]{1,0:T(1,128)S(1)}, u32[]{:S(2)}, u32[]{:S(2)}) collective-permute-start(f32[1,512]{1,0:T(1,128)S(1)} %add.19.after_ref.refs_0_), channel_id=1, source_target_pairs={{0,6},{1,7},{2,0},{3,1},{4,2},{5,3},{6,4},{7,5},{8,14},{9,15},{10,... | collective-permute-start | bytes 6152 | tf_op jit(solution)/shard_map/ppermute | solution.py:240
  17.2 6.5 %collective-permute-start.2 = (f32[1,512]{1,0:T(1,128)S(1)}, f32[1,512]{1,0:T(1,128)S(1)}, u32[]{:S(2)}, u32[]{:S(2)}) collective-permute-start(f32[1,512]{1,0:T(1,128)S(1)} %add.19.after_ref.refs_0_), channel_id=1, source_target_pairs={{0,4},{1,5},{2,6},{3,7},{4,0},{5,1},{6,2},{7,3},{8,12},{9,13},{10,... | collective-permute-start | bytes 6152 | tf_op jit(solution)/shard_map/ppermute | solution.py:240
  17.2 6.5 %collective-permute-start.1 = (f32[1,512]{1,0:T(1,128)S(1)}, f32[1,512]{1,0:T(1,128)S(1)}, u32[]{:S(2)}, u32[]{:S(2)}) collective-permute-start(f32[1,512]{1,0:T(1,128)S(1)} %add.19.after_ref.refs_0_), channel_id=1, source_target_pairs={{0,2},{1,3},{2,4},{3,5},{4,6},{5,7},{6,0},{7,1},{8,10},{9,11},{10,... | collective-permute-start | bytes 6152 | tf_op jit(solution)/shard_map/ppermute | solution.py:240
  17.6 0.9 %copy-start.1 = (s32[512,128]{1,0:T(8,128)S(1)}, s32[512,128]{1,0:T(8,128)}, u32[]{:S(2)}) copy-start(s32[512,128]{1,0:T(8,128)} %m_ref.15) | copy-start | bytes 786436
  18.6 0.9 %copy-start.3 = (s32[512,128]{1,0:T(8,128)S(1)}, s32[512,128]{1,0:T(8,128)}, u32[]{:S(2)}) copy-start(s32[512,128]{1,0:T(8,128)} %d_ref.15) | copy-start | bytes 786436
  19.5 0.9 %copy-start.5 = (f32[512,128]{1,0:T(8,128)S(1)}, f32[512,128]{1,0:T(8,128)}, u32[]{:S(2)}) copy-start(f32[512,128]{1,0:T(8,128)} %a_ref.15) | copy-start | bytes 786436
  23.6 6.8 %copy-start.10 = (f32[512]{0:T(512)S(1)}, f32[512]{0:T(512)}, u32[]{:S(2)}) copy-start(f32[512]{0:T(512)} %param.18) | copy-start | bytes 6148
  24.3 6.0 %collective-permute-start.6 = (f32[1,512]{1,0:T(1,128)S(1)}, f32[1,512]{1,0:T(1,128)S(1)}, u32[]{:S(2)}, u32[]{:S(2)}) collective-permute-start(f32[1,512]{1,0:T(1,128)S(1)} %get-tuple-element.48.after_ref.refs_0_), channel_id=1, source_target_pairs={{0,24},{8,0},{16,8},{24,16},{1,25},{9,1},{17,9},{25,17},{2,26},{10... | collective-permute-start | bytes 6152 | tf_op jit(solution)/shard_map/ppermute | solution.py:240
  26.1 4.2 %collective-permute-start.5 = (f32[1,512]{1,0:T(1,128)S(1)}, f32[1,512]{1,0:T(1,128)S(1)}, u32[]{:S(2)}, u32[]{:S(2)}) collective-permute-start(f32[1,512]{1,0:T(1,128)S(1)} %get-tuple-element.48.after_ref.refs_0_), channel_id=1, source_target_pairs={{0,16},{8,24},{16,0},{24,8},{1,17},{9,25},{17,1},{25,9},{2,18},{10... | collective-permute-start | bytes 6152 | tf_op jit(solution)/shard_map/ppermute | solution.py:240
  27.4 3.0 %collective-permute-start.4 = (f32[1,512]{1,0:T(1,128)S(1)}, f32[1,512]{1,0:T(1,128)S(1)}, u32[]{:S(2)}, u32[]{:S(2)}) collective-permute-start(f32[1,512]{1,0:T(1,128)S(1)} %get-tuple-element.48.after_ref.refs_0_), channel_id=1, source_target_pairs={{0,8},{8,16},{16,24},{24,0},{1,9},{9,17},{17,25},{25,1},{2,10},{10... | collective-permute-start | bytes 6152 | tf_op jit(solution)/shard_map/ppermute | solution.py:240
  31.0 2.7 %collective-permute-start.7 = (f32[1,512]{1,0:T(1,128)S(1)}, f32[1,512]{1,0:T(1,128)S(1)}, u32[]{:S(2)}, u32[]{:S(2)}) collective-permute-start(f32[1,512]{1,0:T(1,128)S(1)} %get-tuple-element.51.after_ref), channel_id=1, source_target_pairs={{0,1},{1,0},{2,3},{3,2},{4,5},{5,4},{6,7},{7,6},{8,9},{9,8},{10,11... | collective-permute-start | bytes 6152 | tf_op jit(solution)/shard_map/ppermute | solution.py:235
  33.8 6.6 %collective-permute-start.10 = (f32[1,512]{1,0:T(1,128)S(1)}, f32[1,512]{1,0:T(1,128)S(1)}, u32[]{:S(2)}, u32[]{:S(2)}) collective-permute-start(f32[1,512]{1,0:T(1,128)S(1)} %add.21.after_ref.refs_0_), channel_id=1, source_target_pairs={{0,6},{1,7},{2,0},{3,1},{4,2},{5,3},{6,4},{7,5},{8,14},{9,15},{10,... | collective-permute-start | bytes 6152 | tf_op jit(solution)/shard_map/ppermute | solution.py:240
  36.5 3.9 %collective-permute-start.9 = (f32[1,512]{1,0:T(1,128)S(1)}, f32[1,512]{1,0:T(1,128)S(1)}, u32[]{:S(2)}, u32[]{:S(2)}) collective-permute-start(f32[1,512]{1,0:T(1,128)S(1)} %add.21.after_ref.refs_0_), channel_id=1, source_target_pairs={{0,4},{1,5},{2,6},{3,7},{4,0},{5,1},{6,2},{7,3},{8,12},{9,13},{10,... | collective-permute-start | bytes 6152 | tf_op jit(solution)/shard_map/ppermute | solution.py:240
  37.2 4.2 %collective-permute-start.8 = (f32[1,512]{1,0:T(1,128)S(1)}, f32[1,512]{1,0:T(1,128)S(1)}, u32[]{:S(2)}, u32[]{:S(2)}) collective-permute-start(f32[1,512]{1,0:T(1,128)S(1)} %add.21.after_ref.refs_0_), channel_id=1, source_target_pairs={{0,2},{1,3},{2,4},{3,5},{4,6},{5,7},{6,0},{7,1},{8,10},{9,11},{10,... | collective-permute-start | bytes 6152 | tf_op jit(solution)/shard_map/ppermute | solution.py:240
  41.7 7.1 %collective-permute-start.13 = (f32[1,512]{1,0:T(1,128)S(1)}, f32[1,512]{1,0:T(1,128)S(1)}, u32[]{:S(2)}, u32[]{:S(2)}) collective-permute-start(f32[1,512]{1,0:T(1,128)S(1)} %get-tuple-element.55.after_ref.refs_0_), channel_id=1, source_target_pairs={{0,24},{8,0},{16,8},{24,16},{1,25},{9,1},{17,9},{25,17},{2,26},{10... | collective-permute-start | bytes 6152 | tf_op jit(solution)/shard_map/ppermute | solution.py:240
  44.5 4.3 %collective-permute-start.12 = (f32[1,512]{1,0:T(1,128)S(1)}, f32[1,512]{1,0:T(1,128)S(1)}, u32[]{:S(2)}, u32[]{:S(2)}) collective-permute-start(f32[1,512]{1,0:T(1,128)S(1)} %get-tuple-element.55.after_ref.refs_0_), channel_id=1, source_target_pairs={{0,16},{8,24},{16,0},{24,8},{1,17},{9,25},{17,1},{25,9},{2,18},{10... | collective-permute-start | bytes 6152 | tf_op jit(solution)/shard_map/ppermute | solution.py:240
  44.9 3.9 %collective-permute-start.11 = (f32[1,512]{1,0:T(1,128)S(1)}, f32[1,512]{1,0:T(1,128)S(1)}, u32[]{:S(2)}, u32[]{:S(2)}) collective-permute-start(f32[1,512]{1,0:T(1,128)S(1)} %get-tuple-element.55.after_ref.refs_0_), channel_id=1, source_target_pairs={{0,8},{8,16},{16,24},{24,0},{1,9},{9,17},{17,25},{25,1},{2,10},{10... | collective-permute-start | bytes 6152 | tf_op jit(solution)/shard_map/ppermute | solution.py:240
  49.2 9.0 %copy-start.11 = (s32[512]{0:T(512)S(1)}, s32[512]{0:T(512)}, u32[]{:S(2)}) copy-start(s32[512]{0:T(512)} %param.19) | copy-start | bytes 6148
  49.2 3.2 %collective-permute-start.14 = (f32[1,512]{1,0:T(1,128)S(1)}, f32[1,512]{1,0:T(1,128)S(1)}, u32[]{:S(2)}, u32[]{:S(2)}) collective-permute-start(f32[1,512]{1,0:T(1,128)S(1)} %get-tuple-element.58.after_ref), channel_id=1, source_target_pairs={{0,1},{1,0},{2,3},{3,2},{4,5},{5,4},{6,7},{7,6},{8,9},{9,8},{10,11... | collective-permute-start | bytes 6152 | tf_op jit(solution)/shard_map/ppermute | solution.py:235
  52.5 5.0 %collective-permute-start.17 = (f32[1,512]{1,0:T(1,128)S(1)}, f32[1,512]{1,0:T(1,128)S(1)}, u32[]{:S(2)}, u32[]{:S(2)}) collective-permute-start(f32[1,512]{1,0:T(1,128)S(1)} %add.22.after_ref.refs_0_), channel_id=1, source_target_pairs={{0,6},{1,7},{2,0},{3,1},{4,2},{5,3},{6,4},{7,5},{8,14},{9,15},{10,... | collective-permute-start | bytes 6152 | tf_op jit(solution)/shard_map/ppermute | solution.py:240
  54.0 3.5 %collective-permute-start.16 = (f32[1,512]{1,0:T(1,128)S(1)}, f32[1,512]{1,0:T(1,128)S(1)}, u32[]{:S(2)}, u32[]{:S(2)}) collective-permute-start(f32[1,512]{1,0:T(1,128)S(1)} %add.22.after_ref.refs_0_), channel_id=1, source_target_pairs={{0,4},{1,5},{2,6},{3,7},{4,0},{5,1},{6,2},{7,3},{8,12},{9,13},{10,... | collective-permute-start | bytes 6152 | tf_op jit(solution)/shard_map/ppermute | solution.py:240
  54.0 4.2 %collective-permute-start.15 = (f32[1,512]{1,0:T(1,128)S(1)}, f32[1,512]{1,0:T(1,128)S(1)}, u32[]{:S(2)}, u32[]{:S(2)}) collective-permute-start(f32[1,512]{1,0:T(1,128)S(1)} %add.22.after_ref.refs_0_), channel_id=1, source_target_pairs={{0,2},{1,3},{2,4},{3,5},{4,6},{5,7},{6,0},{7,1},{8,10},{9,11},{10,... | collective-permute-start | bytes 6152 | tf_op jit(solution)/shard_map/ppermute | solution.py:240
  60.2 3.2 %collective-permute-start.18 = (f32[32,32,128]{2,1,0:T(8,128)S(1)}, f32[32,32,128]{2,1,0:T(8,128)S(1)}, u32[]{:S(2)}, u32[]{:S(2)}) collective-permute-start(f32[32,32,128]{2,1,0:T(8,128)S(1)} %get-tuple-element.80), channel_id=1, source_target_pairs={{0,8},{8,0},{16,24},{24,16},{1,9},{9,1},{17,25},{25,17},{2,10},{10... | collective-permute-start | bytes 1572872 | tf_op jit(solution)/shard_map/ppermute | solution.py:235
  63.5 8.0 %collective-permute-start.19 = (f32[16,32,128]{2,1,0:T(8,128)S(1)}, f32[16,32,128]{2,1,0:T(8,128)S(1)}, u32[]{:S(2)}, u32[]{:S(2)}) collective-permute-start(f32[16,32,128]{2,1,0:T(8,128)S(1)} %slice.9), channel_id=1, source_target_pairs={{0,16},{8,24},{16,0},{24,8},{1,17},{9,25},{17,1},{25,9},{2,18},{10... | collective-permute-start | bytes 786440 | tf_op jit(solution)/shard_map/ppermute | solution.py:240

commit v2 on v1

--- a/solution.py
+++ b/solution.py
@@ -15,6 +15,7 @@
 DAYS = 64
 LANES = 128
 GROUP = 16
+UNROLL = 64
 
 half_span = 11
 
@@ -84,7 +85,30 @@
     return jnp.sum(out, axis=0, keepdims=True)
 
 
-def gibbs_body(x_ref, y_ref, rr_ref, cr_ref, pen_ref, khi_ref, klo_ref, r_ref):
+def gibbs_body(x_hbm, y_hbm, rr_hbm, cr_hbm, pen_hbm, f_hbm, m_hbm, d_hbm, a_hbm, *refs):
+    khi_ref, klo_ref, r_ref, f_ref, m_ref, d_ref, a_ref = refs[:7]
+    x_ref, y_ref, rr_ref, cr_ref, pen_ref, sems = refs[7:]
+    me = lax.axis_index("cohort")
+    copies = [
+        pltpu.make_async_copy(src, dst, sems.at[k])
+        for k, (src, dst) in enumerate(
+            (
+                (x_hbm, x_ref),
+                (y_hbm, y_ref),
+                (rr_hbm, rr_ref),
+                (cr_hbm, cr_ref),
+                (pen_hbm, pen_ref),
+                (f_hbm.at[me], f_ref),
+                (m_hbm, m_ref),
+                (d_hbm, d_ref),
+                (a_hbm, a_ref),
+            )
+        )
+    ]
+    for copy in copies:
+        copy.start()
+    for copy in copies[:5]:
+        copy.wait()
     n, m = x_ref.shape[0], y_ref.shape[0]
     regions = pen_ref.shape[0]
     inv_root = 1.0 / math.sqrt(x_ref.shape[1])
@@ -105,18 +129,25 @@
     khi_ref[...] = hi
     klo_ref[...] = lo
     r_ref[...] = rows_of(jnp.ones((1, m), f32), khi_ref, klo_ref)
-
-
-def gibbs_call(x, y, rr, cr, penalty):
+    for copy in copies[5:]:
+        copy.wait()
+
+
+def gibbs_call(x, y, rr, cr, penalty, table, merchants, days, amounts):
     n, m = x.shape[0], y.shape[0]
+    args = (x, y, rr, cr, penalty)
+    records = (merchants, days, amounts)
     return pl.pallas_call(
         gibbs_body,
-        in_specs=[VMEM] * 5,
-        out_specs=[VMEM] * 3,
-        out_shape=[pltpu.VMEM((n, m), bf16), pltpu.VMEM((n, m), bf16), pltpu.VMEM((1, n), f32)],
+        in_specs=[ANY] * 9,
+        out_specs=[VMEM] * 7,
+        out_shape=[pltpu.VMEM((n, m), bf16), pltpu.VMEM((n, m), bf16), pltpu.VMEM((1, n), f32)]
+        + [pltpu.VMEM(table.shape[1:], f32)]
+        + [pltpu.VMEM(r.shape, r.dtype) for r in records],
+        scratch_shapes=[pltpu.VMEM(r.shape, r.dtype) for r in args] + [pltpu.SemaphoreType.DMA((9,))],
         compiler_params=PARAMS,
         name="gibbs",
-    )(x, y, rr, cr, penalty)
+    )(*args, table, *records)
 
 
 def step_body(apply, parts, mass_ref, khi_ref, klo_ref, *refs):
@@ -147,14 +178,16 @@
     merch_iota = lax.broadcasted_iota(jnp.int32, (MERCH_DEV, LANES), 0).astype(f32).astype(bf16)
     one, zero = jnp.ones((MERCH_DEV, LANES), bf16), jnp.zeros((MERCH_DEV, LANES), bf16)
 
+    size = math.gcd(count, UNROLL)
+
     def group(step, carry):
-        start = pl.multiple_of(step * GROUP, GROUP)
-        rows_in = pl.ds(first + start, GROUP)
+        start = pl.multiple_of(step * size, size)
+        rows_in = pl.ds(first + start, size)
         merch = m_ref[rows_in, :].astype(f32).astype(bf16)
         days = d_ref[rows_in, :]
         amounts = a_ref[rows_in, :]
         tables = []
-        for i in range(GROUP):
+        for i in range(size):
             day = jnp.broadcast_to(days[i : i + 1, :], (t_count, LANES))
             coef = jnp.take_along_axis(filt, day, axis=1, mode="promise_in_bounds")
             chi, clo = split2(coef * amounts[i : i + 1, :])
@@ -164,11 +197,11 @@
             )
             tables.append(both[:t_count] + both[t_count:])
         hi, lo = split2(jnp.swapaxes(jnp.stack(tables, 0), 0, 1))
-        hi_ref[:, pl.ds(start, GROUP), :] = hi
-        lo_ref[:, pl.ds(start, GROUP), :] = lo
+        hi_ref[:, pl.ds(start, size), :] = hi
+        lo_ref[:, pl.ds(start, size), :] = lo
         return carry
 
-    lax.fori_loop(0, count // GROUP, group, 0)
+    lax.fori_loop(0, count // size, group, 0)
     tok_ref[...] = jnp.zeros_like(tok_ref)
 
 
@@ -271,7 +304,6 @@
                 dest = ((y + step) % n_y) * 2 + core
                 rows.extend(range(dest * t_dev, (dest + 1) * t_dev))
         table[me, :, :DAYS] = henderson[rows]
-    filt = lax.dynamic_index_in_dim(jnp.asarray(table), lax.axis_index("cohort"), 0, keepdims=False)
 
     windows = 3 * ITERS + 2
     state = {"first": 0, "left": windows}
@@ -290,18 +322,28 @@
 
     def over_cell(partial):
         other = swap(partial, "cell", n_cell, 1)
-        tokens = fill(partial, 3)
+        tokens = fill(partial, 4)
         if tokens:
             partial, other, _ = lax.optimization_barrier((partial, other, tokens[0]))
         partial = partial + other
         others = [shift(partial, "cell", n_cell, 2, k) for k in range(1, n_cell // 2)]
-        return [partial] + others, fill(partial, 5)
+        return [partial] + others, fill(partial, 4)
 
     def over_cohort(partial):
         others = [shift(partial, "cohort", n_cohort, 1, k) for k in range(1, n_cohort)]
         return [partial] + others, fill(partial, 4)
 
-    khi, klo, partial = gibbs_call(cohort_features, cell_features, row(cohort_region), row(cell_region), penalty)
+    khi, klo, partial, filt, spend_merchant, spend_day, spend_amount = gibbs_call(
+        cohort_features,
+        cell_features,
+        row(cohort_region),
+        row(cell_region),
+        penalty,
+        jnp.asarray(table),
+        spend_merchant,
+        spend_day,
+        spend_amount,
+    )
     for _ in range(ITERS):
         partials, tokens = over_cell(partial)
         cohort_scale, partial = step_call(cols_of, "cols", row(cohort_mass), khi, klo, partials, tokens)

time: 73.5 us -> 71.2 us (0.969)
  Pallas kernels: 28.9 us -> 25.4 us
  waiting for transfers between devices: 8.09 us -> 10.4 us
  local copies, waits for them, and re-layouts: 11 us -> 10.2 us
    pallas_call x8, Pallas kernels: 21.9 us -> 17.8 us  [table_call(): pl.pallas_call(functools.partial(table_body, first, count), in_specs=[VME...]
    ppermute x16, waiting for transfers between devices: 8.08 us -> 10.4 us  [shift(): lax.ppermute(x, axis, [(b * pair + r, (b + step) % blocks * pair + r) for...]
    ppermute x16, starting transfers between devices: 18.3 us -> 16.9 us  [shift(): lax.ppermute(x, axis, [(b * pair + r, (b + step) % blocks * pair + r) for...]
    ppermute x4, starting transfers between devices: 4.31 us -> 5.52 us  [swap(): return lax.ppermute(x, axis, [(i, i ^ mask) for i in range(size)])]
    squeeze x1 -> x0, local copies, waits for them, and re-layouts: 0.76 us -> none  [per_device(): lax.dynamic_index_in_dim(jnp.asarray(table), lax.axis_index('cohort'), 0,...]
    unnamed x29 -> x25, local copies, waits for them, and re-layouts: 10.2 us -> 10.2 us
  transfers between devices with their start and end apart: 20 -> 20, of which waited for: 3 -> 6; matrix products, arithmetic and copies ran while one was open for 2% -> 1% of each run, Pallas kernels for 33% -> 28%
where the time goes in v2:
time: 71.2 us; the launch traced here: 70.1 us
  Pallas kernels  25.4 us (36%)
  starting transfers between devices  22.4 us (31%)
  waiting for transfers between devices  10.4 us (15%)
  local copies, waits for them, and re-layouts  10.2 us (14%)
  between operations  0.84 us (1%)
  other arithmetic  0.83 us (1%)
    pallas_call x8, Pallas kernels, table_call(): pl.pallas_call(functools.partial(table_body, first, count), in_specs=[VME...  17.8 us
    ppermute x16, starting transfers between devices, shift(): lax.ppermute(x, axis, [(b * pair + r, (b + step) % blocks * pair + r) for...  16.9 us
    ppermute x16, waiting for transfers between devices, shift(): lax.ppermute(x, axis, [(b * pair + r, (b + step) % blocks * pair + r) for...  10.4 us
    unnamed x25, local copies, waits for them, and re-layouts  10.2 us
    ppermute x4, starting transfers between devices, swap(): return lax.ppermute(x, axis, [(i, i ^ mask) for i in range(size)])  5.52 us
    pallas_call x2, Pallas kernels, spread_call(): pl.pallas_call(functools.partial(spread_body, t_first, t_count, counts, l...  4.01 us
    pallas_call x4, Pallas kernels, step_call(): pl.pallas_call(functools.partial(step_body, apply, len(partials)), in_spe...  1.97 us
    pallas_call x1, Pallas kernels, gibbs_call(): pl.pallas_call(gibbs_body, in_specs=[ANY] * 9, out_specs=[VMEM] * 7, out_...  1.58 us
  transfers between devices with their start and end apart: 20, of which 6 were waited for; matrix products, arithmetic and copies ran while one was open for 1% of the time, Pallas kernels for 28%

profile of v2, /device:TPU:1, one launch (start us, length us, event | category | flops | bytes accessed | tf_op | source)
XLA Modules:
  0.0 70.1 jit_solution(16995645730887019790)
XLA Ops:
  0.6 0.7 copy-done.10
  1.3 0.9 %copy-done = s32[512,128]{1,0:T(8,128)S(1)} copy-done((s32[512,128]{1,0:T(8,128)S(1)}, s32[512,128]{1,0:T(8,128)}, u32[]{:S(2)}) %copy-start) | copy-done | bytes 262168
  2.3 0.9 %copy-done.1 = s32[512,128]{1,0:T(8,128)S(1)} copy-done((s32[512,128]{1,0:T(8,128)S(1)}, s32[512,128]{1,0:T(8,128)}, u32[]{:S(2)}) %copy-start.1) | copy-done | bytes 262168
  3.2 0.9 %copy-done.2 = f32[512,128]{1,0:T(8,128)S(1)} copy-done((f32[512,128]{1,0:T(8,128)S(1)}, f32[512,128]{1,0:T(8,128)}, u32[]{:S(2)}) %copy-start.2) | copy-done | bytes 262168
  4.2 0.9 %copy-done.3 = bf16[512,128]{1,0:T(8,128)(2,1)S(1)} copy-done((bf16[512,128]{1,0:T(8,128)(2,1)S(1)}, bf16[512,128]{1,0:T(8,128)(2,1)}, u32[]{:S(2)}) %copy-start.3) | copy-done | bytes 131096
  5.1 0.9 %copy-done.4 = bf16[512,128]{1,0:T(8,128)(2,1)S(1)} copy-done((bf16[512,128]{1,0:T(8,128)(2,1)S(1)}, bf16[512,128]{1,0:T(8,128)(2,1)}, u32[]{:S(2)}) %copy-start.4) | copy-done | bytes 131096
  6.0 0.9 %copy-done.5 = f32[4,64,128]{2,1,0:T(8,128)S(1)} copy-done((f32[4,64,128]{2,1,0:T(8,128)S(1)}, f32[4,64,128]{2,1,0:T(8,128)}, u32[]{:S(2)}) %copy-start.5) | copy-done | bytes 131096
  6.9 0.7 %copy-done.6 = f32[32,32]{1,0:T(8,128)S(1)} copy-done((f32[32,32]{1,0:T(8,128)S(1)}, f32[32,32]{1,0:T(8,128)}, u32[]{:S(2)}) %copy-start.6) | copy-done | bytes 4120
  7.6 0.7 copy-done.11
  8.3 1.6 %gibbs.1 = (bf16[512,512]{1,0:T(8,128)(2,1)S(1)}, bf16[512,512]{1,0:T(8,128)(2,1)S(1)}, f32[1,512]{1,0:T(1,128)S(1)}, f32[64,128]{1,0:T(8,128)S(1)}, s32[512,128...) custom-call(bf16[512,128]{1,0:T(8,128)(2,1)S(1)} %copy-done.3, bf16[512,128]{1,0:T(8,128)(2,1)S(1)} %copy-done.4, ...), custom_call_target="tpu_custom_call" | custom-call | tf_op jit(solution)/shard_map/gibbs/pallas_call | solution.py:140
  9.9 2.1 %collective-permute-start = (f32[1,512]{1,0:T(1,128)S(1)}, f32[1,512]{1,0:T(1,128)S(1)}, u32[]{:S(2)}, u32[]{:S(2)}) collective-permute-start(f32[1,512]{1,0:T(1,128)S(1)} %get-tuple-element.49.after_ref), channel_id=1, source_target_pairs={{0,1},{1,0},{2,3},{3,2},{4,5},{5,4},{6,7},{7,6},{8,9},{9,8},{10,11... | collective-permute-start | bytes 6152 | tf_op jit(solution)/shard_map/ppermute | solution.py:268
  12.0 2.6 %tables.12 = (bf16[64,64,128]{2,1,0:T(8,128)(2,1)S(1)}, bf16[64,64,128]{2,1,0:T(8,128)(2,1)S(1)}, f32[8,128]{1,0:T(8,128)}) custom-call(f32[64,128]{1,0:T(8,128)S(1)} %get-tuple-element.51.f_ref, s32[512,128]{1,0:T(8,128)S(1)} %get-tuple-element.52.m_ref, s32[512,128]{1,0:T(8,128)S(1)} %get-tuple-element.53.d_ref, f32[512,128]{1,0:T(8,128)S(1)} %get-tuple-element.54.a_ref, ...), custom_call_target="tpu_custom_call" | custom-call | flops 268435456 | bytes 6400000 | tf_op jit(solution)/shard_map/tables/pallas_call | solution.py:210
  14.6 0.0 collective-permute-done
  14.6 3.4 %collective-permute-start.3 = (f32[1,512]{1,0:T(1,128)S(1)}, f32[1,512]{1,0:T(1,128)S(1)}, u32[]{:S(2)}, u32[]{:S(2)}) collective-permute-start(f32[1,512]{1,0:T(1,128)S(1)} %add.15.after_ref.refs_0_), channel_id=1, source_target_pairs={{0,6},{1,7},{2,0},{3,1},{4,2},{5,3},{6,4},{7,5},{8,14},{9,15},{10,... | collective-permute-start | bytes 6152 | tf_op jit(solution)/shard_map/ppermute | solution.py:273
  18.0 0.0 collective-permute-start.2
  18.0 0.4 collective-permute-start.1
  18.4 2.0 %tables.8 = (bf16[64,64,128]{2,1,0:T(8,128)(2,1)S(1)}, bf16[64,64,128]{2,1,0:T(8,128)(2,1)S(1)}, f32[8,128]{1,0:T(8,128)S(1)}) custom-call(f32[64,128]{1,0:T(8,128)S(1)} %get-tuple-element.51.f_ref, s32[512,128]{1,0:T(8,128)S(1)} %get-tuple-element.52.m_ref, s32[512,128]{1,0:T(8,128)S(1)} %get-tuple-element.53.d_ref, ...), custom_call_target="tpu_custom_call" | custom-call | flops 268435456 | bytes 6400000 | tf_op jit(solution)/shard_map/tables/pallas_call | solution.py:210
  20.4 0.0 collective-permute-done.3.refs_3_
  20.4 0.9 %collective-permute-done.2.refs_2_ = f32[1,512]{1,0:T(1,128)S(1)} collective-permute-done((f32[1,512]{1,0:T(1,128)S(1)}, f32[1,512]{1,0:T(1,128)S(1)}, u32[]{:S(2)}, u32[]{:S(2)}) %collective-permute-start.2) | collective-permute-done | bytes 2080 | tf_op jit(solution)/shard_map/ppermute | solution.py:273
  21.3 0.9 %collective-permute-done.1.refs_1_ = f32[1,512]{1,0:T(1,128)S(1)} collective-permute-done((f32[1,512]{1,0:T(1,128)S(1)}, f32[1,512]{1,0:T(1,128)S(1)}, u32[]{:S(2)}, u32[]{:S(2)}) %collective-permute-start.1) | collective-permute-done | bytes 2080 | tf_op jit(solution)/shard_map/ppermute | solution.py:273
  22.2 0.7 copy-done.7
  22.9 0.7 cols.2
  23.6 2.4 %collective-permute-start.6 = (f32[1,512]{1,0:T(1,128)S(1)}, f32[1,512]{1,0:T(1,128)S(1)}, u32[]{:S(2)}, u32[]{:S(2)}) collective-permute-start(f32[1,512]{1,0:T(1,128)S(1)} %get-tuple-element.56.after_ref.refs_0_), channel_id=1, source_target_pairs={{0,24},{8,0},{16,8},{24,16},{1,25},{9,1},{17,9},{25,17},{2,26},{10... | collective-permute-start | bytes 6152 | tf_op jit(solution)/shard_map/ppermute | solution.py:273
  25.9 1.2 %collective-permute-start.5 = (f32[1,512]{1,0:T(1,128)S(1)}, f32[1,512]{1,0:T(1,128)S(1)}, u32[]{:S(2)}, u32[]{:S(2)}) collective-permute-start(f32[1,512]{1,0:T(1,128)S(1)} %get-tuple-element.56.after_ref.refs_0_), channel_id=1, source_target_pairs={{0,16},{8,24},{16,0},{24,8},{1,17},{9,25},{17,1},{25,9},{2,18},{10... | collective-permute-start | bytes 6152 | tf_op jit(solution)/shard_map/ppermute | solution.py:273
  27.2 0.4 collective-permute-start.4
  27.6 2.0 %tables.9 = (bf16[64,64,128]{2,1,0:T(8,128)(2,1)S(1)}, bf16[64,64,128]{2,1,0:T(8,128)(2,1)S(1)}, f32[8,128]{1,0:T(8,128)S(1)}) custom-call(f32[64,128]{1,0:T(8,128)S(1)} %get-tuple-element.51.f_ref, s32[512,128]{1,0:T(8,128)S(1)} %get-tuple-element.52.m_ref, s32[512,128]{1,0:T(8,128)S(1)} %get-tuple-element.53.d_ref, ...), custom_call_target="tpu_custom_call" | custom-call | flops 268435456 | bytes 6400000 | tf_op jit(solution)/shard_map/tables/pallas_call | solution.py:210
  29.6 0.0 copy-start.8
  29.6 0.0 collective-permute-done.6.refs_3_
  29.6 0.0 collective-permute-done.5.refs_2_
  29.6 0.6 copy-done.8
  30.3 0.7 rows.2
  30.9 0.6 collective-permute-start.7
  31.6 2.6 %tables.13 = (bf16[64,64,128]{2,1,0:T(8,128)(2,1)S(1)}, bf16[64,64,128]{2,1,0:T(8,128)(2,1)S(1)}, f32[8,128]{1,0:T(8,128)}) custom-call(f32[64,128]{1,0:T(8,128)S(1)} %get-tuple-element.51.f_ref, s32[512,128]{1,0:T(8,128)S(1)} %get-tuple-element.52.m_ref, s32[512,128]{1,0:T(8,128)S(1)} %get-tuple-element.53.d_ref, f32[512,128]{1,0:T(8,128)S(1)} %get-tuple-element.54.a_ref, ...), custom_call_target="tpu_custom_call" | custom-call | flops 268435456 | bytes 6400000 | tf_op jit(solution)/shard_map/tables/pallas_call | solution.py:210
  34.2 0.3 collective-permute-start.10
  34.5 0.8 %collective-permute-start.9 = (f32[1,512]{1,0:T(1,128)S(1)}, f32[1,512]{1,0:T(1,128)S(1)}, u32[]{:S(2)}, u32[]{:S(2)}) collective-permute-start(f32[1,512]{1,0:T(1,128)S(1)} %add.16.after_ref.refs_0_), channel_id=1, source_target_pairs={{0,4},{1,5},{2,6},{3,7},{4,0},{5,1},{6,2},{7,3},{8,12},{9,13},{10,... | collective-permute-start | bytes 6152 | tf_op jit(solution)/shard_map/ppermute | solution.py:273
  35.3 1.2 %collective-permute-start.8 = (f32[1,512]{1,0:T(1,128)S(1)}, f32[1,512]{1,0:T(1,128)S(1)}, u32[]{:S(2)}, u32[]{:S(2)}) collective-permute-start(f32[1,512]{1,0:T(1,128)S(1)} %add.16.after_ref.refs_0_), channel_id=1, source_target_pairs={{0,2},{1,3},{2,4},{3,5},{4,6},{5,7},{6,0},{7,1},{8,10},{9,11},{10,... | collective-permute-start | bytes 6152 | tf_op jit(solution)/shard_map/ppermute | solution.py:273
  36.6 2.0 %tables.10 = (bf16[64,64,128]{2,1,0:T(8,128)(2,1)S(1)}, bf16[64,64,128]{2,1,0:T(8,128)(2,1)S(1)}, f32[8,128]{1,0:T(8,128)S(1)}) custom-call(f32[64,128]{1,0:T(8,128)S(1)} %get-tuple-element.51.f_ref, s32[512,128]{1,0:T(8,128)S(1)} %get-tuple-element.52.m_ref, s32[512,128]{1,0:T(8,128)S(1)} %get-tuple-element.53.d_ref, ...), custom_call_target="tpu_custom_call" | custom-call | flops 268435456 | bytes 6400000 | tf_op jit(solution)/shard_map/tables/pallas_call | solution.py:210
  38.5 0.0 collective-permute-done.9.refs_2_
  38.6 1.0 %collective-permute-done.8.refs_1_ = f32[1,512]{1,0:T(1,128)S(1)} collective-permute-done((f32[1,512]{1,0:T(1,128)S(1)}, f32[1,512]{1,0:T(1,128)S(1)}, u32[]{:S(2)}, u32[]{:S(2)}) %collective-permute-start.8) | collective-permute-done | bytes 2080 | tf_op jit(solution)/shard_map/ppermute | solution.py:273
  39.5 0.3 cols.3
  39.8 2.2 %collective-permute-start.13 = (f32[1,512]{1,0:T(1,128)S(1)}, f32[1,512]{1,0:T(1,128)S(1)}, u32[]{:S(2)}, u32[]{:S(2)}) collective-permute-start(f32[1,512]{1,0:T(1,128)S(1)} %get-tuple-element.63.after_ref.refs_0_), channel_id=1, source_target_pairs={{0,24},{8,0},{16,8},{24,16},{1,25},{9,1},{17,9},{25,17},{2,26},{10... | collective-permute-start | bytes 6152 | tf_op jit(solution)/shard_map/ppermute | solution.py:273
  42.0 0.3 collective-permute-start.12
  42.4 1.4 %collective-permute-start.11 = (f32[1,512]{1,0:T(1,128)S(1)}, f32[1,512]{1,0:T(1,128)S(1)}, u32[]{:S(2)}, u32[]{:S(2)}) collective-permute-start(f32[1,512]{1,0:T(1,128)S(1)} %get-tuple-element.63.after_ref.refs_0_), channel_id=1, source_target_pairs={{0,8},{8,16},{16,24},{24,0},{1,9},{9,17},{17,25},{25,1},{2,10},{10... | collective-permute-start | bytes 6152 | tf_op jit(solution)/shard_map/ppermute | solution.py:273
  43.8 2.0 %tables.11 = (bf16[64,64,128]{2,1,0:T(8,128)(2,1)S(1)}, bf16[64,64,128]{2,1,0:T(8,128)(2,1)S(1)}, f32[8,128]{1,0:T(8,128)S(1)}) custom-call(f32[64,128]{1,0:T(8,128)S(1)} %get-tuple-element.51.f_ref, s32[512,128]{1,0:T(8,128)S(1)} %get-tuple-element.52.m_ref, s32[512,128]{1,0:T(8,128)S(1)} %get-tuple-element.53.d_ref, ...), custom_call_target="tpu_custom_call" | custom-call | flops 268435456 | bytes 6400000 | tf_op jit(solution)/shard_map/tables/pallas_call | solution.py:210
  45.7 0.0 collective-permute-done.12.refs_2_
  45.7 0.0 collective-permute-done.11.refs_1_
  45.8 0.4 rows.3
  46.2 0.9 %collective-permute-start.14 = (f32[1,512]{1,0:T(1,128)S(1)}, f32[1,512]{1,0:T(1,128)S(1)}, u32[]{:S(2)}, u32[]{:S(2)}) collective-permute-start(f32[1,512]{1,0:T(1,128)S(1)} %get-tuple-element.66.after_ref), channel_id=1, source_target_pairs={{0,1},{1,0},{2,3},{3,2},{4,5},{5,4},{6,7},{7,6},{8,9},{9,8},{10,11... | collective-permute-start | bytes 6152 | tf_op jit(solution)/shard_map/ppermute | solution.py:268
  47.0 2.6 %tables.14 = (bf16[64,64,128]{2,1,0:T(8,128)(2,1)S(1)}, bf16[64,64,128]{2,1,0:T(8,128)(2,1)S(1)}, f32[8,128]{1,0:T(8,128)}) custom-call(f32[64,128]{1,0:T(8,128)S(1)} %get-tuple-element.51.f_ref, s32[512,128]{1,0:T(8,128)S(1)} %get-tuple-element.52.m_ref, s32[512,128]{1,0:T(8,128)S(1)} %get-tuple-element.53.d_ref, f32[512,128]{1,0:T(8,128)S(1)} %get-tuple-element.54.a_ref, ...), custom_call_target="tpu_custom_call" | custom-call | flops 268435456 | bytes 6400000 | tf_op jit(solution)/shard_map/tables/pallas_call | solution.py:210
  49.7 0.7 %collective-permute-start.17 = (f32[1,512]{1,0:T(1,128)S(1)}, f32[1,512]{1,0:T(1,128)S(1)}, u32[]{:S(2)}, u32[]{:S(2)}) collective-permute-start(f32[1,512]{1,0:T(1,128)S(1)} %add.17.after_ref.refs_0_), channel_id=1, source_target_pairs={{0,6},{1,7},{2,0},{3,1},{4,2},{5,3},{6,4},{7,5},{8,14},{9,15},{10,... | collective-permute-start | bytes 6152 | tf_op jit(solution)/shard_map/ppermute | solution.py:273
  50.4 0.8 %collective-permute-start.15 = (f32[1,512]{1,0:T(1,128)S(1)}, f32[1,512]{1,0:T(1,128)S(1)}, u32[]{:S(2)}, u32[]{:S(2)}) collective-permute-start(f32[1,512]{1,0:T(1,128)S(1)} %add.17.after_ref.refs_0_), channel_id=1, source_target_pairs={{0,2},{1,3},{2,4},{3,5},{4,6},{5,7},{6,0},{7,1},{8,10},{9,11},{10,... | collective-permute-start | bytes 6152 | tf_op jit(solution)/shard_map/ppermute | solution.py:273
  51.2 2.0 %tables.15 = (bf16[64,64,128]{2,1,0:T(8,128)(2,1)S(1)}, bf16[64,64,128]{2,1,0:T(8,128)(2,1)S(1)}, f32[8,128]{1,0:T(8,128)S(1)}) custom-call(f32[64,128]{1,0:T(8,128)S(1)} %get-tuple-element.51.f_ref, s32[512,128]{1,0:T(8,128)S(1)} %get-tuple-element.52.m_ref, s32[512,128]{1,0:T(8,128)S(1)} %get-tuple-element.53.d_ref, ...), custom_call_target="tpu_custom_call" | custom-call | flops 268435456 | bytes 6400000 | tf_op jit(solution)/shard_map/tables/pallas_call | solution.py:210
  53.2 0.0 collective-permute-done.17.refs_3_
  53.2 0.5 collective-permute-done.16.refs_2_
  53.7 0.9 %collective-permute-done.15.refs_1_ = f32[1,512]{1,0:T(1,128)S(1)} collective-permute-done((f32[1,512]{1,0:T(1,128)S(1)}, f32[1,512]{1,0:T(1,128)S(1)}, u32[]{:S(2)}, u32[]{:S(2)}) %collective-permute-start.15) | collective-permute-done | bytes 2080 | tf_op jit(solution)/shard_map/ppermute | solution.py:273
  54.6 0.7 copy-done.9
  55.3 2.0 %spread.2 = (f32[32,32,128]{2,1,0:T(8,128)S(1)}, f32[1,512]{1,0:T(1,128)}) custom-call(s32[1,512]{1,0:T(1,128)S(1)} %bitcast.12, f32[1,512]{1,0:T(1,128)S(1)} %get-tuple-element.62.u_ref, f32[1,512]{1,0:T(1,128)S(1)} %add.17.after_ref.refs_0_, f32[1,512]{1,0:T(1,128)S(1)} %collective-permute-done.15.refs_1_, f32[1,512]{1,0:T(1,128)S(1)} %collective-permute-done.16.refs_2_, ...), custom_call_target="tpu_custom_call" | custom-call | tf_op jit(solution)/shard_map/spread/pallas_call | solution.py:254
  57.3 1.9 %collective-permute-start.18 = (f32[32,32,128]{2,1,0:T(8,128)S(1)}, f32[32,32,128]{2,1,0:T(8,128)S(1)}, u32[]{:S(2)}, u32[]{:S(2)}) collective-permute-start(f32[32,32,128]{2,1,0:T(8,128)S(1)} %get-tuple-element.88), channel_id=1, source_target_pairs={{0,8},{8,0},{16,24},{24,16},{1,9},{9,1},{17,25},{25,17},{2,10},{10... | collective-permute-start | bytes 1572872 | tf_op jit(solution)/shard_map/ppermute | solution.py:268
  59.2 2.0 %spread.3 = (f32[32,32,128]{2,1,0:T(8,128)S(1)}, f32[1,512]{1,0:T(1,128)}) custom-call(s32[1,512]{1,0:T(1,128)S(1)} %bitcast.13, f32[1,512]{1,0:T(1,128)S(1)} %get-tuple-element.62.u_ref, f32[1,512]{1,0:T(1,128)S(1)} %add.17.after_ref.refs_0_, f32[1,512]{1,0:T(1,128)S(1)} %collective-permute-done.15.refs_1_, f32[1,512]{1,0:T(1,128)S(1)} %collective-permute-done.16.refs_2_, ...), custom_call_target="tpu_custom_call" | custom-call | tf_op jit(solution)/shard_map/spread/pallas_call | solution.py:254
  61.2 0.1 add.18
  61.4 1.2 %collective-permute-start.19 = (f32[16,32,128]{2,1,0:T(8,128)S(1)}, f32[16,32,128]{2,1,0:T(8,128)S(1)}, u32[]{:S(2)}, u32[]{:S(2)}) collective-permute-start(f32[16,32,128]{2,1,0:T(8,128)S(1)} %slice.9), channel_id=1, source_target_pairs={{0,16},{8,24},{16,0},{24,8},{1,17},{9,25},{17,1},{25,9},{2,18},{10... | collective-permute-start | bytes 786440 | tf_op jit(solution)/shard_map/ppermute | solution.py:273
  62.6 0.6 copy.15
  63.2 6.2 %collective-permute-done.19 = f32[16,32,128]{2,1,0:T(8,128)S(1)} collective-permute-done((f32[16,32,128]{2,1,0:T(8,128)S(1)}, f32[16,32,128]{2,1,0:T(8,128)S(1)}, u32[]{:S(2)}, u32[]{:S(2)}) %collective-permute-start.19) | collective-permute-done | bytes 262176 | tf_op jit(solution)/shard_map/ppermute | solution.py:273
  69.4 0.7 %slice_add_fusion = f32[16,32,128]{2,1,0:T(8,128)} fusion(f32[16,32,128]{2,1,0:T(8,128)S(1)} %collective-permute-done.19, f32[32,32,128]{2,1,0:T(8,128)S(1)} %add.18), kind=kLoop, calls=%fused_computation | loop fusion | flops 65536 | bytes 786432 | tf_op jit(solution)/shard_map/add | solution.py:361
  (22 shorter events, 0.1 us)
Async XLA Ops:
  0.6 0.7 copy-start.10
  1.3 0.9 %copy-start = (s32[512,128]{1,0:T(8,128)S(1)}, s32[512,128]{1,0:T(8,128)}, u32[]{:S(2)}) copy-start(s32[512,128]{1,0:T(8,128)} %m_hbm.1) | copy-start | bytes 786436
  2.3 0.9 %copy-start.1 = (s32[512,128]{1,0:T(8,128)S(1)}, s32[512,128]{1,0:T(8,128)}, u32[]{:S(2)}) copy-start(s32[512,128]{1,0:T(8,128)} %d_hbm.1) | copy-start | bytes 786436
  3.2 0.9 %copy-start.2 = (f32[512,128]{1,0:T(8,128)S(1)}, f32[512,128]{1,0:T(8,128)}, u32[]{:S(2)}) copy-start(f32[512,128]{1,0:T(8,128)} %a_hbm.1) | copy-start | bytes 786436
  4.2 0.9 %copy-start.3 = (bf16[512,128]{1,0:T(8,128)(2,1)S(1)}, bf16[512,128]{1,0:T(8,128)(2,1)}, u32[]{:S(2)}) copy-start(bf16[512,128]{1,0:T(8,128)(2,1)} %x_hbm.1) | copy-start | bytes 393220
  5.1 0.9 %copy-start.4 = (bf16[512,128]{1,0:T(8,128)(2,1)S(1)}, bf16[512,128]{1,0:T(8,128)(2,1)}, u32[]{:S(2)}) copy-start(bf16[512,128]{1,0:T(8,128)(2,1)} %y_hbm.1) | copy-start | bytes 393220
  6.0 0.9 %copy-start.5 = (f32[4,64,128]{2,1,0:T(8,128)S(1)}, f32[4,64,128]{2,1,0:T(8,128)}, u32[]{:S(2)}) copy-start(f32[4,64,128]{2,1,0:T(8,128)} %constant.2.clone.f_hbm) | copy-start | bytes 393220
  6.9 0.7 %copy-start.6 = (f32[32,32]{1,0:T(8,128)S(1)}, f32[32,32]{1,0:T(8,128)}, u32[]{:S(2)}) copy-start(f32[32,32]{1,0:T(8,128)} %pen_hbm.1) | copy-start | bytes 12292
  7.6 0.7 copy-start.11
  9.9 4.7 %collective-permute-start = (f32[1,512]{1,0:T(1,128)S(1)}, f32[1,512]{1,0:T(1,128)S(1)}, u32[]{:S(2)}, u32[]{:S(2)}) collective-permute-start(f32[1,512]{1,0:T(1,128)S(1)} %get-tuple-element.49.after_ref), channel_id=1, source_target_pairs={{0,1},{1,0},{2,3},{3,2},{4,5},{5,4},{6,7},{7,6},{8,9},{9,8},{10,11... | collective-permute-start | bytes 6152 | tf_op jit(solution)/shard_map/ppermute | solution.py:268
  14.6 5.8 %collective-permute-start.3 = (f32[1,512]{1,0:T(1,128)S(1)}, f32[1,512]{1,0:T(1,128)S(1)}, u32[]{:S(2)}, u32[]{:S(2)}) collective-permute-start(f32[1,512]{1,0:T(1,128)S(1)} %add.15.after_ref.refs_0_), channel_id=1, source_target_pairs={{0,6},{1,7},{2,0},{3,1},{4,2},{5,3},{6,4},{7,5},{8,14},{9,15},{10,... | collective-permute-start | bytes 6152 | tf_op jit(solution)/shard_map/ppermute | solution.py:273
  18.0 3.3 %collective-permute-start.2 = (f32[1,512]{1,0:T(1,128)S(1)}, f32[1,512]{1,0:T(1,128)S(1)}, u32[]{:S(2)}, u32[]{:S(2)}) collective-permute-start(f32[1,512]{1,0:T(1,128)S(1)} %add.15.after_ref.refs_0_), channel_id=1, source_target_pairs={{0,4},{1,5},{2,6},{3,7},{4,0},{5,1},{6,2},{7,3},{8,12},{9,13},{10,... | collective-permute-start | bytes 6152 | tf_op jit(solution)/shard_map/ppermute | solution.py:273
  18.0 4.2 %collective-permute-start.1 = (f32[1,512]{1,0:T(1,128)S(1)}, f32[1,512]{1,0:T(1,128)S(1)}, u32[]{:S(2)}, u32[]{:S(2)}) collective-permute-start(f32[1,512]{1,0:T(1,128)S(1)} %add.15.after_ref.refs_0_), channel_id=1, source_target_pairs={{0,2},{1,3},{2,4},{3,5},{4,6},{5,7},{6,0},{7,1},{8,10},{9,11},{10,... | collective-permute-start | bytes 6152 | tf_op jit(solution)/shard_map/ppermute | solution.py:273
  22.2 0.7 copy-start.7
  23.6 6.1 %collective-permute-start.6 = (f32[1,512]{1,0:T(1,128)S(1)}, f32[1,512]{1,0:T(1,128)S(1)}, u32[]{:S(2)}, u32[]{:S(2)}) collective-permute-start(f32[1,512]{1,0:T(1,128)S(1)} %get-tuple-element.56.after_ref.refs_0_), channel_id=1, source_target_pairs={{0,24},{8,0},{16,8},{24,16},{1,25},{9,1},{17,9},{25,17},{2,26},{10... | collective-permute-start | bytes 6152 | tf_op jit(solution)/shard_map/ppermute | solution.py:273
  25.9 3.7 %collective-permute-start.5 = (f32[1,512]{1,0:T(1,128)S(1)}, f32[1,512]{1,0:T(1,128)S(1)}, u32[]{:S(2)}, u32[]{:S(2)}) collective-permute-start(f32[1,512]{1,0:T(1,128)S(1)} %get-tuple-element.56.after_ref.refs_0_), channel_id=1, source_target_pairs={{0,16},{8,24},{16,0},{24,8},{1,17},{9,25},{17,1},{25,9},{2,18},{10... | collective-permute-start | bytes 6152 | tf_op jit(solution)/shard_map/ppermute | solution.py:273
  27.2 2.5 %collective-permute-start.4 = (f32[1,512]{1,0:T(1,128)S(1)}, f32[1,512]{1,0:T(1,128)S(1)}, u32[]{:S(2)}, u32[]{:S(2)}) collective-permute-start(f32[1,512]{1,0:T(1,128)S(1)} %get-tuple-element.56.after_ref.refs_0_), channel_id=1, source_target_pairs={{0,8},{8,16},{16,24},{24,0},{1,9},{9,17},{17,25},{25,1},{2,10},{10... | collective-permute-start | bytes 6152 | tf_op jit(solution)/shard_map/ppermute | solution.py:273
  29.6 0.7 copy-start.8
  30.9 3.3 %collective-permute-start.7 = (f32[1,512]{1,0:T(1,128)S(1)}, f32[1,512]{1,0:T(1,128)S(1)}, u32[]{:S(2)}, u32[]{:S(2)}) collective-permute-start(f32[1,512]{1,0:T(1,128)S(1)} %get-tuple-element.59.after_ref), channel_id=1, source_target_pairs={{0,1},{1,0},{2,3},{3,2},{4,5},{5,4},{6,7},{7,6},{8,9},{9,8},{10,11... | collective-permute-start | bytes 6152 | tf_op jit(solution)/shard_map/ppermute | solution.py:268
  34.2 4.3 %collective-permute-start.10 = (f32[1,512]{1,0:T(1,128)S(1)}, f32[1,512]{1,0:T(1,128)S(1)}, u32[]{:S(2)}, u32[]{:S(2)}) collective-permute-start(f32[1,512]{1,0:T(1,128)S(1)} %add.16.after_ref.refs_0_), channel_id=1, source_target_pairs={{0,6},{1,7},{2,0},{3,1},{4,2},{5,3},{6,4},{7,5},{8,14},{9,15},{10,... | collective-permute-start | bytes 6152 | tf_op jit(solution)/shard_map/ppermute | solution.py:273
  34.5 4.0 %collective-permute-start.9 = (f32[1,512]{1,0:T(1,128)S(1)}, f32[1,512]{1,0:T(1,128)S(1)}, u32[]{:S(2)}, u32[]{:S(2)}) collective-permute-start(f32[1,512]{1,0:T(1,128)S(1)} %add.16.after_ref.refs_0_), channel_id=1, source_target_pairs={{0,4},{1,5},{2,6},{3,7},{4,0},{5,1},{6,2},{7,3},{8,12},{9,13},{10,... | collective-permute-start | bytes 6152 | tf_op jit(solution)/shard_map/ppermute | solution.py:273
  35.3 4.2 %collective-permute-start.8 = (f32[1,512]{1,0:T(1,128)S(1)}, f32[1,512]{1,0:T(1,128)S(1)}, u32[]{:S(2)}, u32[]{:S(2)}) collective-permute-start(f32[1,512]{1,0:T(1,128)S(1)} %add.16.after_ref.refs_0_), channel_id=1, source_target_pairs={{0,2},{1,3},{2,4},{3,5},{4,6},{5,7},{6,0},{7,1},{8,10},{9,11},{10,... | collective-permute-start | bytes 6152 | tf_op jit(solution)/shard_map/ppermute | solution.py:273
  39.8 5.9 %collective-permute-start.13 = (f32[1,512]{1,0:T(1,128)S(1)}, f32[1,512]{1,0:T(1,128)S(1)}, u32[]{:S(2)}, u32[]{:S(2)}) collective-permute-start(f32[1,512]{1,0:T(1,128)S(1)} %get-tuple-element.63.after_ref.refs_0_), channel_id=1, source_target_pairs={{0,24},{8,0},{16,8},{24,16},{1,25},{9,1},{17,9},{25,17},{2,26},{10... | collective-permute-start | bytes 6152 | tf_op jit(solution)/shard_map/ppermute | solution.py:273
  42.0 3.7 %collective-permute-start.12 = (f32[1,512]{1,0:T(1,128)S(1)}, f32[1,512]{1,0:T(1,128)S(1)}, u32[]{:S(2)}, u32[]{:S(2)}) collective-permute-start(f32[1,512]{1,0:T(1,128)S(1)} %get-tuple-element.63.after_ref.refs_0_), channel_id=1, source_target_pairs={{0,16},{8,24},{16,0},{24,8},{1,17},{9,25},{17,1},{25,9},{2,18},{10... | collective-permute-start | bytes 6152 | tf_op jit(solution)/shard_map/ppermute | solution.py:273
  42.4 3.4 %collective-permute-start.11 = (f32[1,512]{1,0:T(1,128)S(1)}, f32[1,512]{1,0:T(1,128)S(1)}, u32[]{:S(2)}, u32[]{:S(2)}) collective-permute-start(f32[1,512]{1,0:T(1,128)S(1)} %get-tuple-element.63.after_ref.refs_0_), channel_id=1, source_target_pairs={{0,8},{8,16},{16,24},{24,0},{1,9},{9,17},{17,25},{25,1},{2,10},{10... | collective-permute-start | bytes 6152 | tf_op jit(solution)/shard_map/ppermute | solution.py:273
  46.2 3.5 %collective-permute-start.14 = (f32[1,512]{1,0:T(1,128)S(1)}, f32[1,512]{1,0:T(1,128)S(1)}, u32[]{:S(2)}, u32[]{:S(2)}) collective-permute-start(f32[1,512]{1,0:T(1,128)S(1)} %get-tuple-element.66.after_ref), channel_id=1, source_target_pairs={{0,1},{1,0},{2,3},{3,2},{4,5},{5,4},{6,7},{7,6},{8,9},{9,8},{10,11... | collective-permute-start | bytes 6152 | tf_op jit(solution)/shard_map/ppermute | solution.py:268
  49.7 3.5 %collective-permute-start.17 = (f32[1,512]{1,0:T(1,128)S(1)}, f32[1,512]{1,0:T(1,128)S(1)}, u32[]{:S(2)}, u32[]{:S(2)}) collective-permute-start(f32[1,512]{1,0:T(1,128)S(1)} %add.17.after_ref.refs_0_), channel_id=1, source_target_pairs={{0,6},{1,7},{2,0},{3,1},{4,2},{5,3},{6,4},{7,5},{8,14},{9,15},{10,... | collective-permute-start | bytes 6152 | tf_op jit(solution)/shard_map/ppermute | solution.py:273
  50.4 3.3 %collective-permute-start.16 = (f32[1,512]{1,0:T(1,128)S(1)}, f32[1,512]{1,0:T(1,128)S(1)}, u32[]{:S(2)}, u32[]{:S(2)}) collective-permute-start(f32[1,512]{1,0:T(1,128)S(1)} %add.17.after_ref.refs_0_), channel_id=1, source_target_pairs={{0,4},{1,5},{2,6},{3,7},{4,0},{5,1},{6,2},{7,3},{8,12},{9,13},{10,... | collective-permute-start | bytes 6152 | tf_op jit(solution)/shard_map/ppermute | solution.py:273
  50.4 4.2 %collective-permute-start.15 = (f32[1,512]{1,0:T(1,128)S(1)}, f32[1,512]{1,0:T(1,128)S(1)}, u32[]{:S(2)}, u32[]{:S(2)}) collective-permute-start(f32[1,512]{1,0:T(1,128)S(1)} %add.17.after_ref.refs_0_), channel_id=1, source_target_pairs={{0,2},{1,3},{2,4},{3,5},{4,6},{5,7},{6,0},{7,1},{8,10},{9,11},{10,... | collective-permute-start | bytes 6152 | tf_op jit(solution)/shard_map/ppermute | solution.py:273
  54.6 0.7 copy-start.9
  57.3 3.9 %collective-permute-start.18 = (f32[32,32,128]{2,1,0:T(8,128)S(1)}, f32[32,32,128]{2,1,0:T(8,128)S(1)}, u32[]{:S(2)}, u32[]{:S(2)}) collective-permute-start(f32[32,32,128]{2,1,0:T(8,128)S(1)} %get-tuple-element.88), channel_id=1, source_target_pairs={{0,8},{8,0},{16,24},{24,16},{1,9},{9,1},{17,25},{25,17},{2,10},{10... | collective-permute-start | bytes 1572872 | tf_op jit(solution)/shard_map/ppermute | solution.py:268
  61.4 8.0 %collective-permute-start.19 = (f32[16,32,128]{2,1,0:T(8,128)S(1)}, f32[16,32,128]{2,1,0:T(8,128)S(1)}, u32[]{:S(2)}, u32[]{:S(2)}) collective-permute-start(f32[16,32,128]{2,1,0:T(8,128)S(1)} %slice.9), channel_id=1, source_target_pairs={{0,16},{8,24},{16,0},{24,8},{1,17},{9,25},{17,1},{25,9},{2,18},{10... | collective-permute-start | bytes 786440 | tf_op jit(solution)/shard_map/ppermute | solution.py:273

commit v3 on v0

v3 whole, which is shorter than its diff:
```python
import functools
import math

import jax
import jax.numpy as jnp
import numpy as np
from jax import lax
from jax.experimental import pallas as pl
from jax.experimental.pallas import tpu as pltpu
from jax.sharding import PartitionSpec as P

ITERS = 2
SEG = 32
MERCH_DEV = 128
DAYS = 64
LANES = 128
CHUNKS = 4
UNROLL = 64

half_span = 11

f32 = jnp.float32
bf16 = jnp.bfloat16
VMEM = pl.BlockSpec(memory_space=pltpu.VMEM)
ANY = pl.BlockSpec(memory_space=pl.ANY)
HBM = pl.BlockSpec(memory_space=pltpu.HBM)
PARAMS = pltpu.CompilerParams(vmem_limit_bytes=20 * 2**20)


def filter_table(day_count):
    outer = 13.0
    coeffs = []
    for offset_days in range(-half_span, half_span + 1):
        sq = float(offset_days * offset_days)
        top = (
            315.0
            * ((outer - 1) ** 2 - sq)
            * (outer**2 - sq)
            * ((outer + 1) ** 2 - sq)
            * (3 * outer**2 - 16 - 11 * sq)
        )
        bottom = (
            8
            * outer
            * (outer**2 - 1)
            * (4 * outer**2 - 1)
            * (4 * outer**2 - 9)
            * (4 * outer**2 - 25)
        )
        coeffs.append(top / bottom)
    matrix = np.zeros((day_count, day_count))
    for row_day in range(day_count):
        for offset_days in range(-half_span, half_span + 1):
            col_day = row_day + offset_days
            if 0 <= col_day < day_count:
                matrix[row_day, col_day] = coeffs[offset_days + half_span]
        matrix[row_day] = matrix[row_day] / matrix[row_day].sum()
    return matrix


def split2(x):
    hi = x.astype(bf16)
    return hi, (x - hi.astype(f32)).astype(bf16)


def split_rows(x):
    hi = x.astype(bf16)
    rest = x - hi.astype(f32)
    mid = rest.astype(bf16)
    low = (rest - mid.astype(f32)).astype(bf16)
    return jnp.concatenate([hi, mid, low, jnp.zeros((5, x.shape[1]), bf16)], 0)


def dot_rows(rows, k, dims):
    return lax.dot_general(rows, k, (dims, ((), ())), preferred_element_type=f32)


def cols_of(us, blocks):
    out = 0.0
    for u, (khi, klo) in zip(us, blocks):
        rows = split_rows(u)
        out = out + dot_rows(rows, khi[...], ((1,), (0,))) + dot_rows(rows, klo[...], ((1,), (0,)))
    return jnp.sum(out, axis=0, keepdims=True)


def rows_of(vs, blocks):
    out = 0.0
    for v, (khi, klo) in zip(vs, blocks):
        rows = split_rows(v)
        out = out + dot_rows(rows, khi[...], ((1,), (1,))) + dot_rows(rows, klo[...], ((1,), (1,)))
    return jnp.sum(out, axis=0, keepdims=True)


def kernel_block(x, y, row_region, col_region, penalty):
    n, m = x.shape[0], y.shape[0]
    regions = penalty.shape[0]
    inv_root = 1.0 / math.sqrt(x.shape[1])
    inner = dot_rows(x, y, ((1,), (1,)))
    row_hot = (lax.broadcasted_iota(jnp.int32, (regions, n), 0) == row_region).astype(f32).astype(bf16)
    col_hot = (lax.broadcasted_iota(jnp.int32, (regions, m), 0) == col_region).astype(f32).astype(bf16)
    phi, plo = split2(penalty)
    qhi = jnp.dot(phi, col_hot, preferred_element_type=f32).astype(bf16)
    qlo = jnp.dot(plo, col_hot, preferred_element_type=f32).astype(bf16)
    pen = dot_rows(jnp.concatenate([row_hot, row_hot], 0), jnp.concatenate([qhi, qlo], 0), ((0,), (0,)))
    return split2(jnp.exp(inner * inv_root - pen))


def run_copies(pairs, sems):
    copies = [pltpu.make_async_copy(src, dst, sems.at[k]) for k, (src, dst) in enumerate(pairs)]
    for copy in copies:
        copy.start()
    return copies


def first_body(
    x_hbm, y_hbm, rr_hbm, cr_hbm, pen_hbm, rr4_hbm, seg4_hbm, mass4_hbm, cr4_hbm, cm4_hbm, f_hbm, m_hbm, d_hbm, a_hbm,
    khi_ref, klo_ref, r_ref, xpack_ref, ypack_ref, seg_ref, mass_ref, cm_ref, pen_ref, cr_ref, rr_ref, xb_ref, yb_ref,
    f_ref, m_ref, d_ref, a_ref, rr4_ref, seg4_ref, cr4_ref, sems,
):
    me = lax.axis_index("cohort")
    n, m = xb_ref.shape[0], yb_ref.shape[0]
    p, q = n // LANES, m // LANES
    copies = run_copies(
        (
            (x_hbm, xb_ref),
            (y_hbm, yb_ref),
            (rr_hbm, rr_ref),
            (cr_hbm, cr_ref),
            (pen_hbm, pen_ref),
            (rr4_hbm, rr4_ref),
            (seg4_hbm, seg4_ref),
            (mass4_hbm, xpack_ref.at[pl.ds(n + 2 * p, p), :]),
            (cr4_hbm, cr4_ref),
            (cm4_hbm, ypack_ref.at[pl.ds(m + q, q), :]),
            (mass4_hbm, mass_ref),
            (cm4_hbm, cm_ref),
            (seg4_hbm, seg_ref),
            (f_hbm.at[me], f_ref),
            (m_hbm, m_ref),
            (d_hbm, d_ref),
            (a_hbm, a_ref),
        ),
        sems,
    )
    for copy in copies[:5]:
        copy.wait()
    hi, lo = kernel_block(xb_ref[...], yb_ref[...], rr_ref[...], cr_ref[...], pen_ref[...])
    khi_ref[...] = hi
    klo_ref[...] = lo
    r_ref[...] = rows_of([jnp.ones((1, m), f32)], [(khi_ref, klo_ref)])
    xpack_ref[0:n, :] = xb_ref[...].astype(f32)
    ypack_ref[0:m, :] = yb_ref[...].astype(f32)
    for copy in copies[5:]:
        copy.wait()
    xpack_ref[n : n + p, :] = rr4_ref[...].astype(f32)
    xpack_ref[n + p : n + 2 * p, :] = seg4_ref[...].astype(f32)
    ypack_ref[m : m + q, :] = cr4_ref[...].astype(f32)


def first_call(x, y, rr, cr, penalty, mass, cm, seg, table, records):
    n, m = x.shape[0], y.shape[0]
    p, q = n // LANES, m // LANES
    row = lambda v: v.reshape(1, -1)
    block = lambda v: v.reshape(-1, LANES)
    i32 = jnp.int32
    out = [
        ((n, m), bf16),
        ((n, m), bf16),
        ((1, n), f32),
        ((n + 3 * p, LANES), f32),
        ((m + 2 * q, LANES), f32),
        ((p, LANES), i32),
        ((p, LANES), f32),
        ((q, LANES), f32),
        (penalty.shape, f32),
        ((1, m), i32),
        ((1, n), i32),
        (x.shape, bf16),
        (y.shape, bf16),
        (table.shape[1:], f32),
    ] + [(r.shape, r.dtype) for r in records]
    return pl.pallas_call(
        first_body,
        in_specs=[HBM] * 14,
        out_specs=[VMEM] * len(out),
        out_shape=[pltpu.VMEM(shape, dtype) for shape, dtype in out],
        scratch_shapes=[
            pltpu.VMEM((p, LANES), i32),
            pltpu.VMEM((p, LANES), i32),
            pltpu.VMEM((q, LANES), i32),
            pltpu.SemaphoreType.DMA((17,)),
        ],
        compiler_params=PARAMS,
        name="first",
    )(x, y, row(rr), row(cr), penalty, block(rr), block(seg), block(mass), block(cr), block(cm), table, *records)


def flat(block):
    return jnp.concatenate([block[k : k + 1, :] for k in range(block.shape[0])], 1)


def rest_body(counts, x_ref, y_ref, rr_ref, cr_ref, pen_ref, *refs):
    n_x, n_y = counts
    xpacks, ypacks = refs[:n_x], refs[n_x : n_x + n_y]
    outs = refs[n_x + n_y :]
    n, m = x_ref.shape[0], y_ref.shape[0]
    p, q = n // LANES, m // LANES
    xs = [(x_ref[...], rr_ref[...])]
    for pack in xpacks:
        xs.append((pack[0:n, :].astype(bf16), flat(pack[n : n + p, :]).astype(jnp.int32)))
    ys = [(y_ref[...], cr_ref[...])]
    for pack in ypacks:
        ys.append((pack[0:m, :].astype(bf16), flat(pack[m : m + q, :]).astype(jnp.int32)))
    pen = pen_ref[...]
    k = 0
    for i, (x, rr) in enumerate(xs):
        for j, (y, cr) in enumerate(ys):
            if i or j:
                outs[k][...], outs[k + 1][...] = kernel_block(x, y, rr, cr, pen)
                k += 2


def rest_call(x, y, rr, cr, penalty, xpacks, ypacks, after):
    n, m = x.shape[0], y.shape[0]
    blocks = (1 + len(xpacks)) * (1 + len(ypacks)) - 1
    out = pl.pallas_call(
        lambda *refs: rest_body(
            (len(xpacks), len(ypacks)), *refs[: 5 + len(xpacks) + len(ypacks)], *refs[-2 * blocks :]
        ),
        in_specs=[VMEM] * (5 + len(xpacks) + len(ypacks)) + [ANY] * len(after),
        out_specs=[VMEM] * (2 * blocks),
        out_shape=[pltpu.VMEM((n, m), bf16)] * (2 * blocks),
        compiler_params=PARAMS,
        cost_estimate=pl.CostEstimate(
            flops=2 * blocks * n * m * LANES, transcendentals=blocks * n * m, bytes_accessed=blocks * n * m * 4
        ),
        name="rest",
    )(x, y, rr, cr, penalty, *xpacks, *ypacks, *after)
    return [(out[2 * k], out[2 * k + 1]) for k in range(blocks)]


def total_of(refs):
    total = refs[0][...]
    for ref in refs[1:]:
        total = total + ref[...]
    return total


def cols_body(n, groups, packs, block_count, mass_ref, *refs):
    p = n // LANES
    at = 0
    sums = []
    for count in groups:
        sums.append(total_of(refs[at : at + count]))
        at += count
    pack_refs = refs[at : at + packs]
    blocks = [(refs[at + packs + 2 * k], refs[at + packs + 2 * k + 1]) for k in range(block_count)]
    u_ref, c_ref = refs[-2:]
    masses = [flat(mass_ref[...])] + [flat(pack[n + 2 * p : n + 3 * p, :]) for pack in pack_refs]
    if len(groups) == 1:
        sums = [sums[0][:, k * n : (k + 1) * n] for k in range(len(masses))]
    us = [mass / part for mass, part in zip(masses, sums)]
    u_ref[...] = jnp.concatenate(us, 1)
    width = block_count // len(masses)
    c_ref[...] = jnp.concatenate(
        [cols_of(us, [blocks[i * width + j] for i in range(len(masses))]) for j in range(width)], 1
    )


def cols_call(mass, n, partial_groups, packs, blocks, after):
    partials = [part for group in partial_groups for part in group]
    parts = 1 + len(packs)
    m = blocks[0][0].shape[1]
    width = len(blocks) // parts
    args = [mass, *partials, *packs, *[ref for block in blocks for ref in block]]
    return pl.pallas_call(
        lambda *refs: cols_body(
            n, [len(group) for group in partial_groups], len(packs), len(blocks), *refs[: len(args)], *refs[-2:]
        ),
        in_specs=[VMEM] * len(args) + [ANY] * len(after),
        out_specs=[VMEM] * 2,
        out_shape=[pltpu.VMEM((1, parts * n), f32), pltpu.VMEM((1, width * m), f32)],
        compiler_params=PARAMS,
        name="cols",
    )(*args, *after)


def rows_body(m, packs, parts, block_count, mass_ref, *refs):
    q = m // LANES
    total = total_of(refs[:parts])
    pack_refs = refs[parts : parts + packs]
    blocks = [(refs[parts + packs + 2 * k], refs[parts + packs + 2 * k + 1]) for k in range(block_count)]
    v_ref, r_ref = refs[-2:]
    masses = [flat(mass_ref[...])] + [flat(pack[m + q : m + 2 * q, :]) for pack in pack_refs]
    vs = [mass / total[:, k * m : (k + 1) * m] for k, mass in enumerate(masses)]
    v_ref[...] = vs[0]
    width = len(masses)
    r_ref[...] = jnp.concatenate(
        [rows_of(vs, blocks[i * width : (i + 1) * width]) for i in range(block_count // width)], 1
    )


def rows_call(mass, partials, packs, blocks, after):
    n, m = blocks[0][0].shape
    width = 1 + len(packs)
    args = [mass, *partials, *packs, *[ref for block in blocks for ref in block]]
    return pl.pallas_call(
        lambda *refs: rows_body(m, len(packs), len(partials), len(blocks), *refs[: len(args)], *refs[-2:]),
        in_specs=[VMEM] * len(args) + [ANY] * len(after),
        out_specs=[VMEM] * 2,
        out_shape=[
            jax.ShapeDtypeStruct((1, m), f32),
            pltpu.VMEM((1, len(blocks) // width * n), f32),
        ],
        compiler_params=PARAMS,
        name="rows",
    )(*args, *after)


def table_body(count, filt, read, hi_ref, lo_ref):
    t_count = filt.shape[0]
    merch_iota = lax.broadcasted_iota(jnp.int32, (MERCH_DEV, LANES), 0).astype(f32).astype(bf16)
    one, zero = jnp.ones((MERCH_DEV, LANES), bf16), jnp.zeros((MERCH_DEV, LANES), bf16)
    size = math.gcd(count, UNROLL)

    def group(step, carry):
        start = pl.multiple_of(step * size, size)
        merch, days, amounts = read(start, size)
        merch = merch.astype(f32).astype(bf16)
        days = days.astype(jnp.int32)
        tables = []
        for i in range(size):
            day = jnp.broadcast_to(days[i : i + 1, :], (t_count, LANES))
            coef = jnp.take_along_axis(filt, day, axis=1, mode="promise_in_bounds")
            chi, clo = split2(coef * amounts[i : i + 1, :])
            hot = jnp.where(merch_iota == merch[i : i + 1, :], one, zero)
            both = dot_rows(jnp.concatenate([chi, clo], 0), hot, ((1,), (1,)))
            tables.append(both[:t_count] + both[t_count:])
        hi, lo = split2(jnp.swapaxes(jnp.stack(tables, 0), 0, 1))
        hi_ref[:, pl.ds(start, size), :] = hi
        lo_ref[:, pl.ds(start, size), :] = lo
        return carry

    lax.fori_loop(0, count // size, group, 0)


def own_body(first, count, f_ref, m_ref, d_ref, a_ref, hi_ref, lo_ref, pack_ref):
    rows = pl.ds(first, count)
    pack_ref[0:count, :] = m_ref[rows, :].astype(f32)
    pack_ref[count : 2 * count, :] = d_ref[rows, :].astype(f32)
    pack_ref[2 * count : 3 * count, :] = a_ref[rows, :]

    def read(start, size):
        at = pl.ds(first + start, size)
        return m_ref[at, :], d_ref[at, :], a_ref[at, :]

    table_body(count, f_ref[...], read, hi_ref, lo_ref)


def other_body(count, f_ref, pack_ref, hi_ref, lo_ref, token_ref):
    def read(start, size):
        return tuple(pack_ref[pl.ds(k * count + start, size), :] for k in range(3))

    table_body(count, f_ref[...], read, hi_ref, lo_ref)
    token_ref[...] = jnp.zeros_like(token_ref)


def table_call(body, filt, args, count, extra, after):
    t_count = filt.shape[0]
    hi, lo, pack = pl.pallas_call(
        lambda *refs: body(*refs[: 1 + len(args)], *refs[-3:]),
        in_specs=[VMEM] * (1 + len(args)) + [ANY] * len(after),
        out_specs=[VMEM] * 3,
        out_shape=[pltpu.VMEM((t_count, count, LANES), bf16)] * 2 + [pltpu.VMEM((extra, LANES), f32)],
        compiler_params=PARAMS,
        cost_estimate=pl.CostEstimate(
            flops=4 * count * t_count * LANES * LANES, transcendentals=0, bytes_accessed=count * 80000
        ),
        name="tables",
    )(filt, *args, *after)
    return (hi, lo), pack


def spread_body(n, t_first, t_count, parts, packs, count, seg_ref, u_ref, *refs):
    p = n // LANES
    w = u_ref[...] * total_of(refs[:parts])
    pack_refs = refs[parts : parts + packs]
    pair_refs = refs[parts + packs : parts + packs + 2 * count]
    o_ref, w_ref = refs[-2:]
    w_ref[...] = w[:, :n]
    seg = jnp.concatenate(
        [flat(seg_ref[...])] + [flat(pack[n + p : n + 2 * p, :]).astype(jnp.int32) for pack in pack_refs], 1
    )
    hot = lax.broadcasted_iota(jnp.int32, (SEG, w.shape[1]), 0) == seg
    whi, wlo = split2(jnp.where(hot, w, 0.0))
    both = jnp.concatenate([whi, wlo], 0)

    def take(part, t):
        return jnp.concatenate(
            [jnp.concatenate([pair_refs[2 * k + part][t + q] for k in range(count)], 0) for q in range(2)], 1
        )

    for t in range(t_first, t_first + t_count, 2):
        two = jnp.dot(both, take(0, t), preferred_element_type=f32)
        out = two[:SEG] + two[SEG:] + jnp.dot(whi, take(1, t), preferred_element_type=f32)
        o_ref[t - t_first] = out[:, :LANES]
        o_ref[t - t_first + 1] = out[:, LANES:]


def spread_call(n, seg, u, partials, packs, pairs, t_first, t_count, after):
    refs = [ref for pair in pairs for ref in pair]
    args = [seg, u, *partials, *packs, *refs]
    return pl.pallas_call(
        lambda *refs: spread_body(
            n, t_first, t_count, len(partials), len(packs), len(pairs), *refs[: len(args)], *refs[-2:]
        ),
        in_specs=[VMEM] * len(args) + [ANY] * len(after),
        out_specs=[VMEM] * 2,
        out_shape=[pltpu.VMEM((t_count, SEG, LANES), f32), jax.ShapeDtypeStruct((1, n), f32)],
        compiler_params=PARAMS,
        name="spread",
    )(*args, *after)


def move(x, axis, size, pair, step, flip):
    blocks = size // pair
    return lax.ppermute(
        x,
        axis,
        [(b * pair + r, ((b + step) % blocks) * pair + (r ^ flip)) for b in range(blocks) for r in range(pair)],
    )


def gate(x, *after):
    return lax.optimization_barrier((x, *after))[0]


def per_device(
    n_cohort,
    n_cell,
    cohort_features,
    cell_features,
    cohort_region,
    cell_region,
    penalty,
    cohort_mass,
    cell_mass,
    cohort_segment,
    spend_merchant,
    spend_day,
    spend_amount,
):
    n = cohort_features.shape[0]
    t_dev = DAYS // n_cohort
    n_y, n_z = n_cohort // 2, n_cell // 2
    table = np.zeros((n_cohort, 2 * t_dev, LANES), np.float32)
    henderson = filter_table(DAYS)
    for me in range(n_cohort):
        for k, dest in enumerate((me ^ 1, me)):
            table[me, k * t_dev : (k + 1) * t_dev, :DAYS] = henderson[dest * t_dev : (dest + 1) * t_dev]

    over_y = lambda x, step: move(x, "cohort", n_cohort, 2, step, 0)
    core = lambda x: move(x, "cohort", n_cohort, 2, 0, 1)
    along_z = lambda x: [x] + [move(x, "cell", n_cell, 2, step, 0) for step in range(1, n_z)]

    (
        khi, klo, partial, xpack, ypack, seg, mass, cmass, pen, creg, rreg, xb, yb, filt, *records
    ) = first_call(
        cohort_features, cell_features, cohort_region, cell_region, penalty, cohort_mass, cell_mass, cohort_segment,
        jnp.asarray(table), (spend_merchant, spend_day, spend_amount),
    )
    count = n // CHUNKS
    own, sends = [], []

    def own_tables(after):
        first = len(own) * count
        pair, pack = table_call(functools.partial(own_body, first, count), filt, records, count, 3 * count, after)
        own.append(pair)
        sends.append(pack)
        return pack

    lines = along_z(partial)
    xpacks = [over_y(xpack, step) for step in range(1, n_y)]
    ypacks = [move(ypack, "cell", n_cell, 2, 0, 1)]
    token = own_tables([partial])
    token = own_tables([token])
    part = gate(sum(lines), token)
    whole = [part, move(part, "cell", n_cell, 2, 0, 1)]
    groups = [whole]
    for step in range(1, n_y):
        groups.append([both_axes(part, n_cohort, n_cell, step, flip) for flip in range(2)])
    token = own_tables([part])
    token = own_tables([token])
    blocks = [(khi, klo)] + rest_call(xb, yb, rreg, creg, pen, xpacks, ypacks, [token])
    cohort_scale, column = cols_call(mass, n, groups, xpacks, blocks, [token])
    others = []
    gated = column
    waiting = [(step, chunk) for chunk in range(CHUNKS) for step in range(1, n_y)]
    arrived = [over_y(gate(sends[chunk], gated), step) for step, chunk in waiting]
    per_window = -(-len(arrived) // 2)
    token = None
    for iteration in range(ITERS):
        after = [] if token is None else [token]
        cell_scale, partial = rows_call(cmass, [column, core(column)], ypacks, blocks, after)
        lines = along_z(partial)
        token = partial
        for pack in arrived[iteration * per_window : (iteration + 1) * per_window]:
            pair, token = table_call(functools.partial(other_body, count), filt, [pack], count, 8, [token])
            others.append(pair)
        if iteration < ITERS - 1:
            cohort_scale, column = cols_call(mass, n, [lines], xpacks, blocks, [token])
            token = None
    pairs = own + [others[k] for step in range(1, n_y) for k in range(len(waiting)) if waiting[k][0] == step]
    away, weights = spread_call(n, seg, cohort_scale, lines, xpacks, pairs, 0, t_dev, [token])
    mine, _ = spread_call(n, seg, cohort_scale, lines, xpacks, pairs, t_dev, t_dev, [token])
    out = mine + core(away)
    return (weights.reshape(-1), cell_scale.reshape(-1), out)


def both_axes(x, n_cohort, n_cell, step, flip):
    pairs = []
    blocks = n_cohort // 2
    for b in range(blocks):
        for c in range(2):
            for cell in range(n_cell):
                source = (b * 2 + c) * n_cell + cell
                target = (((b + step) % blocks) * 2 + c) * n_cell + (cell ^ flip)
                pairs.append((source, target))
    return lax.ppermute(x, ("cohort", "cell"), pairs)


def solution(mesh):
    return jax.shard_map(
        functools.partial(per_device, mesh.shape["cohort"], mesh.shape["cell"]),
        mesh=mesh,
        in_specs=(
            P("cohort", None),
            P("cell", None),
            P("cohort"),
            P("cell"),
            P(),
            P("cohort"),
            P("cell"),
            P("cohort"),
            P("cohort", "cell"),
            P("cohort", "cell"),
            P("cohort", "cell"),
        ),
        out_specs=(P("cohort"), P("cell"), P("cohort", None, "cell")),
        check_vma=False,
    )
```

time: 186 us -> 75.4 us (0.41)
  blocking collectives: 66.7 us -> 0 us
  matrix products: 61 us -> 0 us
  Pallas kernels: 0 us -> 36.9 us
  starting transfers between devices: 0.04 us -> 26.7 us
  waiting for transfers between devices: 26 us -> 2.83 us
  between operations: 14.1 us -> 0.92 us
  other arithmetic: 6.73 us -> 0.75 us
  local copies, waits for them, and re-layouts: 8.94 us -> 6.92 us
    psum x5 -> x0, blocking collectives: 66.7 us -> none  [the longest x3 48.1 us: finish_rows(): summed = lax.psum(partial_value, 'cell')]
    dot_general x25 -> x0, matrix products: 61 us -> none  [the longest x8 32 us: one_group(): jnp.einsum('brd,brm->bdm', day_values, merch_hot, precision=lax.Precision...]
    pallas_call x0 -> x16, Pallas kernels: none -> 36.9 us  [the longest x8 24.6 us: table_call(): pl.pallas_call(lambda *refs: body(*refs[:1 + len(args)], *refs[-3:]), in_...]
    ppermute x0 -> x21, starting transfers between devices: none -> 26.7 us  [the longest x19 24.3 us: move(): lax.ppermute(x, axis, [(b * pair + r, (b + step) % blocks * pair + (r ^ f...]
    reduce_scatter x1 -> x0, waiting for transfers between devices: 25.9 us -> none  [per_device(): lax.psum_scatter(trend_all.reshape(DAYS, SEG, merch_local), 'cohort', sca...]
    mul x9 -> x0, other arithmetic: 6.7 us -> none  [the longest x8 6.69 us: one_group(): values = group_weights[:, None] * group_amounts]
    eq x16 -> x0, local copies, waits for them, and re-layouts: 6.32 us -> none  [the longest x8 6.27 us: one_group(): group_merch[:, :, None] == merch_iota[None, None, :]]
    unnamed x13 -> x24, local copies, waits for them, and re-layouts: 1.7 us -> 6.92 us
  transfers between devices with their start and end apart: 1 -> 21, of which waited for: 1 -> 3; matrix products, arithmetic and copies ran while one was open for 0% -> 0% of each run, Pallas kernels for 0% -> 43%
where the time goes in v3:
time: 75.4 us; the launch traced here: 75 us
  Pallas kernels  36.9 us (49%)
  starting transfers between devices  26.7 us (35%)
  local copies, waits for them, and re-layouts  6.92 us (9%)
  waiting for transfers between devices  2.83 us (4%)
  between operations  0.92 us (1%)
    pallas_call x8, Pallas kernels, table_call(): pl.pallas_call(lambda *refs: body(*refs[:1 + len(args)], *refs[-3:]), in_...  24.6 us
    ppermute x19, starting transfers between devices, move(): lax.ppermute(x, axis, [(b * pair + r, (b + step) % blocks * pair + (r ^ f...  24.3 us
    unnamed x24, local copies, waits for them, and re-layouts  6.92 us
    pallas_call x2, Pallas kernels, spread_call(): pl.pallas_call(lambda *refs: spread_body(n, t_first, t_count, len(partial...  3.97 us
    pallas_call x2, Pallas kernels, rows_call(): pl.pallas_call(lambda *refs: rows_body(m, len(packs), len(partials), len(...  3.21 us
    ppermute x19, waiting for transfers between devices, move(): lax.ppermute(x, axis, [(b * pair + r, (b + step) % blocks * pair + (r ^ f...  2.82 us
    ppermute x2, starting transfers between devices, both_axes(): return lax.ppermute(x, ('cohort', 'cell'), pairs)  2.4 us
    pallas_call x2, Pallas kernels, cols_call(): pl.pallas_call(lambda *refs: cols_body(n, [len(group) for group in partia...  1.81 us
  transfers between devices with their start and end apart: 21, of which 3 were waited for; matrix products, arithmetic and copies ran while one was open for 0% of the time, Pallas kernels for 43%

profile of v3, /device:TPU:1, one launch (start us, length us, event | category | flops | bytes accessed | tf_op | source)
XLA Modules:
  0.0 75.0 jit_solution(10742627021960093312)
XLA Ops:
  0.7 0.6 copy-done.11
  1.3 0.0 copy-done.10
  1.3 0.0 copy-done.9
  1.3 0.0 copy-done.8
  1.4 0.0 copy-done.7
  1.4 0.9 %copy-done = s32[512,128]{1,0:T(8,128)S(1)} copy-done((s32[512,128]{1,0:T(8,128)S(1)}, s32[512,128]{1,0:T(8,128)}, u32[]{:S(2)}) %copy-start) | copy-done | bytes 262168
  2.3 0.9 %copy-done.1 = s32[512,128]{1,0:T(8,128)S(1)} copy-done((s32[512,128]{1,0:T(8,128)S(1)}, s32[512,128]{1,0:T(8,128)}, u32[]{:S(2)}) %copy-start.1) | copy-done | bytes 262168
  3.3 0.9 %copy-done.2 = f32[512,128]{1,0:T(8,128)S(1)} copy-done((f32[512,128]{1,0:T(8,128)S(1)}, f32[512,128]{1,0:T(8,128)}, u32[]{:S(2)}) %copy-start.2) | copy-done | bytes 262168
  4.2 0.9 %copy-done.3 = bf16[512,128]{1,0:T(8,128)(2,1)S(1)} copy-done((bf16[512,128]{1,0:T(8,128)(2,1)S(1)}, bf16[512,128]{1,0:T(8,128)(2,1)}, u32[]{:S(2)}) %copy-start.3) | copy-done | bytes 131096
  5.1 0.9 %copy-done.4 = bf16[512,128]{1,0:T(8,128)(2,1)S(1)} copy-done((bf16[512,128]{1,0:T(8,128)(2,1)S(1)}, bf16[512,128]{1,0:T(8,128)(2,1)}, u32[]{:S(2)}) %copy-start.4) | copy-done | bytes 131096
  6.0 0.8 %copy-done.5 = f32[4,32,128]{2,1,0:T(8,128)S(1)} copy-done((f32[4,32,128]{2,1,0:T(8,128)S(1)}, f32[4,32,128]{2,1,0:T(8,128)}, u32[]{:S(2)}) %copy-start.5) | copy-done | bytes 65560
  6.9 0.7 copy-done.6
  7.6 1.7 %first.1 = (bf16[512,512]{1,0:T(8,128)(2,1)S(1)}, bf16[512,512]{1,0:T(8,128)(2,1)S(1)}, f32[1,512]{1,0:T(1,128)S(1)}, f32[524,128]{1,0:T(8,128)S(1)}, f32[520,12...) custom-call(bf16[512,128]{1,0:T(8,128)(2,1)S(1)} %copy-done.3, ...), custom_call_target="tpu_custom_call" | custom-call | tf_op jit(solution)/shard_map/first/pallas_call | solution.py:182
  9.3 2.2 %collective-permute-start = (f32[1,512]{1,0:T(1,128)S(1)}, f32[1,512]{1,0:T(1,128)S(1)}, u32[]{:S(2)}, u32[]{:S(2)}) collective-permute-start(f32[1,512]{1,0:T(1,128)S(1)} %get-tuple-element.67.refs_4_), channel_id=1, source_target_pairs={{0,2},{1,3},{2,4},{3,5},{4,6},{5,7},{6,0},{7,1},{8,10},{9,11},{10,... | collective-permute-start | bytes 6152 | tf_op jit(solution)/shard_map/ppermute | solution.py:427
  11.5 2.3 %collective-permute-start.1 = (f32[1,512]{1,0:T(1,128)S(1)}, f32[1,512]{1,0:T(1,128)S(1)}, u32[]{:S(2)}, u32[]{:S(2)}) collective-permute-start(f32[1,512]{1,0:T(1,128)S(1)} %get-tuple-element.67.refs_4_), channel_id=1, source_target_pairs={{0,4},{1,5},{2,6},{3,7},{4,0},{5,1},{6,2},{7,3},{8,12},{9,13},{10,... | collective-permute-start | bytes 6152 | tf_op jit(solution)/shard_map/ppermute | solution.py:427
  13.8 1.1 %collective-permute-start.2 = (f32[1,512]{1,0:T(1,128)S(1)}, f32[1,512]{1,0:T(1,128)S(1)}, u32[]{:S(2)}, u32[]{:S(2)}) collective-permute-start(f32[1,512]{1,0:T(1,128)S(1)} %get-tuple-element.67.refs_4_), channel_id=1, source_target_pairs={{0,6},{1,7},{2,0},{3,1},{4,2},{5,3},{6,4},{7,5},{8,14},{9,15},{10,... | collective-permute-start | bytes 6152 | tf_op jit(solution)/shard_map/ppermute | solution.py:427
  14.8 1.2 %collective-permute-start.6 = (f32[524,128]{1,0:T(8,128)S(1)}, f32[524,128]{1,0:T(8,128)S(1)}, u32[]{:S(2)}, u32[]{:S(2)}) collective-permute-start(f32[524,128]{1,0:T(8,128)S(1)} %get-tuple-element.75), channel_id=1, source_target_pairs={{0,16},{8,24},{16,0},{24,8},{1,17},{9,25},{17,1},{25,9},{2,18},{10... | collective-permute-start | bytes 804872 | tf_op jit(solution)/shard_map/ppermute | solution.py:427
  16.1 1.2 %collective-permute-start.7 = (f32[520,128]{1,0:T(8,128)S(1)}, f32[520,128]{1,0:T(8,128)S(1)}, u32[]{:S(2)}, u32[]{:S(2)}) collective-permute-start(f32[520,128]{1,0:T(8,128)S(1)} %get-tuple-element.83), channel_id=1, source_target_pairs={{0,1},{1,0},{2,3},{3,2},{4,5},{5,4},{6,7},{7,6},{8,9},{9,8},{10,11... | collective-permute-start | bytes 798728 | tf_op jit(solution)/shard_map/ppermute | solution.py:427
  17.3 3.1 %tables.8 = (bf16[32,128,128]{2,1,0:T(8,128)(2,1)S(1)}, bf16[32,128,128]{2,1,0:T(8,128)(2,1)S(1)}, f32[384,128]{1,0:T(8,128)S(1)}) custom-call(f32[32,128]{1,0:T(8,128)S(1)} %get-tuple-element.68.refs_0_, s32[512,128]{1,0:T(8,128)S(1)} %get-tuple-element.69.refs_1_, s32[512,128]{1,0:T(8,128)S(1)} %get-tuple-element.70.refs_2_, ...), custom_call_target="tpu_custom_call" | custom-call | flops 268435456 | bytes 10240000 | tf_op jit(solution)/shard_map/tables/pallas_call | solution.py:370
  20.4 3.1 %tables.9 = (bf16[32,128,128]{2,1,0:T(8,128)(2,1)S(1)}, bf16[32,128,128]{2,1,0:T(8,128)(2,1)S(1)}, f32[384,128]{1,0:T(8,128)S(1)}) custom-call(f32[32,128]{1,0:T(8,128)S(1)} %get-tuple-element.68.refs_0_, s32[512,128]{1,0:T(8,128)S(1)} %get-tuple-element.69.refs_1_, s32[512,128]{1,0:T(8,128)S(1)} %get-tuple-element.70.refs_2_, ...), custom_call_target="tpu_custom_call" | custom-call | flops 268435456 | bytes 10240000 | tf_op jit(solution)/shard_map/tables/pallas_call | solution.py:370
  23.5 0.0 collective-permute-done
  23.6 0.3 collective-permute-start.3
  23.9 0.2 collective-permute-start.4
  24.1 2.2 %collective-permute-start.5 = (f32[1,512]{1,0:T(1,128)S(1)}, f32[1,512]{1,0:T(1,128)S(1)}, u32[]{:S(2)}, u32[]{:S(2)}) collective-permute-start(f32[1,512]{1,0:T(1,128)S(1)} %add_add_fusion.refs_4_.refs_1_), channel_id=1, source_target_pairs={{0,17},{1,16},{2,19},{3,18},{4,21},{5,20},{6,23},{7,22},{8,25},{9,... | collective-permute-start | bytes 6152 | tf_op jit(solution)/shard_map/ppermute | solution.py:529
  26.3 3.0 %tables.10 = (bf16[32,128,128]{2,1,0:T(8,128)(2,1)S(1)}, bf16[32,128,128]{2,1,0:T(8,128)(2,1)S(1)}, f32[384,128]{1,0:T(8,128)S(1)}) custom-call(f32[32,128]{1,0:T(8,128)S(1)} %get-tuple-element.68.refs_0_, s32[512,128]{1,0:T(8,128)S(1)} %get-tuple-element.69.refs_1_, s32[512,128]{1,0:T(8,128)S(1)} %get-tuple-element.70.refs_2_, ...), custom_call_target="tpu_custom_call" | custom-call | flops 268435456 | bytes 10240000 | tf_op jit(solution)/shard_map/tables/pallas_call | solution.py:370
  29.3 3.1 %tables.11 = (bf16[32,128,128]{2,1,0:T(8,128)(2,1)S(1)}, bf16[32,128,128]{2,1,0:T(8,128)(2,1)S(1)}, f32[384,128]{1,0:T(8,128)S(1)}) custom-call(f32[32,128]{1,0:T(8,128)S(1)} %get-tuple-element.68.refs_0_, s32[512,128]{1,0:T(8,128)S(1)} %get-tuple-element.69.refs_1_, s32[512,128]{1,0:T(8,128)S(1)} %get-tuple-element.70.refs_2_, ...), custom_call_target="tpu_custom_call" | custom-call | flops 268435456 | bytes 10240000 | tf_op jit(solution)/shard_map/tables/pallas_call | solution.py:370
  32.4 0.0 collective-permute-done.7.refs_6_.refs_3_
  32.4 0.0 collective-permute-done.6.refs_5_.refs_6_
  32.4 1.6 %rest.1 = (bf16[512,512]{1,0:T(8,128)(2,1)S(1)}, bf16[512,512]{1,0:T(8,128)(2,1)S(1)}, bf16[512,512]{1,0:T(8,128)(2,1)S(1)}, bf16[512,512]{1,0:T(8,128)(2,1)S(1)...) custom-call(bf16[512,128]{1,0:T(8,128)(2,1)S(1)} %get-tuple-element.78.refs_0_, ...), custom_call_target="tpu_custom_call" | custom-call | flops 201326592 | bytes 3145728 | tf_op jit(solution)/shard_map/rest/pallas_call | solution.py:226
  34.1 0.0 collective-permute-done.3.refs_2_
  34.1 0.0 collective-permute-done.4.refs_3_
  34.1 1.1 %cols.2 = (f32[1,1024]{1,0:T(1,128)}, f32[1,1024]{1,0:T(1,128)S(1)}) custom-call(f32[4,128]{1,0:T(4,128)S(1)} %get-tuple-element.65.refs_0_, f32[1,512]{1,0:T(1,128)S(1)} %add_add_fusion.refs_4_.refs_1_, f32[1,512]{1,0:T(1,128)S(1)} %collective-permute-done.3.refs_2_, f32[1,512]{1,0:T(1,128)S(1)} %collective-permute-done.4.refs_3_, ...), custom_call_target="tpu_custom_call" | custom-call | tf_op jit(solution)/shard_map/cols/pallas_call | solution.py:276
  35.2 0.2 collective-permute-start.13
  35.5 1.2 %collective-permute-start.12 = (f32[384,128]{1,0:T(8,128)S(1)}, f32[384,128]{1,0:T(8,128)S(1)}, u32[]{:S(2)}, u32[]{:S(2)}) collective-permute-start(f32[384,128]{1,0:T(8,128)S(1)} %get-tuple-element.94), channel_id=1, source_target_pairs={{0,16},{8,24},{16,0},{24,8},{1,17},{9,25},{17,1},{25,9},{2,18},{10... | collective-permute-start | bytes 589832 | tf_op jit(solution)/shard_map/ppermute | solution.py:427
  36.7 0.2 collective-permute-start.18
  36.9 1.2 %collective-permute-start.19 = (f32[384,128]{1,0:T(8,128)S(1)}, f32[384,128]{1,0:T(8,128)S(1)}, u32[]{:S(2)}, u32[]{:S(2)}) collective-permute-start(f32[384,128]{1,0:T(8,128)S(1)} %get-tuple-element.116.refs_7_.refs_14_), channel_id=1, source_target_pairs={{0,16},{8,24},{16,0},{24,8},{1,17},{9,25},{17,1},{25,9},{2,18},{10... | collective-permute-start | bytes 589832 | tf_op jit(solution)/shard_map/ppermute | solution.py:427
  38.2 4.0 %collective-permute-start.8 = (f32[1,1024]{1,0:T(1,128)S(1)}, f32[1,1024]{1,0:T(1,128)S(1)}, u32[]{:S(2)}, u32[]{:S(2)}) collective-permute-start(f32[1,1024]{1,0:T(1,128)S(1)} %get-tuple-element.92.refs_1_), channel_id=1, source_target_pairs={{0,8},{8,0},{16,24},{24,16},{1,9},{9,1},{17,25},{25,17},{2,10},{10... | collective-permute-start | bytes 12296 | tf_op jit(solution)/shard_map/ppermute | solution.py:427
  42.2 0.8 %collective-permute-done.8.refs_2_ = f32[1,1024]{1,0:T(1,128)S(1)} collective-permute-done((f32[1,1024]{1,0:T(1,128)S(1)}, f32[1,1024]{1,0:T(1,128)S(1)}, u32[]{:S(2)}, u32[]{:S(2)}) %collective-permute-start.8) | collective-permute-done | bytes 4128 | tf_op jit(solution)/shard_map/ppermute | solution.py:427
  43.0 1.6 %rows.2 = (f32[1,512]{1,0:T(1,128)}, f32[1,1024]{1,0:T(1,128)S(1)}) custom-call(f32[4,128]{1,0:T(4,128)S(1)} %get-tuple-element.66.refs_0_, f32[1,1024]{1,0:T(1,128)S(1)} %get-tuple-element.92.refs_1_, f32[1,1024]{1,0:T(1,128)S(1)} %collective-permute-done.8.refs_2_, f32[520,128]{1,0:T(8,128)S(1)} %collective-permute-done.7.refs_6_.refs_3_, ...), custom_call_target="tpu_custom_call" | custom-call | tf_op jit(solution)/shard_map/rows/pallas_call | solution.py:307
  44.6 0.1 collective-permute-start.10
  44.7 0.0 collective-permute-done.13.refs_1_
  44.7 2.4 %collective-permute-start.11 = (f32[1,1024]{1,0:T(1,128)S(1)}, f32[1,1024]{1,0:T(1,128)S(1)}, u32[]{:S(2)}, u32[]{:S(2)}) collective-permute-start(f32[1,1024]{1,0:T(1,128)S(1)} %get-tuple-element.93.refs_2_.refs_1_), channel_id=1, source_target_pairs={{0,6},{1,7},{2,0},{3,1},{4,2},{5,3},{6,4},{7,5},{8,14},{9,15},{10,... | collective-permute-start | bytes 12296 | tf_op jit(solution)/shard_map/ppermute | solution.py:427
  47.1 3.0 %tables.12 = (bf16[32,128,128]{2,1,0:T(8,128)(2,1)S(1)}, bf16[32,128,128]{2,1,0:T(8,128)(2,1)S(1)}, f32[8,128]{1,0:T(8,128)S(1)}) custom-call(f32[32,128]{1,0:T(8,128)S(1)} %get-tuple-element.68.refs_0_, f32[384,128]{1,0:T(8,128)S(1)} %collective-permute-done.13.refs_1_, f32[1,1024]{1,0:T(1,128)S(1)} %get-tuple-element.93.refs_2_.refs_1_), custom_call_target="tpu_custom_call" | custom-call | flops 268435456 | bytes 10240000 | tf_op jit(solution)/shard_map/tables/pallas_call | solution.py:370
  50.2 0.2 collective-permute-start.9
  50.4 3.1 %tables.13 = (bf16[32,128,128]{2,1,0:T(8,128)(2,1)S(1)}, bf16[32,128,128]{2,1,0:T(8,128)(2,1)S(1)}, f32[8,128]{1,0:T(8,128)S(1)}) custom-call(f32[32,128]{1,0:T(8,128)S(1)} %get-tuple-element.68.refs_0_, f32[384,128]{1,0:T(8,128)S(1)} %collective-permute-done.12.refs_1_, f32[8,128]{1,0:T(8,128)S(1)} %get-tuple-element.96.refs_2_), custom_call_target="tpu_custom_call" | custom-call | flops 268435456 | bytes 10240000 | tf_op jit(solution)/shard_map/tables/pallas_call | solution.py:370
  53.5 0.0 collective-permute-done.11.refs_4_
  53.5 1.1 %collective-permute-done.9.refs_2_ = f32[1,1024]{1,0:T(1,128)S(1)} collective-permute-done((f32[1,1024]{1,0:T(1,128)S(1)}, f32[1,1024]{1,0:T(1,128)S(1)}, u32[]{:S(2)}, u32[]{:S(2)}) %collective-permute-start.9) | collective-permute-done | bytes 4128 | tf_op jit(solution)/shard_map/ppermute | solution.py:427
  54.7 0.7 cols.3
  55.3 2.1 %collective-permute-start.14 = (f32[1,1024]{1,0:T(1,128)S(1)}, f32[1,1024]{1,0:T(1,128)S(1)}, u32[]{:S(2)}, u32[]{:S(2)}) collective-permute-start(f32[1,1024]{1,0:T(1,128)S(1)} %get-tuple-element.99.refs_1_), channel_id=1, source_target_pairs={{0,8},{8,0},{16,24},{24,16},{1,9},{9,1},{17,25},{25,17},{2,10},{10... | collective-permute-start | bytes 12296 | tf_op jit(solution)/shard_map/ppermute | solution.py:427
  57.5 0.8 %collective-permute-done.14.refs_2_ = f32[1,1024]{1,0:T(1,128)S(1)} collective-permute-done((f32[1,1024]{1,0:T(1,128)S(1)}, f32[1,1024]{1,0:T(1,128)S(1)}, u32[]{:S(2)}, u32[]{:S(2)}) %collective-permute-start.14) | collective-permute-done | bytes 4128 | tf_op jit(solution)/shard_map/ppermute | solution.py:427
  58.3 1.6 %rows.3 = (f32[1,512]{1,0:T(1,128)}, f32[1,1024]{1,0:T(1,128)S(1)}) custom-call(f32[4,128]{1,0:T(4,128)S(1)} %get-tuple-element.66.refs_0_, f32[1,1024]{1,0:T(1,128)S(1)} %get-tuple-element.99.refs_1_, f32[1,1024]{1,0:T(1,128)S(1)} %collective-permute-done.14.refs_2_, f32[520,128]{1,0:T(8,128)S(1)} %collective-permute-done.7.refs_6_.refs_3_, ...), custom_call_target="tpu_custom_call" | custom-call | tf_op jit(solution)/shard_map/rows/pallas_call | solution.py:307
  59.9 0.0 collective-permute-start.15
  59.9 1.5 %collective-permute-start.16 = (f32[1,1024]{1,0:T(1,128)S(1)}, f32[1,1024]{1,0:T(1,128)S(1)}, u32[]{:S(2)}, u32[]{:S(2)}) collective-permute-start(f32[1,1024]{1,0:T(1,128)S(1)} %get-tuple-element.100.refs_2_), channel_id=1, source_target_pairs={{0,4},{1,5},{2,6},{3,7},{4,0},{5,1},{6,2},{7,3},{8,12},{9,13},{10,... | collective-permute-start | bytes 12296 | tf_op jit(solution)/shard_map/ppermute | solution.py:427
  61.4 1.7 %collective-permute-start.17 = (f32[1,1024]{1,0:T(1,128)S(1)}, f32[1,1024]{1,0:T(1,128)S(1)}, u32[]{:S(2)}, u32[]{:S(2)}) collective-permute-start(f32[1,1024]{1,0:T(1,128)S(1)} %get-tuple-element.100.refs_2_), channel_id=1, source_target_pairs={{0,6},{1,7},{2,0},{3,1},{4,2},{5,3},{6,4},{7,5},{8,14},{9,15},{10,... | collective-permute-start | bytes 12296 | tf_op jit(solution)/shard_map/ppermute | solution.py:427
  63.2 0.0 collective-permute-done.18.refs_1_
  63.2 3.1 %tables.14 = (bf16[32,128,128]{2,1,0:T(8,128)(2,1)S(1)}, bf16[32,128,128]{2,1,0:T(8,128)(2,1)S(1)}, f32[8,128]{1,0:T(8,128)S(1)}) custom-call(f32[32,128]{1,0:T(8,128)S(1)} %get-tuple-element.68.refs_0_, f32[384,128]{1,0:T(8,128)S(1)} %collective-permute-done.18.refs_1_, f32[1,1024]{1,0:T(1,128)S(1)} %get-tuple-element.100.refs_2_), custom_call_target="tpu_custom_call" | custom-call | flops 268435456 | bytes 10240000 | tf_op jit(solution)/shard_map/tables/pallas_call | solution.py:370
  66.2 0.0 collective-permute-done.19.refs_1_
  66.3 3.1 %tables.15 = (bf16[32,128,128]{2,1,0:T(8,128)(2,1)S(1)}, bf16[32,128,128]{2,1,0:T(8,128)(2,1)S(1)}, f32[8,128]{1,0:T(8,128)S(1)}) custom-call(f32[32,128]{1,0:T(8,128)S(1)} %get-tuple-element.68.refs_0_, f32[384,128]{1,0:T(8,128)S(1)} %collective-permute-done.19.refs_1_, f32[8,128]{1,0:T(8,128)S(1)} %get-tuple-element.117.refs_2_), custom_call_target="tpu_custom_call" | custom-call | flops 268435456 | bytes 10240000 | tf_op jit(solution)/shard_map/tables/pallas_call | solution.py:370
  69.4 0.0 collective-permute-done.15.refs_3_
  69.4 0.0 collective-permute-done.17.refs_5_
  69.4 2.0 %spread.2 = (f32[16,32,128]{2,1,0:T(8,128)S(1)}, f32[1,512]{1,0:T(1,128)}) custom-call(s32[4,128]{1,0:T(4,128)S(1)} %get-tuple-element.64.refs_0_, f32[1,1024]{1,0:T(1,128)S(1)} %get-tuple-element.98.refs_1_, f32[1,1024]{1,0:T(1,128)S(1)} %get-tuple-element.100.refs_2_, f32[1,1024]{1,0:T(1,128)S(1)} %collective-permute-done.15.refs_3_, ...), custom_call_target="tpu_custom_call" | custom-call | tf_op jit(solution)/shard_map/spread/pallas_call | solution.py:413
  71.4 0.9 %collective-permute-start.20 = (f32[16,32,128]{2,1,0:T(8,128)S(1)}, f32[16,32,128]{2,1,0:T(8,128)S(1)}, u32[]{:S(2)}, u32[]{:S(2)}) collective-permute-start(f32[16,32,128]{2,1,0:T(8,128)S(1)} %get-tuple-element.124), channel_id=1, source_target_pairs={{0,8},{8,0},{16,24},{24,16},{1,9},{9,1},{17,25},{25,17},{2,10},{10... | collective-permute-start | bytes 786440 | tf_op jit(solution)/shard_map/ppermute | solution.py:427
  72.3 2.0 %spread.3 = (f32[16,32,128]{2,1,0:T(8,128)S(1)}, f32[1,512]{1,0:T(1,128)}) custom-call(s32[4,128]{1,0:T(4,128)S(1)} %get-tuple-element.64.refs_0_, f32[1,1024]{1,0:T(1,128)S(1)} %get-tuple-element.98.refs_1_, f32[1,1024]{1,0:T(1,128)S(1)} %get-tuple-element.100.refs_2_, f32[1,1024]{1,0:T(1,128)S(1)} %collective-permute-done.15.refs_3_, ...), custom_call_target="tpu_custom_call" | custom-call | tf_op jit(solution)/shard_map/spread/pallas_call | solution.py:413
  74.3 0.7 add.15
  (20 shorter events, 0.0 us)
Async XLA Ops:
  0.6 0.7 copy-start.11
  0.6 0.7 copy-start.10
  0.7 0.7 copy-start.9
  0.7 0.7 copy-start.8
  0.7 0.7 copy-start.7
  1.4 0.9 %copy-start = (s32[512,128]{1,0:T(8,128)S(1)}, s32[512,128]{1,0:T(8,128)}, u32[]{:S(2)}) copy-start(s32[512,128]{1,0:T(8,128)} %m_hbm.1) | copy-start | bytes 786436
  2.3 0.9 %copy-start.1 = (s32[512,128]{1,0:T(8,128)S(1)}, s32[512,128]{1,0:T(8,128)}, u32[]{:S(2)}) copy-start(s32[512,128]{1,0:T(8,128)} %d_hbm.1) | copy-start | bytes 786436
  3.3 0.9 %copy-start.2 = (f32[512,128]{1,0:T(8,128)S(1)}, f32[512,128]{1,0:T(8,128)}, u32[]{:S(2)}) copy-start(f32[512,128]{1,0:T(8,128)} %a_hbm.1) | copy-start | bytes 786436
  4.2 0.9 %copy-start.3 = (bf16[512,128]{1,0:T(8,128)(2,1)S(1)}, bf16[512,128]{1,0:T(8,128)(2,1)}, u32[]{:S(2)}) copy-start(bf16[512,128]{1,0:T(8,128)(2,1)} %x_hbm.1) | copy-start | bytes 393220
  5.1 0.9 %copy-start.4 = (bf16[512,128]{1,0:T(8,128)(2,1)S(1)}, bf16[512,128]{1,0:T(8,128)(2,1)}, u32[]{:S(2)}) copy-start(bf16[512,128]{1,0:T(8,128)(2,1)} %y_hbm.1) | copy-start | bytes 393220
  6.0 0.8 %copy-start.5 = (f32[4,32,128]{2,1,0:T(8,128)S(1)}, f32[4,32,128]{2,1,0:T(8,128)}, u32[]{:S(2)}) copy-start(f32[4,32,128]{2,1,0:T(8,128)} %constant.2.clone.f_hbm) | copy-start | bytes 196612
  6.9 0.7 copy-start.6
  9.3 14.2 %collective-permute-start = (f32[1,512]{1,0:T(1,128)S(1)}, f32[1,512]{1,0:T(1,128)S(1)}, u32[]{:S(2)}, u32[]{:S(2)}) collective-permute-start(f32[1,512]{1,0:T(1,128)S(1)} %get-tuple-element.67.refs_4_), channel_id=1, source_target_pairs={{0,2},{1,3},{2,4},{3,5},{4,6},{5,7},{6,0},{7,1},{8,10},{9,11},{10,... | collective-permute-start | bytes 6152 | tf_op jit(solution)/shard_map/ppermute | solution.py:427
  11.5 12.1 %collective-permute-start.1 = (f32[1,512]{1,0:T(1,128)S(1)}, f32[1,512]{1,0:T(1,128)S(1)}, u32[]{:S(2)}, u32[]{:S(2)}) collective-permute-start(f32[1,512]{1,0:T(1,128)S(1)} %get-tuple-element.67.refs_4_), channel_id=1, source_target_pairs={{0,4},{1,5},{2,6},{3,7},{4,0},{5,1},{6,2},{7,3},{8,12},{9,13},{10,... | collective-permute-start | bytes 6152 | tf_op jit(solution)/shard_map/ppermute | solution.py:427
  13.8 9.8 %collective-permute-start.2 = (f32[1,512]{1,0:T(1,128)S(1)}, f32[1,512]{1,0:T(1,128)S(1)}, u32[]{:S(2)}, u32[]{:S(2)}) collective-permute-start(f32[1,512]{1,0:T(1,128)S(1)} %get-tuple-element.67.refs_4_), channel_id=1, source_target_pairs={{0,6},{1,7},{2,0},{3,1},{4,2},{5,3},{6,4},{7,5},{8,14},{9,15},{10,... | collective-permute-start | bytes 6152 | tf_op jit(solution)/shard_map/ppermute | solution.py:427
  14.8 17.6 %collective-permute-start.6 = (f32[524,128]{1,0:T(8,128)S(1)}, f32[524,128]{1,0:T(8,128)S(1)}, u32[]{:S(2)}, u32[]{:S(2)}) collective-permute-start(f32[524,128]{1,0:T(8,128)S(1)} %get-tuple-element.75), channel_id=1, source_target_pairs={{0,16},{8,24},{16,0},{24,8},{1,17},{9,25},{17,1},{25,9},{2,18},{10... | collective-permute-start | bytes 804872 | tf_op jit(solution)/shard_map/ppermute | solution.py:427
  16.1 16.3 %collective-permute-start.7 = (f32[520,128]{1,0:T(8,128)S(1)}, f32[520,128]{1,0:T(8,128)S(1)}, u32[]{:S(2)}, u32[]{:S(2)}) collective-permute-start(f32[520,128]{1,0:T(8,128)S(1)} %get-tuple-element.83), channel_id=1, source_target_pairs={{0,1},{1,0},{2,3},{3,2},{4,5},{5,4},{6,7},{7,6},{8,9},{9,8},{10,11... | collective-permute-start | bytes 798728 | tf_op jit(solution)/shard_map/ppermute | solution.py:427
  23.6 10.5 %collective-permute-start.3 = (f32[1,512]{1,0:T(1,128)S(1)}, f32[1,512]{1,0:T(1,128)S(1)}, u32[]{:S(2)}, u32[]{:S(2)}) collective-permute-start(f32[1,512]{1,0:T(1,128)S(1)} %add_add_fusion.refs_4_.refs_1_), channel_id=1, source_target_pairs={{0,1},{1,0},{2,3},{3,2},{4,5},{5,4},{6,7},{7,6},{8,9},{9,8},{10,11... | collective-permute-start | bytes 6152 | tf_op jit(solution)/shard_map/ppermute | solution.py:427
  23.9 10.2 %collective-permute-start.4 = (f32[1,512]{1,0:T(1,128)S(1)}, f32[1,512]{1,0:T(1,128)S(1)}, u32[]{:S(2)}, u32[]{:S(2)}) collective-permute-start(f32[1,512]{1,0:T(1,128)S(1)} %add_add_fusion.refs_4_.refs_1_), channel_id=1, source_target_pairs={{0,16},{1,17},{2,18},{3,19},{4,20},{5,21},{6,22},{7,23},{8,24},{9,... | collective-permute-start | bytes 6152 | tf_op jit(solution)/shard_map/ppermute | solution.py:529
  24.1 10.0 %collective-permute-start.5 = (f32[1,512]{1,0:T(1,128)S(1)}, f32[1,512]{1,0:T(1,128)S(1)}, u32[]{:S(2)}, u32[]{:S(2)}) collective-permute-start(f32[1,512]{1,0:T(1,128)S(1)} %add_add_fusion.refs_4_.refs_1_), channel_id=1, source_target_pairs={{0,17},{1,16},{2,19},{3,18},{4,21},{5,20},{6,23},{7,22},{8,25},{9,... | collective-permute-start | bytes 6152 | tf_op jit(solution)/shard_map/ppermute | solution.py:529
  35.2 9.5 %collective-permute-start.13 = (f32[384,128]{1,0:T(8,128)S(1)}, f32[384,128]{1,0:T(8,128)S(1)}, u32[]{:S(2)}, u32[]{:S(2)}) collective-permute-start(f32[384,128]{1,0:T(8,128)S(1)} %get-tuple-element.95.refs_4_), channel_id=1, source_target_pairs={{0,16},{8,24},{16,0},{24,8},{1,17},{9,25},{17,1},{25,9},{2,18},{10... | collective-permute-start | bytes 589832 | tf_op jit(solution)/shard_map/ppermute | solution.py:427
  35.5 14.7 %collective-permute-start.12 = (f32[384,128]{1,0:T(8,128)S(1)}, f32[384,128]{1,0:T(8,128)S(1)}, u32[]{:S(2)}, u32[]{:S(2)}) collective-permute-start(f32[384,128]{1,0:T(8,128)S(1)} %get-tuple-element.94), channel_id=1, source_target_pairs={{0,16},{8,24},{16,0},{24,8},{1,17},{9,25},{17,1},{25,9},{2,18},{10... | collective-permute-start | bytes 589832 | tf_op jit(solution)/shard_map/ppermute | solution.py:427
  36.7 26.4 %collective-permute-start.18 = (f32[384,128]{1,0:T(8,128)S(1)}, f32[384,128]{1,0:T(8,128)S(1)}, u32[]{:S(2)}, u32[]{:S(2)}) collective-permute-start(f32[384,128]{1,0:T(8,128)S(1)} %get-tuple-element.113.refs_4_), channel_id=1, source_target_pairs={{0,16},{8,24},{16,0},{24,8},{1,17},{9,25},{17,1},{25,9},{2,18},{10... | collective-permute-start | bytes 589832 | tf_op jit(solution)/shard_map/ppermute | solution.py:427
  36.9 29.3 %collective-permute-start.19 = (f32[384,128]{1,0:T(8,128)S(1)}, f32[384,128]{1,0:T(8,128)S(1)}, u32[]{:S(2)}, u32[]{:S(2)}) collective-permute-start(f32[384,128]{1,0:T(8,128)S(1)} %get-tuple-element.116.refs_7_.refs_14_), channel_id=1, source_target_pairs={{0,16},{8,24},{16,0},{24,8},{1,17},{9,25},{17,1},{25,9},{2,18},{10... | collective-permute-start | bytes 589832 | tf_op jit(solution)/shard_map/ppermute | solution.py:427
  38.2 4.9 %collective-permute-start.8 = (f32[1,1024]{1,0:T(1,128)S(1)}, f32[1,1024]{1,0:T(1,128)S(1)}, u32[]{:S(2)}, u32[]{:S(2)}) collective-permute-start(f32[1,1024]{1,0:T(1,128)S(1)} %get-tuple-element.92.refs_1_), channel_id=1, source_target_pairs={{0,8},{8,0},{16,24},{24,16},{1,9},{9,1},{17,25},{25,17},{2,10},{10... | collective-permute-start | bytes 12296 | tf_op jit(solution)/shard_map/ppermute | solution.py:427
  44.6 8.9 %collective-permute-start.10 = (f32[1,1024]{1,0:T(1,128)S(1)}, f32[1,1024]{1,0:T(1,128)S(1)}, u32[]{:S(2)}, u32[]{:S(2)}) collective-permute-start(f32[1,1024]{1,0:T(1,128)S(1)} %get-tuple-element.93.refs_2_.refs_1_), channel_id=1, source_target_pairs={{0,4},{1,5},{2,6},{3,7},{4,0},{5,1},{6,2},{7,3},{8,12},{9,13},{10,... | collective-permute-start | bytes 12296 | tf_op jit(solution)/shard_map/ppermute | solution.py:427
  44.7 8.8 %collective-permute-start.11 = (f32[1,1024]{1,0:T(1,128)S(1)}, f32[1,1024]{1,0:T(1,128)S(1)}, u32[]{:S(2)}, u32[]{:S(2)}) collective-permute-start(f32[1,1024]{1,0:T(1,128)S(1)} %get-tuple-element.93.refs_2_.refs_1_), channel_id=1, source_target_pairs={{0,6},{1,7},{2,0},{3,1},{4,2},{5,3},{6,4},{7,5},{8,14},{9,15},{10,... | collective-permute-start | bytes 12296 | tf_op jit(solution)/shard_map/ppermute | solution.py:427
  50.2 4.5 %collective-permute-start.9 = (f32[1,1024]{1,0:T(1,128)S(1)}, f32[1,1024]{1,0:T(1,128)S(1)}, u32[]{:S(2)}, u32[]{:S(2)}) collective-permute-start(f32[1,1024]{1,0:T(1,128)S(1)} %get-tuple-element.93.refs_2_.refs_1_), channel_id=1, source_target_pairs={{0,2},{1,3},{2,4},{3,5},{4,6},{5,7},{6,0},{7,1},{8,10},{9,11},{10,... | collective-permute-start | bytes 12296 | tf_op jit(solution)/shard_map/ppermute | solution.py:427
  55.3 2.9 %collective-permute-start.14 = (f32[1,1024]{1,0:T(1,128)S(1)}, f32[1,1024]{1,0:T(1,128)S(1)}, u32[]{:S(2)}, u32[]{:S(2)}) collective-permute-start(f32[1,1024]{1,0:T(1,128)S(1)} %get-tuple-element.99.refs_1_), channel_id=1, source_target_pairs={{0,8},{8,0},{16,24},{24,16},{1,9},{9,1},{17,25},{25,17},{2,10},{10... | collective-permute-start | bytes 12296 | tf_op jit(solution)/shard_map/ppermute | solution.py:427
  59.9 9.5 %collective-permute-start.15 = (f32[1,1024]{1,0:T(1,128)S(1)}, f32[1,1024]{1,0:T(1,128)S(1)}, u32[]{:S(2)}, u32[]{:S(2)}) collective-permute-start(f32[1,1024]{1,0:T(1,128)S(1)} %get-tuple-element.100.refs_2_), channel_id=1, source_target_pairs={{0,2},{1,3},{2,4},{3,5},{4,6},{5,7},{6,0},{7,1},{8,10},{9,11},{10,... | collective-permute-start | bytes 12296 | tf_op jit(solution)/shard_map/ppermute | solution.py:427
  59.9 9.5 %collective-permute-start.16 = (f32[1,1024]{1,0:T(1,128)S(1)}, f32[1,1024]{1,0:T(1,128)S(1)}, u32[]{:S(2)}, u32[]{:S(2)}) collective-permute-start(f32[1,1024]{1,0:T(1,128)S(1)} %get-tuple-element.100.refs_2_), channel_id=1, source_target_pairs={{0,4},{1,5},{2,6},{3,7},{4,0},{5,1},{6,2},{7,3},{8,12},{9,13},{10,... | collective-permute-start | bytes 12296 | tf_op jit(solution)/shard_map/ppermute | solution.py:427
  61.4 7.9 %collective-permute-start.17 = (f32[1,1024]{1,0:T(1,128)S(1)}, f32[1,1024]{1,0:T(1,128)S(1)}, u32[]{:S(2)}, u32[]{:S(2)}) collective-permute-start(f32[1,1024]{1,0:T(1,128)S(1)} %get-tuple-element.100.refs_2_), channel_id=1, source_target_pairs={{0,6},{1,7},{2,0},{3,1},{4,2},{5,3},{6,4},{7,5},{8,14},{9,15},{10,... | collective-permute-start | bytes 12296 | tf_op jit(solution)/shard_map/ppermute | solution.py:427
  71.4 2.9 %collective-permute-start.20 = (f32[16,32,128]{2,1,0:T(8,128)S(1)}, f32[16,32,128]{2,1,0:T(8,128)S(1)}, u32[]{:S(2)}, u32[]{:S(2)}) collective-permute-start(f32[16,32,128]{2,1,0:T(8,128)S(1)} %get-tuple-element.124), channel_id=1, source_target_pairs={{0,8},{8,0},{16,24},{24,16},{1,9},{9,1},{17,25},{25,17},{2,10},{10... | collective-permute-start | bytes 786440 | tf_op jit(solution)/shard_map/ppermute | solution.py:427

commit v4 on v3

--- a/solution.py
+++ b/solution.py
@@ -192,7 +192,14 @@
         ],
         compiler_params=PARAMS,
         name="first",
-    )(x, y, row(rr), row(cr), penalty, block(rr), block(seg), block(mass), block(cr), block(cm), table, *records)
+    )(
+        *[
+            pltpu.with_memory_space_constraint(arg, pltpu.HBM)
+            for arg in (
+                x, y, row(rr), row(cr), penalty, block(rr), block(seg), block(mass), block(cr), block(cm), table, *records
+            )
+        ]
+    )
 
 
 def flat(block):

time: 75.4 us -> 68.7 us (0.911)
  local copies, waits for them, and re-layouts: 6.92 us -> 0 us
    unnamed x24 -> x0, local copies, waits for them, and re-layouts: 6.92 us -> none
  transfers between devices with their start and end apart: 21 -> 21, of which waited for: 3 -> 3; matrix products, arithmetic and copies ran while one was open for 0% -> 0% of each run, Pallas kernels for 43% -> 47%
where the time goes in v4:
time: 68.7 us; the launch traced here: 68.6 us
  Pallas kernels  37.5 us (55%)
  starting transfers between devices  26.7 us (39%)
  waiting for transfers between devices  2.82 us (4%)
  between operations  0.87 us (1%)
  other arithmetic  0.75 us (1%)
    pallas_call x8, Pallas kernels, table_call(): pl.pallas_call(lambda *refs: body(*refs[:1 + len(args)], *refs[-3:]), in_...  24.6 us
    ppermute x19, starting transfers between devices, move(): lax.ppermute(x, axis, [(b * pair + r, (b + step) % blocks * pair + (r ^ f...  24.3 us
    pallas_call x2, Pallas kernels, spread_call(): pl.pallas_call(lambda *refs: spread_body(n, t_first, t_count, len(partial...  3.97 us
    pallas_call x2, Pallas kernels, rows_call(): pl.pallas_call(lambda *refs: rows_body(m, len(packs), len(partials), len(...  3.21 us
    ppermute x19, waiting for transfers between devices, move(): lax.ppermute(x, axis, [(b * pair + r, (b + step) % blocks * pair + (r ^ f...  2.82 us
    ppermute x2, starting transfers between devices, both_axes(): return lax.ppermute(x, ('cohort', 'cell'), pairs)  2.4 us
    pallas_call x1, Pallas kernels, first_call(): pl.pallas_call(first_body, in_specs=[HBM] * 14, out_specs=[VMEM] * len(ou...  2.25 us
    pallas_call x2, Pallas kernels, cols_call(): pl.pallas_call(lambda *refs: cols_body(n, [len(group) for group in partia...  1.81 us
  transfers between devices with their start and end apart: 21, of which 3 were waited for; matrix products, arithmetic and copies ran while one was open for 0% of the time, Pallas kernels for 47%

profile of v4, /device:TPU:1, one launch (start us, length us, event | category | flops | bytes accessed | tf_op | source)
XLA Modules:
  0.0 68.6 jit_solution(1418821733676081633)
XLA Ops:
  0.6 2.3 %first.1 = (bf16[512,512]{1,0:T(8,128)(2,1)S(1)}, bf16[512,512]{1,0:T(8,128)(2,1)S(1)}, f32[1,512]{1,0:T(1,128)S(1)}, f32[524,128]{1,0:T(8,128)S(1)}, f32[520,12...) custom-call(bf16[512,128]{1,0:T(8,128)(2,1)} %x_hbm.1, ...), custom_call_target="tpu_custom_call" | custom-call | tf_op jit(solution)/shard_map/first/pallas_call | solution.py:182
  2.9 2.2 %collective-permute-start = (f32[1,512]{1,0:T(1,128)S(1)}, f32[1,512]{1,0:T(1,128)S(1)}, u32[]{:S(2)}, u32[]{:S(2)}) collective-permute-start(f32[1,512]{1,0:T(1,128)S(1)} %get-tuple-element.67.refs_4_), channel_id=1, source_target_pairs={{0,2},{1,3},{2,4},{3,5},{4,6},{5,7},{6,0},{7,1},{8,10},{9,11},{10,... | collective-permute-start | bytes 6152 | tf_op jit(solution)/shard_map/ppermute | solution.py:434
  5.1 2.3 %collective-permute-start.1 = (f32[1,512]{1,0:T(1,128)S(1)}, f32[1,512]{1,0:T(1,128)S(1)}, u32[]{:S(2)}, u32[]{:S(2)}) collective-permute-start(f32[1,512]{1,0:T(1,128)S(1)} %get-tuple-element.67.refs_4_), channel_id=1, source_target_pairs={{0,4},{1,5},{2,6},{3,7},{4,0},{5,1},{6,2},{7,3},{8,12},{9,13},{10,... | collective-permute-start | bytes 6152 | tf_op jit(solution)/shard_map/ppermute | solution.py:434
  7.4 1.1 %collective-permute-start.2 = (f32[1,512]{1,0:T(1,128)S(1)}, f32[1,512]{1,0:T(1,128)S(1)}, u32[]{:S(2)}, u32[]{:S(2)}) collective-permute-start(f32[1,512]{1,0:T(1,128)S(1)} %get-tuple-element.67.refs_4_), channel_id=1, source_target_pairs={{0,6},{1,7},{2,0},{3,1},{4,2},{5,3},{6,4},{7,5},{8,14},{9,15},{10,... | collective-permute-start | bytes 6152 | tf_op jit(solution)/shard_map/ppermute | solution.py:434
  8.4 1.2 %collective-permute-start.6 = (f32[524,128]{1,0:T(8,128)S(1)}, f32[524,128]{1,0:T(8,128)S(1)}, u32[]{:S(2)}, u32[]{:S(2)}) collective-permute-start(f32[524,128]{1,0:T(8,128)S(1)} %get-tuple-element.75), channel_id=1, source_target_pairs={{0,16},{8,24},{16,0},{24,8},{1,17},{9,25},{17,1},{25,9},{2,18},{10... | collective-permute-start | bytes 804872 | tf_op jit(solution)/shard_map/ppermute | solution.py:434
  9.7 1.2 %collective-permute-start.7 = (f32[520,128]{1,0:T(8,128)S(1)}, f32[520,128]{1,0:T(8,128)S(1)}, u32[]{:S(2)}, u32[]{:S(2)}) collective-permute-start(f32[520,128]{1,0:T(8,128)S(1)} %get-tuple-element.83), channel_id=1, source_target_pairs={{0,1},{1,0},{2,3},{3,2},{4,5},{5,4},{6,7},{7,6},{8,9},{9,8},{10,11... | collective-permute-start | bytes 798728 | tf_op jit(solution)/shard_map/ppermute | solution.py:434
  10.9 3.1 %tables.8 = (bf16[32,128,128]{2,1,0:T(8,128)(2,1)S(1)}, bf16[32,128,128]{2,1,0:T(8,128)(2,1)S(1)}, f32[384,128]{1,0:T(8,128)S(1)}) custom-call(f32[32,128]{1,0:T(8,128)S(1)} %get-tuple-element.68.refs_0_, s32[512,128]{1,0:T(8,128)S(1)} %get-tuple-element.69.refs_1_, s32[512,128]{1,0:T(8,128)S(1)} %get-tuple-element.70.refs_2_, ...), custom_call_target="tpu_custom_call" | custom-call | flops 268435456 | bytes 10240000 | tf_op jit(solution)/shard_map/tables/pallas_call | solution.py:377
  14.0 3.1 %tables.9 = (bf16[32,128,128]{2,1,0:T(8,128)(2,1)S(1)}, bf16[32,128,128]{2,1,0:T(8,128)(2,1)S(1)}, f32[384,128]{1,0:T(8,128)S(1)}) custom-call(f32[32,128]{1,0:T(8,128)S(1)} %get-tuple-element.68.refs_0_, s32[512,128]{1,0:T(8,128)S(1)} %get-tuple-element.69.refs_1_, s32[512,128]{1,0:T(8,128)S(1)} %get-tuple-element.70.refs_2_, ...), custom_call_target="tpu_custom_call" | custom-call | flops 268435456 | bytes 10240000 | tf_op jit(solution)/shard_map/tables/pallas_call | solution.py:377
  17.1 0.0 collective-permute-done
  17.1 0.0 collective-permute-done.1
  17.1 0.0 collective-permute-done.2
  17.2 0.3 collective-permute-start.3
  17.5 0.2 collective-permute-start.4
  17.7 2.2 %collective-permute-start.5 = (f32[1,512]{1,0:T(1,128)S(1)}, f32[1,512]{1,0:T(1,128)S(1)}, u32[]{:S(2)}, u32[]{:S(2)}) collective-permute-start(f32[1,512]{1,0:T(1,128)S(1)} %add_add_fusion.refs_4_.refs_1_), channel_id=1, source_target_pairs={{0,17},{1,16},{2,19},{3,18},{4,21},{5,20},{6,23},{7,22},{8,25},{9,... | collective-permute-start | bytes 6152 | tf_op jit(solution)/shard_map/ppermute | solution.py:536
  19.9 3.0 %tables.10 = (bf16[32,128,128]{2,1,0:T(8,128)(2,1)S(1)}, bf16[32,128,128]{2,1,0:T(8,128)(2,1)S(1)}, f32[384,128]{1,0:T(8,128)S(1)}) custom-call(f32[32,128]{1,0:T(8,128)S(1)} %get-tuple-element.68.refs_0_, s32[512,128]{1,0:T(8,128)S(1)} %get-tuple-element.69.refs_1_, s32[512,128]{1,0:T(8,128)S(1)} %get-tuple-element.70.refs_2_, ...), custom_call_target="tpu_custom_call" | custom-call | flops 268435456 | bytes 10240000 | tf_op jit(solution)/shard_map/tables/pallas_call | solution.py:377
  22.9 3.1 %tables.11 = (bf16[32,128,128]{2,1,0:T(8,128)(2,1)S(1)}, bf16[32,128,128]{2,1,0:T(8,128)(2,1)S(1)}, f32[384,128]{1,0:T(8,128)S(1)}) custom-call(f32[32,128]{1,0:T(8,128)S(1)} %get-tuple-element.68.refs_0_, s32[512,128]{1,0:T(8,128)S(1)} %get-tuple-element.69.refs_1_, s32[512,128]{1,0:T(8,128)S(1)} %get-tuple-element.70.refs_2_, ...), custom_call_target="tpu_custom_call" | custom-call | flops 268435456 | bytes 10240000 | tf_op jit(solution)/shard_map/tables/pallas_call | solution.py:377
  26.0 0.0 collective-permute-done.7.refs_6_.refs_3_
  26.0 0.0 collective-permute-done.6.refs_5_.refs_6_
  26.0 1.6 %rest.1 = (bf16[512,512]{1,0:T(8,128)(2,1)S(1)}, bf16[512,512]{1,0:T(8,128)(2,1)S(1)}, bf16[512,512]{1,0:T(8,128)(2,1)S(1)}, bf16[512,512]{1,0:T(8,128)(2,1)S(1)...) custom-call(bf16[512,128]{1,0:T(8,128)(2,1)S(1)} %get-tuple-element.78.refs_0_, ...), custom_call_target="tpu_custom_call" | custom-call | flops 201326592 | bytes 3145728 | tf_op jit(solution)/shard_map/rest/pallas_call | solution.py:233
  27.7 0.0 collective-permute-done.3.refs_2_
  27.7 0.0 collective-permute-done.4.refs_3_
  27.7 0.0 collective-permute-done.5.refs_4_
  27.7 1.1 %cols.2 = (f32[1,1024]{1,0:T(1,128)}, f32[1,1024]{1,0:T(1,128)S(1)}) custom-call(f32[4,128]{1,0:T(4,128)S(1)} %get-tuple-element.65.refs_0_, f32[1,512]{1,0:T(1,128)S(1)} %add_add_fusion.refs_4_.refs_1_, f32[1,512]{1,0:T(1,128)S(1)} %collective-permute-done.3.refs_2_, f32[1,512]{1,0:T(1,128)S(1)} %collective-permute-done.4.refs_3_, ...), custom_call_target="tpu_custom_call" | custom-call | tf_op jit(solution)/shard_map/cols/pallas_call | solution.py:283
  28.8 0.2 collective-permute-start.13
  29.1 1.2 %collective-permute-start.12 = (f32[384,128]{1,0:T(8,128)S(1)}, f32[384,128]{1,0:T(8,128)S(1)}, u32[]{:S(2)}, u32[]{:S(2)}) collective-permute-start(f32[384,128]{1,0:T(8,128)S(1)} %get-tuple-element.94), channel_id=1, source_target_pairs={{0,16},{8,24},{16,0},{24,8},{1,17},{9,25},{17,1},{25,9},{2,18},{10... | collective-permute-start | bytes 589832 | tf_op jit(solution)/shard_map/ppermute | solution.py:434
  30.3 0.2 collective-permute-start.18
  30.5 1.2 %collective-permute-start.19 = (f32[384,128]{1,0:T(8,128)S(1)}, f32[384,128]{1,0:T(8,128)S(1)}, u32[]{:S(2)}, u32[]{:S(2)}) collective-permute-start(f32[384,128]{1,0:T(8,128)S(1)} %get-tuple-element.116.refs_7_.refs_14_), channel_id=1, source_target_pairs={{0,16},{8,24},{16,0},{24,8},{1,17},{9,25},{17,1},{25,9},{2,18},{10... | collective-permute-start | bytes 589832 | tf_op jit(solution)/shard_map/ppermute | solution.py:434
  31.8 4.0 %collective-permute-start.8 = (f32[1,1024]{1,0:T(1,128)S(1)}, f32[1,1024]{1,0:T(1,128)S(1)}, u32[]{:S(2)}, u32[]{:S(2)}) collective-permute-start(f32[1,1024]{1,0:T(1,128)S(1)} %get-tuple-element.92.refs_1_), channel_id=1, source_target_pairs={{0,8},{8,0},{16,24},{24,16},{1,9},{9,1},{17,25},{25,17},{2,10},{10... | collective-permute-start | bytes 12296 | tf_op jit(solution)/shard_map/ppermute | solution.py:434
  35.8 0.8 %collective-permute-done.8.refs_2_ = f32[1,1024]{1,0:T(1,128)S(1)} collective-permute-done((f32[1,1024]{1,0:T(1,128)S(1)}, f32[1,1024]{1,0:T(1,128)S(1)}, u32[]{:S(2)}, u32[]{:S(2)}) %collective-permute-start.8) | collective-permute-done | bytes 4128 | tf_op jit(solution)/shard_map/ppermute | solution.py:434
  36.6 1.6 %rows.2 = (f32[1,512]{1,0:T(1,128)}, f32[1,1024]{1,0:T(1,128)S(1)}) custom-call(f32[4,128]{1,0:T(4,128)S(1)} %get-tuple-element.66.refs_0_, f32[1,1024]{1,0:T(1,128)S(1)} %get-tuple-element.92.refs_1_, f32[1,1024]{1,0:T(1,128)S(1)} %collective-permute-done.8.refs_2_, f32[520,128]{1,0:T(8,128)S(1)} %collective-permute-done.7.refs_6_.refs_3_, ...), custom_call_target="tpu_custom_call" | custom-call | tf_op jit(solution)/shard_map/rows/pallas_call | solution.py:314
  38.2 0.1 collective-permute-start.10
  38.3 0.0 collective-permute-done.13.refs_1_
  38.3 2.4 %collective-permute-start.11 = (f32[1,1024]{1,0:T(1,128)S(1)}, f32[1,1024]{1,0:T(1,128)S(1)}, u32[]{:S(2)}, u32[]{:S(2)}) collective-permute-start(f32[1,1024]{1,0:T(1,128)S(1)} %get-tuple-element.93.refs_2_.refs_1_), channel_id=1, source_target_pairs={{0,6},{1,7},{2,0},{3,1},{4,2},{5,3},{6,4},{7,5},{8,14},{9,15},{10,... | collective-permute-start | bytes 12296 | tf_op jit(solution)/shard_map/ppermute | solution.py:434
  40.7 3.0 %tables.12 = (bf16[32,128,128]{2,1,0:T(8,128)(2,1)S(1)}, bf16[32,128,128]{2,1,0:T(8,128)(2,1)S(1)}, f32[8,128]{1,0:T(8,128)S(1)}) custom-call(f32[32,128]{1,0:T(8,128)S(1)} %get-tuple-element.68.refs_0_, f32[384,128]{1,0:T(8,128)S(1)} %collective-permute-done.13.refs_1_, f32[1,1024]{1,0:T(1,128)S(1)} %get-tuple-element.93.refs_2_.refs_1_), custom_call_target="tpu_custom_call" | custom-call | flops 268435456 | bytes 10240000 | tf_op jit(solution)/shard_map/tables/pallas_call | solution.py:377
  43.8 0.0 collective-permute-done.12.refs_1_
  43.8 0.2 collective-permute-start.9
  44.0 3.1 %tables.13 = (bf16[32,128,128]{2,1,0:T(8,128)(2,1)S(1)}, bf16[32,128,128]{2,1,0:T(8,128)(2,1)S(1)}, f32[8,128]{1,0:T(8,128)S(1)}) custom-call(f32[32,128]{1,0:T(8,128)S(1)} %get-tuple-element.68.refs_0_, f32[384,128]{1,0:T(8,128)S(1)} %collective-permute-done.12.refs_1_, f32[8,128]{1,0:T(8,128)S(1)} %get-tuple-element.96.refs_2_), custom_call_target="tpu_custom_call" | custom-call | flops 268435456 | bytes 10240000 | tf_op jit(solution)/shard_map/tables/pallas_call | solution.py:377
  47.1 0.0 collective-permute-done.10.refs_3_
  47.1 0.0 collective-permute-done.11.refs_4_
  47.1 1.1 %collective-permute-done.9.refs_2_ = f32[1,1024]{1,0:T(1,128)S(1)} collective-permute-done((f32[1,1024]{1,0:T(1,128)S(1)}, f32[1,1024]{1,0:T(1,128)S(1)}, u32[]{:S(2)}, u32[]{:S(2)}) %collective-permute-start.9) | collective-permute-done | bytes 4128 | tf_op jit(solution)/shard_map/ppermute | solution.py:434
  48.3 0.7 cols.3
  48.9 2.1 %collective-permute-start.14 = (f32[1,1024]{1,0:T(1,128)S(1)}, f32[1,1024]{1,0:T(1,128)S(1)}, u32[]{:S(2)}, u32[]{:S(2)}) collective-permute-start(f32[1,1024]{1,0:T(1,128)S(1)} %get-tuple-element.99.refs_1_), channel_id=1, source_target_pairs={{0,8},{8,0},{16,24},{24,16},{1,9},{9,1},{17,25},{25,17},{2,10},{10... | collective-permute-start | bytes 12296 | tf_op jit(solution)/shard_map/ppermute | solution.py:434
  51.1 0.8 %collective-permute-done.14.refs_2_ = f32[1,1024]{1,0:T(1,128)S(1)} collective-permute-done((f32[1,1024]{1,0:T(1,128)S(1)}, f32[1,1024]{1,0:T(1,128)S(1)}, u32[]{:S(2)}, u32[]{:S(2)}) %collective-permute-start.14) | collective-permute-done | bytes 4128 | tf_op jit(solution)/shard_map/ppermute | solution.py:434
  51.9 1.6 %rows.3 = (f32[1,512]{1,0:T(1,128)}, f32[1,1024]{1,0:T(1,128)S(1)}) custom-call(f32[4,128]{1,0:T(4,128)S(1)} %get-tuple-element.66.refs_0_, f32[1,1024]{1,0:T(1,128)S(1)} %get-tuple-element.99.refs_1_, f32[1,1024]{1,0:T(1,128)S(1)} %collective-permute-done.14.refs_2_, f32[520,128]{1,0:T(8,128)S(1)} %collective-permute-done.7.refs_6_.refs_3_, ...), custom_call_target="tpu_custom_call" | custom-call | tf_op jit(solution)/shard_map/rows/pallas_call | solution.py:314
  53.5 0.0 collective-permute-start.15
  53.5 1.5 %collective-permute-start.16 = (f32[1,1024]{1,0:T(1,128)S(1)}, f32[1,1024]{1,0:T(1,128)S(1)}, u32[]{:S(2)}, u32[]{:S(2)}) collective-permute-start(f32[1,1024]{1,0:T(1,128)S(1)} %get-tuple-element.100.refs_2_), channel_id=1, source_target_pairs={{0,4},{1,5},{2,6},{3,7},{4,0},{5,1},{6,2},{7,3},{8,12},{9,13},{10,... | collective-permute-start | bytes 12296 | tf_op jit(solution)/shard_map/ppermute | solution.py:434
  55.0 1.7 %collective-permute-start.17 = (f32[1,1024]{1,0:T(1,128)S(1)}, f32[1,1024]{1,0:T(1,128)S(1)}, u32[]{:S(2)}, u32[]{:S(2)}) collective-permute-start(f32[1,1024]{1,0:T(1,128)S(1)} %get-tuple-element.100.refs_2_), channel_id=1, source_target_pairs={{0,6},{1,7},{2,0},{3,1},{4,2},{5,3},{6,4},{7,5},{8,14},{9,15},{10,... | collective-permute-start | bytes 12296 | tf_op jit(solution)/shard_map/ppermute | solution.py:434
  56.8 0.0 collective-permute-done.18.refs_1_
  56.8 3.1 %tables.14 = (bf16[32,128,128]{2,1,0:T(8,128)(2,1)S(1)}, bf16[32,128,128]{2,1,0:T(8,128)(2,1)S(1)}, f32[8,128]{1,0:T(8,128)S(1)}) custom-call(f32[32,128]{1,0:T(8,128)S(1)} %get-tuple-element.68.refs_0_, f32[384,128]{1,0:T(8,128)S(1)} %collective-permute-done.18.refs_1_, f32[1,1024]{1,0:T(1,128)S(1)} %get-tuple-element.100.refs_2_), custom_call_target="tpu_custom_call" | custom-call | flops 268435456 | bytes 10240000 | tf_op jit(solution)/shard_map/tables/pallas_call | solution.py:377
  59.9 0.0 collective-permute-done.19.refs_1_
  59.9 3.1 %tables.15 = (bf16[32,128,128]{2,1,0:T(8,128)(2,1)S(1)}, bf16[32,128,128]{2,1,0:T(8,128)(2,1)S(1)}, f32[8,128]{1,0:T(8,128)S(1)}) custom-call(f32[32,128]{1,0:T(8,128)S(1)} %get-tuple-element.68.refs_0_, f32[384,128]{1,0:T(8,128)S(1)} %collective-permute-done.19.refs_1_, f32[8,128]{1,0:T(8,128)S(1)} %get-tuple-element.117.refs_2_), custom_call_target="tpu_custom_call" | custom-call | flops 268435456 | bytes 10240000 | tf_op jit(solution)/shard_map/tables/pallas_call | solution.py:377
  63.0 0.0 collective-permute-done.15.refs_3_
  63.0 0.0 collective-permute-done.16.refs_4_
  63.0 0.0 collective-permute-done.17.refs_5_
  63.0 2.0 %spread.2 = (f32[16,32,128]{2,1,0:T(8,128)S(1)}, f32[1,512]{1,0:T(1,128)}) custom-call(s32[4,128]{1,0:T(4,128)S(1)} %get-tuple-element.64.refs_0_, f32[1,1024]{1,0:T(1,128)S(1)} %get-tuple-element.98.refs_1_, f32[1,1024]{1,0:T(1,128)S(1)} %get-tuple-element.100.refs_2_, f32[1,1024]{1,0:T(1,128)S(1)} %collective-permute-done.15.refs_3_, ...), custom_call_target="tpu_custom_call" | custom-call | tf_op jit(solution)/shard_map/spread/pallas_call | solution.py:420
  65.0 0.9 %collective-permute-start.20 = (f32[16,32,128]{2,1,0:T(8,128)S(1)}, f32[16,32,128]{2,1,0:T(8,128)S(1)}, u32[]{:S(2)}, u32[]{:S(2)}) collective-permute-start(f32[16,32,128]{2,1,0:T(8,128)S(1)} %get-tuple-element.124), channel_id=1, source_target_pairs={{0,8},{8,0},{16,24},{24,16},{1,9},{9,1},{17,25},{25,17},{2,10},{10... | collective-permute-start | bytes 786440 | tf_op jit(solution)/shard_map/ppermute | solution.py:434
  65.9 2.0 %spread.3 = (f32[16,32,128]{2,1,0:T(8,128)S(1)}, f32[1,512]{1,0:T(1,128)}) custom-call(s32[4,128]{1,0:T(4,128)S(1)} %get-tuple-element.64.refs_0_, f32[1,1024]{1,0:T(1,128)S(1)} %get-tuple-element.98.refs_1_, f32[1,1024]{1,0:T(1,128)S(1)} %get-tuple-element.100.refs_2_, f32[1,1024]{1,0:T(1,128)S(1)} %collective-permute-done.15.refs_3_, ...), custom_call_target="tpu_custom_call" | custom-call | tf_op jit(solution)/shard_map/spread/pallas_call | solution.py:420
  67.9 0.0 collective-permute-done.20
  67.9 0.7 %add.15 = f32[16,32,128]{2,1,0:T(8,128)} add(f32[16,32,128]{2,1,0:T(8,128)S(1)} %get-tuple-element.123, f32[16,32,128]{2,1,0:T(8,128)S(1)} %collective-permute-done.20) | non-fusion elementwise | flops 65536 | bytes 786432 | tf_op jit(solution)/shard_map/add | solution.py:523
  (1 shorter events, 0.0 us)
Async XLA Ops:
  2.9 14.2 %collective-permute-start = (f32[1,512]{1,0:T(1,128)S(1)}, f32[1,512]{1,0:T(1,128)S(1)}, u32[]{:S(2)}, u32[]{:S(2)}) collective-permute-start(f32[1,512]{1,0:T(1,128)S(1)} %get-tuple-element.67.refs_4_), channel_id=1, source_target_pairs={{0,2},{1,3},{2,4},{3,5},{4,6},{5,7},{6,0},{7,1},{8,10},{9,11},{10,... | collective-permute-start | bytes 6152 | tf_op jit(solution)/shard_map/ppermute | solution.py:434
  5.1 12.0 %collective-permute-start.1 = (f32[1,512]{1,0:T(1,128)S(1)}, f32[1,512]{1,0:T(1,128)S(1)}, u32[]{:S(2)}, u32[]{:S(2)}) collective-permute-start(f32[1,512]{1,0:T(1,128)S(1)} %get-tuple-element.67.refs_4_), channel_id=1, source_target_pairs={{0,4},{1,5},{2,6},{3,7},{4,0},{5,1},{6,2},{7,3},{8,12},{9,13},{10,... | collective-permute-start | bytes 6152 | tf_op jit(solution)/shard_map/ppermute | solution.py:434
  7.4 9.7 %collective-permute-start.2 = (f32[1,512]{1,0:T(1,128)S(1)}, f32[1,512]{1,0:T(1,128)S(1)}, u32[]{:S(2)}, u32[]{:S(2)}) collective-permute-start(f32[1,512]{1,0:T(1,128)S(1)} %get-tuple-element.67.refs_4_), channel_id=1, source_target_pairs={{0,6},{1,7},{2,0},{3,1},{4,2},{5,3},{6,4},{7,5},{8,14},{9,15},{10,... | collective-permute-start | bytes 6152 | tf_op jit(solution)/shard_map/ppermute | solution.py:434
  8.4 17.6 %collective-permute-start.6 = (f32[524,128]{1,0:T(8,128)S(1)}, f32[524,128]{1,0:T(8,128)S(1)}, u32[]{:S(2)}, u32[]{:S(2)}) collective-permute-start(f32[524,128]{1,0:T(8,128)S(1)} %get-tuple-element.75), channel_id=1, source_target_pairs={{0,16},{8,24},{16,0},{24,8},{1,17},{9,25},{17,1},{25,9},{2,18},{10... | collective-permute-start | bytes 804872 | tf_op jit(solution)/shard_map/ppermute | solution.py:434
  9.7 16.3 %collective-permute-start.7 = (f32[520,128]{1,0:T(8,128)S(1)}, f32[520,128]{1,0:T(8,128)S(1)}, u32[]{:S(2)}, u32[]{:S(2)}) collective-permute-start(f32[520,128]{1,0:T(8,128)S(1)} %get-tuple-element.83), channel_id=1, source_target_pairs={{0,1},{1,0},{2,3},{3,2},{4,5},{5,4},{6,7},{7,6},{8,9},{9,8},{10,11... | collective-permute-start | bytes 798728 | tf_op jit(solution)/shard_map/ppermute | solution.py:434
  17.2 10.5 %collective-permute-start.3 = (f32[1,512]{1,0:T(1,128)S(1)}, f32[1,512]{1,0:T(1,128)S(1)}, u32[]{:S(2)}, u32[]{:S(2)}) collective-permute-start(f32[1,512]{1,0:T(1,128)S(1)} %add_add_fusion.refs_4_.refs_1_), channel_id=1, source_target_pairs={{0,1},{1,0},{2,3},{3,2},{4,5},{5,4},{6,7},{7,6},{8,9},{9,8},{10,11... | collective-permute-start | bytes 6152 | tf_op jit(solution)/shard_map/ppermute | solution.py:434
  17.5 10.2 %collective-permute-start.4 = (f32[1,512]{1,0:T(1,128)S(1)}, f32[1,512]{1,0:T(1,128)S(1)}, u32[]{:S(2)}, u32[]{:S(2)}) collective-permute-start(f32[1,512]{1,0:T(1,128)S(1)} %add_add_fusion.refs_4_.refs_1_), channel_id=1, source_target_pairs={{0,16},{1,17},{2,18},{3,19},{4,20},{5,21},{6,22},{7,23},{8,24},{9,... | collective-permute-start | bytes 6152 | tf_op jit(solution)/shard_map/ppermute | solution.py:536
  17.7 10.0 %collective-permute-start.5 = (f32[1,512]{1,0:T(1,128)S(1)}, f32[1,512]{1,0:T(1,128)S(1)}, u32[]{:S(2)}, u32[]{:S(2)}) collective-permute-start(f32[1,512]{1,0:T(1,128)S(1)} %add_add_fusion.refs_4_.refs_1_), channel_id=1, source_target_pairs={{0,17},{1,16},{2,19},{3,18},{4,21},{5,20},{6,23},{7,22},{8,25},{9,... | collective-permute-start | bytes 6152 | tf_op jit(solution)/shard_map/ppermute | solution.py:536
  28.8 9.5 %collective-permute-start.13 = (f32[384,128]{1,0:T(8,128)S(1)}, f32[384,128]{1,0:T(8,128)S(1)}, u32[]{:S(2)}, u32[]{:S(2)}) collective-permute-start(f32[384,128]{1,0:T(8,128)S(1)} %get-tuple-element.95.refs_4_), channel_id=1, source_target_pairs={{0,16},{8,24},{16,0},{24,8},{1,17},{9,25},{17,1},{25,9},{2,18},{10... | collective-permute-start | bytes 589832 | tf_op jit(solution)/shard_map/ppermute | solution.py:434
  29.1 14.7 %collective-permute-start.12 = (f32[384,128]{1,0:T(8,128)S(1)}, f32[384,128]{1,0:T(8,128)S(1)}, u32[]{:S(2)}, u32[]{:S(2)}) collective-permute-start(f32[384,128]{1,0:T(8,128)S(1)} %get-tuple-element.94), channel_id=1, source_target_pairs={{0,16},{8,24},{16,0},{24,8},{1,17},{9,25},{17,1},{25,9},{2,18},{10... | collective-permute-start | bytes 589832 | tf_op jit(solution)/shard_map/ppermute | solution.py:434
  30.3 26.5 %collective-permute-start.18 = (f32[384,128]{1,0:T(8,128)S(1)}, f32[384,128]{1,0:T(8,128)S(1)}, u32[]{:S(2)}, u32[]{:S(2)}) collective-permute-start(f32[384,128]{1,0:T(8,128)S(1)} %get-tuple-element.113.refs_4_), channel_id=1, source_target_pairs={{0,16},{8,24},{16,0},{24,8},{1,17},{9,25},{17,1},{25,9},{2,18},{10... | collective-permute-start | bytes 589832 | tf_op jit(solution)/shard_map/ppermute | solution.py:434
  30.5 29.3 %collective-permute-start.19 = (f32[384,128]{1,0:T(8,128)S(1)}, f32[384,128]{1,0:T(8,128)S(1)}, u32[]{:S(2)}, u32[]{:S(2)}) collective-permute-start(f32[384,128]{1,0:T(8,128)S(1)} %get-tuple-element.116.refs_7_.refs_14_), channel_id=1, source_target_pairs={{0,16},{8,24},{16,0},{24,8},{1,17},{9,25},{17,1},{25,9},{2,18},{10... | collective-permute-start | bytes 589832 | tf_op jit(solution)/shard_map/ppermute | solution.py:434
  31.8 4.9 %collective-permute-start.8 = (f32[1,1024]{1,0:T(1,128)S(1)}, f32[1,1024]{1,0:T(1,128)S(1)}, u32[]{:S(2)}, u32[]{:S(2)}) collective-permute-start(f32[1,1024]{1,0:T(1,128)S(1)} %get-tuple-element.92.refs_1_), channel_id=1, source_target_pairs={{0,8},{8,0},{16,24},{24,16},{1,9},{9,1},{17,25},{25,17},{2,10},{10... | collective-permute-start | bytes 12296 | tf_op jit(solution)/shard_map/ppermute | solution.py:434
  38.2 8.9 %collective-permute-start.10 = (f32[1,1024]{1,0:T(1,128)S(1)}, f32[1,1024]{1,0:T(1,128)S(1)}, u32[]{:S(2)}, u32[]{:S(2)}) collective-permute-start(f32[1,1024]{1,0:T(1,128)S(1)} %get-tuple-element.93.refs_2_.refs_1_), channel_id=1, source_target_pairs={{0,4},{1,5},{2,6},{3,7},{4,0},{5,1},{6,2},{7,3},{8,12},{9,13},{10,... | collective-permute-start | bytes 12296 | tf_op jit(solution)/shard_map/ppermute | solution.py:434
  38.3 8.8 %collective-permute-start.11 = (f32[1,1024]{1,0:T(1,128)S(1)}, f32[1,1024]{1,0:T(1,128)S(1)}, u32[]{:S(2)}, u32[]{:S(2)}) collective-permute-start(f32[1,1024]{1,0:T(1,128)S(1)} %get-tuple-element.93.refs_2_.refs_1_), channel_id=1, source_target_pairs={{0,6},{1,7},{2,0},{3,1},{4,2},{5,3},{6,4},{7,5},{8,14},{9,15},{10,... | collective-permute-start | bytes 12296 | tf_op jit(solution)/shard_map/ppermute | solution.py:434
  43.8 4.5 %collective-permute-start.9 = (f32[1,1024]{1,0:T(1,128)S(1)}, f32[1,1024]{1,0:T(1,128)S(1)}, u32[]{:S(2)}, u32[]{:S(2)}) collective-permute-start(f32[1,1024]{1,0:T(1,128)S(1)} %get-tuple-element.93.refs_2_.refs_1_), channel_id=1, source_target_pairs={{0,2},{1,3},{2,4},{3,5},{4,6},{5,7},{6,0},{7,1},{8,10},{9,11},{10,... | collective-permute-start | bytes 12296 | tf_op jit(solution)/shard_map/ppermute | solution.py:434
  48.9 2.9 %collective-permute-start.14 = (f32[1,1024]{1,0:T(1,128)S(1)}, f32[1,1024]{1,0:T(1,128)S(1)}, u32[]{:S(2)}, u32[]{:S(2)}) collective-permute-start(f32[1,1024]{1,0:T(1,128)S(1)} %get-tuple-element.99.refs_1_), channel_id=1, source_target_pairs={{0,8},{8,0},{16,24},{24,16},{1,9},{9,1},{17,25},{25,17},{2,10},{10... | collective-permute-start | bytes 12296 | tf_op jit(solution)/shard_map/ppermute | solution.py:434
  53.5 9.5 %collective-permute-start.15 = (f32[1,1024]{1,0:T(1,128)S(1)}, f32[1,1024]{1,0:T(1,128)S(1)}, u32[]{:S(2)}, u32[]{:S(2)}) collective-permute-start(f32[1,1024]{1,0:T(1,128)S(1)} %get-tuple-element.100.refs_2_), channel_id=1, source_target_pairs={{0,2},{1,3},{2,4},{3,5},{4,6},{5,7},{6,0},{7,1},{8,10},{9,11},{10,... | collective-permute-start | bytes 12296 | tf_op jit(solution)/shard_map/ppermute | solution.py:434
  53.5 9.5 %collective-permute-start.16 = (f32[1,1024]{1,0:T(1,128)S(1)}, f32[1,1024]{1,0:T(1,128)S(1)}, u32[]{:S(2)}, u32[]{:S(2)}) collective-permute-start(f32[1,1024]{1,0:T(1,128)S(1)} %get-tuple-element.100.refs_2_), channel_id=1, source_target_pairs={{0,4},{1,5},{2,6},{3,7},{4,0},{5,1},{6,2},{7,3},{8,12},{9,13},{10,... | collective-permute-start | bytes 12296 | tf_op jit(solution)/shard_map/ppermute | solution.py:434
  55.0 7.9 %collective-permute-start.17 = (f32[1,1024]{1,0:T(1,128)S(1)}, f32[1,1024]{1,0:T(1,128)S(1)}, u32[]{:S(2)}, u32[]{:S(2)}) collective-permute-start(f32[1,1024]{1,0:T(1,128)S(1)} %get-tuple-element.100.refs_2_), channel_id=1, source_target_pairs={{0,6},{1,7},{2,0},{3,1},{4,2},{5,3},{6,4},{7,5},{8,14},{9,15},{10,... | collective-permute-start | bytes 12296 | tf_op jit(solution)/shard_map/ppermute | solution.py:434
  65.0 2.9 %collective-permute-start.20 = (f32[16,32,128]{2,1,0:T(8,128)S(1)}, f32[16,32,128]{2,1,0:T(8,128)S(1)}, u32[]{:S(2)}, u32[]{:S(2)}) collective-permute-start(f32[16,32,128]{2,1,0:T(8,128)S(1)} %get-tuple-element.124), channel_id=1, source_target_pairs={{0,8},{8,0},{16,24},{24,16},{1,9},{9,1},{17,25},{25,17},{2,10},{10... | collective-permute-start | bytes 786440 | tf_op jit(solution)/shard_map/ppermute | solution.py:434

commit v5 on v3

v5 whole, which is shorter than its diff:
```python
import functools
import math

import jax
import jax.numpy as jnp
import numpy as np
from jax import lax
from jax.experimental import pallas as pl
from jax.experimental.pallas import tpu as pltpu
from jax.sharding import PartitionSpec as P

ITERS = 2
SEG = 32
MERCH_DEV = 128
DAYS = 64
LANES = 128
UNROLL = 128

half_span = 11

f32 = jnp.float32
bf16 = jnp.bfloat16
VMEM = pl.BlockSpec(memory_space=pltpu.VMEM)
ANY = pl.BlockSpec(memory_space=pl.ANY)
HBM = pl.BlockSpec(memory_space=pltpu.HBM)
PARAMS = pltpu.CompilerParams(vmem_limit_bytes=20 * 2**20)


def filter_table(day_count):
    outer = 13.0
    coeffs = []
    for offset_days in range(-half_span, half_span + 1):
        sq = float(offset_days * offset_days)
        top = (
            315.0
            * ((outer - 1) ** 2 - sq)
            * (outer**2 - sq)
            * ((outer + 1) ** 2 - sq)
            * (3 * outer**2 - 16 - 11 * sq)
        )
        bottom = (
            8
            * outer
            * (outer**2 - 1)
            * (4 * outer**2 - 1)
            * (4 * outer**2 - 9)
            * (4 * outer**2 - 25)
        )
        coeffs.append(top / bottom)
    matrix = np.zeros((day_count, day_count))
    for row_day in range(day_count):
        for offset_days in range(-half_span, half_span + 1):
            col_day = row_day + offset_days
            if 0 <= col_day < day_count:
                matrix[row_day, col_day] = coeffs[offset_days + half_span]
        matrix[row_day] = matrix[row_day] / matrix[row_day].sum()
    return matrix


def split2(x):
    hi = x.astype(bf16)
    return hi, (x - hi.astype(f32)).astype(bf16)


def split_rows(x):
    hi = x.astype(bf16)
    rest = x - hi.astype(f32)
    mid = rest.astype(bf16)
    low = (rest - mid.astype(f32)).astype(bf16)
    return jnp.concatenate([hi, mid, low, jnp.zeros((5, x.shape[1]), bf16)], 0)


def dot_rows(rows, k, dims):
    return lax.dot_general(rows, k, (dims, ((), ())), preferred_element_type=f32)


def cols_of(us, blocks):
    out = 0.0
    for u, (khi, klo) in zip(us, blocks):
        rows = split_rows(u)
        out = out + dot_rows(rows, khi[...], ((1,), (0,))) + dot_rows(rows, klo[...], ((1,), (0,)))
    return jnp.sum(out, axis=0, keepdims=True)


def rows_of(vs, blocks):
    out = 0.0
    for v, (khi, klo) in zip(vs, blocks):
        rows = split_rows(v)
        out = out + dot_rows(rows, khi[...], ((1,), (1,))) + dot_rows(rows, klo[...], ((1,), (1,)))
    return jnp.sum(out, axis=0, keepdims=True)


def kernel_block(x, y, row_region, col_region, penalty):
    n, m = x.shape[0], y.shape[0]
    regions = penalty.shape[0]
    inv_root = 1.0 / math.sqrt(x.shape[1])
    inner = dot_rows(x, y, ((1,), (1,)))
    row_hot = (lax.broadcasted_iota(jnp.int32, (regions, n), 0) == row_region).astype(f32).astype(bf16)
    col_hot = (lax.broadcasted_iota(jnp.int32, (regions, m), 0) == col_region).astype(f32).astype(bf16)
    phi, plo = split2(penalty)
    qhi = jnp.dot(phi, col_hot, preferred_element_type=f32).astype(bf16)
    qlo = jnp.dot(plo, col_hot, preferred_element_type=f32).astype(bf16)
    pen = dot_rows(jnp.concatenate([row_hot, row_hot], 0), jnp.concatenate([qhi, qlo], 0), ((0,), (0,)))
    return split2(jnp.exp(inner * inv_root - pen))


def run_copies(pairs, sems):
    copies = [pltpu.make_async_copy(src, dst, sems.at[k]) for k, (src, dst) in enumerate(pairs)]
    for copy in copies:
        copy.start()
    return copies


def first_body(
    x_hbm, y_hbm, rr_hbm, seg_hbm, mass_hbm, cr_hbm, cm_hbm, f_hbm, m_hbm, d_hbm, a_hbm,
    xpack_ref, ypack_ref, rpack_ref, f_ref, xb_ref, yb_ref, rr_ref, seg_ref, cr_ref, m_ref, d_ref, sems,
):
    me = lax.axis_index("cohort")
    n, m = xb_ref.shape[0], yb_ref.shape[0]
    p, q = n // LANES, m // LANES
    copies = run_copies(
        (
            (x_hbm, xb_ref),
            (rr_hbm, rr_ref),
            (seg_hbm, seg_ref),
            (mass_hbm, xpack_ref.at[pl.ds(n + 2 * p, p), :]),
            (y_hbm, yb_ref),
            (cr_hbm, cr_ref),
            (cm_hbm, ypack_ref.at[pl.ds(m + q, q), :]),
            (m_hbm, m_ref),
            (d_hbm, d_ref),
            (a_hbm, rpack_ref.at[pl.ds(2 * n, n), :]),
            (f_hbm.at[me], f_ref),
        ),
        sems,
    )
    for copy in copies:
        copy.wait()
    xpack_ref[0:n, :] = xb_ref[...].astype(f32)
    xpack_ref[n : n + p, :] = rr_ref[...].astype(f32)
    xpack_ref[n + p : n + 2 * p, :] = seg_ref[...].astype(f32)
    ypack_ref[0:m, :] = yb_ref[...].astype(f32)
    ypack_ref[m : m + q, :] = cr_ref[...].astype(f32)
    rpack_ref[0:n, :] = m_ref[...].astype(f32)
    rpack_ref[n : 2 * n, :] = d_ref[...].astype(f32)


def first_call(x, y, rr, seg, mass, cr, cm, table, records):
    n, m = x.shape[0], y.shape[0]
    p, q = n // LANES, m // LANES
    block = lambda v: v.reshape(-1, LANES)
    i32 = jnp.int32
    out = [(n + 3 * p, LANES), (m + 2 * q, LANES), (3 * n, LANES), table.shape[1:]]
    args = (x, y, block(rr), block(seg), block(mass), block(cr), block(cm), table, *records)
    return pl.pallas_call(
        first_body,
        in_specs=[HBM] * len(args),
        out_specs=[VMEM] * len(out),
        out_shape=[pltpu.VMEM(shape, f32) for shape in out],
        scratch_shapes=[
            pltpu.VMEM(x.shape, bf16),
            pltpu.VMEM(y.shape, bf16),
            pltpu.VMEM((p, LANES), i32),
            pltpu.VMEM((p, LANES), i32),
            pltpu.VMEM((q, LANES), i32),
            pltpu.VMEM((n, LANES), i32),
            pltpu.VMEM((n, LANES), i32),
            pltpu.SemaphoreType.DMA((len(args),)),
        ],
        compiler_params=PARAMS,
        name="first",
    )(*[pltpu.with_memory_space_constraint(arg, pltpu.HBM) for arg in args])


def flat(block):
    return jnp.concatenate([block[k : k + 1, :] for k in range(block.shape[0])], 1)


def gibbs_body(n, m, packs_x, packs_y, *refs):
    xpacks, ypacks, pen_ref = refs[:packs_x], refs[packs_x : packs_x + packs_y], refs[packs_x + packs_y]
    outs = refs[packs_x + packs_y + 1 : -1]
    r_ref = refs[-1]
    p, q = n // LANES, m // LANES
    pen = pen_ref[...]
    xs = [(pack[0:n, :].astype(bf16), flat(pack[n : n + p, :]).astype(jnp.int32)) for pack in xpacks]
    ys = [(pack[0:m, :].astype(bf16), flat(pack[m : m + q, :]).astype(jnp.int32)) for pack in ypacks]
    k = 0
    sums = []
    for x, rr in xs:
        blocks = []
        for y, cr in ys:
            outs[k][...], outs[k + 1][...] = kernel_block(x, y, rr, cr, pen)
            blocks.append((outs[k], outs[k + 1]))
            k += 2
        sums.append(rows_of([jnp.ones((1, m), f32)] * len(ys), blocks))
    r_ref[...] = jnp.concatenate(sums, 1)


def gibbs_call(n, m, xpacks, ypacks, penalty, after):
    blocks = len(xpacks) * len(ypacks)
    args = [*xpacks, *ypacks, penalty]
    *out, sums = pl.pallas_call(
        lambda *refs: gibbs_body(n, m, len(xpacks), len(ypacks), *refs[: len(args)], *refs[-2 * blocks - 1 :]),
        in_specs=[VMEM] * len(args) + [ANY] * len(after),
        out_specs=[VMEM] * (2 * blocks + 1),
        out_shape=[pltpu.VMEM((n, m), bf16)] * (2 * blocks) + [pltpu.VMEM((1, len(xpacks) * n), f32)],
        compiler_params=PARAMS,
        cost_estimate=pl.CostEstimate(
            flops=2 * blocks * n * m * LANES, transcendentals=blocks * n * m, bytes_accessed=blocks * n * m * 4
        ),
        name="gibbs",
    )(*args, *after)
    return [(out[2 * k], out[2 * k + 1]) for k in range(blocks)], sums


def total_of(refs):
    total = refs[0][...]
    for ref in refs[1:]:
        total = total + ref[...]
    return total


def cols_body(n, parts, packs, block_count, *refs):
    p = n // LANES
    total = total_of(refs[:parts])
    pack_refs = refs[parts : parts + packs]
    rest = refs[parts + packs :]
    blocks = [(rest[2 * k], rest[2 * k + 1]) for k in range(block_count)]
    u_ref, c_ref = refs[-2:]
    us = [flat(pack[n + 2 * p : n + 3 * p, :]) / total[:, k * n : (k + 1) * n] for k, pack in enumerate(pack_refs)]
    u_ref[...] = jnp.concatenate(us, 1)
    width = block_count // packs
    c_ref[...] = jnp.concatenate([cols_of(us, blocks[j::width]) for j in range(width)], 1)


def rows_body(m, parts, packs, block_count, *refs):
    q = m // LANES
    total = total_of(refs[:parts])
    pack_refs = refs[parts : parts + packs]
    rest = refs[parts + packs :]
    blocks = [(rest[2 * k], rest[2 * k + 1]) for k in range(block_count)]
    v_ref, r_ref = refs[-2:]
    vs = [flat(pack[m + q : m + 2 * q, :]) / total[:, k * m : (k + 1) * m] for k, pack in enumerate(pack_refs)]
    v_ref[...] = vs[0]
    r_ref[...] = jnp.concatenate([rows_of(vs, blocks[i : i + packs]) for i in range(0, block_count, packs)], 1)


def half_step(body, name, size, partials, packs, blocks, outs, after):
    args = [*partials, *packs, *[ref for block in blocks for ref in block]]
    return pl.pallas_call(
        lambda *refs: body(size, len(partials), len(packs), len(blocks), *refs[: len(args)], *refs[-2:]),
        in_specs=[VMEM] * len(args) + [ANY] * len(after),
        out_specs=[VMEM] * 2,
        out_shape=outs,
        compiler_params=PARAMS,
        name=name,
    )(*args, *after)


def table_body(n, first, count, f_ref, pack_ref, hi_ref, lo_ref, token_ref):
    filt = f_ref[...]
    t_count = filt.shape[0]
    merch_rows = lax.broadcasted_iota(jnp.int32, (MERCH_DEV, LANES), 0).astype(f32).astype(bf16)
    merch_cols = lax.broadcasted_iota(jnp.int32, (LANES, MERCH_DEV), 1).astype(f32).astype(bf16)
    one, zero = jnp.ones((MERCH_DEV, LANES), bf16), jnp.zeros((MERCH_DEV, LANES), bf16)
    size = math.gcd(count, UNROLL)

    def group(step, carry):
        start = pl.multiple_of(step * size, size)
        merch = pack_ref[pl.ds(first + start, size), :]
        days = pack_ref[pl.ds(n + first + start, size), :].astype(jnp.int32)
        amounts = pack_ref[pl.ds(2 * n + first + start, size), :]
        turned = jnp.transpose(merch).astype(bf16)
        merch = merch.astype(bf16)
        tables = []
        for i in range(size):
            day = jnp.broadcast_to(days[i : i + 1, :], (t_count, LANES))
            coef = jnp.take_along_axis(filt, day, axis=1, mode="promise_in_bounds")
            both = jnp.concatenate(split2(coef * amounts[i : i + 1, :]), 0)
            if i % 2:
                hot = jnp.where(merch_cols == jnp.broadcast_to(turned[:, i : i + 1], merch_cols.shape), one, zero)
                both = dot_rows(both, hot, ((1,), (0,)))
            else:
                hot = jnp.where(merch_rows == merch[i : i + 1, :], one, zero)
                both = dot_rows(both, hot, ((1,), (1,)))
            tables.append(both[:t_count] + both[t_count:])
        hi, lo = split2(jnp.swapaxes(jnp.stack(tables, 0), 0, 1))
        hi_ref[:, pl.ds(start, size), :] = hi
        lo_ref[:, pl.ds(start, size), :] = lo
        return carry

    lax.fori_loop(0, count // size, group, 0)
    token_ref[...] = jnp.zeros_like(token_ref)


def table_call(filt, pack, n, first, count, after):
    t_count = filt.shape[0]
    hi, lo, token = pl.pallas_call(
        lambda *refs: table_body(n, first, count, *refs[:2], *refs[-3:]),
        in_specs=[VMEM] * 2 + [ANY] * len(after),
        out_specs=[VMEM] * 3,
        out_shape=[pltpu.VMEM((t_count, count, LANES), bf16)] * 2 + [pltpu.VMEM((8, LANES), f32)],
        compiler_params=PARAMS,
        cost_estimate=pl.CostEstimate(
            flops=4 * count * t_count * LANES * LANES, transcendentals=0, bytes_accessed=count * 60000
        ),
        name="tables",
    )(filt, pack, *after)
    return (hi, lo), token


def spread_body(n, t_first, t_count, parts, packs, count, u_ref, *refs):
    p = n // LANES
    w = u_ref[...] * total_of(refs[:parts])
    pack_refs = refs[parts : parts + packs]
    pair_refs = refs[parts + packs : parts + packs + 2 * count]
    o_ref, w_ref = refs[-2:]
    w_ref[...] = w[:, :n]
    seg = jnp.concatenate([flat(pack[n + p : n + 2 * p, :]).astype(jnp.int32) for pack in pack_refs], 1)
    hot = lax.broadcasted_iota(jnp.int32, (SEG, w.shape[1]), 0) == seg
    whi, wlo = split2(jnp.where(hot, w, 0.0))
    both = jnp.concatenate([whi, wlo], 0)

    def take(part, t):
        return jnp.concatenate(
            [jnp.concatenate([pair_refs[2 * k + part][t + q] for k in range(count)], 0) for q in range(2)], 1
        )

    for t in range(t_first, t_first + t_count, 2):
        two = jnp.dot(both, take(0, t), preferred_element_type=f32)
        out = two[:SEG] + two[SEG:] + jnp.dot(whi, take(1, t), preferred_element_type=f32)
        o_ref[t - t_first] = out[:, :LANES]
        o_ref[t - t_first + 1] = out[:, LANES:]


def spread_call(n, u, partials, packs, pairs, t_first, t_count, after):
    refs = [ref for pair in pairs for ref in pair]
    args = [u, *partials, *packs, *refs]
    return pl.pallas_call(
        lambda *refs: spread_body(
            n, t_first, t_count, len(partials), len(packs), len(pairs), *refs[: len(args)], *refs[-2:]
        ),
        in_specs=[VMEM] * len(args) + [ANY] * len(after),
        out_specs=[VMEM] * 2,
        out_shape=[pltpu.VMEM((t_count, SEG, LANES), f32), jax.ShapeDtypeStruct((1, n), f32)],
        compiler_params=PARAMS,
        name="spread",
    )(*args, *after)


def move(x, axis, size, pair, step, flip):
    blocks = size // pair

    def away(b):
        return b ^ step if blocks & (blocks - 1) == 0 else (b + step) % blocks

    return lax.ppermute(
        x, axis, [(b * pair + r, away(b) * pair + (r ^ flip)) for b in range(blocks) for r in range(pair)]
    )


def gate(x, *after):
    return lax.optimization_barrier((x, *after))[0]


def per_device(
    n_cohort,
    n_cell,
    cohort_features,
    cell_features,
    cohort_region,
    cell_region,
    penalty,
    cohort_mass,
    cell_mass,
    cohort_segment,
    spend_merchant,
    spend_day,
    spend_amount,
):
    n, m = cohort_features.shape[0], cell_features.shape[0]
    t_dev = DAYS // n_cohort
    n_y, n_z = n_cohort // 2, n_cell // 2
    table = np.zeros((n_cohort, 2 * t_dev, LANES), np.float32)
    henderson = filter_table(DAYS)
    for me in range(n_cohort):
        for k, dest in enumerate((me ^ 1, me)):
            table[me, k * t_dev : (k + 1) * t_dev, :DAYS] = henderson[dest * t_dev : (dest + 1) * t_dev]

    over_y = lambda x: [move(x, "cohort", n_cohort, 2, step, 0) for step in range(1, n_y)]
    core = lambda x: move(x, "cohort", n_cohort, 2, 0, 1)
    along_z = lambda x: [x] + [move(x, "cell", n_cell, 2, step, 0) for step in range(1, n_z)]

    xpack, ypack, rpack, filt = first_call(
        cohort_features, cell_features, cohort_region, cohort_segment, cohort_mass, cell_region, cell_mass,
        jnp.asarray(table), (spend_merchant, spend_day, spend_amount),
    )
    xpacks = [xpack] + over_y(xpack)
    ypacks = [ypack, move(ypack, "cell", n_cell, 2, 0, 1)]
    rpacks = over_y(rpack)
    pairs = {}

    def tables(source, pack, first, count, token):
        pairs[source, first], token = table_call(filt, pack, n, first, count, [token])
        return token

    early = 3 * n // 4
    token = tables(0, rpack, 0, early, filt)
    blocks, partial = gibbs_call(n, m, xpacks, ypacks, penalty, [token])
    row_sums = lambda: pltpu.VMEM((1, len(xpacks) * n), f32)
    col_sums = lambda: pltpu.VMEM((1, len(ypacks) * m), f32)
    lines = along_z(partial)
    token = tables(0, rpack, early, n - early, partial)
    for iteration in range(ITERS):
        cohort_scale, column = half_step(
            cols_body, "cols", n, lines, xpacks, blocks, [row_sums(), col_sums()], [token]
        )
        cell_scale, partial = half_step(
            rows_body, "rows", m, [column, core(column)], ypacks, blocks,
            [jax.ShapeDtypeStruct((1, m), f32), row_sums()], [],
        )
        lines = along_z(partial)
        token = partial
        part = n // ITERS
        for source, pack in enumerate(rpacks):
            token = tables(1 + source, pack, iteration * part, part, token)
    ordered = [pairs[key] for key in sorted(pairs)]
    away, weights = spread_call(n, cohort_scale, lines, xpacks, ordered, 0, t_dev, [token])
    mine, _ = spread_call(n, cohort_scale, lines, xpacks, ordered, t_dev, t_dev, [token])
    out = mine + core(away)
    return (weights.reshape(-1), cell_scale.reshape(-1), out)


def solution(mesh):
    return jax.shard_map(
        functools.partial(per_device, mesh.shape["cohort"], mesh.shape["cell"]),
        mesh=mesh,
        in_specs=(
            P("cohort", None),
            P("cell", None),
            P("cohort"),
            P("cell"),
            P(),
            P("cohort"),
            P("cell"),
            P("cohort"),
            P("cohort", "cell"),
            P("cohort", "cell"),
            P("cohort", "cell"),
        ),
        out_specs=(P("cohort"), P("cell"), P("cohort", None, "cell")),
        check_vma=False,
    )
```

time: 75.4 us -> 70 us (0.928)
  waiting for transfers between devices: 2.83 us -> 17.3 us
  starting transfers between devices: 26.7 us -> 19.7 us
  local copies, waits for them, and re-layouts: 6.92 us -> 0.01 us
  Pallas kernels: 36.9 us -> 31.3 us
    ppermute x21 -> x15, waiting for transfers between devices: 2.83 us -> 17.3 us  [move(): lax.ppermute(x, axis, [(b * pair + r, away(b) * pair + (r ^ flip)) for b...]
    ppermute x21 -> x15, starting transfers between devices: 26.7 us -> 19.7 us  [move(): lax.ppermute(x, axis, [(b * pair + r, away(b) * pair + (r ^ flip)) for b...]
    unnamed x24 -> x2, local copies, waits for them, and re-layouts: 6.92 us -> 0.01 us
    pallas_call x14 -> x10, Pallas kernels: 32.9 us -> 27.3 us  [the longest x4 18.1 us: table_call(): pl.pallas_call(lambda *refs: table_body(n, first, count, *refs[:2], *refs...]
  transfers between devices with their start and end apart: 21 -> 15, of which waited for: 3 -> 4; matrix products, arithmetic and copies ran while one was open for 0% -> 0% of each run, Pallas kernels for 43% -> 37%
where the time goes in v5:
time: 70 us; the launch traced here: 69.8 us
  Pallas kernels  31.3 us (45%)
  starting transfers between devices  19.7 us (28%)
  waiting for transfers between devices  17.3 us (25%)
  between operations  0.78 us (1%)
  other arithmetic  0.74 us (1%)
    ppermute x15, starting transfers between devices, move(): lax.ppermute(x, axis, [(b * pair + r, away(b) * pair + (r ^ flip)) for b...  19.7 us
    pallas_call x4, Pallas kernels, table_call(): pl.pallas_call(lambda *refs: table_body(n, first, count, *refs[:2], *refs...  18.1 us
    ppermute x15, waiting for transfers between devices, move(): lax.ppermute(x, axis, [(b * pair + r, away(b) * pair + (r ^ flip)) for b...  17.3 us
    pallas_call x4, Pallas kernels, half_step(): pl.pallas_call(lambda *refs: body(size, len(partials), len(packs), len(bl...  5.02 us
    pallas_call x2, Pallas kernels, spread_call(): pl.pallas_call(lambda *refs: spread_body(n, t_first, t_count, len(partial...  3.96 us
    pallas_call x1, Pallas kernels, gibbs_call(): pl.pallas_call(lambda *refs: gibbs_body(n, m, len(xpacks), len(ypacks), *...  2.73 us
    pallas_call x1, Pallas kernels, first_call(): pl.pallas_call(first_body, in_specs=[HBM] * len(args), out_specs=[VMEM] *...  1.5 us
  transfers between devices with their start and end apart: 15, of which 4 were waited for; matrix products, arithmetic and copies ran while one was open for 0% of the time, Pallas kernels for 37%

profile of v5, /device:TPU:1, one launch (start us, length us, event | category | flops | bytes accessed | tf_op | source)
XLA Modules:
  0.0 69.8 jit_solution(16068878221032980772)
XLA Ops:
  0.6 0.0 copy-start
  0.6 1.5 %first.1 = (f32[524,128]{1,0:T(8,128)S(1)}, f32[520,128]{1,0:T(8,128)S(1)}, f32[1536,128]{1,0:T(8,128)S(1)}, f32[32,128]{1,0:T(8,128)S(1)}) custom-call(bf16[512,128]{1,0:T(8,128)(2,1)} %x_hbm.1, bf16[512,128]{1,0:T(8,128)(2,1)} %y_hbm.1, s32[4,128]{1,0:T(4,128)} %bitcast.7, s32[4,128]{1,0:T(4,128)} %bitcast.8, f32[4,128]{1,0:T(4,128)} %bitcast.9, ...), custom_call_target="tpu_custom_call" | custom-call | tf_op jit(solution)/shard_map/first/pallas_call | solution.py:155
  2.1 2.1 %collective-permute-start.9 = (f32[1536,128]{1,0:T(8,128)S(1)}, f32[1536,128]{1,0:T(8,128)S(1)}, u32[]{:S(2)}, u32[]{:S(2)}) collective-permute-start(f32[1536,128]{1,0:T(8,128)S(1)} %get-tuple-element.40.refs_1_), channel_id=1, source_target_pairs={{0,16},{8,24},{16,0},{24,8},{1,17},{9,25},{17,1},{25,9},{2,18},{10... | collective-permute-start | bytes 2359304 | tf_op jit(solution)/shard_map/ppermute | solution.py:357
  4.3 0.1 collective-permute-start
  4.4 1.4 %collective-permute-start.1 = (f32[520,128]{1,0:T(8,128)S(1)}, f32[520,128]{1,0:T(8,128)S(1)}, u32[]{:S(2)}, u32[]{:S(2)}) collective-permute-start(f32[520,128]{1,0:T(8,128)S(1)} %get-tuple-element.38.refs_2_), channel_id=1, source_target_pairs={{0,1},{1,0},{2,3},{3,2},{4,5},{5,4},{6,7},{7,6},{8,9},{9,8},{10,11... | collective-permute-start | bytes 798728 | tf_op jit(solution)/shard_map/ppermute | solution.py:357
  5.7 6.7 %tables.4 = (bf16[32,384,128]{2,1,0:T(8,128)(2,1)S(1)}, bf16[32,384,128]{2,1,0:T(8,128)(2,1)S(1)}, f32[8,128]{1,0:T(8,128)S(1)}) custom-call(f32[32,128]{1,0:T(8,128)S(1)} %get-tuple-element.39.refs_0_.refs_2_, f32[1536,128]{1,0:T(8,128)S(1)} %get-tuple-element.40.refs_1_, f32[32,128]{1,0:T(8,128)S(1)} %get-tuple-element.39.refs_0_.refs_2_), custom_call_target="tpu_custom_call" | custom-call | flops 805306368 | bytes 23040000 | tf_op jit(solution)/shard_map/tables/pallas_call | solution.py:298
  12.4 0.0 collective-permute-done.1.refs_3_
  12.4 14.9 %collective-permute-done.refs_1_.refs_5_.refs_6_ = f32[524,128]{1,0:T(8,128)S(1)} collective-permute-done((f32[524,128]{1,0:T(8,128)S(1)}, f32[524,128]{1,0:T(8,128)S(1)}, u32[]{:S(2)}, u32[]{:S(2)}) %collective-permute-start) | collective-permute-done | bytes 268320 | tf_op jit(solution)/shard_map/ppermute | solution.py:357
  27.3 0.0 copy-done
  27.3 2.7 %gibbs.1 = (bf16[512,512]{1,0:T(8,128)(2,1)S(1)}, bf16[512,512]{1,0:T(8,128)(2,1)S(1)}, bf16[512,512]{1,0:T(8,128)(2,1)S(1)}, bf16[512,512]{1,0:T(8,128)(2,1)S(1...) custom-call(f32[524,128]{1,0:T(8,128)S(1)} %get-tuple-element.37.ref, ...), custom_call_target="tpu_custom_call" | custom-call | flops 268435456 | bytes 4194304 | tf_op jit(solution)/shard_map/gibbs/pallas_call | solution.py:202
  30.1 3.3 %collective-permute-start.4 = (f32[1,1024]{1,0:T(1,128)S(1)}, f32[1,1024]{1,0:T(1,128)S(1)}, u32[]{:S(2)}, u32[]{:S(2)}) collective-permute-start(f32[1,1024]{1,0:T(1,128)S(1)} %get-tuple-element.42.refs_2_.refs_0_), channel_id=1, source_target_pairs={{0,6},{1,7},{2,4},{3,5},{4,2},{5,3},{6,0},{7,1},{8,14},{9,15},{10,... | collective-permute-start | bytes 12296 | tf_op jit(solution)/shard_map/ppermute | solution.py:357
  33.4 0.0 collective-permute-start.3
  33.4 0.4 collective-permute-start.2
  33.7 2.2 %tables.5 = (bf16[32,128,128]{2,1,0:T(8,128)(2,1)S(1)}, bf16[32,128,128]{2,1,0:T(8,128)(2,1)S(1)}, f32[8,128]{1,0:T(8,128)S(1)}) custom-call(f32[32,128]{1,0:T(8,128)S(1)} %get-tuple-element.39.refs_0_.refs_2_, f32[1536,128]{1,0:T(8,128)S(1)} %get-tuple-element.40.refs_1_, f32[1,1024]{1,0:T(1,128)S(1)} %get-tuple-element.42.refs_2_.refs_0_), custom_call_target="tpu_custom_call" | custom-call | flops 268435456 | bytes 7680000 | tf_op jit(solution)/shard_map/tables/pallas_call | solution.py:298
  36.0 0.0 collective-permute-done.4.refs_3_
  36.0 0.7 %collective-permute-done.3.refs_2_ = f32[1,1024]{1,0:T(1,128)S(1)} collective-permute-done((f32[1,1024]{1,0:T(1,128)S(1)}, f32[1,1024]{1,0:T(1,128)S(1)}, u32[]{:S(2)}, u32[]{:S(2)}) %collective-permute-start.3) | collective-permute-done | bytes 4128 | tf_op jit(solution)/shard_map/ppermute | solution.py:357
  36.7 0.0 collective-permute-done.2.refs_1_
  36.7 1.1 %cols.2 = (f32[1,1024]{1,0:T(1,128)}, f32[1,1024]{1,0:T(1,128)S(1)}) custom-call(f32[1,1024]{1,0:T(1,128)S(1)} %get-tuple-element.42.refs_2_.refs_0_, f32[1,1024]{1,0:T(1,128)S(1)} %collective-permute-done.2.refs_1_, f32[1,1024]{1,0:T(1,128)S(1)} %collective-permute-done.3.refs_2_, f32[1,1024]{1,0:T(1,128)S(1)} %collective-permute-done.4.refs_3_, ...), custom_call_target="tpu_custom_call" | custom-call | tf_op jit(solution)/shard_map/cols/pallas_call | solution.py:250
  37.9 3.0 %collective-permute-start.5 = (f32[1,1024]{1,0:T(1,128)S(1)}, f32[1,1024]{1,0:T(1,128)S(1)}, u32[]{:S(2)}, u32[]{:S(2)}) collective-permute-start(f32[1,1024]{1,0:T(1,128)S(1)} %get-tuple-element.52.refs_0_), channel_id=1, source_target_pairs={{0,8},{8,0},{16,24},{24,16},{1,9},{9,1},{17,25},{25,17},{2,10},{10... | collective-permute-start | bytes 12296 | tf_op jit(solution)/shard_map/ppermute | solution.py:357
  40.9 0.8 %collective-permute-done.5.refs_1_ = f32[1,1024]{1,0:T(1,128)S(1)} collective-permute-done((f32[1,1024]{1,0:T(1,128)S(1)}, f32[1,1024]{1,0:T(1,128)S(1)}, u32[]{:S(2)}, u32[]{:S(2)}) %collective-permute-start.5) | collective-permute-done | bytes 4128 | tf_op jit(solution)/shard_map/ppermute | solution.py:357
  41.7 1.6 %rows.2 = (f32[1,512]{1,0:T(1,128)}, f32[1,1024]{1,0:T(1,128)S(1)}) custom-call(f32[1,1024]{1,0:T(1,128)S(1)} %get-tuple-element.52.refs_0_, f32[1,1024]{1,0:T(1,128)S(1)} %collective-permute-done.5.refs_1_, f32[520,128]{1,0:T(8,128)S(1)} %get-tuple-element.38.refs_2_, f32[520,128]{1,0:T(8,128)S(1)} %collective-permute-done.1.refs_3_, ...), custom_call_target="tpu_custom_call" | custom-call | tf_op jit(solution)/shard_map/rows/pallas_call | solution.py:250
  43.3 1.9 %collective-permute-start.8 = (f32[1,1024]{1,0:T(1,128)S(1)}, f32[1,1024]{1,0:T(1,128)S(1)}, u32[]{:S(2)}, u32[]{:S(2)}) collective-permute-start(f32[1,1024]{1,0:T(1,128)S(1)} %get-tuple-element.53.refs_2_.refs_0_), channel_id=1, source_target_pairs={{0,6},{1,7},{2,4},{3,5},{4,2},{5,3},{6,0},{7,1},{8,14},{9,15},{10,... | collective-permute-start | bytes 12296 | tf_op jit(solution)/shard_map/ppermute | solution.py:357
  45.2 0.0 collective-permute-start.7
  45.2 1.7 %collective-permute-start.6 = (f32[1,1024]{1,0:T(1,128)S(1)}, f32[1,1024]{1,0:T(1,128)S(1)}, u32[]{:S(2)}, u32[]{:S(2)}) collective-permute-start(f32[1,1024]{1,0:T(1,128)S(1)} %get-tuple-element.53.refs_2_.refs_0_), channel_id=1, source_target_pairs={{0,2},{1,3},{2,0},{3,1},{4,6},{5,7},{6,4},{7,5},{8,10},{9,11},{10,... | collective-permute-start | bytes 12296 | tf_op jit(solution)/shard_map/ppermute | solution.py:357
  46.8 0.0 collective-permute-done.9.refs_1_
  46.8 4.5 %tables.6 = (bf16[32,256,128]{2,1,0:T(8,128)(2,1)S(1)}, bf16[32,256,128]{2,1,0:T(8,128)(2,1)S(1)}, f32[8,128]{1,0:T(8,128)S(1)}) custom-call(f32[32,128]{1,0:T(8,128)S(1)} %get-tuple-element.39.refs_0_.refs_2_, f32[1536,128]{1,0:T(8,128)S(1)} %collective-permute-done.9.refs_1_, f32[1,1024]{1,0:T(1,128)S(1)} %get-tuple-element.53.refs_2_.refs_0_), custom_call_target="tpu_custom_call" | custom-call | flops 536870912 | bytes 15360000 | tf_op jit(solution)/shard_map/tables/pallas_call | solution.py:298
  51.3 0.0 collective-permute-done.8.refs_3_
  51.3 0.0 collective-permute-done.7.refs_2_
  51.3 0.0 collective-permute-done.6.refs_1_
  51.4 0.7 cols.3
  52.0 1.2 %collective-permute-start.10 = (f32[1,1024]{1,0:T(1,128)S(1)}, f32[1,1024]{1,0:T(1,128)S(1)}, u32[]{:S(2)}, u32[]{:S(2)}) collective-permute-start(f32[1,1024]{1,0:T(1,128)S(1)} %get-tuple-element.56.refs_0_), channel_id=1, source_target_pairs={{0,8},{8,0},{16,24},{24,16},{1,9},{9,1},{17,25},{25,17},{2,10},{10... | collective-permute-start | bytes 12296 | tf_op jit(solution)/shard_map/ppermute | solution.py:357
  53.3 0.8 %collective-permute-done.10.refs_1_ = f32[1,1024]{1,0:T(1,128)S(1)} collective-permute-done((f32[1,1024]{1,0:T(1,128)S(1)}, f32[1,1024]{1,0:T(1,128)S(1)}, u32[]{:S(2)}, u32[]{:S(2)}) %collective-permute-start.10) | collective-permute-done | bytes 4128 | tf_op jit(solution)/shard_map/ppermute | solution.py:357
  54.1 1.6 %rows.3 = (f32[1,512]{1,0:T(1,128)}, f32[1,1024]{1,0:T(1,128)S(1)}) custom-call(f32[1,1024]{1,0:T(1,128)S(1)} %get-tuple-element.56.refs_0_, f32[1,1024]{1,0:T(1,128)S(1)} %collective-permute-done.10.refs_1_, f32[520,128]{1,0:T(8,128)S(1)} %get-tuple-element.38.refs_2_, f32[520,128]{1,0:T(8,128)S(1)} %collective-permute-done.1.refs_3_, ...), custom_call_target="tpu_custom_call" | custom-call | tf_op jit(solution)/shard_map/rows/pallas_call | solution.py:250
  55.7 1.9 %collective-permute-start.13 = (f32[1,1024]{1,0:T(1,128)S(1)}, f32[1,1024]{1,0:T(1,128)S(1)}, u32[]{:S(2)}, u32[]{:S(2)}) collective-permute-start(f32[1,1024]{1,0:T(1,128)S(1)} %get-tuple-element.57.refs_2_.refs_1_), channel_id=1, source_target_pairs={{0,6},{1,7},{2,4},{3,5},{4,2},{5,3},{6,0},{7,1},{8,14},{9,15},{10,... | collective-permute-start | bytes 12296 | tf_op jit(solution)/shard_map/ppermute | solution.py:357
  57.6 0.0 collective-permute-start.12
  57.6 1.7 %collective-permute-start.11 = (f32[1,1024]{1,0:T(1,128)S(1)}, f32[1,1024]{1,0:T(1,128)S(1)}, u32[]{:S(2)}, u32[]{:S(2)}) collective-permute-start(f32[1,1024]{1,0:T(1,128)S(1)} %get-tuple-element.57.refs_2_.refs_1_), channel_id=1, source_target_pairs={{0,2},{1,3},{2,0},{3,1},{4,6},{5,7},{6,4},{7,5},{8,10},{9,11},{10,... | collective-permute-start | bytes 12296 | tf_op jit(solution)/shard_map/ppermute | solution.py:357
  59.3 4.6 %tables.7 = (bf16[32,256,128]{2,1,0:T(8,128)(2,1)S(1)}, bf16[32,256,128]{2,1,0:T(8,128)(2,1)S(1)}, f32[8,128]{1,0:T(8,128)S(1)}) custom-call(f32[32,128]{1,0:T(8,128)S(1)} %get-tuple-element.39.refs_0_.refs_2_, f32[1536,128]{1,0:T(8,128)S(1)} %collective-permute-done.9.refs_1_, f32[1,1024]{1,0:T(1,128)S(1)} %get-tuple-element.57.refs_2_.refs_1_), custom_call_target="tpu_custom_call" | custom-call | flops 536870912 | bytes 15360000 | tf_op jit(solution)/shard_map/tables/pallas_call | solution.py:298
  63.9 0.0 collective-permute-done.13.refs_4_
  63.9 0.0 collective-permute-done.12.refs_3_
  63.9 0.0 collective-permute-done.11.refs_2_
  63.9 2.0 %spread.2 = (f32[16,32,128]{2,1,0:T(8,128)S(1)}, f32[1,512]{1,0:T(1,128)}) custom-call(f32[1,1024]{1,0:T(1,128)S(1)} %get-tuple-element.55.refs_0_, f32[1,1024]{1,0:T(1,128)S(1)} %get-tuple-element.57.refs_2_.refs_1_, f32[1,1024]{1,0:T(1,128)S(1)} %collective-permute-done.11.refs_2_, f32[1,1024]{1,0:T(1,128)S(1)} %collective-permute-done.12.refs_3_, ...), custom_call_target="tpu_custom_call" | custom-call | tf_op jit(solution)/shard_map/spread/pallas_call | solution.py:339
  65.9 1.2 %collective-permute-start.14 = (f32[16,32,128]{2,1,0:T(8,128)S(1)}, f32[16,32,128]{2,1,0:T(8,128)S(1)}, u32[]{:S(2)}, u32[]{:S(2)}) collective-permute-start(f32[16,32,128]{2,1,0:T(8,128)S(1)} %get-tuple-element.70), channel_id=1, source_target_pairs={{0,8},{8,0},{16,24},{24,16},{1,9},{9,1},{17,25},{25,17},{2,10},{10... | collective-permute-start | bytes 786440 | tf_op jit(solution)/shard_map/ppermute | solution.py:357
  67.1 2.0 %spread.3 = (f32[16,32,128]{2,1,0:T(8,128)S(1)}, f32[1,512]{1,0:T(1,128)}) custom-call(f32[1,1024]{1,0:T(1,128)S(1)} %get-tuple-element.55.refs_0_, f32[1,1024]{1,0:T(1,128)S(1)} %get-tuple-element.57.refs_2_.refs_1_, f32[1,1024]{1,0:T(1,128)S(1)} %collective-permute-done.11.refs_2_, f32[1,1024]{1,0:T(1,128)S(1)} %collective-permute-done.12.refs_3_, ...), custom_call_target="tpu_custom_call" | custom-call | tf_op jit(solution)/shard_map/spread/pallas_call | solution.py:339
  69.1 0.0 collective-permute-done.14
  69.1 0.7 %add.3 = f32[16,32,128]{2,1,0:T(8,128)} add(f32[16,32,128]{2,1,0:T(8,128)S(1)} %get-tuple-element.69, f32[16,32,128]{2,1,0:T(8,128)S(1)} %collective-permute-done.14) | non-fusion elementwise | flops 65536 | bytes 786432 | tf_op jit(solution)/shard_map/add | solution.py:430
Async XLA Ops:
  0.6 26.7 %copy-start = (f32[32,32]{1,0:T(8,128)S(1)}, f32[32,32]{1,0:T(8,128)}, u32[]{:S(2)}) copy-start(f32[32,32]{1,0:T(8,128)} %refs_4_.1) | copy-start | bytes 12292
  2.1 44.7 %collective-permute-start.9 = (f32[1536,128]{1,0:T(8,128)S(1)}, f32[1536,128]{1,0:T(8,128)S(1)}, u32[]{:S(2)}, u32[]{:S(2)}) collective-permute-start(f32[1536,128]{1,0:T(8,128)S(1)} %get-tuple-element.40.refs_1_), channel_id=1, source_target_pairs={{0,16},{8,24},{16,0},{24,8},{1,17},{9,25},{17,1},{25,9},{2,18},{10... | collective-permute-start | bytes 2359304 | tf_op jit(solution)/shard_map/ppermute | solution.py:357
  4.3 23.1 %collective-permute-start = (f32[524,128]{1,0:T(8,128)S(1)}, f32[524,128]{1,0:T(8,128)S(1)}, u32[]{:S(2)}, u32[]{:S(2)}) collective-permute-start(f32[524,128]{1,0:T(8,128)S(1)} %get-tuple-element.37.refs_0_.refs_4_.refs_5_), channel_id=1, source_target_pairs={{0,16},{8,24},{16,0},{24,8},{1,17},{9,25},{17,1},{25,9},{2,18},{10... | collective-permute-start | bytes 804872 | tf_op jit(solution)/shard_map/ppermute | solution.py:357
  4.4 8.1 %collective-permute-start.1 = (f32[520,128]{1,0:T(8,128)S(1)}, f32[520,128]{1,0:T(8,128)S(1)}, u32[]{:S(2)}, u32[]{:S(2)}) collective-permute-start(f32[520,128]{1,0:T(8,128)S(1)} %get-tuple-element.38.refs_2_), channel_id=1, source_target_pairs={{0,1},{1,0},{2,3},{3,2},{4,5},{5,4},{6,7},{7,6},{8,9},{9,8},{10,11... | collective-permute-start | bytes 798728 | tf_op jit(solution)/shard_map/ppermute | solution.py:357
  30.1 5.9 %collective-permute-start.4 = (f32[1,1024]{1,0:T(1,128)S(1)}, f32[1,1024]{1,0:T(1,128)S(1)}, u32[]{:S(2)}, u32[]{:S(2)}) collective-permute-start(f32[1,1024]{1,0:T(1,128)S(1)} %get-tuple-element.42.refs_2_.refs_0_), channel_id=1, source_target_pairs={{0,6},{1,7},{2,4},{3,5},{4,2},{5,3},{6,0},{7,1},{8,14},{9,15},{10,... | collective-permute-start | bytes 12296 | tf_op jit(solution)/shard_map/ppermute | solution.py:357
  33.4 3.4 %collective-permute-start.3 = (f32[1,1024]{1,0:T(1,128)S(1)}, f32[1,1024]{1,0:T(1,128)S(1)}, u32[]{:S(2)}, u32[]{:S(2)}) collective-permute-start(f32[1,1024]{1,0:T(1,128)S(1)} %get-tuple-element.42.refs_2_.refs_0_), channel_id=1, source_target_pairs={{0,4},{1,5},{2,6},{3,7},{4,0},{5,1},{6,2},{7,3},{8,12},{9,13},{10,... | collective-permute-start | bytes 12296 | tf_op jit(solution)/shard_map/ppermute | solution.py:357
  33.4 3.4 %collective-permute-start.2 = (f32[1,1024]{1,0:T(1,128)S(1)}, f32[1,1024]{1,0:T(1,128)S(1)}, u32[]{:S(2)}, u32[]{:S(2)}) collective-permute-start(f32[1,1024]{1,0:T(1,128)S(1)} %get-tuple-element.42.refs_2_.refs_0_), channel_id=1, source_target_pairs={{0,2},{1,3},{2,0},{3,1},{4,6},{5,7},{6,4},{7,5},{8,10},{9,11},{10,... | collective-permute-start | bytes 12296 | tf_op jit(solution)/shard_map/ppermute | solution.py:357
  37.9 3.8 %collective-permute-start.5 = (f32[1,1024]{1,0:T(1,128)S(1)}, f32[1,1024]{1,0:T(1,128)S(1)}, u32[]{:S(2)}, u32[]{:S(2)}) collective-permute-start(f32[1,1024]{1,0:T(1,128)S(1)} %get-tuple-element.52.refs_0_), channel_id=1, source_target_pairs={{0,8},{8,0},{16,24},{24,16},{1,9},{9,1},{17,25},{25,17},{2,10},{10... | collective-permute-start | bytes 12296 | tf_op jit(solution)/shard_map/ppermute | solution.py:357
  43.3 8.0 %collective-permute-start.8 = (f32[1,1024]{1,0:T(1,128)S(1)}, f32[1,1024]{1,0:T(1,128)S(1)}, u32[]{:S(2)}, u32[]{:S(2)}) collective-permute-start(f32[1,1024]{1,0:T(1,128)S(1)} %get-tuple-element.53.refs_2_.refs_0_), channel_id=1, source_target_pairs={{0,6},{1,7},{2,4},{3,5},{4,2},{5,3},{6,0},{7,1},{8,14},{9,15},{10,... | collective-permute-start | bytes 12296 | tf_op jit(solution)/shard_map/ppermute | solution.py:357
  45.2 6.2 %collective-permute-start.7 = (f32[1,1024]{1,0:T(1,128)S(1)}, f32[1,1024]{1,0:T(1,128)S(1)}, u32[]{:S(2)}, u32[]{:S(2)}) collective-permute-start(f32[1,1024]{1,0:T(1,128)S(1)} %get-tuple-element.53.refs_2_.refs_0_), channel_id=1, source_target_pairs={{0,4},{1,5},{2,6},{3,7},{4,0},{5,1},{6,2},{7,3},{8,12},{9,13},{10,... | collective-permute-start | bytes 12296 | tf_op jit(solution)/shard_map/ppermute | solution.py:357
  45.2 6.2 %collective-permute-start.6 = (f32[1,1024]{1,0:T(1,128)S(1)}, f32[1,1024]{1,0:T(1,128)S(1)}, u32[]{:S(2)}, u32[]{:S(2)}) collective-permute-start(f32[1,1024]{1,0:T(1,128)S(1)} %get-tuple-element.53.refs_2_.refs_0_), channel_id=1, source_target_pairs={{0,2},{1,3},{2,0},{3,1},{4,6},{5,7},{6,4},{7,5},{8,10},{9,11},{10,... | collective-permute-start | bytes 12296 | tf_op jit(solution)/shard_map/ppermute | solution.py:357
  52.0 2.1 %collective-permute-start.10 = (f32[1,1024]{1,0:T(1,128)S(1)}, f32[1,1024]{1,0:T(1,128)S(1)}, u32[]{:S(2)}, u32[]{:S(2)}) collective-permute-start(f32[1,1024]{1,0:T(1,128)S(1)} %get-tuple-element.56.refs_0_), channel_id=1, source_target_pairs={{0,8},{8,0},{16,24},{24,16},{1,9},{9,1},{17,25},{25,17},{2,10},{10... | collective-permute-start | bytes 12296 | tf_op jit(solution)/shard_map/ppermute | solution.py:357
  55.7 8.2 %collective-permute-start.13 = (f32[1,1024]{1,0:T(1,128)S(1)}, f32[1,1024]{1,0:T(1,128)S(1)}, u32[]{:S(2)}, u32[]{:S(2)}) collective-permute-start(f32[1,1024]{1,0:T(1,128)S(1)} %get-tuple-element.57.refs_2_.refs_1_), channel_id=1, source_target_pairs={{0,6},{1,7},{2,4},{3,5},{4,2},{5,3},{6,0},{7,1},{8,14},{9,15},{10,... | collective-permute-start | bytes 12296 | tf_op jit(solution)/shard_map/ppermute | solution.py:357
  57.6 6.3 %collective-permute-start.12 = (f32[1,1024]{1,0:T(1,128)S(1)}, f32[1,1024]{1,0:T(1,128)S(1)}, u32[]{:S(2)}, u32[]{:S(2)}) collective-permute-start(f32[1,1024]{1,0:T(1,128)S(1)} %get-tuple-element.57.refs_2_.refs_1_), channel_id=1, source_target_pairs={{0,4},{1,5},{2,6},{3,7},{4,0},{5,1},{6,2},{7,3},{8,12},{9,13},{10,... | collective-permute-start | bytes 12296 | tf_op jit(solution)/shard_map/ppermute | solution.py:357
  57.6 6.3 %collective-permute-start.11 = (f32[1,1024]{1,0:T(1,128)S(1)}, f32[1,1024]{1,0:T(1,128)S(1)}, u32[]{:S(2)}, u32[]{:S(2)}) collective-permute-start(f32[1,1024]{1,0:T(1,128)S(1)} %get-tuple-element.57.refs_2_.refs_1_), channel_id=1, source_target_pairs={{0,2},{1,3},{2,0},{3,1},{4,6},{5,7},{6,4},{7,5},{8,10},{9,11},{10,... | collective-permute-start | bytes 12296 | tf_op jit(solution)/shard_map/ppermute | solution.py:357
  65.9 3.2 %collective-permute-start.14 = (f32[16,32,128]{2,1,0:T(8,128)S(1)}, f32[16,32,128]{2,1,0:T(8,128)S(1)}, u32[]{:S(2)}, u32[]{:S(2)}) collective-permute-start(f32[16,32,128]{2,1,0:T(8,128)S(1)} %get-tuple-element.70), channel_id=1, source_target_pairs={{0,8},{8,0},{16,24},{24,16},{1,9},{9,1},{17,25},{25,17},{2,10},{10... | collective-permute-start | bytes 786440 | tf_op jit(solution)/shard_map/ppermute | solution.py:357

commit v6 on v5

--- a/solution.py
+++ b/solution.py
@@ -397,7 +397,7 @@
     )
     xpacks = [xpack] + over_y(xpack)
     ypacks = [ypack, move(ypack, "cell", n_cell, 2, 0, 1)]
-    rpacks = over_y(rpack)
+    rpacks = over_y(gate(rpack, *xpacks))
     pairs = {}
 
     def tables(source, pack, first, count, token):

time: 70 us -> 62.9 us (0.90)
  waiting for transfers between devices: 17.3 us -> 8.91 us
  starting transfers between devices: 19.7 us -> 21 us
    ppermute x15, waiting for transfers between devices: 17.3 us -> 8.91 us  [move(): lax.ppermute(x, axis, [(b * pair + r, away(b) * pair + (r ^ flip)) for b...]
    ppermute x15, starting transfers between devices: 19.7 us -> 21 us  [move(): lax.ppermute(x, axis, [(b * pair + r, away(b) * pair + (r ^ flip)) for b...]
  transfers between devices with their start and end apart: 15 -> 15, of which waited for: 4 -> 4; matrix products, arithmetic and copies ran while one was open for 0% -> 0% of each run, Pallas kernels for 37% -> 41%
where the time goes in v6:
time: 62.9 us; the launch traced here: 62.7 us
  Pallas kernels  31.3 us (50%)
  starting transfers between devices  21 us (33%)
  waiting for transfers between devices  8.91 us (14%)
  between operations  0.78 us (1%)
  other arithmetic  0.74 us (1%)
    ppermute x15, starting transfers between devices, move(): lax.ppermute(x, axis, [(b * pair + r, away(b) * pair + (r ^ flip)) for b...  21 us
    pallas_call x4, Pallas kernels, table_call(): pl.pallas_call(lambda *refs: table_body(n, first, count, *refs[:2], *refs...  18.1 us
    ppermute x15, waiting for transfers between devices, move(): lax.ppermute(x, axis, [(b * pair + r, away(b) * pair + (r ^ flip)) for b...  8.91 us
    pallas_call x4, Pallas kernels, half_step(): pl.pallas_call(lambda *refs: body(size, len(partials), len(packs), len(bl...  5.02 us
    pallas_call x2, Pallas kernels, spread_call(): pl.pallas_call(lambda *refs: spread_body(n, t_first, t_count, len(partial...  3.96 us
    pallas_call x1, Pallas kernels, gibbs_call(): pl.pallas_call(lambda *refs: gibbs_body(n, m, len(xpacks), len(ypacks), *...  2.74 us
    pallas_call x1, Pallas kernels, first_call(): pl.pallas_call(first_body, in_specs=[HBM] * len(args), out_specs=[VMEM] *...  1.5 us
  transfers between devices with their start and end apart: 15, of which 4 were waited for; matrix products, arithmetic and copies ran while one was open for 0% of the time, Pallas kernels for 41%

profile of v6, /device:TPU:1, one launch (start us, length us, event | category | flops | bytes accessed | tf_op | source)
XLA Modules:
  0.0 62.7 jit_solution(2123301841720761299)
XLA Ops:
  0.6 0.0 copy-start
  0.6 1.5 %first.1 = (f32[524,128]{1,0:T(8,128)S(1)}, f32[520,128]{1,0:T(8,128)S(1)}, f32[1536,128]{1,0:T(8,128)S(1)}, f32[32,128]{1,0:T(8,128)S(1)}) custom-call(bf16[512,128]{1,0:T(8,128)(2,1)} %x_hbm.1, bf16[512,128]{1,0:T(8,128)(2,1)} %y_hbm.1, s32[4,128]{1,0:T(4,128)} %bitcast.7, s32[4,128]{1,0:T(4,128)} %bitcast.8, f32[4,128]{1,0:T(4,128)} %bitcast.9, ...), custom_call_target="tpu_custom_call" | custom-call | tf_op jit(solution)/shard_map/first/pallas_call | solution.py:155
  2.1 2.1 %collective-permute-start = (f32[524,128]{1,0:T(8,128)S(1)}, f32[524,128]{1,0:T(8,128)S(1)}, u32[]{:S(2)}, u32[]{:S(2)}) collective-permute-start(f32[524,128]{1,0:T(8,128)S(1)} %get-tuple-element.38.refs_0_.refs_4_.refs_5_), channel_id=1, source_target_pairs={{0,16},{8,24},{16,0},{24,8},{1,17},{9,25},{17,1},{25,9},{2,18},{10... | collective-permute-start | bytes 804872 | tf_op jit(solution)/shard_map/ppermute | solution.py:357
  4.3 6.2 %collective-permute-done.refs_1_.refs_5_.refs_6_ = f32[524,128]{1,0:T(8,128)S(1)} collective-permute-done((f32[524,128]{1,0:T(8,128)S(1)}, f32[524,128]{1,0:T(8,128)S(1)}, u32[]{:S(2)}, u32[]{:S(2)}) %collective-permute-start) | collective-permute-done | bytes 268320 | tf_op jit(solution)/shard_map/ppermute | solution.py:357
  10.5 1.1 %collective-permute-start.9 = (f32[1536,128]{1,0:T(8,128)S(1)}, f32[1536,128]{1,0:T(8,128)S(1)}, u32[]{:S(2)}, u32[]{:S(2)}) collective-permute-start(f32[1536,128]{1,0:T(8,128)S(1)} %get-tuple-element.55.refs_1_), channel_id=1, source_target_pairs={{0,16},{8,24},{16,0},{24,8},{1,17},{9,25},{17,1},{25,9},{2,18},{10... | collective-permute-start | bytes 2359304 | tf_op jit(solution)/shard_map/ppermute | solution.py:357
  11.6 1.2 %collective-permute-start.1 = (f32[520,128]{1,0:T(8,128)S(1)}, f32[520,128]{1,0:T(8,128)S(1)}, u32[]{:S(2)}, u32[]{:S(2)}) collective-permute-start(f32[520,128]{1,0:T(8,128)S(1)} %get-tuple-element.39.refs_2_), channel_id=1, source_target_pairs={{0,1},{1,0},{2,3},{3,2},{4,5},{5,4},{6,7},{7,6},{8,9},{9,8},{10,11... | collective-permute-start | bytes 798728 | tf_op jit(solution)/shard_map/ppermute | solution.py:357
  12.8 6.7 %tables.4 = (bf16[32,384,128]{2,1,0:T(8,128)(2,1)S(1)}, bf16[32,384,128]{2,1,0:T(8,128)(2,1)S(1)}, f32[8,128]{1,0:T(8,128)S(1)}) custom-call(f32[32,128]{1,0:T(8,128)S(1)} %get-tuple-element.40.refs_0_.refs_2_, f32[1536,128]{1,0:T(8,128)S(1)} %get-tuple-element.55.refs_1_, f32[32,128]{1,0:T(8,128)S(1)} %get-tuple-element.40.refs_0_.refs_2_), custom_call_target="tpu_custom_call" | custom-call | flops 805306368 | bytes 23040000 | tf_op jit(solution)/shard_map/tables/pallas_call | solution.py:298
  19.6 0.0 collective-permute-done.1.refs_3_
  19.6 0.0 copy-done
  19.6 2.7 %gibbs.1 = (bf16[512,512]{1,0:T(8,128)(2,1)S(1)}, bf16[512,512]{1,0:T(8,128)(2,1)S(1)}, bf16[512,512]{1,0:T(8,128)(2,1)S(1)}, bf16[512,512]{1,0:T(8,128)(2,1)S(1...) custom-call(f32[524,128]{1,0:T(8,128)S(1)} %get-tuple-element.38.ref, ...), custom_call_target="tpu_custom_call" | custom-call | flops 268435456 | bytes 4194304 | tf_op jit(solution)/shard_map/gibbs/pallas_call | solution.py:202
  22.3 3.4 %collective-permute-start.4 = (f32[1,1024]{1,0:T(1,128)S(1)}, f32[1,1024]{1,0:T(1,128)S(1)}, u32[]{:S(2)}, u32[]{:S(2)}) collective-permute-start(f32[1,1024]{1,0:T(1,128)S(1)} %get-tuple-element.43.refs_2_.refs_0_), channel_id=1, source_target_pairs={{0,6},{1,7},{2,4},{3,5},{4,2},{5,3},{6,0},{7,1},{8,14},{9,15},{10,... | collective-permute-start | bytes 12296 | tf_op jit(solution)/shard_map/ppermute | solution.py:357
  25.7 0.0 collective-permute-start.3
  25.7 0.4 collective-permute-start.2
  26.1 2.2 %tables.5 = (bf16[32,128,128]{2,1,0:T(8,128)(2,1)S(1)}, bf16[32,128,128]{2,1,0:T(8,128)(2,1)S(1)}, f32[8,128]{1,0:T(8,128)S(1)}) custom-call(f32[32,128]{1,0:T(8,128)S(1)} %get-tuple-element.40.refs_0_.refs_2_, f32[1536,128]{1,0:T(8,128)S(1)} %get-tuple-element.55.refs_1_, f32[1,1024]{1,0:T(1,128)S(1)} %get-tuple-element.43.refs_2_.refs_0_), custom_call_target="tpu_custom_call" | custom-call | flops 268435456 | bytes 7680000 | tf_op jit(solution)/shard_map/tables/pallas_call | solution.py:298
  28.3 0.0 collective-permute-done.4.refs_3_
  28.3 1.0 %collective-permute-done.3.refs_2_ = f32[1,1024]{1,0:T(1,128)S(1)} collective-permute-done((f32[1,1024]{1,0:T(1,128)S(1)}, f32[1,1024]{1,0:T(1,128)S(1)}, u32[]{:S(2)}, u32[]{:S(2)}) %collective-permute-start.3) | collective-permute-done | bytes 4128 | tf_op jit(solution)/shard_map/ppermute | solution.py:357
  29.4 0.0 collective-permute-done.2.refs_1_
  29.4 1.1 %cols.2 = (f32[1,1024]{1,0:T(1,128)}, f32[1,1024]{1,0:T(1,128)S(1)}) custom-call(f32[1,1024]{1,0:T(1,128)S(1)} %get-tuple-element.43.refs_2_.refs_0_, f32[1,1024]{1,0:T(1,128)S(1)} %collective-permute-done.2.refs_1_, f32[1,1024]{1,0:T(1,128)S(1)} %collective-permute-done.3.refs_2_, f32[1,1024]{1,0:T(1,128)S(1)} %collective-permute-done.4.refs_3_, ...), custom_call_target="tpu_custom_call" | custom-call | tf_op jit(solution)/shard_map/cols/pallas_call | solution.py:250
  30.5 3.2 %collective-permute-start.5 = (f32[1,1024]{1,0:T(1,128)S(1)}, f32[1,1024]{1,0:T(1,128)S(1)}, u32[]{:S(2)}, u32[]{:S(2)}) collective-permute-start(f32[1,1024]{1,0:T(1,128)S(1)} %get-tuple-element.53.refs_0_), channel_id=1, source_target_pairs={{0,8},{8,0},{16,24},{24,16},{1,9},{9,1},{17,25},{25,17},{2,10},{10... | collective-permute-start | bytes 12296 | tf_op jit(solution)/shard_map/ppermute | solution.py:357
  33.7 0.8 %collective-permute-done.5.refs_1_ = f32[1,1024]{1,0:T(1,128)S(1)} collective-permute-done((f32[1,1024]{1,0:T(1,128)S(1)}, f32[1,1024]{1,0:T(1,128)S(1)}, u32[]{:S(2)}, u32[]{:S(2)}) %collective-permute-start.5) | collective-permute-done | bytes 4128 | tf_op jit(solution)/shard_map/ppermute | solution.py:357
  34.6 1.6 %rows.2 = (f32[1,512]{1,0:T(1,128)}, f32[1,1024]{1,0:T(1,128)S(1)}) custom-call(f32[1,1024]{1,0:T(1,128)S(1)} %get-tuple-element.53.refs_0_, f32[1,1024]{1,0:T(1,128)S(1)} %collective-permute-done.5.refs_1_, f32[520,128]{1,0:T(8,128)S(1)} %get-tuple-element.39.refs_2_, f32[520,128]{1,0:T(8,128)S(1)} %collective-permute-done.1.refs_3_, ...), custom_call_target="tpu_custom_call" | custom-call | tf_op jit(solution)/shard_map/rows/pallas_call | solution.py:250
  36.2 1.9 %collective-permute-start.8 = (f32[1,1024]{1,0:T(1,128)S(1)}, f32[1,1024]{1,0:T(1,128)S(1)}, u32[]{:S(2)}, u32[]{:S(2)}) collective-permute-start(f32[1,1024]{1,0:T(1,128)S(1)} %get-tuple-element.54.refs_2_.refs_0_), channel_id=1, source_target_pairs={{0,6},{1,7},{2,4},{3,5},{4,2},{5,3},{6,0},{7,1},{8,14},{9,15},{10,... | collective-permute-start | bytes 12296 | tf_op jit(solution)/shard_map/ppermute | solution.py:357
  38.1 0.0 collective-permute-start.7
  38.1 1.7 %collective-permute-start.6 = (f32[1,1024]{1,0:T(1,128)S(1)}, f32[1,1024]{1,0:T(1,128)S(1)}, u32[]{:S(2)}, u32[]{:S(2)}) collective-permute-start(f32[1,1024]{1,0:T(1,128)S(1)} %get-tuple-element.54.refs_2_.refs_0_), channel_id=1, source_target_pairs={{0,2},{1,3},{2,0},{3,1},{4,6},{5,7},{6,4},{7,5},{8,10},{9,11},{10,... | collective-permute-start | bytes 12296 | tf_op jit(solution)/shard_map/ppermute | solution.py:357
  39.7 0.0 collective-permute-done.9.refs_1_
  39.7 4.5 %tables.6 = (bf16[32,256,128]{2,1,0:T(8,128)(2,1)S(1)}, bf16[32,256,128]{2,1,0:T(8,128)(2,1)S(1)}, f32[8,128]{1,0:T(8,128)S(1)}) custom-call(f32[32,128]{1,0:T(8,128)S(1)} %get-tuple-element.40.refs_0_.refs_2_, f32[1536,128]{1,0:T(8,128)S(1)} %collective-permute-done.9.refs_1_, f32[1,1024]{1,0:T(1,128)S(1)} %get-tuple-element.54.refs_2_.refs_0_), custom_call_target="tpu_custom_call" | custom-call | flops 536870912 | bytes 15360000 | tf_op jit(solution)/shard_map/tables/pallas_call | solution.py:298
  44.2 0.0 collective-permute-done.8.refs_3_
  44.2 0.0 collective-permute-done.7.refs_2_
  44.2 0.0 collective-permute-done.6.refs_1_
  44.2 0.7 %cols.3 = (f32[1,1024]{1,0:T(1,128)S(1)}, f32[1,1024]{1,0:T(1,128)S(1)}) custom-call(f32[1,1024]{1,0:T(1,128)S(1)} %get-tuple-element.54.refs_2_.refs_0_, f32[1,1024]{1,0:T(1,128)S(1)} %collective-permute-done.6.refs_1_, f32[1,1024]{1,0:T(1,128)S(1)} %collective-permute-done.7.refs_2_, f32[1,1024]{1,0:T(1,128)S(1)} %collective-permute-done.8.refs_3_, ...), custom_call_target="tpu_custom_call" | custom-call | tf_op jit(solution)/shard_map/cols/pallas_call | solution.py:250
  44.9 1.2 %collective-permute-start.10 = (f32[1,1024]{1,0:T(1,128)S(1)}, f32[1,1024]{1,0:T(1,128)S(1)}, u32[]{:S(2)}, u32[]{:S(2)}) collective-permute-start(f32[1,1024]{1,0:T(1,128)S(1)} %get-tuple-element.58.refs_0_), channel_id=1, source_target_pairs={{0,8},{8,0},{16,24},{24,16},{1,9},{9,1},{17,25},{25,17},{2,10},{10... | collective-permute-start | bytes 12296 | tf_op jit(solution)/shard_map/ppermute | solution.py:357
  46.2 0.8 %collective-permute-done.10.refs_1_ = f32[1,1024]{1,0:T(1,128)S(1)} collective-permute-done((f32[1,1024]{1,0:T(1,128)S(1)}, f32[1,1024]{1,0:T(1,128)S(1)}, u32[]{:S(2)}, u32[]{:S(2)}) %collective-permute-start.10) | collective-permute-done | bytes 4128 | tf_op jit(solution)/shard_map/ppermute | solution.py:357
  47.0 1.6 %rows.3 = (f32[1,512]{1,0:T(1,128)}, f32[1,1024]{1,0:T(1,128)S(1)}) custom-call(f32[1,1024]{1,0:T(1,128)S(1)} %get-tuple-element.58.refs_0_, f32[1,1024]{1,0:T(1,128)S(1)} %collective-permute-done.10.refs_1_, f32[520,128]{1,0:T(8,128)S(1)} %get-tuple-element.39.refs_2_, f32[520,128]{1,0:T(8,128)S(1)} %collective-permute-done.1.refs_3_, ...), custom_call_target="tpu_custom_call" | custom-call | tf_op jit(solution)/shard_map/rows/pallas_call | solution.py:250
  48.6 1.9 %collective-permute-start.13 = (f32[1,1024]{1,0:T(1,128)S(1)}, f32[1,1024]{1,0:T(1,128)S(1)}, u32[]{:S(2)}, u32[]{:S(2)}) collective-permute-start(f32[1,1024]{1,0:T(1,128)S(1)} %get-tuple-element.59.refs_2_.refs_1_), channel_id=1, source_target_pairs={{0,6},{1,7},{2,4},{3,5},{4,2},{5,3},{6,0},{7,1},{8,14},{9,15},{10,... | collective-permute-start | bytes 12296 | tf_op jit(solution)/shard_map/ppermute | solution.py:357
  50.5 0.0 collective-permute-start.12
  50.5 1.7 %collective-permute-start.11 = (f32[1,1024]{1,0:T(1,128)S(1)}, f32[1,1024]{1,0:T(1,128)S(1)}, u32[]{:S(2)}, u32[]{:S(2)}) collective-permute-start(f32[1,1024]{1,0:T(1,128)S(1)} %get-tuple-element.59.refs_2_.refs_1_), channel_id=1, source_target_pairs={{0,2},{1,3},{2,0},{3,1},{4,6},{5,7},{6,4},{7,5},{8,10},{9,11},{10,... | collective-permute-start | bytes 12296 | tf_op jit(solution)/shard_map/ppermute | solution.py:357
  52.1 4.6 %tables.7 = (bf16[32,256,128]{2,1,0:T(8,128)(2,1)S(1)}, bf16[32,256,128]{2,1,0:T(8,128)(2,1)S(1)}, f32[8,128]{1,0:T(8,128)S(1)}) custom-call(f32[32,128]{1,0:T(8,128)S(1)} %get-tuple-element.40.refs_0_.refs_2_, f32[1536,128]{1,0:T(8,128)S(1)} %collective-permute-done.9.refs_1_, f32[1,1024]{1,0:T(1,128)S(1)} %get-tuple-element.59.refs_2_.refs_1_), custom_call_target="tpu_custom_call" | custom-call | flops 536870912 | bytes 15360000 | tf_op jit(solution)/shard_map/tables/pallas_call | solution.py:298
  56.8 0.0 collective-permute-done.13.refs_4_
  56.8 0.0 collective-permute-done.12.refs_3_
  56.8 0.0 collective-permute-done.11.refs_2_
  56.8 2.0 %spread.2 = (f32[16,32,128]{2,1,0:T(8,128)S(1)}, f32[1,512]{1,0:T(1,128)}) custom-call(f32[1,1024]{1,0:T(1,128)S(1)} %get-tuple-element.57.refs_0_, f32[1,1024]{1,0:T(1,128)S(1)} %get-tuple-element.59.refs_2_.refs_1_, f32[1,1024]{1,0:T(1,128)S(1)} %collective-permute-done.11.refs_2_, f32[1,1024]{1,0:T(1,128)S(1)} %collective-permute-done.12.refs_3_, ...), custom_call_target="tpu_custom_call" | custom-call | tf_op jit(solution)/shard_map/spread/pallas_call | solution.py:339
  58.8 1.2 %collective-permute-start.14 = (f32[16,32,128]{2,1,0:T(8,128)S(1)}, f32[16,32,128]{2,1,0:T(8,128)S(1)}, u32[]{:S(2)}, u32[]{:S(2)}) collective-permute-start(f32[16,32,128]{2,1,0:T(8,128)S(1)} %get-tuple-element.72), channel_id=1, source_target_pairs={{0,8},{8,0},{16,24},{24,16},{1,9},{9,1},{17,25},{25,17},{2,10},{10... | collective-permute-start | bytes 786440 | tf_op jit(solution)/shard_map/ppermute | solution.py:357
  60.0 2.0 %spread.3 = (f32[16,32,128]{2,1,0:T(8,128)S(1)}, f32[1,512]{1,0:T(1,128)}) custom-call(f32[1,1024]{1,0:T(1,128)S(1)} %get-tuple-element.57.refs_0_, f32[1,1024]{1,0:T(1,128)S(1)} %get-tuple-element.59.refs_2_.refs_1_, f32[1,1024]{1,0:T(1,128)S(1)} %collective-permute-done.11.refs_2_, f32[1,1024]{1,0:T(1,128)S(1)} %collective-permute-done.12.refs_3_, ...), custom_call_target="tpu_custom_call" | custom-call | tf_op jit(solution)/shard_map/spread/pallas_call | solution.py:339
  62.0 0.0 collective-permute-done.14
  62.0 0.7 %add.3 = f32[16,32,128]{2,1,0:T(8,128)} add(f32[16,32,128]{2,1,0:T(8,128)S(1)} %get-tuple-element.71, f32[16,32,128]{2,1,0:T(8,128)S(1)} %collective-permute-done.14) | non-fusion elementwise | flops 65536 | bytes 786432 | tf_op jit(solution)/shard_map/add | solution.py:430
Async XLA Ops:
  0.6 18.9 %copy-start = (f32[32,32]{1,0:T(8,128)S(1)}, f32[32,32]{1,0:T(8,128)}, u32[]{:S(2)}) copy-start(f32[32,32]{1,0:T(8,128)} %refs_4_.1) | copy-start | bytes 12292
  2.1 8.3 %collective-permute-start = (f32[524,128]{1,0:T(8,128)S(1)}, f32[524,128]{1,0:T(8,128)S(1)}, u32[]{:S(2)}, u32[]{:S(2)}) collective-permute-start(f32[524,128]{1,0:T(8,128)S(1)} %get-tuple-element.38.refs_0_.refs_4_.refs_5_), channel_id=1, source_target_pairs={{0,16},{8,24},{16,0},{24,8},{1,17},{9,25},{17,1},{25,9},{2,18},{10... | collective-permute-start | bytes 804872 | tf_op jit(solution)/shard_map/ppermute | solution.py:357
  10.5 29.2 %collective-permute-start.9 = (f32[1536,128]{1,0:T(8,128)S(1)}, f32[1536,128]{1,0:T(8,128)S(1)}, u32[]{:S(2)}, u32[]{:S(2)}) collective-permute-start(f32[1536,128]{1,0:T(8,128)S(1)} %get-tuple-element.55.refs_1_), channel_id=1, source_target_pairs={{0,16},{8,24},{16,0},{24,8},{1,17},{9,25},{17,1},{25,9},{2,18},{10... | collective-permute-start | bytes 2359304 | tf_op jit(solution)/shard_map/ppermute | solution.py:357
  11.6 7.9 %collective-permute-start.1 = (f32[520,128]{1,0:T(8,128)S(1)}, f32[520,128]{1,0:T(8,128)S(1)}, u32[]{:S(2)}, u32[]{:S(2)}) collective-permute-start(f32[520,128]{1,0:T(8,128)S(1)} %get-tuple-element.39.refs_2_), channel_id=1, source_target_pairs={{0,1},{1,0},{2,3},{3,2},{4,5},{5,4},{6,7},{7,6},{8,9},{9,8},{10,11... | collective-permute-start | bytes 798728 | tf_op jit(solution)/shard_map/ppermute | solution.py:357
  22.3 6.0 %collective-permute-start.4 = (f32[1,1024]{1,0:T(1,128)S(1)}, f32[1,1024]{1,0:T(1,128)S(1)}, u32[]{:S(2)}, u32[]{:S(2)}) collective-permute-start(f32[1,1024]{1,0:T(1,128)S(1)} %get-tuple-element.43.refs_2_.refs_0_), channel_id=1, source_target_pairs={{0,6},{1,7},{2,4},{3,5},{4,2},{5,3},{6,0},{7,1},{8,14},{9,15},{10,... | collective-permute-start | bytes 12296 | tf_op jit(solution)/shard_map/ppermute | solution.py:357
  25.7 3.7 %collective-permute-start.3 = (f32[1,1024]{1,0:T(1,128)S(1)}, f32[1,1024]{1,0:T(1,128)S(1)}, u32[]{:S(2)}, u32[]{:S(2)}) collective-permute-start(f32[1,1024]{1,0:T(1,128)S(1)} %get-tuple-element.43.refs_2_.refs_0_), channel_id=1, source_target_pairs={{0,4},{1,5},{2,6},{3,7},{4,0},{5,1},{6,2},{7,3},{8,12},{9,13},{10,... | collective-permute-start | bytes 12296 | tf_op jit(solution)/shard_map/ppermute | solution.py:357
  25.7 3.7 %collective-permute-start.2 = (f32[1,1024]{1,0:T(1,128)S(1)}, f32[1,1024]{1,0:T(1,128)S(1)}, u32[]{:S(2)}, u32[]{:S(2)}) collective-permute-start(f32[1,1024]{1,0:T(1,128)S(1)} %get-tuple-element.43.refs_2_.refs_0_), channel_id=1, source_target_pairs={{0,2},{1,3},{2,0},{3,1},{4,6},{5,7},{6,4},{7,5},{8,10},{9,11},{10,... | collective-permute-start | bytes 12296 | tf_op jit(solution)/shard_map/ppermute | solution.py:357
  30.5 4.1 %collective-permute-start.5 = (f32[1,1024]{1,0:T(1,128)S(1)}, f32[1,1024]{1,0:T(1,128)S(1)}, u32[]{:S(2)}, u32[]{:S(2)}) collective-permute-start(f32[1,1024]{1,0:T(1,128)S(1)} %get-tuple-element.53.refs_0_), channel_id=1, source_target_pairs={{0,8},{8,0},{16,24},{24,16},{1,9},{9,1},{17,25},{25,17},{2,10},{10... | collective-permute-start | bytes 12296 | tf_op jit(solution)/shard_map/ppermute | solution.py:357
  36.2 8.0 %collective-permute-start.8 = (f32[1,1024]{1,0:T(1,128)S(1)}, f32[1,1024]{1,0:T(1,128)S(1)}, u32[]{:S(2)}, u32[]{:S(2)}) collective-permute-start(f32[1,1024]{1,0:T(1,128)S(1)} %get-tuple-element.54.refs_2_.refs_0_), channel_id=1, source_target_pairs={{0,6},{1,7},{2,4},{3,5},{4,2},{5,3},{6,0},{7,1},{8,14},{9,15},{10,... | collective-permute-start | bytes 12296 | tf_op jit(solution)/shard_map/ppermute | solution.py:357
  38.1 6.2 %collective-permute-start.7 = (f32[1,1024]{1,0:T(1,128)S(1)}, f32[1,1024]{1,0:T(1,128)S(1)}, u32[]{:S(2)}, u32[]{:S(2)}) collective-permute-start(f32[1,1024]{1,0:T(1,128)S(1)} %get-tuple-element.54.refs_2_.refs_0_), channel_id=1, source_target_pairs={{0,4},{1,5},{2,6},{3,7},{4,0},{5,1},{6,2},{7,3},{8,12},{9,13},{10,... | collective-permute-start | bytes 12296 | tf_op jit(solution)/shard_map/ppermute | solution.py:357
  38.1 6.2 %collective-permute-start.6 = (f32[1,1024]{1,0:T(1,128)S(1)}, f32[1,1024]{1,0:T(1,128)S(1)}, u32[]{:S(2)}, u32[]{:S(2)}) collective-permute-start(f32[1,1024]{1,0:T(1,128)S(1)} %get-tuple-element.54.refs_2_.refs_0_), channel_id=1, source_target_pairs={{0,2},{1,3},{2,0},{3,1},{4,6},{5,7},{6,4},{7,5},{8,10},{9,11},{10,... | collective-permute-start | bytes 12296 | tf_op jit(solution)/shard_map/ppermute | solution.py:357
  44.9 2.1 %collective-permute-start.10 = (f32[1,1024]{1,0:T(1,128)S(1)}, f32[1,1024]{1,0:T(1,128)S(1)}, u32[]{:S(2)}, u32[]{:S(2)}) collective-permute-start(f32[1,1024]{1,0:T(1,128)S(1)} %get-tuple-element.58.refs_0_), channel_id=1, source_target_pairs={{0,8},{8,0},{16,24},{24,16},{1,9},{9,1},{17,25},{25,17},{2,10},{10... | collective-permute-start | bytes 12296 | tf_op jit(solution)/shard_map/ppermute | solution.py:357
  48.6 8.2 %collective-permute-start.13 = (f32[1,1024]{1,0:T(1,128)S(1)}, f32[1,1024]{1,0:T(1,128)S(1)}, u32[]{:S(2)}, u32[]{:S(2)}) collective-permute-start(f32[1,1024]{1,0:T(1,128)S(1)} %get-tuple-element.59.refs_2_.refs_1_), channel_id=1, source_target_pairs={{0,6},{1,7},{2,4},{3,5},{4,2},{5,3},{6,0},{7,1},{8,14},{9,15},{10,... | collective-permute-start | bytes 12296 | tf_op jit(solution)/shard_map/ppermute | solution.py:357
  50.5 6.3 %collective-permute-start.12 = (f32[1,1024]{1,0:T(1,128)S(1)}, f32[1,1024]{1,0:T(1,128)S(1)}, u32[]{:S(2)}, u32[]{:S(2)}) collective-permute-start(f32[1,1024]{1,0:T(1,128)S(1)} %get-tuple-element.59.refs_2_.refs_1_), channel_id=1, source_target_pairs={{0,4},{1,5},{2,6},{3,7},{4,0},{5,1},{6,2},{7,3},{8,12},{9,13},{10,... | collective-permute-start | bytes 12296 | tf_op jit(solution)/shard_map/ppermute | solution.py:357
  50.5 6.3 %collective-permute-start.11 = (f32[1,1024]{1,0:T(1,128)S(1)}, f32[1,1024]{1,0:T(1,128)S(1)}, u32[]{:S(2)}, u32[]{:S(2)}) collective-permute-start(f32[1,1024]{1,0:T(1,128)S(1)} %get-tuple-element.59.refs_2_.refs_1_), channel_id=1, source_target_pairs={{0,2},{1,3},{2,0},{3,1},{4,6},{5,7},{6,4},{7,5},{8,10},{9,11},{10,... | collective-permute-start | bytes 12296 | tf_op jit(solution)/shard_map/ppermute | solution.py:357
  58.8 3.2 %collective-permute-start.14 = (f32[16,32,128]{2,1,0:T(8,128)S(1)}, f32[16,32,128]{2,1,0:T(8,128)S(1)}, u32[]{:S(2)}, u32[]{:S(2)}) collective-permute-start(f32[16,32,128]{2,1,0:T(8,128)S(1)} %get-tuple-element.72), channel_id=1, source_target_pairs={{0,8},{8,0},{16,24},{24,16},{1,9},{9,1},{17,25},{25,17},{2,10},{10... | collective-permute-start | bytes 786440 | tf_op jit(solution)/shard_map/ppermute | solution.py:357

commit v7 on v6

--- a/solution.py
+++ b/solution.py
@@ -397,36 +397,49 @@
     )
     xpacks = [xpack] + over_y(xpack)
     ypacks = [ypack, move(ypack, "cell", n_cell, 2, 0, 1)]
-    rpacks = over_y(gate(rpack, *xpacks))
     pairs = {}
-
-    def tables(source, pack, first, count, token):
-        pairs[source, first], token = table_call(filt, pack, n, first, count, [token])
-        return token
-
-    early = 3 * n // 4
-    token = tables(0, rpack, 0, early, filt)
-    blocks, partial = gibbs_call(n, m, xpacks, ypacks, penalty, [token])
-    row_sums = lambda: pltpu.VMEM((1, len(xpacks) * n), f32)
-    col_sums = lambda: pltpu.VMEM((1, len(ypacks) * m), f32)
+    unit = n // 8
+
+    def tables(source, first, units, *after):
+        for size in (units & ~1, units & 1):
+            if size:
+                pack = rpack if source == 0 else rpacks[source - 1]
+                pairs[source, first], token = table_call(filt, pack, n, first * unit, size * unit, after)
+                after, first = [token], first + size
+        return after
+
+    def others(first, units, *after):
+        for source in range(1, n_y):
+            after = tables(source, first, units, *after)
+        return after
+
+    after = tables(0, 0, 6, filt)
+    rpacks = over_y(gate(rpack, *xpacks, *ypacks, *after))
+    blocks, partial = gibbs_call(n, m, xpacks, ypacks, penalty, after)
+    row_sums = pltpu.VMEM((1, len(xpacks) * n), f32)
+    col_sums = pltpu.VMEM((1, len(ypacks) * m), f32)
+    fills = [
+        [lambda *after: tables(0, 6, 1, *after), lambda *after: tables(0, 7, 1, *after)],
+        [lambda *after: others(0, 4, *after), lambda *after: others(4, 1, *after)],
+        [lambda *after: others(5, 3, *after)],
+    ]
     lines = along_z(partial)
-    token = tables(0, rpack, early, n - early, partial)
+    after = fills[0][0](partial)
     for iteration in range(ITERS):
         cohort_scale, column = half_step(
-            cols_body, "cols", n, lines, xpacks, blocks, [row_sums(), col_sums()], [token]
+            cols_body, "cols", n, lines, xpacks, blocks, [row_sums, col_sums], after
         )
+        sibling = core(column)
+        after = fills[iteration][1](column)
         cell_scale, partial = half_step(
-            rows_body, "rows", m, [column, core(column)], ypacks, blocks,
-            [jax.ShapeDtypeStruct((1, m), f32), row_sums()], [],
+            rows_body, "rows", m, [column, sibling], ypacks, blocks,
+            [jax.ShapeDtypeStruct((1, m), f32), row_sums], after,
         )
         lines = along_z(partial)
-        token = partial
-        part = n // ITERS
-        for source, pack in enumerate(rpacks):
-            token = tables(1 + source, pack, iteration * part, part, token)
+        after = fills[iteration + 1][0](partial)
     ordered = [pairs[key] for key in sorted(pairs)]
-    away, weights = spread_call(n, cohort_scale, lines, xpacks, ordered, 0, t_dev, [token])
-    mine, _ = spread_call(n, cohort_scale, lines, xpacks, ordered, t_dev, t_dev, [token])
+    away, weights = spread_call(n, cohort_scale, lines, xpacks, ordered, 0, t_dev, after)
+    mine, _ = spread_call(n, cohort_scale, lines, xpacks, ordered, t_dev, t_dev, after)
     out = mine + core(away)
     return (weights.reshape(-1), cell_scale.reshape(-1), out)
 

time: 62.9 us -> 54.4 us (0.86)
  waiting for transfers between devices: 8.91 us -> 1.75 us
  starting transfers between devices: 21 us -> 19.2 us
    ppermute x15, waiting for transfers between devices: 8.91 us -> 1.75 us  [move(): lax.ppermute(x, axis, [(b * pair + r, away(b) * pair + (r ^ flip)) for b...]
    ppermute x15, starting transfers between devices: 21 us -> 19.2 us  [move(): lax.ppermute(x, axis, [(b * pair + r, away(b) * pair + (r ^ flip)) for b...]
    pallas_call x4 -> x7, Pallas kernels: 18.1 us -> 18.5 us  [table_call(): pl.pallas_call(lambda *refs: table_body(n, first, count, *refs[:2], *refs...]
  transfers between devices with their start and end apart: 15 -> 15, of which waited for: 4 -> 1; matrix products, arithmetic and copies ran while one was open for 0% -> 0% of each run, Pallas kernels for 41% -> 48%
where the time goes in v7:
time: 54.4 us; the launch traced here: 54.3 us
  Pallas kernels  31.7 us (58%)
  starting transfers between devices  19.2 us (35%)
  waiting for transfers between devices  1.75 us (3%)
  between operations  0.82 us (2%)
  other arithmetic  0.74 us (1%)
    ppermute x15, starting transfers between devices, move(): lax.ppermute(x, axis, [(b * pair + r, away(b) * pair + (r ^ flip)) for b...  19.2 us
    pallas_call x7, Pallas kernels, table_call(): pl.pallas_call(lambda *refs: table_body(n, first, count, *refs[:2], *refs...  18.5 us
    pallas_call x4, Pallas kernels, half_step(): pl.pallas_call(lambda *refs: body(size, len(partials), len(packs), len(bl...  5.03 us
    pallas_call x2, Pallas kernels, spread_call(): pl.pallas_call(lambda *refs: spread_body(n, t_first, t_count, len(partial...  3.97 us
    pallas_call x1, Pallas kernels, gibbs_call(): pl.pallas_call(lambda *refs: gibbs_body(n, m, len(xpacks), len(ypacks), *...  2.73 us
    ppermute x15, waiting for transfers between devices, move(): lax.ppermute(x, axis, [(b * pair + r, away(b) * pair + (r ^ flip)) for b...  1.75 us
    pallas_call x1, Pallas kernels, first_call(): pl.pallas_call(first_body, in_specs=[HBM] * len(args), out_specs=[VMEM] *...  1.5 us
  transfers between devices with their start and end apart: 15, of which 1 were waited for; matrix products, arithmetic and copies ran while one was open for 0% of the time, Pallas kernels for 48%

profile of v7, /device:TPU:1, one launch (start us, length us, event | category | flops | bytes accessed | tf_op | source)
XLA Modules:
  0.0 54.3 jit_solution(1019023708940806776)
XLA Ops:
  0.6 0.0 copy-start
  0.6 1.5 %first.1 = (f32[524,128]{1,0:T(8,128)S(1)}, f32[520,128]{1,0:T(8,128)S(1)}, f32[1536,128]{1,0:T(8,128)S(1)}, f32[32,128]{1,0:T(8,128)S(1)}) custom-call(bf16[512,128]{1,0:T(8,128)(2,1)} %x_hbm.1, bf16[512,128]{1,0:T(8,128)(2,1)} %y_hbm.1, s32[4,128]{1,0:T(4,128)} %bitcast.7, s32[4,128]{1,0:T(4,128)} %bitcast.8, f32[4,128]{1,0:T(4,128)} %bitcast.9, ...), custom_call_target="tpu_custom_call" | custom-call | tf_op jit(solution)/shard_map/first/pallas_call | solution.py:155
  2.1 2.1 %collective-permute-start = (f32[524,128]{1,0:T(8,128)S(1)}, f32[524,128]{1,0:T(8,128)S(1)}, u32[]{:S(2)}, u32[]{:S(2)}) collective-permute-start(f32[524,128]{1,0:T(8,128)S(1)} %get-tuple-element.47.refs_0_.refs_4_.refs_5_), channel_id=1, source_target_pairs={{0,16},{8,24},{16,0},{24,8},{1,17},{9,25},{17,1},{25,9},{2,18},{10... | collective-permute-start | bytes 804872 | tf_op jit(solution)/shard_map/ppermute | solution.py:357
  4.3 1.2 %collective-permute-start.1 = (f32[520,128]{1,0:T(8,128)S(1)}, f32[520,128]{1,0:T(8,128)S(1)}, u32[]{:S(2)}, u32[]{:S(2)}) collective-permute-start(f32[520,128]{1,0:T(8,128)S(1)} %get-tuple-element.48.refs_2_), channel_id=1, source_target_pairs={{0,1},{1,0},{2,3},{3,2},{4,5},{5,4},{6,7},{7,6},{8,9},{9,8},{10,11... | collective-permute-start | bytes 798728 | tf_op jit(solution)/shard_map/ppermute | solution.py:357
  5.5 6.7 %tables.7 = (bf16[32,384,128]{2,1,0:T(8,128)(2,1)S(1)}, bf16[32,384,128]{2,1,0:T(8,128)(2,1)S(1)}, f32[8,128]{1,0:T(8,128)S(1)}) custom-call(f32[32,128]{1,0:T(8,128)S(1)} %get-tuple-element.49.refs_0_.refs_2_, f32[1536,128]{1,0:T(8,128)S(1)} %get-tuple-element.65.refs_1_, f32[32,128]{1,0:T(8,128)S(1)} %get-tuple-element.49.refs_0_.refs_2_), custom_call_target="tpu_custom_call" | custom-call | flops 805306368 | bytes 23040000 | tf_op jit(solution)/shard_map/tables/pallas_call | solution.py:298
  12.2 0.0 collective-permute-done.1.refs_3_
  12.2 0.0 collective-permute-done.refs_1_.refs_5_.refs_6_
  12.2 0.3 collective-permute-start.9
  12.5 0.0 copy-done
  12.5 2.7 %gibbs.1 = (bf16[512,512]{1,0:T(8,128)(2,1)S(1)}, bf16[512,512]{1,0:T(8,128)(2,1)S(1)}, bf16[512,512]{1,0:T(8,128)(2,1)S(1)}, bf16[512,512]{1,0:T(8,128)(2,1)S(1...) custom-call(f32[524,128]{1,0:T(8,128)S(1)} %get-tuple-element.47.ref, ...), custom_call_target="tpu_custom_call" | custom-call | flops 268435456 | bytes 4194304 | tf_op jit(solution)/shard_map/gibbs/pallas_call | solution.py:202
  15.2 3.4 %collective-permute-start.4 = (f32[1,1024]{1,0:T(1,128)S(1)}, f32[1,1024]{1,0:T(1,128)S(1)}, u32[]{:S(2)}, u32[]{:S(2)}) collective-permute-start(f32[1,1024]{1,0:T(1,128)S(1)} %get-tuple-element.52.refs_2_.refs_0_), channel_id=1, source_target_pairs={{0,6},{1,7},{2,4},{3,5},{4,2},{5,3},{6,0},{7,1},{8,14},{9,15},{10,... | collective-permute-start | bytes 12296 | tf_op jit(solution)/shard_map/ppermute | solution.py:357
  18.6 0.0 collective-permute-start.3
  18.6 0.4 collective-permute-start.2
  19.0 1.3 %tables.8 = (bf16[32,64,128]{2,1,0:T(8,128)(2,1)S(1)}, bf16[32,64,128]{2,1,0:T(8,128)(2,1)S(1)}, f32[8,128]{1,0:T(8,128)S(1)}) custom-call(f32[32,128]{1,0:T(8,128)S(1)} %get-tuple-element.49.refs_0_.refs_2_, f32[1536,128]{1,0:T(8,128)S(1)} %get-tuple-element.65.refs_1_, f32[1,1024]{1,0:T(1,128)S(1)} %get-tuple-element.52.refs_2_.refs_0_), custom_call_target="tpu_custom_call" | custom-call | flops 134217728 | bytes 3840000 | tf_op jit(solution)/shard_map/tables/pallas_call | solution.py:298
  20.3 0.0 collective-permute-done.4.refs_3_
  20.3 1.7 %collective-permute-done.3.refs_2_ = f32[1,1024]{1,0:T(1,128)S(1)} collective-permute-done((f32[1,1024]{1,0:T(1,128)S(1)}, f32[1,1024]{1,0:T(1,128)S(1)}, u32[]{:S(2)}, u32[]{:S(2)}) %collective-permute-start.3) | collective-permute-done | bytes 4128 | tf_op jit(solution)/shard_map/ppermute | solution.py:357
  22.0 0.0 collective-permute-done.2.refs_1_
  22.0 1.1 %cols.2 = (f32[1,1024]{1,0:T(1,128)}, f32[1,1024]{1,0:T(1,128)S(1)}) custom-call(f32[1,1024]{1,0:T(1,128)S(1)} %get-tuple-element.52.refs_2_.refs_0_, f32[1,1024]{1,0:T(1,128)S(1)} %collective-permute-done.2.refs_1_, f32[1,1024]{1,0:T(1,128)S(1)} %collective-permute-done.3.refs_2_, f32[1,1024]{1,0:T(1,128)S(1)} %collective-permute-done.4.refs_3_, ...), custom_call_target="tpu_custom_call" | custom-call | tf_op jit(solution)/shard_map/cols/pallas_call | solution.py:250
  23.1 2.9 %collective-permute-start.5 = (f32[1,1024]{1,0:T(1,128)S(1)}, f32[1,1024]{1,0:T(1,128)S(1)}, u32[]{:S(2)}, u32[]{:S(2)}) collective-permute-start(f32[1,1024]{1,0:T(1,128)S(1)} %get-tuple-element.62.refs_2_.refs_0_), channel_id=1, source_target_pairs={{0,8},{8,0},{16,24},{24,16},{1,9},{9,1},{17,25},{25,17},{2,10},{10... | collective-permute-start | bytes 12296 | tf_op jit(solution)/shard_map/ppermute | solution.py:357
  26.1 1.3 %tables.9 = (bf16[32,64,128]{2,1,0:T(8,128)(2,1)S(1)}, bf16[32,64,128]{2,1,0:T(8,128)(2,1)S(1)}, f32[8,128]{1,0:T(8,128)S(1)}) custom-call(f32[32,128]{1,0:T(8,128)S(1)} %get-tuple-element.49.refs_0_.refs_2_, f32[1536,128]{1,0:T(8,128)S(1)} %get-tuple-element.65.refs_1_, f32[1,1024]{1,0:T(1,128)S(1)} %get-tuple-element.62.refs_2_.refs_0_), custom_call_target="tpu_custom_call" | custom-call | flops 134217728 | bytes 3840000 | tf_op jit(solution)/shard_map/tables/pallas_call | solution.py:298
  27.3 0.0 collective-permute-done.5.refs_1_
  27.4 1.6 %rows.2 = (f32[1,512]{1,0:T(1,128)}, f32[1,1024]{1,0:T(1,128)S(1)}) custom-call(f32[1,1024]{1,0:T(1,128)S(1)} %get-tuple-element.62.refs_2_.refs_0_, f32[1,1024]{1,0:T(1,128)S(1)} %collective-permute-done.5.refs_1_, f32[520,128]{1,0:T(8,128)S(1)} %get-tuple-element.48.refs_2_, f32[520,128]{1,0:T(8,128)S(1)} %collective-permute-done.1.refs_3_, ...), custom_call_target="tpu_custom_call" | custom-call | tf_op jit(solution)/shard_map/rows/pallas_call | solution.py:250
  29.0 1.2 %collective-permute-start.8 = (f32[1,1024]{1,0:T(1,128)S(1)}, f32[1,1024]{1,0:T(1,128)S(1)}, u32[]{:S(2)}, u32[]{:S(2)}) collective-permute-start(f32[1,1024]{1,0:T(1,128)S(1)} %get-tuple-element.64.refs_2_.refs_0_), channel_id=1, source_target_pairs={{0,6},{1,7},{2,4},{3,5},{4,2},{5,3},{6,0},{7,1},{8,14},{9,15},{10,... | collective-permute-start | bytes 12296 | tf_op jit(solution)/shard_map/ppermute | solution.py:357
  30.2 0.6 %collective-permute-start.7 = (f32[1,1024]{1,0:T(1,128)S(1)}, f32[1,1024]{1,0:T(1,128)S(1)}, u32[]{:S(2)}, u32[]{:S(2)}) collective-permute-start(f32[1,1024]{1,0:T(1,128)S(1)} %get-tuple-element.64.refs_2_.refs_0_), channel_id=1, source_target_pairs={{0,4},{1,5},{2,6},{3,7},{4,0},{5,1},{6,2},{7,3},{8,12},{9,13},{10,... | collective-permute-start | bytes 12296 | tf_op jit(solution)/shard_map/ppermute | solution.py:357
  30.7 1.8 %collective-permute-start.6 = (f32[1,1024]{1,0:T(1,128)S(1)}, f32[1,1024]{1,0:T(1,128)S(1)}, u32[]{:S(2)}, u32[]{:S(2)}) collective-permute-start(f32[1,1024]{1,0:T(1,128)S(1)} %get-tuple-element.64.refs_2_.refs_0_), channel_id=1, source_target_pairs={{0,2},{1,3},{2,0},{3,1},{4,6},{5,7},{6,4},{7,5},{8,10},{9,11},{10,... | collective-permute-start | bytes 12296 | tf_op jit(solution)/shard_map/ppermute | solution.py:357
  32.5 0.0 collective-permute-done.9.refs_1_
  32.5 4.6 %tables.10 = (bf16[32,256,128]{2,1,0:T(8,128)(2,1)S(1)}, bf16[32,256,128]{2,1,0:T(8,128)(2,1)S(1)}, f32[8,128]{1,0:T(8,128)S(1)}) custom-call(f32[32,128]{1,0:T(8,128)S(1)} %get-tuple-element.49.refs_0_.refs_2_, f32[1536,128]{1,0:T(8,128)S(1)} %collective-permute-done.9.refs_1_, f32[1,1024]{1,0:T(1,128)S(1)} %get-tuple-element.64.refs_2_.refs_0_), custom_call_target="tpu_custom_call" | custom-call | flops 536870912 | bytes 15360000 | tf_op jit(solution)/shard_map/tables/pallas_call | solution.py:298
  37.1 0.0 collective-permute-done.8.refs_3_
  37.1 0.0 collective-permute-done.7.refs_2_
  37.1 0.0 collective-permute-done.6.refs_1_
  37.1 0.7 %cols.3 = (f32[1,1024]{1,0:T(1,128)S(1)}, f32[1,1024]{1,0:T(1,128)S(1)}) custom-call(f32[1,1024]{1,0:T(1,128)S(1)} %get-tuple-element.64.refs_2_.refs_0_, f32[1,1024]{1,0:T(1,128)S(1)} %collective-permute-done.6.refs_1_, f32[1,1024]{1,0:T(1,128)S(1)} %collective-permute-done.7.refs_2_, f32[1,1024]{1,0:T(1,128)S(1)} %collective-permute-done.8.refs_3_, ...), custom_call_target="tpu_custom_call" | custom-call | tf_op jit(solution)/shard_map/cols/pallas_call | solution.py:250
  37.8 0.9 %collective-permute-start.10 = (f32[1,1024]{1,0:T(1,128)S(1)}, f32[1,1024]{1,0:T(1,128)S(1)}, u32[]{:S(2)}, u32[]{:S(2)}) collective-permute-start(f32[1,1024]{1,0:T(1,128)S(1)} %get-tuple-element.68.refs_2_.refs_0_), channel_id=1, source_target_pairs={{0,8},{8,0},{16,24},{24,16},{1,9},{9,1},{17,25},{25,17},{2,10},{10... | collective-permute-start | bytes 12296 | tf_op jit(solution)/shard_map/ppermute | solution.py:357
  38.7 1.2 %tables.11 = (bf16[32,64,128]{2,1,0:T(8,128)(2,1)S(1)}, bf16[32,64,128]{2,1,0:T(8,128)(2,1)S(1)}, f32[8,128]{1,0:T(8,128)S(1)}) custom-call(f32[32,128]{1,0:T(8,128)S(1)} %get-tuple-element.49.refs_0_.refs_2_, f32[1536,128]{1,0:T(8,128)S(1)} %collective-permute-done.9.refs_1_, f32[1,1024]{1,0:T(1,128)S(1)} %get-tuple-element.68.refs_2_.refs_0_), custom_call_target="tpu_custom_call" | custom-call | flops 134217728 | bytes 3840000 | tf_op jit(solution)/shard_map/tables/pallas_call | solution.py:298
  39.9 0.0 collective-permute-done.10.refs_1_
  40.0 1.6 %rows.3 = (f32[1,512]{1,0:T(1,128)}, f32[1,1024]{1,0:T(1,128)S(1)}) custom-call(f32[1,1024]{1,0:T(1,128)S(1)} %get-tuple-element.68.refs_2_.refs_0_, f32[1,1024]{1,0:T(1,128)S(1)} %collective-permute-done.10.refs_1_, f32[520,128]{1,0:T(8,128)S(1)} %get-tuple-element.48.refs_2_, f32[520,128]{1,0:T(8,128)S(1)} %collective-permute-done.1.refs_3_, ...), custom_call_target="tpu_custom_call" | custom-call | tf_op jit(solution)/shard_map/rows/pallas_call | solution.py:250
  41.6 2.2 %collective-permute-start.13 = (f32[1,1024]{1,0:T(1,128)S(1)}, f32[1,1024]{1,0:T(1,128)S(1)}, u32[]{:S(2)}, u32[]{:S(2)}) collective-permute-start(f32[1,1024]{1,0:T(1,128)S(1)} %get-tuple-element.70.refs_2_.refs_1_), channel_id=1, source_target_pairs={{0,6},{1,7},{2,4},{3,5},{4,2},{5,3},{6,0},{7,1},{8,14},{9,15},{10,... | collective-permute-start | bytes 12296 | tf_op jit(solution)/shard_map/ppermute | solution.py:357
  43.8 0.0 collective-permute-start.12
  43.8 1.4 %collective-permute-start.11 = (f32[1,1024]{1,0:T(1,128)S(1)}, f32[1,1024]{1,0:T(1,128)S(1)}, u32[]{:S(2)}, u32[]{:S(2)}) collective-permute-start(f32[1,1024]{1,0:T(1,128)S(1)} %get-tuple-element.70.refs_2_.refs_1_), channel_id=1, source_target_pairs={{0,2},{1,3},{2,0},{3,1},{4,6},{5,7},{6,4},{7,5},{8,10},{9,11},{10,... | collective-permute-start | bytes 12296 | tf_op jit(solution)/shard_map/ppermute | solution.py:357
  45.1 2.2 %tables.12 = (bf16[32,128,128]{2,1,0:T(8,128)(2,1)S(1)}, bf16[32,128,128]{2,1,0:T(8,128)(2,1)S(1)}, f32[8,128]{1,0:T(8,128)S(1)}) custom-call(f32[32,128]{1,0:T(8,128)S(1)} %get-tuple-element.49.refs_0_.refs_2_, f32[1536,128]{1,0:T(8,128)S(1)} %collective-permute-done.9.refs_1_, f32[1,1024]{1,0:T(1,128)S(1)} %get-tuple-element.70.refs_2_.refs_1_), custom_call_target="tpu_custom_call" | custom-call | flops 268435456 | bytes 7680000 | tf_op jit(solution)/shard_map/tables/pallas_call | solution.py:298
  47.4 1.3 %tables.13 = (bf16[32,64,128]{2,1,0:T(8,128)(2,1)S(1)}, bf16[32,64,128]{2,1,0:T(8,128)(2,1)S(1)}, f32[8,128]{1,0:T(8,128)S(1)}) custom-call(f32[32,128]{1,0:T(8,128)S(1)} %get-tuple-element.49.refs_0_.refs_2_, f32[1536,128]{1,0:T(8,128)S(1)} %collective-permute-done.9.refs_1_, f32[8,128]{1,0:T(8,128)S(1)} %get-tuple-element.83.refs_2_), custom_call_target="tpu_custom_call" | custom-call | flops 134217728 | bytes 3840000 | tf_op jit(solution)/shard_map/tables/pallas_call | solution.py:298
  48.6 0.0 collective-permute-done.13.refs_4_
  48.7 0.0 collective-permute-done.12.refs_3_
  48.7 0.0 collective-permute-done.11.refs_2_
  48.7 2.0 %spread.2 = (f32[16,32,128]{2,1,0:T(8,128)S(1)}, f32[1,512]{1,0:T(1,128)}) custom-call(f32[1,1024]{1,0:T(1,128)S(1)} %get-tuple-element.67.refs_0_, f32[1,1024]{1,0:T(1,128)S(1)} %get-tuple-element.70.refs_2_.refs_1_, f32[1,1024]{1,0:T(1,128)S(1)} %collective-permute-done.11.refs_2_, f32[1,1024]{1,0:T(1,128)S(1)} %collective-permute-done.12.refs_3_, ...), custom_call_target="tpu_custom_call" | custom-call | tf_op jit(solution)/shard_map/spread/pallas_call | solution.py:339
  50.7 0.9 %collective-permute-start.14 = (f32[16,32,128]{2,1,0:T(8,128)S(1)}, f32[16,32,128]{2,1,0:T(8,128)S(1)}, u32[]{:S(2)}, u32[]{:S(2)}) collective-permute-start(f32[16,32,128]{2,1,0:T(8,128)S(1)} %get-tuple-element.90), channel_id=1, source_target_pairs={{0,8},{8,0},{16,24},{24,16},{1,9},{9,1},{17,25},{25,17},{2,10},{10... | collective-permute-start | bytes 786440 | tf_op jit(solution)/shard_map/ppermute | solution.py:357
  51.5 2.0 %spread.3 = (f32[16,32,128]{2,1,0:T(8,128)S(1)}, f32[1,512]{1,0:T(1,128)}) custom-call(f32[1,1024]{1,0:T(1,128)S(1)} %get-tuple-element.67.refs_0_, f32[1,1024]{1,0:T(1,128)S(1)} %get-tuple-element.70.refs_2_.refs_1_, f32[1,1024]{1,0:T(1,128)S(1)} %collective-permute-done.11.refs_2_, f32[1,1024]{1,0:T(1,128)S(1)} %collective-permute-done.12.refs_3_, ...), custom_call_target="tpu_custom_call" | custom-call | tf_op jit(solution)/shard_map/spread/pallas_call | solution.py:339
  53.5 0.0 collective-permute-done.14
  53.5 0.7 %add.3 = f32[16,32,128]{2,1,0:T(8,128)} add(f32[16,32,128]{2,1,0:T(8,128)S(1)} %get-tuple-element.89, f32[16,32,128]{2,1,0:T(8,128)S(1)} %collective-permute-done.14) | non-fusion elementwise | flops 65536 | bytes 786432 | tf_op jit(solution)/shard_map/add | solution.py:443
Async XLA Ops:
  0.6 11.9 %copy-start = (f32[32,32]{1,0:T(8,128)S(1)}, f32[32,32]{1,0:T(8,128)}, u32[]{:S(2)}) copy-start(f32[32,32]{1,0:T(8,128)} %refs_4_.1) | copy-start | bytes 12292
  2.1 10.1 %collective-permute-start = (f32[524,128]{1,0:T(8,128)S(1)}, f32[524,128]{1,0:T(8,128)S(1)}, u32[]{:S(2)}, u32[]{:S(2)}) collective-permute-start(f32[524,128]{1,0:T(8,128)S(1)} %get-tuple-element.47.refs_0_.refs_4_.refs_5_), channel_id=1, source_target_pairs={{0,16},{8,24},{16,0},{24,8},{1,17},{9,25},{17,1},{25,9},{2,18},{10... | collective-permute-start | bytes 804872 | tf_op jit(solution)/shard_map/ppermute | solution.py:357
  4.3 7.9 %collective-permute-start.1 = (f32[520,128]{1,0:T(8,128)S(1)}, f32[520,128]{1,0:T(8,128)S(1)}, u32[]{:S(2)}, u32[]{:S(2)}) collective-permute-start(f32[520,128]{1,0:T(8,128)S(1)} %get-tuple-element.48.refs_2_), channel_id=1, source_target_pairs={{0,1},{1,0},{2,3},{3,2},{4,5},{5,4},{6,7},{7,6},{8,9},{9,8},{10,11... | collective-permute-start | bytes 798728 | tf_op jit(solution)/shard_map/ppermute | solution.py:357
  12.2 20.3 %collective-permute-start.9 = (f32[1536,128]{1,0:T(8,128)S(1)}, f32[1536,128]{1,0:T(8,128)S(1)}, u32[]{:S(2)}, u32[]{:S(2)}) collective-permute-start(f32[1536,128]{1,0:T(8,128)S(1)} %get-tuple-element.65.refs_1_), channel_id=1, source_target_pairs={{0,16},{8,24},{16,0},{24,8},{1,17},{9,25},{17,1},{25,9},{2,18},{10... | collective-permute-start | bytes 2359304 | tf_op jit(solution)/shard_map/ppermute | solution.py:357
  15.2 5.0 %collective-permute-start.4 = (f32[1,1024]{1,0:T(1,128)S(1)}, f32[1,1024]{1,0:T(1,128)S(1)}, u32[]{:S(2)}, u32[]{:S(2)}) collective-permute-start(f32[1,1024]{1,0:T(1,128)S(1)} %get-tuple-element.52.refs_2_.refs_0_), channel_id=1, source_target_pairs={{0,6},{1,7},{2,4},{3,5},{4,2},{5,3},{6,0},{7,1},{8,14},{9,15},{10,... | collective-permute-start | bytes 12296 | tf_op jit(solution)/shard_map/ppermute | solution.py:357
  18.6 3.4 %collective-permute-start.3 = (f32[1,1024]{1,0:T(1,128)S(1)}, f32[1,1024]{1,0:T(1,128)S(1)}, u32[]{:S(2)}, u32[]{:S(2)}) collective-permute-start(f32[1,1024]{1,0:T(1,128)S(1)} %get-tuple-element.52.refs_2_.refs_0_), channel_id=1, source_target_pairs={{0,4},{1,5},{2,6},{3,7},{4,0},{5,1},{6,2},{7,3},{8,12},{9,13},{10,... | collective-permute-start | bytes 12296 | tf_op jit(solution)/shard_map/ppermute | solution.py:357
  18.6 3.4 %collective-permute-start.2 = (f32[1,1024]{1,0:T(1,128)S(1)}, f32[1,1024]{1,0:T(1,128)S(1)}, u32[]{:S(2)}, u32[]{:S(2)}) collective-permute-start(f32[1,1024]{1,0:T(1,128)S(1)} %get-tuple-element.52.refs_2_.refs_0_), channel_id=1, source_target_pairs={{0,2},{1,3},{2,0},{3,1},{4,6},{5,7},{6,4},{7,5},{8,10},{9,11},{10,... | collective-permute-start | bytes 12296 | tf_op jit(solution)/shard_map/ppermute | solution.py:357
  23.1 4.2 %collective-permute-start.5 = (f32[1,1024]{1,0:T(1,128)S(1)}, f32[1,1024]{1,0:T(1,128)S(1)}, u32[]{:S(2)}, u32[]{:S(2)}) collective-permute-start(f32[1,1024]{1,0:T(1,128)S(1)} %get-tuple-element.62.refs_2_.refs_0_), channel_id=1, source_target_pairs={{0,8},{8,0},{16,24},{24,16},{1,9},{9,1},{17,25},{25,17},{2,10},{10... | collective-permute-start | bytes 12296 | tf_op jit(solution)/shard_map/ppermute | solution.py:357
  29.0 8.1 %collective-permute-start.8 = (f32[1,1024]{1,0:T(1,128)S(1)}, f32[1,1024]{1,0:T(1,128)S(1)}, u32[]{:S(2)}, u32[]{:S(2)}) collective-permute-start(f32[1,1024]{1,0:T(1,128)S(1)} %get-tuple-element.64.refs_2_.refs_0_), channel_id=1, source_target_pairs={{0,6},{1,7},{2,4},{3,5},{4,2},{5,3},{6,0},{7,1},{8,14},{9,15},{10,... | collective-permute-start | bytes 12296 | tf_op jit(solution)/shard_map/ppermute | solution.py:357
  30.2 6.9 %collective-permute-start.7 = (f32[1,1024]{1,0:T(1,128)S(1)}, f32[1,1024]{1,0:T(1,128)S(1)}, u32[]{:S(2)}, u32[]{:S(2)}) collective-permute-start(f32[1,1024]{1,0:T(1,128)S(1)} %get-tuple-element.64.refs_2_.refs_0_), channel_id=1, source_target_pairs={{0,4},{1,5},{2,6},{3,7},{4,0},{5,1},{6,2},{7,3},{8,12},{9,13},{10,... | collective-permute-start | bytes 12296 | tf_op jit(solution)/shard_map/ppermute | solution.py:357
  30.7 6.4 %collective-permute-start.6 = (f32[1,1024]{1,0:T(1,128)S(1)}, f32[1,1024]{1,0:T(1,128)S(1)}, u32[]{:S(2)}, u32[]{:S(2)}) collective-permute-start(f32[1,1024]{1,0:T(1,128)S(1)} %get-tuple-element.64.refs_2_.refs_0_), channel_id=1, source_target_pairs={{0,2},{1,3},{2,0},{3,1},{4,6},{5,7},{6,4},{7,5},{8,10},{9,11},{10,... | collective-permute-start | bytes 12296 | tf_op jit(solution)/shard_map/ppermute | solution.py:357
  37.8 2.2 %collective-permute-start.10 = (f32[1,1024]{1,0:T(1,128)S(1)}, f32[1,1024]{1,0:T(1,128)S(1)}, u32[]{:S(2)}, u32[]{:S(2)}) collective-permute-start(f32[1,1024]{1,0:T(1,128)S(1)} %get-tuple-element.68.refs_2_.refs_0_), channel_id=1, source_target_pairs={{0,8},{8,0},{16,24},{24,16},{1,9},{9,1},{17,25},{25,17},{2,10},{10... | collective-permute-start | bytes 12296 | tf_op jit(solution)/shard_map/ppermute | solution.py:357
  41.6 7.1 %collective-permute-start.13 = (f32[1,1024]{1,0:T(1,128)S(1)}, f32[1,1024]{1,0:T(1,128)S(1)}, u32[]{:S(2)}, u32[]{:S(2)}) collective-permute-start(f32[1,1024]{1,0:T(1,128)S(1)} %get-tuple-element.70.refs_2_.refs_1_), channel_id=1, source_target_pairs={{0,6},{1,7},{2,4},{3,5},{4,2},{5,3},{6,0},{7,1},{8,14},{9,15},{10,... | collective-permute-start | bytes 12296 | tf_op jit(solution)/shard_map/ppermute | solution.py:357
  43.8 4.9 %collective-permute-start.12 = (f32[1,1024]{1,0:T(1,128)S(1)}, f32[1,1024]{1,0:T(1,128)S(1)}, u32[]{:S(2)}, u32[]{:S(2)}) collective-permute-start(f32[1,1024]{1,0:T(1,128)S(1)} %get-tuple-element.70.refs_2_.refs_1_), channel_id=1, source_target_pairs={{0,4},{1,5},{2,6},{3,7},{4,0},{5,1},{6,2},{7,3},{8,12},{9,13},{10,... | collective-permute-start | bytes 12296 | tf_op jit(solution)/shard_map/ppermute | solution.py:357
  43.8 4.9 %collective-permute-start.11 = (f32[1,1024]{1,0:T(1,128)S(1)}, f32[1,1024]{1,0:T(1,128)S(1)}, u32[]{:S(2)}, u32[]{:S(2)}) collective-permute-start(f32[1,1024]{1,0:T(1,128)S(1)} %get-tuple-element.70.refs_2_.refs_1_), channel_id=1, source_target_pairs={{0,2},{1,3},{2,0},{3,1},{4,6},{5,7},{6,4},{7,5},{8,10},{9,11},{10,... | collective-permute-start | bytes 12296 | tf_op jit(solution)/shard_map/ppermute | solution.py:357
  50.7 2.8 %collective-permute-start.14 = (f32[16,32,128]{2,1,0:T(8,128)S(1)}, f32[16,32,128]{2,1,0:T(8,128)S(1)}, u32[]{:S(2)}, u32[]{:S(2)}) collective-permute-start(f32[16,32,128]{2,1,0:T(8,128)S(1)} %get-tuple-element.90), channel_id=1, source_target_pairs={{0,8},{8,0},{16,24},{24,16},{1,9},{9,1},{17,25},{25,17},{2,10},{10... | collective-permute-start | bytes 786440 | tf_op jit(solution)/shard_map/ppermute | solution.py:357

commit v8 on v7

--- a/solution.py
+++ b/solution.py
@@ -62,32 +62,38 @@
     return hi, (x - hi.astype(f32)).astype(bf16)
 
 
-def split_rows(x):
-    hi = x.astype(bf16)
-    rest = x - hi.astype(f32)
-    mid = rest.astype(bf16)
-    low = (rest - mid.astype(f32)).astype(bf16)
-    return jnp.concatenate([hi, mid, low, jnp.zeros((5, x.shape[1]), bf16)], 0)
-
-
 def dot_rows(rows, k, dims):
     return lax.dot_general(rows, k, (dims, ((), ())), preferred_element_type=f32)
 
 
-def cols_of(us, blocks):
-    out = 0.0
-    for u, (khi, klo) in zip(us, blocks):
-        rows = split_rows(u)
-        out = out + dot_rows(rows, khi[...], ((1,), (0,))) + dot_rows(rows, klo[...], ((1,), (0,)))
-    return jnp.sum(out, axis=0, keepdims=True)
-
-
-def rows_of(vs, blocks):
-    out = 0.0
-    for v, (khi, klo) in zip(vs, blocks):
-        rows = split_rows(v)
-        out = out + dot_rows(rows, khi[...], ((1,), (1,))) + dot_rows(rows, klo[...], ((1,), (1,)))
-    return jnp.sum(out, axis=0, keepdims=True)
+def tiles(count):
+    return [slice(at, at + LANES) for at in range(0, count, LANES)]
+
+
+def turn(row):
+    return jnp.transpose(jnp.broadcast_to(row, (LANES, LANES)))
+
+
+def cols_of(u, k_ref):
+    rows, cols = k_ref.shape
+    totals = [0.0] * (cols // LANES)
+    for block in tiles(rows):
+        scale = turn(u[:, block])
+        for j, tile in enumerate(tiles(cols)):
+            totals[j] = totals[j] + jnp.sum((k_ref[block, tile] * scale).reshape(-1, 8, LANES), axis=0)
+    return jnp.concatenate([jnp.sum(total, axis=0, keepdims=True) for total in totals], 1)
+
+
+def rows_of(v, k_ref):
+    rows, cols = k_ref.shape
+    out = []
+    for block in tiles(rows):
+        total = 0.0
+        for tile in tiles(cols):
+            term = k_ref[block, tile]
+            total = total + (term if v is None else term * v[:, tile])
+        out.append(jnp.sum(jnp.transpose(total), axis=0, keepdims=True))
+    return jnp.concatenate(out, 1)
 
 
 def kernel_block(x, y, row_region, col_region, penalty):
@@ -101,7 +107,7 @@
     qhi = jnp.dot(phi, col_hot, preferred_element_type=f32).astype(bf16)
     qlo = jnp.dot(plo, col_hot, preferred_element_type=f32).astype(bf16)
     pen = dot_rows(jnp.concatenate([row_hot, row_hot], 0), jnp.concatenate([qhi, qlo], 0), ((0,), (0,)))
-    return split2(jnp.exp(inner * inv_root - pen))
+    return jnp.exp(inner * inv_root - pen)
 
 
 def run_copies(pairs, sems):
@@ -177,40 +183,32 @@
 
 
 def gibbs_body(n, m, packs_x, packs_y, *refs):
-    xpacks, ypacks, pen_ref = refs[:packs_x], refs[packs_x : packs_x + packs_y], refs[packs_x + packs_y]
-    outs = refs[packs_x + packs_y + 1 : -1]
-    r_ref = refs[-1]
+    xpacks, ypacks = refs[:packs_x], refs[packs_x : packs_x + packs_y]
+    pen_ref, k_ref, r_ref = refs[packs_x + packs_y :]
     p, q = n // LANES, m // LANES
     pen = pen_ref[...]
-    xs = [(pack[0:n, :].astype(bf16), flat(pack[n : n + p, :]).astype(jnp.int32)) for pack in xpacks]
     ys = [(pack[0:m, :].astype(bf16), flat(pack[m : m + q, :]).astype(jnp.int32)) for pack in ypacks]
-    k = 0
-    sums = []
-    for x, rr in xs:
-        blocks = []
-        for y, cr in ys:
-            outs[k][...], outs[k + 1][...] = kernel_block(x, y, rr, cr, pen)
-            blocks.append((outs[k], outs[k + 1]))
-            k += 2
-        sums.append(rows_of([jnp.ones((1, m), f32)] * len(ys), blocks))
-    r_ref[...] = jnp.concatenate(sums, 1)
+    for i, pack in enumerate(xpacks):
+        x, rr = pack[0:n, :].astype(bf16), flat(pack[n : n + p, :]).astype(jnp.int32)
+        for j, (y, cr) in enumerate(ys):
+            k_ref[i * n : (i + 1) * n, j * m : (j + 1) * m] = kernel_block(x, y, rr, cr, pen)
+    r_ref[...] = rows_of(None, k_ref)
 
 
 def gibbs_call(n, m, xpacks, ypacks, penalty, after):
-    blocks = len(xpacks) * len(ypacks)
+    rows, cols = len(xpacks) * n, len(ypacks) * m
     args = [*xpacks, *ypacks, penalty]
-    *out, sums = pl.pallas_call(
-        lambda *refs: gibbs_body(n, m, len(xpacks), len(ypacks), *refs[: len(args)], *refs[-2 * blocks - 1 :]),
+    return pl.pallas_call(
+        lambda *refs: gibbs_body(n, m, len(xpacks), len(ypacks), *refs[: len(args)], *refs[-2:]),
         in_specs=[VMEM] * len(args) + [ANY] * len(after),
-        out_specs=[VMEM] * (2 * blocks + 1),
-        out_shape=[pltpu.VMEM((n, m), bf16)] * (2 * blocks) + [pltpu.VMEM((1, len(xpacks) * n), f32)],
+        out_specs=[VMEM] * 2,
+        out_shape=[pltpu.VMEM((rows, cols), f32), pltpu.VMEM((1, rows), f32)],
         compiler_params=PARAMS,
         cost_estimate=pl.CostEstimate(
-            flops=2 * blocks * n * m * LANES, transcendentals=blocks * n * m, bytes_accessed=blocks * n * m * 4
+            flops=2 * rows * cols * LANES, transcendentals=rows * cols, bytes_accessed=rows * cols * 4
         ),
         name="gibbs",
     )(*args, *after)
-    return [(out[2 * k], out[2 * k + 1]) for k in range(blocks)], sums
 
 
 def total_of(refs):
@@ -220,35 +218,30 @@
     return total
 
 
-def cols_body(n, parts, packs, block_count, *refs):
+def cols_body(n, parts, packs, *refs):
     p = n // LANES
     total = total_of(refs[:parts])
     pack_refs = refs[parts : parts + packs]
-    rest = refs[parts + packs :]
-    blocks = [(rest[2 * k], rest[2 * k + 1]) for k in range(block_count)]
-    u_ref, c_ref = refs[-2:]
-    us = [flat(pack[n + 2 * p : n + 3 * p, :]) / total[:, k * n : (k + 1) * n] for k, pack in enumerate(pack_refs)]
-    u_ref[...] = jnp.concatenate(us, 1)
-    width = block_count // packs
-    c_ref[...] = jnp.concatenate([cols_of(us, blocks[j::width]) for j in range(width)], 1)
-
-
-def rows_body(m, parts, packs, block_count, *refs):
+    k_ref, u_ref, c_ref = refs[parts + packs :]
+    u = jnp.concatenate([flat(pack[n + 2 * p : n + 3 * p, :]) for pack in pack_refs], 1) / total
+    u_ref[...] = u
+    c_ref[...] = cols_of(u, k_ref)
+
+
+def rows_body(m, parts, packs, *refs):
     q = m // LANES
     total = total_of(refs[:parts])
     pack_refs = refs[parts : parts + packs]
-    rest = refs[parts + packs :]
-    blocks = [(rest[2 * k], rest[2 * k + 1]) for k in range(block_count)]
-    v_ref, r_ref = refs[-2:]
-    vs = [flat(pack[m + q : m + 2 * q, :]) / total[:, k * m : (k + 1) * m] for k, pack in enumerate(pack_refs)]
-    v_ref[...] = vs[0]
-    r_ref[...] = jnp.concatenate([rows_of(vs, blocks[i : i + packs]) for i in range(0, block_count, packs)], 1)
-
-
-def half_step(body, name, size, partials, packs, blocks, outs, after):
-    args = [*partials, *packs, *[ref for block in blocks for ref in block]]
+    k_ref, v_ref, r_ref = refs[parts + packs :]
+    v = jnp.concatenate([flat(pack[m + q : m + 2 * q, :]) for pack in pack_refs], 1) / total
+    v_ref[...] = v[:, :m]
+    r_ref[...] = rows_of(v, k_ref)
+
+
+def half_step(body, name, size, partials, packs, kernel, outs, after):
+    args = [*partials, *packs, kernel]
     return pl.pallas_call(
-        lambda *refs: body(size, len(partials), len(packs), len(blocks), *refs[: len(args)], *refs[-2:]),
+        lambda *refs: body(size, len(partials), len(packs), *refs[: len(args)], *refs[-2:]),
         in_specs=[VMEM] * len(args) + [ANY] * len(after),
         out_specs=[VMEM] * 2,
         out_shape=outs,
@@ -415,7 +408,7 @@
 
     after = tables(0, 0, 6, filt)
     rpacks = over_y(gate(rpack, *xpacks, *ypacks, *after))
-    blocks, partial = gibbs_call(n, m, xpacks, ypacks, penalty, after)
+    kernel, partial = gibbs_call(n, m, xpacks, ypacks, penalty, after)
     row_sums = pltpu.VMEM((1, len(xpacks) * n), f32)
     col_sums = pltpu.VMEM((1, len(ypacks) * m), f32)
     fills = [
@@ -427,12 +420,12 @@
     after = fills[0][0](partial)
     for iteration in range(ITERS):
         cohort_scale, column = half_step(
-            cols_body, "cols", n, lines, xpacks, blocks, [row_sums, col_sums], after
+            cols_body, "cols", n, lines, xpacks, kernel, [row_sums, col_sums], after
         )
         sibling = core(column)
         after = fills[iteration][1](column)
         cell_scale, partial = half_step(
-            rows_body, "rows", m, [column, sibling], ypacks, blocks,
+            rows_body, "rows", m, [column, sibling], ypacks, kernel,
             [jax.ShapeDtypeStruct((1, m), f32), row_sums], after,
         )
         lines = along_z(partial)

time: 54.4 us -> 52.5 us (0.965)
  Pallas kernels: 31.7 us -> 28.8 us
  starting transfers between devices: 19.2 us -> 20.2 us
    pallas_call x4, Pallas kernels: 5.03 us -> 3.06 us  [half_step(): pl.pallas_call(lambda *refs: body(size, len(partials), len(packs), *refs[...]
    ppermute x15, starting transfers between devices: 19.2 us -> 20.2 us  [move(): lax.ppermute(x, axis, [(b * pair + r, away(b) * pair + (r ^ flip)) for b...]
    pallas_call x1, Pallas kernels: 2.73 us -> 1.79 us  [gibbs_call(): pl.pallas_call(lambda *refs: gibbs_body(n, m, len(xpacks), len(ypacks), *...]
  transfers between devices with their start and end apart: 15 -> 15, of which waited for: 1 -> 1; matrix products, arithmetic and copies ran while one was open for 0% -> 0% of each run, Pallas kernels for 48% -> 46%
where the time goes in v8:
time: 52.5 us; the launch traced here: 52.3 us
  Pallas kernels  28.8 us (55%)
  starting transfers between devices  20.2 us (38%)
  waiting for transfers between devices  1.77 us (3%)
  between operations  0.81 us (2%)
  other arithmetic  0.74 us (1%)
    ppermute x15, starting transfers between devices, move(): lax.ppermute(x, axis, [(b * pair + r, away(b) * pair + (r ^ flip)) for b...  20.2 us
    pallas_call x7, Pallas kernels, table_call(): pl.pallas_call(lambda *refs: table_body(n, first, count, *refs[:2], *refs...  18.5 us
    pallas_call x2, Pallas kernels, spread_call(): pl.pallas_call(lambda *refs: spread_body(n, t_first, t_count, len(partial...  3.97 us
    pallas_call x4, Pallas kernels, half_step(): pl.pallas_call(lambda *refs: body(size, len(partials), len(packs), *refs[...  3.06 us
    pallas_call x1, Pallas kernels, gibbs_call(): pl.pallas_call(lambda *refs: gibbs_body(n, m, len(xpacks), len(ypacks), *...  1.79 us
    ppermute x15, waiting for transfers between devices, move(): lax.ppermute(x, axis, [(b * pair + r, away(b) * pair + (r ^ flip)) for b...  1.77 us
    pallas_call x1, Pallas kernels, first_call(): pl.pallas_call(first_body, in_specs=[HBM] * len(args), out_specs=[VMEM] *...  1.5 us
  transfers between devices with their start and end apart: 15, of which 1 were waited for; matrix products, arithmetic and copies ran while one was open for 0% of the time, Pallas kernels for 46%

profile of v8, /device:TPU:1, one launch (start us, length us, event | category | flops | bytes accessed | tf_op | source)
XLA Modules:
  0.0 52.3 jit_solution(7020624776100612779)
XLA Ops:
  0.6 0.0 copy-start
  0.6 1.5 %first.1 = (f32[524,128]{1,0:T(8,128)S(1)}, f32[520,128]{1,0:T(8,128)S(1)}, f32[1536,128]{1,0:T(8,128)S(1)}, f32[32,128]{1,0:T(8,128)S(1)}) custom-call(bf16[512,128]{1,0:T(8,128)(2,1)} %x_hbm.1, bf16[512,128]{1,0:T(8,128)(2,1)} %y_hbm.1, s32[4,128]{1,0:T(4,128)} %bitcast.7, s32[4,128]{1,0:T(4,128)} %bitcast.8, f32[4,128]{1,0:T(4,128)} %bitcast.9, ...), custom_call_target="tpu_custom_call" | custom-call | tf_op jit(solution)/shard_map/first/pallas_call | solution.py:161
  2.1 2.1 %collective-permute-start = (f32[524,128]{1,0:T(8,128)S(1)}, f32[524,128]{1,0:T(8,128)S(1)}, u32[]{:S(2)}, u32[]{:S(2)}) collective-permute-start(f32[524,128]{1,0:T(8,128)S(1)} %get-tuple-element.40.refs_0_.refs_4_.refs_5_), channel_id=1, source_target_pairs={{0,16},{8,24},{16,0},{24,8},{1,17},{9,25},{17,1},{25,9},{2,18},{10... | collective-permute-start | bytes 804872 | tf_op jit(solution)/shard_map/ppermute | solution.py:350
  4.3 1.2 %collective-permute-start.1 = (f32[520,128]{1,0:T(8,128)S(1)}, f32[520,128]{1,0:T(8,128)S(1)}, u32[]{:S(2)}, u32[]{:S(2)}) collective-permute-start(f32[520,128]{1,0:T(8,128)S(1)} %get-tuple-element.41.refs_2_), channel_id=1, source_target_pairs={{0,1},{1,0},{2,3},{3,2},{4,5},{5,4},{6,7},{7,6},{8,9},{9,8},{10,11... | collective-permute-start | bytes 798728 | tf_op jit(solution)/shard_map/ppermute | solution.py:350
  5.5 6.7 %tables.7 = (bf16[32,384,128]{2,1,0:T(8,128)(2,1)S(1)}, bf16[32,384,128]{2,1,0:T(8,128)(2,1)S(1)}, f32[8,128]{1,0:T(8,128)S(1)}) custom-call(f32[32,128]{1,0:T(8,128)S(1)} %get-tuple-element.42.refs_0_.refs_2_, f32[1536,128]{1,0:T(8,128)S(1)} %get-tuple-element.51.refs_1_, f32[32,128]{1,0:T(8,128)S(1)} %get-tuple-element.42.refs_0_.refs_2_), custom_call_target="tpu_custom_call" | custom-call | flops 805306368 | bytes 23040000 | tf_op jit(solution)/shard_map/tables/pallas_call | solution.py:291
  12.2 0.0 collective-permute-done.1.refs_3_
  12.2 0.0 collective-permute-done.refs_1_.refs_5_.refs_6_
  12.2 0.3 collective-permute-start.9
  12.5 0.0 copy-done
  12.5 1.8 %gibbs.1 = (f32[1024,1024]{1,0:T(8,128)S(1)}, f32[1,1024]{1,0:T(1,128)S(1)}) custom-call(f32[524,128]{1,0:T(8,128)S(1)} %get-tuple-element.40.refs_0_.refs_4_.refs_5_, f32[524,128]{1,0:T(8,128)S(1)} %collective-permute-done.refs_1_.refs_5_.refs_6_, f32[520,128]{1,0:T(8,128)S(1)} %get-tuple-element.41.refs_2_, f32[520,128]{1,0:T(8,128)S(1)} %collective-permute-done.1.refs_3_, ...), custom_call_target="tpu_custom_call" | custom-call | flops 268435456 | bytes 4194304 | tf_op jit(solution)/shard_map/gibbs/pallas_call | solution.py:201
  14.3 3.4 %collective-permute-start.4 = (f32[1,1024]{1,0:T(1,128)S(1)}, f32[1,1024]{1,0:T(1,128)S(1)}, u32[]{:S(2)}, u32[]{:S(2)}) collective-permute-start(f32[1,1024]{1,0:T(1,128)S(1)} %get-tuple-element.45.refs_2_.refs_0_), channel_id=1, source_target_pairs={{0,6},{1,7},{2,4},{3,5},{4,2},{5,3},{6,0},{7,1},{8,14},{9,15},{10,... | collective-permute-start | bytes 12296 | tf_op jit(solution)/shard_map/ppermute | solution.py:350
  17.7 0.0 collective-permute-start.3
  17.7 0.4 collective-permute-start.2
  18.0 1.2 %tables.8 = (bf16[32,64,128]{2,1,0:T(8,128)(2,1)S(1)}, bf16[32,64,128]{2,1,0:T(8,128)(2,1)S(1)}, f32[8,128]{1,0:T(8,128)S(1)}) custom-call(f32[32,128]{1,0:T(8,128)S(1)} %get-tuple-element.42.refs_0_.refs_2_, f32[1536,128]{1,0:T(8,128)S(1)} %get-tuple-element.51.refs_1_, f32[1,1024]{1,0:T(1,128)S(1)} %get-tuple-element.45.refs_2_.refs_0_), custom_call_target="tpu_custom_call" | custom-call | flops 134217728 | bytes 3840000 | tf_op jit(solution)/shard_map/tables/pallas_call | solution.py:291
  19.3 0.0 collective-permute-done.4.refs_3_
  19.3 1.7 %collective-permute-done.3.refs_2_ = f32[1,1024]{1,0:T(1,128)S(1)} collective-permute-done((f32[1,1024]{1,0:T(1,128)S(1)}, f32[1,1024]{1,0:T(1,128)S(1)}, u32[]{:S(2)}, u32[]{:S(2)}) %collective-permute-start.3) | collective-permute-done | bytes 4128 | tf_op jit(solution)/shard_map/ppermute | solution.py:350
  21.0 0.0 collective-permute-done.2.refs_1_
  21.0 1.0 %cols.2 = (f32[1,1024]{1,0:T(1,128)}, f32[1,1024]{1,0:T(1,128)S(1)}) custom-call(f32[1,1024]{1,0:T(1,128)S(1)} %get-tuple-element.45.refs_2_.refs_0_, f32[1,1024]{1,0:T(1,128)S(1)} %collective-permute-done.2.refs_1_, f32[1,1024]{1,0:T(1,128)S(1)} %collective-permute-done.3.refs_2_, f32[1,1024]{1,0:T(1,128)S(1)} %collective-permute-done.4.refs_3_, ...), custom_call_target="tpu_custom_call" | custom-call | tf_op jit(solution)/shard_map/cols/pallas_call | solution.py:243
  22.0 2.9 %collective-permute-start.5 = (f32[1,1024]{1,0:T(1,128)S(1)}, f32[1,1024]{1,0:T(1,128)S(1)}, u32[]{:S(2)}, u32[]{:S(2)}) collective-permute-start(f32[1,1024]{1,0:T(1,128)S(1)} %get-tuple-element.48.refs_2_.refs_0_), channel_id=1, source_target_pairs={{0,8},{8,0},{16,24},{24,16},{1,9},{9,1},{17,25},{25,17},{2,10},{10... | collective-permute-start | bytes 12296 | tf_op jit(solution)/shard_map/ppermute | solution.py:350
  24.9 1.2 %tables.9 = (bf16[32,64,128]{2,1,0:T(8,128)(2,1)S(1)}, bf16[32,64,128]{2,1,0:T(8,128)(2,1)S(1)}, f32[8,128]{1,0:T(8,128)S(1)}) custom-call(f32[32,128]{1,0:T(8,128)S(1)} %get-tuple-element.42.refs_0_.refs_2_, f32[1536,128]{1,0:T(8,128)S(1)} %get-tuple-element.51.refs_1_, f32[1,1024]{1,0:T(1,128)S(1)} %get-tuple-element.48.refs_2_.refs_0_), custom_call_target="tpu_custom_call" | custom-call | flops 134217728 | bytes 3840000 | tf_op jit(solution)/shard_map/tables/pallas_call | solution.py:291
  26.2 0.0 collective-permute-done.5.refs_1_
  26.2 0.9 %rows.2 = (f32[1,512]{1,0:T(1,128)}, f32[1,1024]{1,0:T(1,128)S(1)}) custom-call(f32[1,1024]{1,0:T(1,128)S(1)} %get-tuple-element.48.refs_2_.refs_0_, f32[1,1024]{1,0:T(1,128)S(1)} %collective-permute-done.5.refs_1_, f32[520,128]{1,0:T(8,128)S(1)} %get-tuple-element.41.refs_2_, f32[520,128]{1,0:T(8,128)S(1)} %collective-permute-done.1.refs_3_, ...), custom_call_target="tpu_custom_call" | custom-call | tf_op jit(solution)/shard_map/rows/pallas_call | solution.py:243
  27.1 1.2 %collective-permute-start.8 = (f32[1,1024]{1,0:T(1,128)S(1)}, f32[1,1024]{1,0:T(1,128)S(1)}, u32[]{:S(2)}, u32[]{:S(2)}) collective-permute-start(f32[1,1024]{1,0:T(1,128)S(1)} %get-tuple-element.50.refs_2_.refs_0_), channel_id=1, source_target_pairs={{0,6},{1,7},{2,4},{3,5},{4,2},{5,3},{6,0},{7,1},{8,14},{9,15},{10,... | collective-permute-start | bytes 12296 | tf_op jit(solution)/shard_map/ppermute | solution.py:350
  28.3 0.6 %collective-permute-start.7 = (f32[1,1024]{1,0:T(1,128)S(1)}, f32[1,1024]{1,0:T(1,128)S(1)}, u32[]{:S(2)}, u32[]{:S(2)}) collective-permute-start(f32[1,1024]{1,0:T(1,128)S(1)} %get-tuple-element.50.refs_2_.refs_0_), channel_id=1, source_target_pairs={{0,4},{1,5},{2,6},{3,7},{4,0},{5,1},{6,2},{7,3},{8,12},{9,13},{10,... | collective-permute-start | bytes 12296 | tf_op jit(solution)/shard_map/ppermute | solution.py:350
  28.8 1.8 %collective-permute-start.6 = (f32[1,1024]{1,0:T(1,128)S(1)}, f32[1,1024]{1,0:T(1,128)S(1)}, u32[]{:S(2)}, u32[]{:S(2)}) collective-permute-start(f32[1,1024]{1,0:T(1,128)S(1)} %get-tuple-element.50.refs_2_.refs_0_), channel_id=1, source_target_pairs={{0,2},{1,3},{2,0},{3,1},{4,6},{5,7},{6,4},{7,5},{8,10},{9,11},{10,... | collective-permute-start | bytes 12296 | tf_op jit(solution)/shard_map/ppermute | solution.py:350
  30.6 0.0 collective-permute-done.9.refs_1_
  30.6 4.7 %tables.10 = (bf16[32,256,128]{2,1,0:T(8,128)(2,1)S(1)}, bf16[32,256,128]{2,1,0:T(8,128)(2,1)S(1)}, f32[8,128]{1,0:T(8,128)S(1)}) custom-call(f32[32,128]{1,0:T(8,128)S(1)} %get-tuple-element.42.refs_0_.refs_2_, f32[1536,128]{1,0:T(8,128)S(1)} %collective-permute-done.9.refs_1_, f32[1,1024]{1,0:T(1,128)S(1)} %get-tuple-element.50.refs_2_.refs_0_), custom_call_target="tpu_custom_call" | custom-call | flops 536870912 | bytes 15360000 | tf_op jit(solution)/shard_map/tables/pallas_call | solution.py:291
  35.3 0.0 collective-permute-done.8.refs_3_
  35.3 0.0 collective-permute-done.7.refs_2_
  35.3 0.0 collective-permute-done.6.refs_1_
  35.3 0.4 cols.3
  35.7 1.7 %collective-permute-start.10 = (f32[1,1024]{1,0:T(1,128)S(1)}, f32[1,1024]{1,0:T(1,128)S(1)}, u32[]{:S(2)}, u32[]{:S(2)}) collective-permute-start(f32[1,1024]{1,0:T(1,128)S(1)} %get-tuple-element.54.refs_2_.refs_0_), channel_id=1, source_target_pairs={{0,8},{8,0},{16,24},{24,16},{1,9},{9,1},{17,25},{25,17},{2,10},{10... | collective-permute-start | bytes 12296 | tf_op jit(solution)/shard_map/ppermute | solution.py:350
  37.4 1.2 %tables.11 = (bf16[32,64,128]{2,1,0:T(8,128)(2,1)S(1)}, bf16[32,64,128]{2,1,0:T(8,128)(2,1)S(1)}, f32[8,128]{1,0:T(8,128)S(1)}) custom-call(f32[32,128]{1,0:T(8,128)S(1)} %get-tuple-element.42.refs_0_.refs_2_, f32[1536,128]{1,0:T(8,128)S(1)} %collective-permute-done.9.refs_1_, f32[1,1024]{1,0:T(1,128)S(1)} %get-tuple-element.54.refs_2_.refs_0_), custom_call_target="tpu_custom_call" | custom-call | flops 134217728 | bytes 3840000 | tf_op jit(solution)/shard_map/tables/pallas_call | solution.py:291
  38.6 0.0 collective-permute-done.10.refs_1_
  38.6 0.9 %rows.3 = (f32[1,512]{1,0:T(1,128)}, f32[1,1024]{1,0:T(1,128)S(1)}) custom-call(f32[1,1024]{1,0:T(1,128)S(1)} %get-tuple-element.54.refs_2_.refs_0_, f32[1,1024]{1,0:T(1,128)S(1)} %collective-permute-done.10.refs_1_, f32[520,128]{1,0:T(8,128)S(1)} %get-tuple-element.41.refs_2_, f32[520,128]{1,0:T(8,128)S(1)} %collective-permute-done.1.refs_3_, ...), custom_call_target="tpu_custom_call" | custom-call | tf_op jit(solution)/shard_map/rows/pallas_call | solution.py:243
  39.5 3.3 %collective-permute-start.13 = (f32[1,1024]{1,0:T(1,128)S(1)}, f32[1,1024]{1,0:T(1,128)S(1)}, u32[]{:S(2)}, u32[]{:S(2)}) collective-permute-start(f32[1,1024]{1,0:T(1,128)S(1)} %get-tuple-element.56.refs_2_.refs_1_), channel_id=1, source_target_pairs={{0,6},{1,7},{2,4},{3,5},{4,2},{5,3},{6,0},{7,1},{8,14},{9,15},{10,... | collective-permute-start | bytes 12296 | tf_op jit(solution)/shard_map/ppermute | solution.py:350
  42.8 0.0 collective-permute-start.12
  42.8 0.3 collective-permute-start.11
  43.1 2.2 %tables.12 = (bf16[32,128,128]{2,1,0:T(8,128)(2,1)S(1)}, bf16[32,128,128]{2,1,0:T(8,128)(2,1)S(1)}, f32[8,128]{1,0:T(8,128)S(1)}) custom-call(f32[32,128]{1,0:T(8,128)S(1)} %get-tuple-element.42.refs_0_.refs_2_, f32[1536,128]{1,0:T(8,128)S(1)} %collective-permute-done.9.refs_1_, f32[1,1024]{1,0:T(1,128)S(1)} %get-tuple-element.56.refs_2_.refs_1_), custom_call_target="tpu_custom_call" | custom-call | flops 268435456 | bytes 7680000 | tf_op jit(solution)/shard_map/tables/pallas_call | solution.py:291
  45.3 1.3 %tables.13 = (bf16[32,64,128]{2,1,0:T(8,128)(2,1)S(1)}, bf16[32,64,128]{2,1,0:T(8,128)(2,1)S(1)}, f32[8,128]{1,0:T(8,128)S(1)}) custom-call(f32[32,128]{1,0:T(8,128)S(1)} %get-tuple-element.42.refs_0_.refs_2_, f32[1536,128]{1,0:T(8,128)S(1)} %collective-permute-done.9.refs_1_, f32[8,128]{1,0:T(8,128)S(1)} %get-tuple-element.69.refs_2_), custom_call_target="tpu_custom_call" | custom-call | flops 134217728 | bytes 3840000 | tf_op jit(solution)/shard_map/tables/pallas_call | solution.py:291
  46.6 0.0 collective-permute-done.13.refs_4_
  46.6 0.0 collective-permute-done.12.refs_3_
  46.6 0.0 collective-permute-done.11.refs_2_
  46.6 2.0 %spread.2 = (f32[16,32,128]{2,1,0:T(8,128)S(1)}, f32[1,512]{1,0:T(1,128)}) custom-call(f32[1,1024]{1,0:T(1,128)S(1)} %get-tuple-element.53.refs_0_, f32[1,1024]{1,0:T(1,128)S(1)} %get-tuple-element.56.refs_2_.refs_1_, f32[1,1024]{1,0:T(1,128)S(1)} %collective-permute-done.11.refs_2_, f32[1,1024]{1,0:T(1,128)S(1)} %collective-permute-done.12.refs_3_, ...), custom_call_target="tpu_custom_call" | custom-call | tf_op jit(solution)/shard_map/spread/pallas_call | solution.py:332
  48.6 1.0 %collective-permute-start.14 = (f32[16,32,128]{2,1,0:T(8,128)S(1)}, f32[16,32,128]{2,1,0:T(8,128)S(1)}, u32[]{:S(2)}, u32[]{:S(2)}) collective-permute-start(f32[16,32,128]{2,1,0:T(8,128)S(1)} %get-tuple-element.76), channel_id=1, source_target_pairs={{0,8},{8,0},{16,24},{24,16},{1,9},{9,1},{17,25},{25,17},{2,10},{10... | collective-permute-start | bytes 786440 | tf_op jit(solution)/shard_map/ppermute | solution.py:350
  49.6 2.0 %spread.3 = (f32[16,32,128]{2,1,0:T(8,128)S(1)}, f32[1,512]{1,0:T(1,128)}) custom-call(f32[1,1024]{1,0:T(1,128)S(1)} %get-tuple-element.53.refs_0_, f32[1,1024]{1,0:T(1,128)S(1)} %get-tuple-element.56.refs_2_.refs_1_, f32[1,1024]{1,0:T(1,128)S(1)} %collective-permute-done.11.refs_2_, f32[1,1024]{1,0:T(1,128)S(1)} %collective-permute-done.12.refs_3_, ...), custom_call_target="tpu_custom_call" | custom-call | tf_op jit(solution)/shard_map/spread/pallas_call | solution.py:332
  51.6 0.0 collective-permute-done.14
  51.6 0.7 %add.3 = f32[16,32,128]{2,1,0:T(8,128)} add(f32[16,32,128]{2,1,0:T(8,128)S(1)} %get-tuple-element.75, f32[16,32,128]{2,1,0:T(8,128)S(1)} %collective-permute-done.14) | non-fusion elementwise | flops 65536 | bytes 786432 | tf_op jit(solution)/shard_map/add | solution.py:436
Async XLA Ops:
  0.6 11.9 %copy-start = (f32[32,32]{1,0:T(8,128)S(1)}, f32[32,32]{1,0:T(8,128)}, u32[]{:S(2)}) copy-start(f32[32,32]{1,0:T(8,128)} %refs_4_.1) | copy-start | bytes 12292
  2.1 10.1 %collective-permute-start = (f32[524,128]{1,0:T(8,128)S(1)}, f32[524,128]{1,0:T(8,128)S(1)}, u32[]{:S(2)}, u32[]{:S(2)}) collective-permute-start(f32[524,128]{1,0:T(8,128)S(1)} %get-tuple-element.40.refs_0_.refs_4_.refs_5_), channel_id=1, source_target_pairs={{0,16},{8,24},{16,0},{24,8},{1,17},{9,25},{17,1},{25,9},{2,18},{10... | collective-permute-start | bytes 804872 | tf_op jit(solution)/shard_map/ppermute | solution.py:350
  4.3 7.9 %collective-permute-start.1 = (f32[520,128]{1,0:T(8,128)S(1)}, f32[520,128]{1,0:T(8,128)S(1)}, u32[]{:S(2)}, u32[]{:S(2)}) collective-permute-start(f32[520,128]{1,0:T(8,128)S(1)} %get-tuple-element.41.refs_2_), channel_id=1, source_target_pairs={{0,1},{1,0},{2,3},{3,2},{4,5},{5,4},{6,7},{7,6},{8,9},{9,8},{10,11... | collective-permute-start | bytes 798728 | tf_op jit(solution)/shard_map/ppermute | solution.py:350
  12.2 18.4 %collective-permute-start.9 = (f32[1536,128]{1,0:T(8,128)S(1)}, f32[1536,128]{1,0:T(8,128)S(1)}, u32[]{:S(2)}, u32[]{:S(2)}) collective-permute-start(f32[1536,128]{1,0:T(8,128)S(1)} %get-tuple-element.51.refs_1_), channel_id=1, source_target_pairs={{0,16},{8,24},{16,0},{24,8},{1,17},{9,25},{17,1},{25,9},{2,18},{10... | collective-permute-start | bytes 2359304 | tf_op jit(solution)/shard_map/ppermute | solution.py:350
  14.3 5.0 %collective-permute-start.4 = (f32[1,1024]{1,0:T(1,128)S(1)}, f32[1,1024]{1,0:T(1,128)S(1)}, u32[]{:S(2)}, u32[]{:S(2)}) collective-permute-start(f32[1,1024]{1,0:T(1,128)S(1)} %get-tuple-element.45.refs_2_.refs_0_), channel_id=1, source_target_pairs={{0,6},{1,7},{2,4},{3,5},{4,2},{5,3},{6,0},{7,1},{8,14},{9,15},{10,... | collective-permute-start | bytes 12296 | tf_op jit(solution)/shard_map/ppermute | solution.py:350
  17.7 3.4 %collective-permute-start.3 = (f32[1,1024]{1,0:T(1,128)S(1)}, f32[1,1024]{1,0:T(1,128)S(1)}, u32[]{:S(2)}, u32[]{:S(2)}) collective-permute-start(f32[1,1024]{1,0:T(1,128)S(1)} %get-tuple-element.45.refs_2_.refs_0_), channel_id=1, source_target_pairs={{0,4},{1,5},{2,6},{3,7},{4,0},{5,1},{6,2},{7,3},{8,12},{9,13},{10,... | collective-permute-start | bytes 12296 | tf_op jit(solution)/shard_map/ppermute | solution.py:350
  17.7 3.4 %collective-permute-start.2 = (f32[1,1024]{1,0:T(1,128)S(1)}, f32[1,1024]{1,0:T(1,128)S(1)}, u32[]{:S(2)}, u32[]{:S(2)}) collective-permute-start(f32[1,1024]{1,0:T(1,128)S(1)} %get-tuple-element.45.refs_2_.refs_0_), channel_id=1, source_target_pairs={{0,2},{1,3},{2,0},{3,1},{4,6},{5,7},{6,4},{7,5},{8,10},{9,11},{10,... | collective-permute-start | bytes 12296 | tf_op jit(solution)/shard_map/ppermute | solution.py:350
  22.0 4.2 %collective-permute-start.5 = (f32[1,1024]{1,0:T(1,128)S(1)}, f32[1,1024]{1,0:T(1,128)S(1)}, u32[]{:S(2)}, u32[]{:S(2)}) collective-permute-start(f32[1,1024]{1,0:T(1,128)S(1)} %get-tuple-element.48.refs_2_.refs_0_), channel_id=1, source_target_pairs={{0,8},{8,0},{16,24},{24,16},{1,9},{9,1},{17,25},{25,17},{2,10},{10... | collective-permute-start | bytes 12296 | tf_op jit(solution)/shard_map/ppermute | solution.py:350
  27.1 8.2 %collective-permute-start.8 = (f32[1,1024]{1,0:T(1,128)S(1)}, f32[1,1024]{1,0:T(1,128)S(1)}, u32[]{:S(2)}, u32[]{:S(2)}) collective-permute-start(f32[1,1024]{1,0:T(1,128)S(1)} %get-tuple-element.50.refs_2_.refs_0_), channel_id=1, source_target_pairs={{0,6},{1,7},{2,4},{3,5},{4,2},{5,3},{6,0},{7,1},{8,14},{9,15},{10,... | collective-permute-start | bytes 12296 | tf_op jit(solution)/shard_map/ppermute | solution.py:350
  28.3 7.0 %collective-permute-start.7 = (f32[1,1024]{1,0:T(1,128)S(1)}, f32[1,1024]{1,0:T(1,128)S(1)}, u32[]{:S(2)}, u32[]{:S(2)}) collective-permute-start(f32[1,1024]{1,0:T(1,128)S(1)} %get-tuple-element.50.refs_2_.refs_0_), channel_id=1, source_target_pairs={{0,4},{1,5},{2,6},{3,7},{4,0},{5,1},{6,2},{7,3},{8,12},{9,13},{10,... | collective-permute-start | bytes 12296 | tf_op jit(solution)/shard_map/ppermute | solution.py:350
  28.8 6.5 %collective-permute-start.6 = (f32[1,1024]{1,0:T(1,128)S(1)}, f32[1,1024]{1,0:T(1,128)S(1)}, u32[]{:S(2)}, u32[]{:S(2)}) collective-permute-start(f32[1,1024]{1,0:T(1,128)S(1)} %get-tuple-element.50.refs_2_.refs_0_), channel_id=1, source_target_pairs={{0,2},{1,3},{2,0},{3,1},{4,6},{5,7},{6,4},{7,5},{8,10},{9,11},{10,... | collective-permute-start | bytes 12296 | tf_op jit(solution)/shard_map/ppermute | solution.py:350
  35.7 2.9 %collective-permute-start.10 = (f32[1,1024]{1,0:T(1,128)S(1)}, f32[1,1024]{1,0:T(1,128)S(1)}, u32[]{:S(2)}, u32[]{:S(2)}) collective-permute-start(f32[1,1024]{1,0:T(1,128)S(1)} %get-tuple-element.54.refs_2_.refs_0_), channel_id=1, source_target_pairs={{0,8},{8,0},{16,24},{24,16},{1,9},{9,1},{17,25},{25,17},{2,10},{10... | collective-permute-start | bytes 12296 | tf_op jit(solution)/shard_map/ppermute | solution.py:350
  39.5 7.1 %collective-permute-start.13 = (f32[1,1024]{1,0:T(1,128)S(1)}, f32[1,1024]{1,0:T(1,128)S(1)}, u32[]{:S(2)}, u32[]{:S(2)}) collective-permute-start(f32[1,1024]{1,0:T(1,128)S(1)} %get-tuple-element.56.refs_2_.refs_1_), channel_id=1, source_target_pairs={{0,6},{1,7},{2,4},{3,5},{4,2},{5,3},{6,0},{7,1},{8,14},{9,15},{10,... | collective-permute-start | bytes 12296 | tf_op jit(solution)/shard_map/ppermute | solution.py:350
  42.8 3.8 %collective-permute-start.12 = (f32[1,1024]{1,0:T(1,128)S(1)}, f32[1,1024]{1,0:T(1,128)S(1)}, u32[]{:S(2)}, u32[]{:S(2)}) collective-permute-start(f32[1,1024]{1,0:T(1,128)S(1)} %get-tuple-element.56.refs_2_.refs_1_), channel_id=1, source_target_pairs={{0,4},{1,5},{2,6},{3,7},{4,0},{5,1},{6,2},{7,3},{8,12},{9,13},{10,... | collective-permute-start | bytes 12296 | tf_op jit(solution)/shard_map/ppermute | solution.py:350
  42.8 3.8 %collective-permute-start.11 = (f32[1,1024]{1,0:T(1,128)S(1)}, f32[1,1024]{1,0:T(1,128)S(1)}, u32[]{:S(2)}, u32[]{:S(2)}) collective-permute-start(f32[1,1024]{1,0:T(1,128)S(1)} %get-tuple-element.56.refs_2_.refs_1_), channel_id=1, source_target_pairs={{0,2},{1,3},{2,0},{3,1},{4,6},{5,7},{6,4},{7,5},{8,10},{9,11},{10,... | collective-permute-start | bytes 12296 | tf_op jit(solution)/shard_map/ppermute | solution.py:350
  48.6 3.0 %collective-permute-start.14 = (f32[16,32,128]{2,1,0:T(8,128)S(1)}, f32[16,32,128]{2,1,0:T(8,128)S(1)}, u32[]{:S(2)}, u32[]{:S(2)}) collective-permute-start(f32[16,32,128]{2,1,0:T(8,128)S(1)} %get-tuple-element.76), channel_id=1, source_target_pairs={{0,8},{8,0},{16,24},{24,16},{1,9},{9,1},{17,25},{25,17},{2,10},{10... | collective-permute-start | bytes 786440 | tf_op jit(solution)/shard_map/ppermute | solution.py:350

commit v9 on v8

--- a/solution.py
+++ b/solution.py
@@ -119,11 +119,12 @@
 
 def first_body(
     x_hbm, y_hbm, rr_hbm, seg_hbm, mass_hbm, cr_hbm, cm_hbm, f_hbm, m_hbm, d_hbm, a_hbm,
-    xpack_ref, ypack_ref, rpack_ref, f_ref, xb_ref, yb_ref, rr_ref, seg_ref, cr_ref, m_ref, d_ref, sems,
+    xpack_ref, ypack_ref, early_ref, late_ref, f_ref, xb_ref, yb_ref, rr_ref, seg_ref, cr_ref, m_ref, d_ref, sems,
 ):
     me = lax.axis_index("cohort")
     n, m = xb_ref.shape[0], yb_ref.shape[0]
     p, q = n // LANES, m // LANES
+    e = early_ref.shape[0] // 3
     copies = run_copies(
         (
             (x_hbm, xb_ref),
@@ -135,7 +136,8 @@
             (cm_hbm, ypack_ref.at[pl.ds(m + q, q), :]),
             (m_hbm, m_ref),
             (d_hbm, d_ref),
-            (a_hbm, rpack_ref.at[pl.ds(2 * n, n), :]),
+            (a_hbm.at[pl.ds(0, e), :], early_ref.at[pl.ds(2 * e, e), :]),
+            (a_hbm.at[pl.ds(e, n - e), :], late_ref.at[pl.ds(2 * (n - e), n - e), :]),
             (f_hbm.at[me], f_ref),
         ),
         sems,
@@ -147,16 +149,18 @@
     xpack_ref[n + p : n + 2 * p, :] = seg_ref[...].astype(f32)
     ypack_ref[0:m, :] = yb_ref[...].astype(f32)
     ypack_ref[m : m + q, :] = cr_ref[...].astype(f32)
-    rpack_ref[0:n, :] = m_ref[...].astype(f32)
-    rpack_ref[n : 2 * n, :] = d_ref[...].astype(f32)
-
-
-def first_call(x, y, rr, seg, mass, cr, cm, table, records):
+    for pack, rows in ((early_ref, slice(0, e)), (late_ref, slice(e, n))):
+        size = rows.stop - rows.start
+        pack[0:size, :] = m_ref[rows, :].astype(f32)
+        pack[size : 2 * size, :] = d_ref[rows, :].astype(f32)
+
+
+def first_call(x, y, rr, seg, mass, cr, cm, table, records, early):
     n, m = x.shape[0], y.shape[0]
     p, q = n // LANES, m // LANES
     block = lambda v: v.reshape(-1, LANES)
     i32 = jnp.int32
-    out = [(n + 3 * p, LANES), (m + 2 * q, LANES), (3 * n, LANES), table.shape[1:]]
+    out = [(n + 3 * p, LANES), (m + 2 * q, LANES), (3 * early, LANES), (3 * (n - early), LANES), table.shape[1:]]
     args = (x, y, block(rr), block(seg), block(mass), block(cr), block(cm), table, *records)
     return pl.pallas_call(
         first_body,
@@ -171,7 +175,7 @@
             pltpu.VMEM((q, LANES), i32),
             pltpu.VMEM((n, LANES), i32),
             pltpu.VMEM((n, LANES), i32),
-            pltpu.SemaphoreType.DMA((len(args),)),
+            pltpu.SemaphoreType.DMA((len(args) + 1,)),
         ],
         compiler_params=PARAMS,
         name="first",
@@ -341,6 +345,21 @@
     )(*args, *after)
 
 
+def add_body(a_ref, b_ref, o_ref):
+    o_ref[...] = a_ref[...] + b_ref[...]
+
+
+def add_call(a, b):
+    return pl.pallas_call(
+        add_body,
+        in_specs=[VMEM] * 2,
+        out_specs=VMEM,
+        out_shape=jax.ShapeDtypeStruct(a.shape, f32),
+        compiler_params=PARAMS,
+        name="last",
+    )(a, b)
+
+
 def move(x, axis, size, pair, step, flip):
     blocks = size // pair
 
@@ -384,20 +403,24 @@
     core = lambda x: move(x, "cohort", n_cohort, 2, 0, 1)
     along_z = lambda x: [x] + [move(x, "cell", n_cell, 2, step, 0) for step in range(1, n_z)]
 
-    xpack, ypack, rpack, filt = first_call(
+    unit = n // 8
+    ahead = 4
+    xpack, ypack, *own, filt = first_call(
         cohort_features, cell_features, cohort_region, cohort_segment, cohort_mass, cell_region, cell_mass,
-        jnp.asarray(table), (spend_merchant, spend_day, spend_amount),
+        jnp.asarray(table), (spend_merchant, spend_day, spend_amount), ahead * unit,
     )
     xpacks = [xpack] + over_y(xpack)
     ypacks = [ypack, move(ypack, "cell", n_cell, 2, 0, 1)]
     pairs = {}
-    unit = n // 8
 
     def tables(source, first, units, *after):
         for size in (units & ~1, units & 1):
             if size:
-                pack = rpack if source == 0 else rpacks[source - 1]
-                pairs[source, first], token = table_call(filt, pack, n, first * unit, size * unit, after)
+                late = int(first >= ahead)
+                pack = own[late] if source == 0 else rpacks[late][source - 1]
+                pairs[source, first], token = table_call(
+                    filt, pack, pack.shape[0] // 3, (first - late * ahead) * unit, size * unit, after
+                )
                 after, first = [token], first + size
         return after
 
@@ -406,34 +429,32 @@
             after = tables(source, first, units, *after)
         return after
 
-    after = tables(0, 0, 6, filt)
-    rpacks = over_y(gate(rpack, *xpacks, *ypacks, *after))
+    after = tables(0, ahead, 2, *tables(0, 0, ahead, filt))
+    rpacks = [over_y(gate(own[0], *xpacks, *ypacks, *after))]
     kernel, partial = gibbs_call(n, m, xpacks, ypacks, penalty, after)
     row_sums = pltpu.VMEM((1, len(xpacks) * n), f32)
     col_sums = pltpu.VMEM((1, len(ypacks) * m), f32)
-    fills = [
-        [lambda *after: tables(0, 6, 1, *after), lambda *after: tables(0, 7, 1, *after)],
-        [lambda *after: others(0, 4, *after), lambda *after: others(4, 1, *after)],
-        [lambda *after: others(5, 3, *after)],
-    ]
     lines = along_z(partial)
-    after = fills[0][0](partial)
+    after = tables(0, ahead + 2, 2, partial)
+    fills = [[(0, 1), (1, 3)], [(4, 1), (5, 3)]]
     for iteration in range(ITERS):
         cohort_scale, column = half_step(
             cols_body, "cols", n, lines, xpacks, kernel, [row_sums, col_sums], after
         )
         sibling = core(column)
-        after = fills[iteration][1](column)
+        if iteration == 0:
+            rpacks.append(over_y(gate(own[1], column)))
+        after = others(*fills[iteration][0], column)
         cell_scale, partial = half_step(
             rows_body, "rows", m, [column, sibling], ypacks, kernel,
             [jax.ShapeDtypeStruct((1, m), f32), row_sums], after,
         )
         lines = along_z(partial)
-        after = fills[iteration + 1][0](partial)
+        after = others(*fills[iteration][1], partial)
     ordered = [pairs[key] for key in sorted(pairs)]
     away, weights = spread_call(n, cohort_scale, lines, xpacks, ordered, 0, t_dev, after)
     mine, _ = spread_call(n, cohort_scale, lines, xpacks, ordered, t_dev, t_dev, after)
-    out = mine + core(away)
+    out = add_call(mine, core(away))
     return (weights.reshape(-1), cell_scale.reshape(-1), out)
 
 

time: 52.5 us -> 52.2 us (level)
  waiting for transfers between devices: 1.77 us -> 0.78 us
  Pallas kernels: 28.8 us -> 29.7 us
  other arithmetic: 0.74 us -> 0 us
    ppermute x15 -> x16, waiting for transfers between devices: 1.77 us -> 0.78 us  [move(): lax.ppermute(x, axis, [(b * pair + r, away(b) * pair + (r ^ flip)) for b...]
    add x1 -> x0, other arithmetic: 0.74 us -> none  [per_device(): out = mine + core(away)]
    pallas_call x0 -> x1, Pallas kernels: none -> 0.73 us  [add_call(): pl.pallas_call(add_body, in_specs=[VMEM] * 2, out_specs=VMEM, out_shape=j...]
    ppermute x15 -> x16, starting transfers between devices: 20.2 us -> 20.7 us  [move(): lax.ppermute(x, axis, [(b * pair + r, away(b) * pair + (r ^ flip)) for b...]
    pallas_call x7 -> x9, Pallas kernels: 18.5 us -> 18.7 us  [table_call(): pl.pallas_call(lambda *refs: table_body(n, first, count, *refs[:2], *refs...]
  transfers between devices with their start and end apart: 15 -> 16, of which waited for: 1 -> 1; matrix products, arithmetic and copies ran while one was open for 0% -> 0% of each run, Pallas kernels for 46% -> 47%
where the time goes in v9:
time: 52.2 us; the launch traced here: 52 us
  Pallas kernels  29.7 us (57%)
  starting transfers between devices  20.7 us (40%)
  between operations  0.83 us (2%)
  waiting for transfers between devices  0.78 us (1%)
    ppermute x16, starting transfers between devices, move(): lax.ppermute(x, axis, [(b * pair + r, away(b) * pair + (r ^ flip)) for b...  20.7 us
    pallas_call x9, Pallas kernels, table_call(): pl.pallas_call(lambda *refs: table_body(n, first, count, *refs[:2], *refs...  18.7 us
    pallas_call x2, Pallas kernels, spread_call(): pl.pallas_call(lambda *refs: spread_body(n, t_first, t_count, len(partial...  3.96 us
    pallas_call x4, Pallas kernels, half_step(): pl.pallas_call(lambda *refs: body(size, len(partials), len(packs), *refs[...  3.06 us
    pallas_call x1, Pallas kernels, gibbs_call(): pl.pallas_call(lambda *refs: gibbs_body(n, m, len(xpacks), len(ypacks), *...  1.78 us
    pallas_call x1, Pallas kernels, first_call(): pl.pallas_call(first_body, in_specs=[HBM] * len(args), out_specs=[VMEM] *...  1.5 us
  transfers between devices with their start and end apart: 16, of which 1 were waited for; matrix products, arithmetic and copies ran while one was open for 0% of the time, Pallas kernels for 47%

profile of v9, /device:TPU:1, one launch (start us, length us, event | category | flops | bytes accessed | tf_op | source)
XLA Modules:
  0.0 52.0 jit_solution(15852699410404970960)
XLA Ops:
  0.6 0.0 copy-start
  0.6 1.5 %first.1 = (f32[524,128]{1,0:T(8,128)S(1)}, f32[520,128]{1,0:T(8,128)S(1)}, f32[768,128]{1,0:T(8,128)S(1)}, f32[768,128]{1,0:T(8,128)S(1)}, f32[32,128]{1,0:T(8,128)S(1)}) custom-call(bf16[512,128]{1,0:T(8,128)(2,1)} %x_hbm.1, bf16[512,128]{1,0:T(8,128)(2,1)} %y_hbm.1, s32[4,128]{1,0:T(4,128)} %bitcast.7, s32[4,128]{1,0:T(4,128)} %bitcast.8, ...), custom_call_target="tpu_custom_call" | custom-call | tf_op jit(solution)/shard_map/first/pallas_call | solution.py:165
  2.1 2.1 %collective-permute-start = (f32[524,128]{1,0:T(8,128)S(1)}, f32[524,128]{1,0:T(8,128)S(1)}, u32[]{:S(2)}, u32[]{:S(2)}) collective-permute-start(f32[524,128]{1,0:T(8,128)S(1)} %get-tuple-element.48.refs_0_.refs_4_.refs_5_), channel_id=1, source_target_pairs={{0,16},{8,24},{16,0},{24,8},{1,17},{9,25},{17,1},{25,9},{2,18},{10... | collective-permute-start | bytes 804872 | tf_op jit(solution)/shard_map/ppermute | solution.py:369
  4.3 1.2 %collective-permute-start.1 = (f32[520,128]{1,0:T(8,128)S(1)}, f32[520,128]{1,0:T(8,128)S(1)}, u32[]{:S(2)}, u32[]{:S(2)}) collective-permute-start(f32[520,128]{1,0:T(8,128)S(1)} %get-tuple-element.49.refs_2_), channel_id=1, source_target_pairs={{0,1},{1,0},{2,3},{3,2},{4,5},{5,4},{6,7},{7,6},{8,9},{9,8},{10,11... | collective-permute-start | bytes 798728 | tf_op jit(solution)/shard_map/ppermute | solution.py:369
  5.5 4.7 %tables.9 = (bf16[32,256,128]{2,1,0:T(8,128)(2,1)S(1)}, bf16[32,256,128]{2,1,0:T(8,128)(2,1)S(1)}, f32[8,128]{1,0:T(8,128)S(1)}) custom-call(f32[32,128]{1,0:T(8,128)S(1)} %get-tuple-element.50.refs_0_.refs_2_, f32[768,128]{1,0:T(8,128)S(1)} %get-tuple-element.59.refs_1_, f32[32,128]{1,0:T(8,128)S(1)} %get-tuple-element.50.refs_0_.refs_2_), custom_call_target="tpu_custom_call" | custom-call | flops 536870912 | bytes 15360000 | tf_op jit(solution)/shard_map/tables/pallas_call | solution.py:295
  10.2 2.2 %tables.10 = (bf16[32,128,128]{2,1,0:T(8,128)(2,1)S(1)}, bf16[32,128,128]{2,1,0:T(8,128)(2,1)S(1)}, f32[8,128]{1,0:T(8,128)S(1)}) custom-call(f32[32,128]{1,0:T(8,128)S(1)} %get-tuple-element.50.refs_0_.refs_2_, f32[768,128]{1,0:T(8,128)S(1)} %get-tuple-element.66.refs_1_, f32[8,128]{1,0:T(8,128)S(1)} %get-tuple-element.53.refs_2_), custom_call_target="tpu_custom_call" | custom-call | flops 268435456 | bytes 7680000 | tf_op jit(solution)/shard_map/tables/pallas_call | solution.py:295
  12.4 0.0 collective-permute-done.1.refs_3_
  12.4 0.0 collective-permute-done.refs_1_.refs_5_.refs_6_
  12.4 0.3 collective-permute-start.6
  12.7 0.0 copy-done
  12.7 1.8 %gibbs.1 = (f32[1024,1024]{1,0:T(8,128)S(1)}, f32[1,1024]{1,0:T(1,128)S(1)}) custom-call(f32[524,128]{1,0:T(8,128)S(1)} %get-tuple-element.48.refs_0_.refs_4_.refs_5_, f32[524,128]{1,0:T(8,128)S(1)} %collective-permute-done.refs_1_.refs_5_.refs_6_, f32[520,128]{1,0:T(8,128)S(1)} %get-tuple-element.49.refs_2_, f32[520,128]{1,0:T(8,128)S(1)} %collective-permute-done.1.refs_3_, ...), custom_call_target="tpu_custom_call" | custom-call | flops 268435456 | bytes 4194304 | tf_op jit(solution)/shard_map/gibbs/pallas_call | solution.py:205
  14.5 3.4 %collective-permute-start.4 = (f32[1,1024]{1,0:T(1,128)S(1)}, f32[1,1024]{1,0:T(1,128)S(1)}, u32[]{:S(2)}, u32[]{:S(2)}) collective-permute-start(f32[1,1024]{1,0:T(1,128)S(1)} %get-tuple-element.55.refs_2_.refs_0_), channel_id=1, source_target_pairs={{0,6},{1,7},{2,4},{3,5},{4,2},{5,3},{6,0},{7,1},{8,14},{9,15},{10,... | collective-permute-start | bytes 12296 | tf_op jit(solution)/shard_map/ppermute | solution.py:369
  17.9 0.0 collective-permute-start.3
  17.9 0.4 collective-permute-start.2
  18.2 2.2 %tables.11 = (bf16[32,128,128]{2,1,0:T(8,128)(2,1)S(1)}, bf16[32,128,128]{2,1,0:T(8,128)(2,1)S(1)}, f32[8,128]{1,0:T(8,128)S(1)}) custom-call(f32[32,128]{1,0:T(8,128)S(1)} %get-tuple-element.50.refs_0_.refs_2_, f32[768,128]{1,0:T(8,128)S(1)} %get-tuple-element.66.refs_1_, f32[1,1024]{1,0:T(1,128)S(1)} %get-tuple-element.55.refs_2_.refs_0_), custom_call_target="tpu_custom_call" | custom-call | flops 268435456 | bytes 7680000 | tf_op jit(solution)/shard_map/tables/pallas_call | solution.py:295
  20.5 0.0 collective-permute-done.4.refs_3_
  20.5 0.7 %collective-permute-done.3.refs_2_ = f32[1,1024]{1,0:T(1,128)S(1)} collective-permute-done((f32[1,1024]{1,0:T(1,128)S(1)}, f32[1,1024]{1,0:T(1,128)S(1)}, u32[]{:S(2)}, u32[]{:S(2)}) %collective-permute-start.3) | collective-permute-done | bytes 4128 | tf_op jit(solution)/shard_map/ppermute | solution.py:369
  21.2 0.0 collective-permute-done.2.refs_1_
  21.2 1.0 %cols.2 = (f32[1,1024]{1,0:T(1,128)}, f32[1,1024]{1,0:T(1,128)S(1)}) custom-call(f32[1,1024]{1,0:T(1,128)S(1)} %get-tuple-element.55.refs_2_.refs_0_, f32[1,1024]{1,0:T(1,128)S(1)} %collective-permute-done.2.refs_1_, f32[1,1024]{1,0:T(1,128)S(1)} %collective-permute-done.3.refs_2_, f32[1,1024]{1,0:T(1,128)S(1)} %collective-permute-done.4.refs_3_, ...), custom_call_target="tpu_custom_call" | custom-call | tf_op jit(solution)/shard_map/cols/pallas_call | solution.py:247
  22.2 1.2 %collective-permute-start.11 = (f32[768,128]{1,0:T(8,128)S(1)}, f32[768,128]{1,0:T(8,128)S(1)}, u32[]{:S(2)}, u32[]{:S(2)}) collective-permute-start(f32[768,128]{1,0:T(8,128)S(1)} %get-tuple-element.66.refs_1_), channel_id=1, source_target_pairs={{0,16},{8,24},{16,0},{24,8},{1,17},{9,25},{17,1},{25,9},{2,18},{10... | collective-permute-start | bytes 1179656 | tf_op jit(solution)/shard_map/ppermute | solution.py:369
  23.4 3.2 %collective-permute-start.5 = (f32[1,1024]{1,0:T(1,128)S(1)}, f32[1,1024]{1,0:T(1,128)S(1)}, u32[]{:S(2)}, u32[]{:S(2)}) collective-permute-start(f32[1,1024]{1,0:T(1,128)S(1)} %get-tuple-element.58.refs_2_.refs_0_), channel_id=1, source_target_pairs={{0,8},{8,0},{16,24},{24,16},{1,9},{9,1},{17,25},{25,17},{2,10},{10... | collective-permute-start | bytes 12296 | tf_op jit(solution)/shard_map/ppermute | solution.py:369
  26.6 0.0 collective-permute-done.6.refs_1_
  26.6 1.2 %tables.12 = (bf16[32,64,128]{2,1,0:T(8,128)(2,1)S(1)}, bf16[32,64,128]{2,1,0:T(8,128)(2,1)S(1)}, f32[8,128]{1,0:T(8,128)S(1)}) custom-call(f32[32,128]{1,0:T(8,128)S(1)} %get-tuple-element.50.refs_0_.refs_2_, f32[768,128]{1,0:T(8,128)S(1)} %collective-permute-done.6.refs_1_, f32[1,1024]{1,0:T(1,128)S(1)} %get-tuple-element.58.refs_2_.refs_0_), custom_call_target="tpu_custom_call" | custom-call | flops 134217728 | bytes 3840000 | tf_op jit(solution)/shard_map/tables/pallas_call | solution.py:295
  27.9 0.0 collective-permute-done.5.refs_1_
  27.9 0.9 %rows.2 = (f32[1,512]{1,0:T(1,128)}, f32[1,1024]{1,0:T(1,128)S(1)}) custom-call(f32[1,1024]{1,0:T(1,128)S(1)} %get-tuple-element.58.refs_2_.refs_0_, f32[1,1024]{1,0:T(1,128)S(1)} %collective-permute-done.5.refs_1_, f32[520,128]{1,0:T(8,128)S(1)} %get-tuple-element.49.refs_2_, f32[520,128]{1,0:T(8,128)S(1)} %collective-permute-done.1.refs_3_, ...), custom_call_target="tpu_custom_call" | custom-call | tf_op jit(solution)/shard_map/rows/pallas_call | solution.py:247
  28.8 1.9 %collective-permute-start.9 = (f32[1,1024]{1,0:T(1,128)S(1)}, f32[1,1024]{1,0:T(1,128)S(1)}, u32[]{:S(2)}, u32[]{:S(2)}) collective-permute-start(f32[1,1024]{1,0:T(1,128)S(1)} %get-tuple-element.61.refs_2_.refs_0_), channel_id=1, source_target_pairs={{0,6},{1,7},{2,4},{3,5},{4,2},{5,3},{6,0},{7,1},{8,14},{9,15},{10,... | collective-permute-start | bytes 12296 | tf_op jit(solution)/shard_map/ppermute | solution.py:369
  30.6 0.0 collective-permute-start.8
  30.6 1.7 %collective-permute-start.7 = (f32[1,1024]{1,0:T(1,128)S(1)}, f32[1,1024]{1,0:T(1,128)S(1)}, u32[]{:S(2)}, u32[]{:S(2)}) collective-permute-start(f32[1,1024]{1,0:T(1,128)S(1)} %get-tuple-element.61.refs_2_.refs_0_), channel_id=1, source_target_pairs={{0,2},{1,3},{2,0},{3,1},{4,6},{5,7},{6,4},{7,5},{8,10},{9,11},{10,... | collective-permute-start | bytes 12296 | tf_op jit(solution)/shard_map/ppermute | solution.py:369
  32.3 2.2 %tables.13 = (bf16[32,128,128]{2,1,0:T(8,128)(2,1)S(1)}, bf16[32,128,128]{2,1,0:T(8,128)(2,1)S(1)}, f32[8,128]{1,0:T(8,128)S(1)}) custom-call(f32[32,128]{1,0:T(8,128)S(1)} %get-tuple-element.50.refs_0_.refs_2_, f32[768,128]{1,0:T(8,128)S(1)} %collective-permute-done.6.refs_1_, f32[1,1024]{1,0:T(1,128)S(1)} %get-tuple-element.61.refs_2_.refs_0_), custom_call_target="tpu_custom_call" | custom-call | flops 268435456 | bytes 7680000 | tf_op jit(solution)/shard_map/tables/pallas_call | solution.py:295
  34.5 1.2 %tables.14 = (bf16[32,64,128]{2,1,0:T(8,128)(2,1)S(1)}, bf16[32,64,128]{2,1,0:T(8,128)(2,1)S(1)}, f32[8,128]{1,0:T(8,128)S(1)}) custom-call(f32[32,128]{1,0:T(8,128)S(1)} %get-tuple-element.50.refs_0_.refs_2_, f32[768,128]{1,0:T(8,128)S(1)} %collective-permute-done.6.refs_1_, f32[8,128]{1,0:T(8,128)S(1)} %get-tuple-element.62.refs_2_), custom_call_target="tpu_custom_call" | custom-call | flops 134217728 | bytes 3840000 | tf_op jit(solution)/shard_map/tables/pallas_call | solution.py:295
  35.8 0.0 collective-permute-done.9.refs_3_
  35.8 0.0 collective-permute-done.8.refs_2_
  35.8 0.0 collective-permute-done.7.refs_1_
  35.8 0.4 cols.3
  36.2 0.9 %collective-permute-start.10 = (f32[1,1024]{1,0:T(1,128)S(1)}, f32[1,1024]{1,0:T(1,128)S(1)}, u32[]{:S(2)}, u32[]{:S(2)}) collective-permute-start(f32[1,1024]{1,0:T(1,128)S(1)} %get-tuple-element.65.refs_2_.refs_0_), channel_id=1, source_target_pairs={{0,8},{8,0},{16,24},{24,16},{1,9},{9,1},{17,25},{25,17},{2,10},{10... | collective-permute-start | bytes 12296 | tf_op jit(solution)/shard_map/ppermute | solution.py:369
  37.1 0.0 collective-permute-done.11.refs_1_
  37.1 1.5 %tables.15 = (bf16[32,64,128]{2,1,0:T(8,128)(2,1)S(1)}, bf16[32,64,128]{2,1,0:T(8,128)(2,1)S(1)}, f32[8,128]{1,0:T(8,128)S(1)}) custom-call(f32[32,128]{1,0:T(8,128)S(1)} %get-tuple-element.50.refs_0_.refs_2_, f32[768,128]{1,0:T(8,128)S(1)} %collective-permute-done.11.refs_1_, f32[1,1024]{1,0:T(1,128)S(1)} %get-tuple-element.65.refs_2_.refs_0_), custom_call_target="tpu_custom_call" | custom-call | flops 134217728 | bytes 3840000 | tf_op jit(solution)/shard_map/tables/pallas_call | solution.py:295
  38.5 0.0 collective-permute-done.10.refs_1_
  38.5 0.9 %rows.3 = (f32[1,512]{1,0:T(1,128)}, f32[1,1024]{1,0:T(1,128)S(1)}) custom-call(f32[1,1024]{1,0:T(1,128)S(1)} %get-tuple-element.65.refs_2_.refs_0_, f32[1,1024]{1,0:T(1,128)S(1)} %collective-permute-done.10.refs_1_, f32[520,128]{1,0:T(8,128)S(1)} %get-tuple-element.49.refs_2_, f32[520,128]{1,0:T(8,128)S(1)} %collective-permute-done.1.refs_3_, ...), custom_call_target="tpu_custom_call" | custom-call | tf_op jit(solution)/shard_map/rows/pallas_call | solution.py:247
  39.4 1.9 %collective-permute-start.14 = (f32[1,1024]{1,0:T(1,128)S(1)}, f32[1,1024]{1,0:T(1,128)S(1)}, u32[]{:S(2)}, u32[]{:S(2)}) collective-permute-start(f32[1,1024]{1,0:T(1,128)S(1)} %get-tuple-element.68.refs_2_.refs_1_), channel_id=1, source_target_pairs={{0,6},{1,7},{2,4},{3,5},{4,2},{5,3},{6,0},{7,1},{8,14},{9,15},{10,... | collective-permute-start | bytes 12296 | tf_op jit(solution)/shard_map/ppermute | solution.py:369
  41.3 0.0 collective-permute-start.13
  41.3 1.7 %collective-permute-start.12 = (f32[1,1024]{1,0:T(1,128)S(1)}, f32[1,1024]{1,0:T(1,128)S(1)}, u32[]{:S(2)}, u32[]{:S(2)}) collective-permute-start(f32[1,1024]{1,0:T(1,128)S(1)} %get-tuple-element.68.refs_2_.refs_1_), channel_id=1, source_target_pairs={{0,2},{1,3},{2,0},{3,1},{4,6},{5,7},{6,4},{7,5},{8,10},{9,11},{10,... | collective-permute-start | bytes 12296 | tf_op jit(solution)/shard_map/ppermute | solution.py:369
  43.0 2.2 %tables.16 = (bf16[32,128,128]{2,1,0:T(8,128)(2,1)S(1)}, bf16[32,128,128]{2,1,0:T(8,128)(2,1)S(1)}, f32[8,128]{1,0:T(8,128)S(1)}) custom-call(f32[32,128]{1,0:T(8,128)S(1)} %get-tuple-element.50.refs_0_.refs_2_, f32[768,128]{1,0:T(8,128)S(1)} %collective-permute-done.11.refs_1_, f32[1,1024]{1,0:T(1,128)S(1)} %get-tuple-element.68.refs_2_.refs_1_), custom_call_target="tpu_custom_call" | custom-call | flops 268435456 | bytes 7680000 | tf_op jit(solution)/shard_map/tables/pallas_call | solution.py:295
  45.2 1.3 %tables.17 = (bf16[32,64,128]{2,1,0:T(8,128)(2,1)S(1)}, bf16[32,64,128]{2,1,0:T(8,128)(2,1)S(1)}, f32[8,128]{1,0:T(8,128)S(1)}) custom-call(f32[32,128]{1,0:T(8,128)S(1)} %get-tuple-element.50.refs_0_.refs_2_, f32[768,128]{1,0:T(8,128)S(1)} %collective-permute-done.11.refs_1_, f32[8,128]{1,0:T(8,128)S(1)} %get-tuple-element.85.refs_2_), custom_call_target="tpu_custom_call" | custom-call | flops 134217728 | bytes 3840000 | tf_op jit(solution)/shard_map/tables/pallas_call | solution.py:295
  46.4 0.0 collective-permute-done.14.refs_4_
  46.5 0.0 collective-permute-done.13.refs_3_
  46.5 0.0 collective-permute-done.12.refs_2_
  46.5 2.0 %spread.2 = (f32[16,32,128]{2,1,0:T(8,128)S(1)}, f32[1,512]{1,0:T(1,128)}) custom-call(f32[1,1024]{1,0:T(1,128)S(1)} %get-tuple-element.64.refs_0_, f32[1,1024]{1,0:T(1,128)S(1)} %get-tuple-element.68.refs_2_.refs_1_, f32[1,1024]{1,0:T(1,128)S(1)} %collective-permute-done.12.refs_2_, f32[1,1024]{1,0:T(1,128)S(1)} %collective-permute-done.13.refs_3_, ...), custom_call_target="tpu_custom_call" | custom-call | tf_op jit(solution)/shard_map/spread/pallas_call | solution.py:336
  48.5 0.9 %collective-permute-start.15 = (f32[16,32,128]{2,1,0:T(8,128)S(1)}, f32[16,32,128]{2,1,0:T(8,128)S(1)}, u32[]{:S(2)}, u32[]{:S(2)}) collective-permute-start(f32[16,32,128]{2,1,0:T(8,128)S(1)} %get-tuple-element.92), channel_id=1, source_target_pairs={{0,8},{8,0},{16,24},{24,16},{1,9},{9,1},{17,25},{25,17},{2,10},{10... | collective-permute-start | bytes 786440 | tf_op jit(solution)/shard_map/ppermute | solution.py:369
  49.3 2.0 %spread.3 = (f32[16,32,128]{2,1,0:T(8,128)S(1)}, f32[1,512]{1,0:T(1,128)}) custom-call(f32[1,1024]{1,0:T(1,128)S(1)} %get-tuple-element.64.refs_0_, f32[1,1024]{1,0:T(1,128)S(1)} %get-tuple-element.68.refs_2_.refs_1_, f32[1,1024]{1,0:T(1,128)S(1)} %collective-permute-done.12.refs_2_, f32[1,1024]{1,0:T(1,128)S(1)} %collective-permute-done.13.refs_3_, ...), custom_call_target="tpu_custom_call" | custom-call | tf_op jit(solution)/shard_map/spread/pallas_call | solution.py:336
  51.3 0.0 collective-permute-done.15.b_ref
  51.3 0.7 %last.1 = f32[16,32,128]{2,1,0:T(8,128)} custom-call(f32[16,32,128]{2,1,0:T(8,128)S(1)} %get-tuple-element.91.a_ref, f32[16,32,128]{2,1,0:T(8,128)S(1)} %collective-permute-done.15.b_ref), custom_call_target="tpu_custom_call" | custom-call | tf_op jit(solution)/shard_map/last/pallas_call | solution.py:353
Async XLA Ops:
  0.6 12.0 %copy-start = (f32[32,32]{1,0:T(8,128)S(1)}, f32[32,32]{1,0:T(8,128)}, u32[]{:S(2)}) copy-start(f32[32,32]{1,0:T(8,128)} %refs_4_.1) | copy-start | bytes 12292
  2.1 10.2 %collective-permute-start = (f32[524,128]{1,0:T(8,128)S(1)}, f32[524,128]{1,0:T(8,128)S(1)}, u32[]{:S(2)}, u32[]{:S(2)}) collective-permute-start(f32[524,128]{1,0:T(8,128)S(1)} %get-tuple-element.48.refs_0_.refs_4_.refs_5_), channel_id=1, source_target_pairs={{0,16},{8,24},{16,0},{24,8},{1,17},{9,25},{17,1},{25,9},{2,18},{10... | collective-permute-start | bytes 804872 | tf_op jit(solution)/shard_map/ppermute | solution.py:369
  4.3 8.1 %collective-permute-start.1 = (f32[520,128]{1,0:T(8,128)S(1)}, f32[520,128]{1,0:T(8,128)S(1)}, u32[]{:S(2)}, u32[]{:S(2)}) collective-permute-start(f32[520,128]{1,0:T(8,128)S(1)} %get-tuple-element.49.refs_2_), channel_id=1, source_target_pairs={{0,1},{1,0},{2,3},{3,2},{4,5},{5,4},{6,7},{7,6},{8,9},{9,8},{10,11... | collective-permute-start | bytes 798728 | tf_op jit(solution)/shard_map/ppermute | solution.py:369
  12.4 14.3 %collective-permute-start.6 = (f32[768,128]{1,0:T(8,128)S(1)}, f32[768,128]{1,0:T(8,128)S(1)}, u32[]{:S(2)}, u32[]{:S(2)}) collective-permute-start(f32[768,128]{1,0:T(8,128)S(1)} %get-tuple-element.59.refs_1_), channel_id=1, source_target_pairs={{0,16},{8,24},{16,0},{24,8},{1,17},{9,25},{17,1},{25,9},{2,18},{10... | collective-permute-start | bytes 1179656 | tf_op jit(solution)/shard_map/ppermute | solution.py:369
  14.5 6.0 %collective-permute-start.4 = (f32[1,1024]{1,0:T(1,128)S(1)}, f32[1,1024]{1,0:T(1,128)S(1)}, u32[]{:S(2)}, u32[]{:S(2)}) collective-permute-start(f32[1,1024]{1,0:T(1,128)S(1)} %get-tuple-element.55.refs_2_.refs_0_), channel_id=1, source_target_pairs={{0,6},{1,7},{2,4},{3,5},{4,2},{5,3},{6,0},{7,1},{8,14},{9,15},{10,... | collective-permute-start | bytes 12296 | tf_op jit(solution)/shard_map/ppermute | solution.py:369
  17.9 3.4 %collective-permute-start.3 = (f32[1,1024]{1,0:T(1,128)S(1)}, f32[1,1024]{1,0:T(1,128)S(1)}, u32[]{:S(2)}, u32[]{:S(2)}) collective-permute-start(f32[1,1024]{1,0:T(1,128)S(1)} %get-tuple-element.55.refs_2_.refs_0_), channel_id=1, source_target_pairs={{0,4},{1,5},{2,6},{3,7},{4,0},{5,1},{6,2},{7,3},{8,12},{9,13},{10,... | collective-permute-start | bytes 12296 | tf_op jit(solution)/shard_map/ppermute | solution.py:369
  17.9 3.4 %collective-permute-start.2 = (f32[1,1024]{1,0:T(1,128)S(1)}, f32[1,1024]{1,0:T(1,128)S(1)}, u32[]{:S(2)}, u32[]{:S(2)}) collective-permute-start(f32[1,1024]{1,0:T(1,128)S(1)} %get-tuple-element.55.refs_2_.refs_0_), channel_id=1, source_target_pairs={{0,2},{1,3},{2,0},{3,1},{4,6},{5,7},{6,4},{7,5},{8,10},{9,11},{10,... | collective-permute-start | bytes 12296 | tf_op jit(solution)/shard_map/ppermute | solution.py:369
  22.2 14.9 %collective-permute-start.11 = (f32[768,128]{1,0:T(8,128)S(1)}, f32[768,128]{1,0:T(8,128)S(1)}, u32[]{:S(2)}, u32[]{:S(2)}) collective-permute-start(f32[768,128]{1,0:T(8,128)S(1)} %get-tuple-element.66.refs_1_), channel_id=1, source_target_pairs={{0,16},{8,24},{16,0},{24,8},{1,17},{9,25},{17,1},{25,9},{2,18},{10... | collective-permute-start | bytes 1179656 | tf_op jit(solution)/shard_map/ppermute | solution.py:369
  23.4 4.5 %collective-permute-start.5 = (f32[1,1024]{1,0:T(1,128)S(1)}, f32[1,1024]{1,0:T(1,128)S(1)}, u32[]{:S(2)}, u32[]{:S(2)}) collective-permute-start(f32[1,1024]{1,0:T(1,128)S(1)} %get-tuple-element.58.refs_2_.refs_0_), channel_id=1, source_target_pairs={{0,8},{8,0},{16,24},{24,16},{1,9},{9,1},{17,25},{25,17},{2,10},{10... | collective-permute-start | bytes 12296 | tf_op jit(solution)/shard_map/ppermute | solution.py:369
  28.8 7.0 %collective-permute-start.9 = (f32[1,1024]{1,0:T(1,128)S(1)}, f32[1,1024]{1,0:T(1,128)S(1)}, u32[]{:S(2)}, u32[]{:S(2)}) collective-permute-start(f32[1,1024]{1,0:T(1,128)S(1)} %get-tuple-element.61.refs_2_.refs_0_), channel_id=1, source_target_pairs={{0,6},{1,7},{2,4},{3,5},{4,2},{5,3},{6,0},{7,1},{8,14},{9,15},{10,... | collective-permute-start | bytes 12296 | tf_op jit(solution)/shard_map/ppermute | solution.py:369
  30.6 5.1 %collective-permute-start.8 = (f32[1,1024]{1,0:T(1,128)S(1)}, f32[1,1024]{1,0:T(1,128)S(1)}, u32[]{:S(2)}, u32[]{:S(2)}) collective-permute-start(f32[1,1024]{1,0:T(1,128)S(1)} %get-tuple-element.61.refs_2_.refs_0_), channel_id=1, source_target_pairs={{0,4},{1,5},{2,6},{3,7},{4,0},{5,1},{6,2},{7,3},{8,12},{9,13},{10,... | collective-permute-start | bytes 12296 | tf_op jit(solution)/shard_map/ppermute | solution.py:369
  30.6 5.1 %collective-permute-start.7 = (f32[1,1024]{1,0:T(1,128)S(1)}, f32[1,1024]{1,0:T(1,128)S(1)}, u32[]{:S(2)}, u32[]{:S(2)}) collective-permute-start(f32[1,1024]{1,0:T(1,128)S(1)} %get-tuple-element.61.refs_2_.refs_0_), channel_id=1, source_target_pairs={{0,2},{1,3},{2,0},{3,1},{4,6},{5,7},{6,4},{7,5},{8,10},{9,11},{10,... | collective-permute-start | bytes 12296 | tf_op jit(solution)/shard_map/ppermute | solution.py:369
  36.2 2.4 %collective-permute-start.10 = (f32[1,1024]{1,0:T(1,128)S(1)}, f32[1,1024]{1,0:T(1,128)S(1)}, u32[]{:S(2)}, u32[]{:S(2)}) collective-permute-start(f32[1,1024]{1,0:T(1,128)S(1)} %get-tuple-element.65.refs_2_.refs_0_), channel_id=1, source_target_pairs={{0,8},{8,0},{16,24},{24,16},{1,9},{9,1},{17,25},{25,17},{2,10},{10... | collective-permute-start | bytes 12296 | tf_op jit(solution)/shard_map/ppermute | solution.py:369
  39.4 7.0 %collective-permute-start.14 = (f32[1,1024]{1,0:T(1,128)S(1)}, f32[1,1024]{1,0:T(1,128)S(1)}, u32[]{:S(2)}, u32[]{:S(2)}) collective-permute-start(f32[1,1024]{1,0:T(1,128)S(1)} %get-tuple-element.68.refs_2_.refs_1_), channel_id=1, source_target_pairs={{0,6},{1,7},{2,4},{3,5},{4,2},{5,3},{6,0},{7,1},{8,14},{9,15},{10,... | collective-permute-start | bytes 12296 | tf_op jit(solution)/shard_map/ppermute | solution.py:369
  41.3 5.2 %collective-permute-start.13 = (f32[1,1024]{1,0:T(1,128)S(1)}, f32[1,1024]{1,0:T(1,128)S(1)}, u32[]{:S(2)}, u32[]{:S(2)}) collective-permute-start(f32[1,1024]{1,0:T(1,128)S(1)} %get-tuple-element.68.refs_2_.refs_1_), channel_id=1, source_target_pairs={{0,4},{1,5},{2,6},{3,7},{4,0},{5,1},{6,2},{7,3},{8,12},{9,13},{10,... | collective-permute-start | bytes 12296 | tf_op jit(solution)/shard_map/ppermute | solution.py:369
  41.3 5.2 %collective-permute-start.12 = (f32[1,1024]{1,0:T(1,128)S(1)}, f32[1,1024]{1,0:T(1,128)S(1)}, u32[]{:S(2)}, u32[]{:S(2)}) collective-permute-start(f32[1,1024]{1,0:T(1,128)S(1)} %get-tuple-element.68.refs_2_.refs_1_), channel_id=1, source_target_pairs={{0,2},{1,3},{2,0},{3,1},{4,6},{5,7},{6,4},{7,5},{8,10},{9,11},{10,... | collective-permute-start | bytes 12296 | tf_op jit(solution)/shard_map/ppermute | solution.py:369
  48.5 2.8 %collective-permute-start.15 = (f32[16,32,128]{2,1,0:T(8,128)S(1)}, f32[16,32,128]{2,1,0:T(8,128)S(1)}, u32[]{:S(2)}, u32[]{:S(2)}) collective-permute-start(f32[16,32,128]{2,1,0:T(8,128)S(1)} %get-tuple-element.92), channel_id=1, source_target_pairs={{0,8},{8,0},{16,24},{24,16},{1,9},{9,1},{17,25},{25,17},{2,10},{10... | collective-permute-start | bytes 786440 | tf_op jit(solution)/shard_map/ppermute | solution.py:369

commit v10 on v9

--- a/solution.py
+++ b/solution.py
@@ -117,23 +117,70 @@
     return copies
 
 
-def first_body(
-    x_hbm, y_hbm, rr_hbm, seg_hbm, mass_hbm, cr_hbm, cm_hbm, f_hbm, m_hbm, d_hbm, a_hbm,
-    xpack_ref, ypack_ref, early_ref, late_ref, f_ref, xb_ref, yb_ref, rr_ref, seg_ref, cr_ref, m_ref, d_ref, sems,
+def packs_body(
+    x_hbm, y_hbm, rr_hbm, seg_hbm, mass_hbm, cr_hbm, cm_hbm,
+    xpack_ref, ypack_ref, xb_ref, yb_ref, rr_ref, seg_ref, cr_ref, sems,
 ):
-    me = lax.axis_index("cohort")
     n, m = xb_ref.shape[0], yb_ref.shape[0]
     p, q = n // LANES, m // LANES
-    e = early_ref.shape[0] // 3
     copies = run_copies(
         (
             (x_hbm, xb_ref),
+            (y_hbm, yb_ref),
             (rr_hbm, rr_ref),
             (seg_hbm, seg_ref),
             (mass_hbm, xpack_ref.at[pl.ds(n + 2 * p, p), :]),
-            (y_hbm, yb_ref),
             (cr_hbm, cr_ref),
             (cm_hbm, ypack_ref.at[pl.ds(m + q, q), :]),
+        ),
+        sems,
+    )
+    for copy in copies:
+        copy.wait()
+    xpack_ref[0:n, :] = xb_ref[...].astype(f32)
+    xpack_ref[n : n + p, :] = rr_ref[...].astype(f32)
+    xpack_ref[n + p : n + 2 * p, :] = seg_ref[...].astype(f32)
+    ypack_ref[0:m, :] = yb_ref[...].astype(f32)
+    ypack_ref[m : m + q, :] = cr_ref[...].astype(f32)
+
+
+def hbm_call(body, name, args, out, scratch):
+    return pl.pallas_call(
+        body,
+        in_specs=[HBM] * len(args),
+        out_specs=[VMEM] * len(out),
+        out_shape=[pltpu.VMEM(shape, f32) for shape in out],
+        scratch_shapes=[*scratch, pltpu.SemaphoreType.DMA((len(args) + 1,))],
+        compiler_params=PARAMS,
+        name=name,
+    )(*[pltpu.with_memory_space_constraint(arg, pltpu.HBM) for arg in args])
+
+
+def packs_call(x, y, rr, seg, mass, cr, cm):
+    n, m = x.shape[0], y.shape[0]
+    p, q = n // LANES, m // LANES
+    block = lambda v: v.reshape(-1, LANES)
+    i32 = jnp.int32
+    return hbm_call(
+        packs_body,
+        "packs",
+        (x, y, block(rr), block(seg), block(mass), block(cr), block(cm)),
+        [(n + 3 * p, LANES), (m + 2 * q, LANES)],
+        [
+            pltpu.VMEM(x.shape, bf16),
+            pltpu.VMEM(y.shape, bf16),
+            pltpu.VMEM((p, LANES), i32),
+            pltpu.VMEM((p, LANES), i32),
+            pltpu.VMEM((q, LANES), i32),
+        ],
+    )
+
+
+def records_body(f_hbm, m_hbm, d_hbm, a_hbm, early_ref, late_ref, f_ref, m_ref, d_ref, sems):
+    me = lax.axis_index("cohort")
+    e, n = early_ref.shape[0] // 3, m_ref.shape[0]
+    copies = run_copies(
+        (
             (m_hbm, m_ref),
             (d_hbm, d_ref),
             (a_hbm.at[pl.ds(0, e), :], early_ref.at[pl.ds(2 * e, e), :]),
@@ -144,42 +191,21 @@
     )
     for copy in copies:
         copy.wait()
-    xpack_ref[0:n, :] = xb_ref[...].astype(f32)
-    xpack_ref[n : n + p, :] = rr_ref[...].astype(f32)
-    xpack_ref[n + p : n + 2 * p, :] = seg_ref[...].astype(f32)
-    ypack_ref[0:m, :] = yb_ref[...].astype(f32)
-    ypack_ref[m : m + q, :] = cr_ref[...].astype(f32)
     for pack, rows in ((early_ref, slice(0, e)), (late_ref, slice(e, n))):
         size = rows.stop - rows.start
         pack[0:size, :] = m_ref[rows, :].astype(f32)
         pack[size : 2 * size, :] = d_ref[rows, :].astype(f32)
 
 
-def first_call(x, y, rr, seg, mass, cr, cm, table, records, early):
-    n, m = x.shape[0], y.shape[0]
-    p, q = n // LANES, m // LANES
-    block = lambda v: v.reshape(-1, LANES)
-    i32 = jnp.int32
-    out = [(n + 3 * p, LANES), (m + 2 * q, LANES), (3 * early, LANES), (3 * (n - early), LANES), table.shape[1:]]
-    args = (x, y, block(rr), block(seg), block(mass), block(cr), block(cm), table, *records)
-    return pl.pallas_call(
-        first_body,
-        in_specs=[HBM] * len(args),
-        out_specs=[VMEM] * len(out),
-        out_shape=[pltpu.VMEM(shape, f32) for shape in out],
-        scratch_shapes=[
-            pltpu.VMEM(x.shape, bf16),
-            pltpu.VMEM(y.shape, bf16),
-            pltpu.VMEM((p, LANES), i32),
-            pltpu.VMEM((p, LANES), i32),
-            pltpu.VMEM((q, LANES), i32),
-            pltpu.VMEM((n, LANES), i32),
-            pltpu.VMEM((n, LANES), i32),
-            pltpu.SemaphoreType.DMA((len(args) + 1,)),
-        ],
-        compiler_params=PARAMS,
-        name="first",
-    )(*[pltpu.with_memory_space_constraint(arg, pltpu.HBM) for arg in args])
+def records_call(table, merchants, days, amounts, early):
+    n = merchants.shape[0]
+    return hbm_call(
+        records_body,
+        "records",
+        (table, merchants, days, amounts),
+        [(3 * early, LANES), (3 * (n - early), LANES), table.shape[1:]],
+        [pltpu.VMEM((n, LANES), jnp.int32), pltpu.VMEM((n, LANES), jnp.int32)],
+    )
 
 
 def flat(block):
@@ -339,25 +365,27 @@
         ),
         in_specs=[VMEM] * len(args) + [ANY] * len(after),
         out_specs=[VMEM] * 2,
-        out_shape=[pltpu.VMEM((t_count, SEG, LANES), f32), jax.ShapeDtypeStruct((1, n), f32)],
+        out_shape=[pltpu.VMEM((t_count, SEG, LANES), f32), pltpu.VMEM((1, n), f32)],
         compiler_params=PARAMS,
         name="spread",
     )(*args, *after)
 
 
-def add_body(a_ref, b_ref, o_ref):
+def last_body(a_ref, b_ref, w_ref, v_ref, o_ref, w_out, v_out):
     o_ref[...] = a_ref[...] + b_ref[...]
-
-
-def add_call(a, b):
+    w_out[...] = w_ref[...]
+    v_out[...] = v_ref[...]
+
+
+def last_call(a, b, w, v):
     return pl.pallas_call(
-        add_body,
-        in_specs=[VMEM] * 2,
-        out_specs=VMEM,
-        out_shape=jax.ShapeDtypeStruct(a.shape, f32),
+        last_body,
+        in_specs=[VMEM] * 4,
+        out_specs=[VMEM] * 3,
+        out_shape=[jax.ShapeDtypeStruct(x.shape, f32) for x in (a, w, v)],
         compiler_params=PARAMS,
         name="last",
-    )(a, b)
+    )(a, b, w, v)
 
 
 def move(x, axis, size, pair, step, flip):
@@ -405,10 +433,10 @@
 
     unit = n // 8
     ahead = 4
-    xpack, ypack, *own, filt = first_call(
-        cohort_features, cell_features, cohort_region, cohort_segment, cohort_mass, cell_region, cell_mass,
-        jnp.asarray(table), (spend_merchant, spend_day, spend_amount), ahead * unit,
-    )
+    xpack, ypack = packs_call(
+        cohort_features, cell_features, cohort_region, cohort_segment, cohort_mass, cell_region, cell_mass
+    )
+    *own, filt = records_call(jnp.asarray(table), spend_merchant, spend_day, spend_amount, ahead * unit)
     xpacks = [xpack] + over_y(xpack)
     ypacks = [ypack, move(ypack, "cell", n_cell, 2, 0, 1)]
     pairs = {}
@@ -447,14 +475,14 @@
         after = others(*fills[iteration][0], column)
         cell_scale, partial = half_step(
             rows_body, "rows", m, [column, sibling], ypacks, kernel,
-            [jax.ShapeDtypeStruct((1, m), f32), row_sums], after,
+            [pltpu.VMEM((1, m), f32), row_sums], after,
         )
         lines = along_z(partial)
         after = others(*fills[iteration][1], partial)
     ordered = [pairs[key] for key in sorted(pairs)]
     away, weights = spread_call(n, cohort_scale, lines, xpacks, ordered, 0, t_dev, after)
     mine, _ = spread_call(n, cohort_scale, lines, xpacks, ordered, t_dev, t_dev, after)
-    out = add_call(mine, core(away))
+    out, weights, cell_scale = last_call(mine, core(away), weights, cell_scale)
     return (weights.reshape(-1), cell_scale.reshape(-1), out)
 
 

time: 52.2 us -> 52.1 us (level)
    pallas_call x2 -> x3, Pallas kernels: 2.23 us -> 3.02 us  [the longest x2 2.27 us: hbm_call(): pl.pallas_call(body, in_specs=[HBM] * len(args), out_specs=[VMEM] * len(o...]
  transfers between devices with their start and end apart: 16 -> 16, of which waited for: 1 -> 1; matrix products, arithmetic and copies ran while one was open for 0% -> 0% of each run, Pallas kernels for 47% -> 50%
where the time goes in v10:
time: 52.1 us; the launch traced here: 52 us
  Pallas kernels  29.6 us (57%)
  starting transfers between devices  20.8 us (40%)
  between operations  0.84 us (2%)
  waiting for transfers between devices  0.77 us (1%)
    ppermute x16, starting transfers between devices, move(): lax.ppermute(x, axis, [(b * pair + r, away(b) * pair + (r ^ flip)) for b...  20.8 us
    pallas_call x9, Pallas kernels, table_call(): pl.pallas_call(lambda *refs: table_body(n, first, count, *refs[:2], *refs...  18.7 us
    pallas_call x2, Pallas kernels, spread_call(): pl.pallas_call(lambda *refs: spread_body(n, t_first, t_count, len(partial...  3.52 us
    pallas_call x4, Pallas kernels, half_step(): pl.pallas_call(lambda *refs: body(size, len(partials), len(packs), *refs[...  2.56 us
    pallas_call x2, Pallas kernels, hbm_call(): pl.pallas_call(body, in_specs=[HBM] * len(args), out_specs=[VMEM] * len(o...  2.27 us
    pallas_call x1, Pallas kernels, gibbs_call(): pl.pallas_call(lambda *refs: gibbs_body(n, m, len(xpacks), len(ypacks), *...  1.78 us
  transfers between devices with their start and end apart: 16, of which 1 were waited for; matrix products, arithmetic and copies ran while one was open for 0% of the time, Pallas kernels for 50%

profile of v10, /device:TPU:1, one launch (start us, length us, event | category | flops | bytes accessed | tf_op | source)
XLA Modules:
  0.0 52.0 jit_solution(3069230842984410553)
XLA Ops:
  0.6 0.0 copy-start
  0.6 1.1 %packs.1 = (f32[524,128]{1,0:T(8,128)S(1)}, f32[520,128]{1,0:T(8,128)S(1)}) custom-call(bf16[512,128]{1,0:T(8,128)(2,1)} %x_hbm.1, bf16[512,128]{1,0:T(8,128)(2,1)} %y_hbm.1, s32[4,128]{1,0:T(4,128)} %bitcast.7, s32[4,128]{1,0:T(4,128)} %bitcast.8, f32[4,128]{1,0:T(4,128)} %bitcast.9, s32[4,128]{1,0:T(4,128)} %bitcast.10, f32[4,128]{1,0:T(4,128)} %bitcast.11), custom_call_target="tpu_custom_call" | custom-call | tf_op jit(solution)/shard_map/packs/pallas_call | solution.py:148
  1.7 2.1 %collective-permute-start = (f32[524,128]{1,0:T(8,128)S(1)}, f32[524,128]{1,0:T(8,128)S(1)}, u32[]{:S(2)}, u32[]{:S(2)}) collective-permute-start(f32[524,128]{1,0:T(8,128)S(1)} %get-tuple-element.51.refs_0_.refs_4_.refs_5_), channel_id=1, source_target_pairs={{0,16},{8,24},{16,0},{24,8},{1,17},{9,25},{17,1},{25,9},{2,18},{10... | collective-permute-start | bytes 804872 | tf_op jit(solution)/shard_map/ppermute | solution.py:397
  3.9 1.2 %collective-permute-start.1 = (f32[520,128]{1,0:T(8,128)S(1)}, f32[520,128]{1,0:T(8,128)S(1)}, u32[]{:S(2)}, u32[]{:S(2)}) collective-permute-start(f32[520,128]{1,0:T(8,128)S(1)} %get-tuple-element.52.refs_2_), channel_id=1, source_target_pairs={{0,1},{1,0},{2,3},{3,2},{4,5},{5,4},{6,7},{7,6},{8,9},{9,8},{10,11... | collective-permute-start | bytes 798728 | tf_op jit(solution)/shard_map/ppermute | solution.py:397
  5.1 1.2 %records.1 = (f32[768,128]{1,0:T(8,128)S(1)}, f32[768,128]{1,0:T(8,128)S(1)}, f32[32,128]{1,0:T(8,128)S(1)}) custom-call(f32[4,32,128]{2,1,0:T(8,128)} %constant.2.clone.f_hbm, s32[512,128]{1,0:T(8,128)} %m_hbm.1, s32[512,128]{1,0:T(8,128)} %d_hbm.1, f32[512,128]{1,0:T(8,128)} %a_hbm.1), custom_call_target="tpu_custom_call" | custom-call | tf_op jit(solution)/shard_map/records/pallas_call | solution.py:148
  6.3 4.7 %tables.9 = (bf16[32,256,128]{2,1,0:T(8,128)(2,1)S(1)}, bf16[32,256,128]{2,1,0:T(8,128)(2,1)S(1)}, f32[8,128]{1,0:T(8,128)S(1)}) custom-call(f32[32,128]{1,0:T(8,128)S(1)} %get-tuple-element.53.refs_0_.refs_2_, f32[768,128]{1,0:T(8,128)S(1)} %get-tuple-element.62.refs_1_, f32[32,128]{1,0:T(8,128)S(1)} %get-tuple-element.53.refs_0_.refs_2_), custom_call_target="tpu_custom_call" | custom-call | flops 536870912 | bytes 15360000 | tf_op jit(solution)/shard_map/tables/pallas_call | solution.py:321
  10.9 2.2 %tables.10 = (bf16[32,128,128]{2,1,0:T(8,128)(2,1)S(1)}, bf16[32,128,128]{2,1,0:T(8,128)(2,1)S(1)}, f32[8,128]{1,0:T(8,128)S(1)}) custom-call(f32[32,128]{1,0:T(8,128)S(1)} %get-tuple-element.53.refs_0_.refs_2_, f32[768,128]{1,0:T(8,128)S(1)} %get-tuple-element.69.refs_1_, f32[8,128]{1,0:T(8,128)S(1)} %get-tuple-element.56.refs_2_), custom_call_target="tpu_custom_call" | custom-call | flops 268435456 | bytes 7680000 | tf_op jit(solution)/shard_map/tables/pallas_call | solution.py:321
  13.1 0.0 collective-permute-done.1.refs_3_
  13.2 0.0 collective-permute-done.refs_1_.refs_5_.refs_6_
  13.2 0.3 collective-permute-start.6
  13.5 0.0 copy-done
  13.5 1.8 %gibbs.1 = (f32[1024,1024]{1,0:T(8,128)S(1)}, f32[1,1024]{1,0:T(1,128)S(1)}) custom-call(f32[524,128]{1,0:T(8,128)S(1)} %get-tuple-element.51.refs_0_.refs_4_.refs_5_, f32[524,128]{1,0:T(8,128)S(1)} %collective-permute-done.refs_1_.refs_5_.refs_6_, f32[520,128]{1,0:T(8,128)S(1)} %get-tuple-element.52.refs_2_, f32[520,128]{1,0:T(8,128)S(1)} %collective-permute-done.1.refs_3_, ...), custom_call_target="tpu_custom_call" | custom-call | flops 268435456 | bytes 4194304 | tf_op jit(solution)/shard_map/gibbs/pallas_call | solution.py:231
  15.2 3.4 %collective-permute-start.4 = (f32[1,1024]{1,0:T(1,128)S(1)}, f32[1,1024]{1,0:T(1,128)S(1)}, u32[]{:S(2)}, u32[]{:S(2)}) collective-permute-start(f32[1,1024]{1,0:T(1,128)S(1)} %get-tuple-element.58.refs_2_.refs_0_), channel_id=1, source_target_pairs={{0,6},{1,7},{2,4},{3,5},{4,2},{5,3},{6,0},{7,1},{8,14},{9,15},{10,... | collective-permute-start | bytes 12296 | tf_op jit(solution)/shard_map/ppermute | solution.py:397
  18.6 0.0 collective-permute-start.3
  18.6 0.4 collective-permute-start.2
  19.0 2.2 %tables.11 = (bf16[32,128,128]{2,1,0:T(8,128)(2,1)S(1)}, bf16[32,128,128]{2,1,0:T(8,128)(2,1)S(1)}, f32[8,128]{1,0:T(8,128)S(1)}) custom-call(f32[32,128]{1,0:T(8,128)S(1)} %get-tuple-element.53.refs_0_.refs_2_, f32[768,128]{1,0:T(8,128)S(1)} %get-tuple-element.69.refs_1_, f32[1,1024]{1,0:T(1,128)S(1)} %get-tuple-element.58.refs_2_.refs_0_), custom_call_target="tpu_custom_call" | custom-call | flops 268435456 | bytes 7680000 | tf_op jit(solution)/shard_map/tables/pallas_call | solution.py:321
  21.2 0.0 collective-permute-done.4.refs_3_
  21.2 0.7 %collective-permute-done.3.refs_2_ = f32[1,1024]{1,0:T(1,128)S(1)} collective-permute-done((f32[1,1024]{1,0:T(1,128)S(1)}, f32[1,1024]{1,0:T(1,128)S(1)}, u32[]{:S(2)}, u32[]{:S(2)}) %collective-permute-start.3) | collective-permute-done | bytes 4128 | tf_op jit(solution)/shard_map/ppermute | solution.py:397
  22.0 0.0 collective-permute-done.2.refs_1_
  22.0 1.0 %cols.2 = (f32[1,1024]{1,0:T(1,128)}, f32[1,1024]{1,0:T(1,128)S(1)}) custom-call(f32[1,1024]{1,0:T(1,128)S(1)} %get-tuple-element.58.refs_2_.refs_0_, f32[1,1024]{1,0:T(1,128)S(1)} %collective-permute-done.2.refs_1_, f32[1,1024]{1,0:T(1,128)S(1)} %collective-permute-done.3.refs_2_, f32[1,1024]{1,0:T(1,128)S(1)} %collective-permute-done.4.refs_3_, ...), custom_call_target="tpu_custom_call" | custom-call | tf_op jit(solution)/shard_map/cols/pallas_call | solution.py:273
  22.9 1.2 %collective-permute-start.11 = (f32[768,128]{1,0:T(8,128)S(1)}, f32[768,128]{1,0:T(8,128)S(1)}, u32[]{:S(2)}, u32[]{:S(2)}) collective-permute-start(f32[768,128]{1,0:T(8,128)S(1)} %get-tuple-element.69.refs_1_), channel_id=1, source_target_pairs={{0,16},{8,24},{16,0},{24,8},{1,17},{9,25},{17,1},{25,9},{2,18},{10... | collective-permute-start | bytes 1179656 | tf_op jit(solution)/shard_map/ppermute | solution.py:397
  24.2 3.2 %collective-permute-start.5 = (f32[1,1024]{1,0:T(1,128)S(1)}, f32[1,1024]{1,0:T(1,128)S(1)}, u32[]{:S(2)}, u32[]{:S(2)}) collective-permute-start(f32[1,1024]{1,0:T(1,128)S(1)} %get-tuple-element.61.refs_2_.refs_0_), channel_id=1, source_target_pairs={{0,8},{8,0},{16,24},{24,16},{1,9},{9,1},{17,25},{25,17},{2,10},{10... | collective-permute-start | bytes 12296 | tf_op jit(solution)/shard_map/ppermute | solution.py:397
  27.4 0.0 collective-permute-done.6.refs_1_
  27.4 1.2 %tables.12 = (bf16[32,64,128]{2,1,0:T(8,128)(2,1)S(1)}, bf16[32,64,128]{2,1,0:T(8,128)(2,1)S(1)}, f32[8,128]{1,0:T(8,128)S(1)}) custom-call(f32[32,128]{1,0:T(8,128)S(1)} %get-tuple-element.53.refs_0_.refs_2_, f32[768,128]{1,0:T(8,128)S(1)} %collective-permute-done.6.refs_1_, f32[1,1024]{1,0:T(1,128)S(1)} %get-tuple-element.61.refs_2_.refs_0_), custom_call_target="tpu_custom_call" | custom-call | flops 134217728 | bytes 3840000 | tf_op jit(solution)/shard_map/tables/pallas_call | solution.py:321
  28.7 0.0 collective-permute-done.5.refs_1_
  28.7 0.9 %rows.2 = (f32[1,512]{1,0:T(1,128)}, f32[1,1024]{1,0:T(1,128)S(1)}) custom-call(f32[1,1024]{1,0:T(1,128)S(1)} %get-tuple-element.61.refs_2_.refs_0_, f32[1,1024]{1,0:T(1,128)S(1)} %collective-permute-done.5.refs_1_, f32[520,128]{1,0:T(8,128)S(1)} %get-tuple-element.52.refs_2_, f32[520,128]{1,0:T(8,128)S(1)} %collective-permute-done.1.refs_3_, ...), custom_call_target="tpu_custom_call" | custom-call | tf_op jit(solution)/shard_map/rows/pallas_call | solution.py:273
  29.5 1.9 %collective-permute-start.9 = (f32[1,1024]{1,0:T(1,128)S(1)}, f32[1,1024]{1,0:T(1,128)S(1)}, u32[]{:S(2)}, u32[]{:S(2)}) collective-permute-start(f32[1,1024]{1,0:T(1,128)S(1)} %get-tuple-element.64.refs_2_.refs_0_), channel_id=1, source_target_pairs={{0,6},{1,7},{2,4},{3,5},{4,2},{5,3},{6,0},{7,1},{8,14},{9,15},{10,... | collective-permute-start | bytes 12296 | tf_op jit(solution)/shard_map/ppermute | solution.py:397
  31.4 0.0 collective-permute-start.8
  31.4 1.7 %collective-permute-start.7 = (f32[1,1024]{1,0:T(1,128)S(1)}, f32[1,1024]{1,0:T(1,128)S(1)}, u32[]{:S(2)}, u32[]{:S(2)}) collective-permute-start(f32[1,1024]{1,0:T(1,128)S(1)} %get-tuple-element.64.refs_2_.refs_0_), channel_id=1, source_target_pairs={{0,2},{1,3},{2,0},{3,1},{4,6},{5,7},{6,4},{7,5},{8,10},{9,11},{10,... | collective-permute-start | bytes 12296 | tf_op jit(solution)/shard_map/ppermute | solution.py:397
  33.1 2.2 %tables.13 = (bf16[32,128,128]{2,1,0:T(8,128)(2,1)S(1)}, bf16[32,128,128]{2,1,0:T(8,128)(2,1)S(1)}, f32[8,128]{1,0:T(8,128)S(1)}) custom-call(f32[32,128]{1,0:T(8,128)S(1)} %get-tuple-element.53.refs_0_.refs_2_, f32[768,128]{1,0:T(8,128)S(1)} %collective-permute-done.6.refs_1_, f32[1,1024]{1,0:T(1,128)S(1)} %get-tuple-element.64.refs_2_.refs_0_), custom_call_target="tpu_custom_call" | custom-call | flops 268435456 | bytes 7680000 | tf_op jit(solution)/shard_map/tables/pallas_call | solution.py:321
  35.3 1.2 %tables.14 = (bf16[32,64,128]{2,1,0:T(8,128)(2,1)S(1)}, bf16[32,64,128]{2,1,0:T(8,128)(2,1)S(1)}, f32[8,128]{1,0:T(8,128)S(1)}) custom-call(f32[32,128]{1,0:T(8,128)S(1)} %get-tuple-element.53.refs_0_.refs_2_, f32[768,128]{1,0:T(8,128)S(1)} %collective-permute-done.6.refs_1_, f32[8,128]{1,0:T(8,128)S(1)} %get-tuple-element.65.refs_2_), custom_call_target="tpu_custom_call" | custom-call | flops 134217728 | bytes 3840000 | tf_op jit(solution)/shard_map/tables/pallas_call | solution.py:321
  36.5 0.0 collective-permute-done.9.refs_3_
  36.6 0.0 collective-permute-done.8.refs_2_
  36.6 0.0 collective-permute-done.7.refs_1_
  36.6 0.4 cols.3
  36.9 0.9 %collective-permute-start.10 = (f32[1,1024]{1,0:T(1,128)S(1)}, f32[1,1024]{1,0:T(1,128)S(1)}, u32[]{:S(2)}, u32[]{:S(2)}) collective-permute-start(f32[1,1024]{1,0:T(1,128)S(1)} %get-tuple-element.68.refs_2_.refs_0_), channel_id=1, source_target_pairs={{0,8},{8,0},{16,24},{24,16},{1,9},{9,1},{17,25},{25,17},{2,10},{10... | collective-permute-start | bytes 12296 | tf_op jit(solution)/shard_map/ppermute | solution.py:397
  37.9 0.0 collective-permute-done.11.refs_1_
  37.9 1.5 %tables.15 = (bf16[32,64,128]{2,1,0:T(8,128)(2,1)S(1)}, bf16[32,64,128]{2,1,0:T(8,128)(2,1)S(1)}, f32[8,128]{1,0:T(8,128)S(1)}) custom-call(f32[32,128]{1,0:T(8,128)S(1)} %get-tuple-element.53.refs_0_.refs_2_, f32[768,128]{1,0:T(8,128)S(1)} %collective-permute-done.11.refs_1_, f32[1,1024]{1,0:T(1,128)S(1)} %get-tuple-element.68.refs_2_.refs_0_), custom_call_target="tpu_custom_call" | custom-call | flops 134217728 | bytes 3840000 | tf_op jit(solution)/shard_map/tables/pallas_call | solution.py:321
  39.3 0.0 collective-permute-done.10.refs_1_
  39.3 0.4 rows.3
  39.7 1.9 %collective-permute-start.14 = (f32[1,1024]{1,0:T(1,128)S(1)}, f32[1,1024]{1,0:T(1,128)S(1)}, u32[]{:S(2)}, u32[]{:S(2)}) collective-permute-start(f32[1,1024]{1,0:T(1,128)S(1)} %get-tuple-element.71.refs_2_.refs_1_), channel_id=1, source_target_pairs={{0,6},{1,7},{2,4},{3,5},{4,2},{5,3},{6,0},{7,1},{8,14},{9,15},{10,... | collective-permute-start | bytes 12296 | tf_op jit(solution)/shard_map/ppermute | solution.py:397
  41.6 0.0 collective-permute-start.13
  41.6 1.7 %collective-permute-start.12 = (f32[1,1024]{1,0:T(1,128)S(1)}, f32[1,1024]{1,0:T(1,128)S(1)}, u32[]{:S(2)}, u32[]{:S(2)}) collective-permute-start(f32[1,1024]{1,0:T(1,128)S(1)} %get-tuple-element.71.refs_2_.refs_1_), channel_id=1, source_target_pairs={{0,2},{1,3},{2,0},{3,1},{4,6},{5,7},{6,4},{7,5},{8,10},{9,11},{10,... | collective-permute-start | bytes 12296 | tf_op jit(solution)/shard_map/ppermute | solution.py:397
  43.3 2.2 %tables.16 = (bf16[32,128,128]{2,1,0:T(8,128)(2,1)S(1)}, bf16[32,128,128]{2,1,0:T(8,128)(2,1)S(1)}, f32[8,128]{1,0:T(8,128)S(1)}) custom-call(f32[32,128]{1,0:T(8,128)S(1)} %get-tuple-element.53.refs_0_.refs_2_, f32[768,128]{1,0:T(8,128)S(1)} %collective-permute-done.11.refs_1_, f32[1,1024]{1,0:T(1,128)S(1)} %get-tuple-element.71.refs_2_.refs_1_), custom_call_target="tpu_custom_call" | custom-call | flops 268435456 | bytes 7680000 | tf_op jit(solution)/shard_map/tables/pallas_call | solution.py:321
  45.5 1.3 %tables.17 = (bf16[32,64,128]{2,1,0:T(8,128)(2,1)S(1)}, bf16[32,64,128]{2,1,0:T(8,128)(2,1)S(1)}, f32[8,128]{1,0:T(8,128)S(1)}) custom-call(f32[32,128]{1,0:T(8,128)S(1)} %get-tuple-element.53.refs_0_.refs_2_, f32[768,128]{1,0:T(8,128)S(1)} %collective-permute-done.11.refs_1_, f32[8,128]{1,0:T(8,128)S(1)} %get-tuple-element.88.refs_2_), custom_call_target="tpu_custom_call" | custom-call | flops 134217728 | bytes 3840000 | tf_op jit(solution)/shard_map/tables/pallas_call | solution.py:321
  46.8 0.0 collective-permute-done.14.refs_4_
  46.8 0.0 collective-permute-done.13.refs_3_
  46.8 0.0 collective-permute-done.12.refs_2_
  46.8 1.5 %spread.3 = (f32[16,32,128]{2,1,0:T(8,128)S(1)}, f32[1,512]{1,0:T(1,128)S(1)}) custom-call(f32[1,1024]{1,0:T(1,128)S(1)} %get-tuple-element.67.refs_0_, f32[1,1024]{1,0:T(1,128)S(1)} %get-tuple-element.71.refs_2_.refs_1_, f32[1,1024]{1,0:T(1,128)S(1)} %collective-permute-done.12.refs_2_, f32[1,1024]{1,0:T(1,128)S(1)} %collective-permute-done.13.refs_3_, ...), custom_call_target="tpu_custom_call" | custom-call | tf_op jit(solution)/shard_map/spread/pallas_call | solution.py:362
  48.4 0.9 %collective-permute-start.15 = (f32[16,32,128]{2,1,0:T(8,128)S(1)}, f32[16,32,128]{2,1,0:T(8,128)S(1)}, u32[]{:S(2)}, u32[]{:S(2)}) collective-permute-start(f32[16,32,128]{2,1,0:T(8,128)S(1)} %get-tuple-element.93), channel_id=1, source_target_pairs={{0,8},{8,0},{16,24},{24,16},{1,9},{9,1},{17,25},{25,17},{2,10},{10... | collective-permute-start | bytes 786440 | tf_op jit(solution)/shard_map/ppermute | solution.py:397
  49.2 2.0 %spread.2 = (f32[16,32,128]{2,1,0:T(8,128)S(1)}, f32[1,512]{1,0:T(1,128)}) custom-call(f32[1,1024]{1,0:T(1,128)S(1)} %get-tuple-element.67.refs_0_, f32[1,1024]{1,0:T(1,128)S(1)} %get-tuple-element.71.refs_2_.refs_1_, f32[1,1024]{1,0:T(1,128)S(1)} %collective-permute-done.12.refs_2_, f32[1,1024]{1,0:T(1,128)S(1)} %collective-permute-done.13.refs_3_, ...), custom_call_target="tpu_custom_call" | custom-call | tf_op jit(solution)/shard_map/spread/pallas_call | solution.py:362
  51.2 0.0 collective-permute-done.15.b_ref
  51.2 0.8 %last.1 = (f32[16,32,128]{2,1,0:T(8,128)}, f32[1,512]{1,0:T(1,128)}, f32[1,512]{1,0:T(1,128)}) custom-call(f32[16,32,128]{2,1,0:T(8,128)S(1)} %get-tuple-element.92.a_ref, f32[16,32,128]{2,1,0:T(8,128)S(1)} %collective-permute-done.15.b_ref, f32[1,512]{1,0:T(1,128)S(1)} %get-tuple-element.94.w_ref, f32[1,512]{1,0:T(1,128)S(1)} %get-tuple-element.95.v_ref), custom_call_target="tpu_custom_call" | custom-call | tf_op jit(solution)/shard_map/last/pallas_call | solution.py:381
Async XLA Ops:
  0.6 12.8 %copy-start = (f32[32,32]{1,0:T(8,128)S(1)}, f32[32,32]{1,0:T(8,128)}, u32[]{:S(2)}) copy-start(f32[32,32]{1,0:T(8,128)} %refs_4_.1) | copy-start | bytes 12292
  1.7 11.4 %collective-permute-start = (f32[524,128]{1,0:T(8,128)S(1)}, f32[524,128]{1,0:T(8,128)S(1)}, u32[]{:S(2)}, u32[]{:S(2)}) collective-permute-start(f32[524,128]{1,0:T(8,128)S(1)} %get-tuple-element.51.refs_0_.refs_4_.refs_5_), channel_id=1, source_target_pairs={{0,16},{8,24},{16,0},{24,8},{1,17},{9,25},{17,1},{25,9},{2,18},{10... | collective-permute-start | bytes 804872 | tf_op jit(solution)/shard_map/ppermute | solution.py:397
  3.9 9.3 %collective-permute-start.1 = (f32[520,128]{1,0:T(8,128)S(1)}, f32[520,128]{1,0:T(8,128)S(1)}, u32[]{:S(2)}, u32[]{:S(2)}) collective-permute-start(f32[520,128]{1,0:T(8,128)S(1)} %get-tuple-element.52.refs_2_), channel_id=1, source_target_pairs={{0,1},{1,0},{2,3},{3,2},{4,5},{5,4},{6,7},{7,6},{8,9},{9,8},{10,11... | collective-permute-start | bytes 798728 | tf_op jit(solution)/shard_map/ppermute | solution.py:397
  13.2 14.2 %collective-permute-start.6 = (f32[768,128]{1,0:T(8,128)S(1)}, f32[768,128]{1,0:T(8,128)S(1)}, u32[]{:S(2)}, u32[]{:S(2)}) collective-permute-start(f32[768,128]{1,0:T(8,128)S(1)} %get-tuple-element.62.refs_1_), channel_id=1, source_target_pairs={{0,16},{8,24},{16,0},{24,8},{1,17},{9,25},{17,1},{25,9},{2,18},{10... | collective-permute-start | bytes 1179656 | tf_op jit(solution)/shard_map/ppermute | solution.py:397
  15.2 6.0 %collective-permute-start.4 = (f32[1,1024]{1,0:T(1,128)S(1)}, f32[1,1024]{1,0:T(1,128)S(1)}, u32[]{:S(2)}, u32[]{:S(2)}) collective-permute-start(f32[1,1024]{1,0:T(1,128)S(1)} %get-tuple-element.58.refs_2_.refs_0_), channel_id=1, source_target_pairs={{0,6},{1,7},{2,4},{3,5},{4,2},{5,3},{6,0},{7,1},{8,14},{9,15},{10,... | collective-permute-start | bytes 12296 | tf_op jit(solution)/shard_map/ppermute | solution.py:397
  18.6 3.4 %collective-permute-start.3 = (f32[1,1024]{1,0:T(1,128)S(1)}, f32[1,1024]{1,0:T(1,128)S(1)}, u32[]{:S(2)}, u32[]{:S(2)}) collective-permute-start(f32[1,1024]{1,0:T(1,128)S(1)} %get-tuple-element.58.refs_2_.refs_0_), channel_id=1, source_target_pairs={{0,4},{1,5},{2,6},{3,7},{4,0},{5,1},{6,2},{7,3},{8,12},{9,13},{10,... | collective-permute-start | bytes 12296 | tf_op jit(solution)/shard_map/ppermute | solution.py:397
  18.6 3.4 %collective-permute-start.2 = (f32[1,1024]{1,0:T(1,128)S(1)}, f32[1,1024]{1,0:T(1,128)S(1)}, u32[]{:S(2)}, u32[]{:S(2)}) collective-permute-start(f32[1,1024]{1,0:T(1,128)S(1)} %get-tuple-element.58.refs_2_.refs_0_), channel_id=1, source_target_pairs={{0,2},{1,3},{2,0},{3,1},{4,6},{5,7},{6,4},{7,5},{8,10},{9,11},{10,... | collective-permute-start | bytes 12296 | tf_op jit(solution)/shard_map/ppermute | solution.py:397
  22.9 14.9 %collective-permute-start.11 = (f32[768,128]{1,0:T(8,128)S(1)}, f32[768,128]{1,0:T(8,128)S(1)}, u32[]{:S(2)}, u32[]{:S(2)}) collective-permute-start(f32[768,128]{1,0:T(8,128)S(1)} %get-tuple-element.69.refs_1_), channel_id=1, source_target_pairs={{0,16},{8,24},{16,0},{24,8},{1,17},{9,25},{17,1},{25,9},{2,18},{10... | collective-permute-start | bytes 1179656 | tf_op jit(solution)/shard_map/ppermute | solution.py:397
  24.2 4.5 %collective-permute-start.5 = (f32[1,1024]{1,0:T(1,128)S(1)}, f32[1,1024]{1,0:T(1,128)S(1)}, u32[]{:S(2)}, u32[]{:S(2)}) collective-permute-start(f32[1,1024]{1,0:T(1,128)S(1)} %get-tuple-element.61.refs_2_.refs_0_), channel_id=1, source_target_pairs={{0,8},{8,0},{16,24},{24,16},{1,9},{9,1},{17,25},{25,17},{2,10},{10... | collective-permute-start | bytes 12296 | tf_op jit(solution)/shard_map/ppermute | solution.py:397
  29.5 7.0 %collective-permute-start.9 = (f32[1,1024]{1,0:T(1,128)S(1)}, f32[1,1024]{1,0:T(1,128)S(1)}, u32[]{:S(2)}, u32[]{:S(2)}) collective-permute-start(f32[1,1024]{1,0:T(1,128)S(1)} %get-tuple-element.64.refs_2_.refs_0_), channel_id=1, source_target_pairs={{0,6},{1,7},{2,4},{3,5},{4,2},{5,3},{6,0},{7,1},{8,14},{9,15},{10,... | collective-permute-start | bytes 12296 | tf_op jit(solution)/shard_map/ppermute | solution.py:397
  31.4 5.1 %collective-permute-start.8 = (f32[1,1024]{1,0:T(1,128)S(1)}, f32[1,1024]{1,0:T(1,128)S(1)}, u32[]{:S(2)}, u32[]{:S(2)}) collective-permute-start(f32[1,1024]{1,0:T(1,128)S(1)} %get-tuple-element.64.refs_2_.refs_0_), channel_id=1, source_target_pairs={{0,4},{1,5},{2,6},{3,7},{4,0},{5,1},{6,2},{7,3},{8,12},{9,13},{10,... | collective-permute-start | bytes 12296 | tf_op jit(solution)/shard_map/ppermute | solution.py:397
  31.4 5.1 %collective-permute-start.7 = (f32[1,1024]{1,0:T(1,128)S(1)}, f32[1,1024]{1,0:T(1,128)S(1)}, u32[]{:S(2)}, u32[]{:S(2)}) collective-permute-start(f32[1,1024]{1,0:T(1,128)S(1)} %get-tuple-element.64.refs_2_.refs_0_), channel_id=1, source_target_pairs={{0,2},{1,3},{2,0},{3,1},{4,6},{5,7},{6,4},{7,5},{8,10},{9,11},{10,... | collective-permute-start | bytes 12296 | tf_op jit(solution)/shard_map/ppermute | solution.py:397
  36.9 2.4 %collective-permute-start.10 = (f32[1,1024]{1,0:T(1,128)S(1)}, f32[1,1024]{1,0:T(1,128)S(1)}, u32[]{:S(2)}, u32[]{:S(2)}) collective-permute-start(f32[1,1024]{1,0:T(1,128)S(1)} %get-tuple-element.68.refs_2_.refs_0_), channel_id=1, source_target_pairs={{0,8},{8,0},{16,24},{24,16},{1,9},{9,1},{17,25},{25,17},{2,10},{10... | collective-permute-start | bytes 12296 | tf_op jit(solution)/shard_map/ppermute | solution.py:397
  39.7 7.1 %collective-permute-start.14 = (f32[1,1024]{1,0:T(1,128)S(1)}, f32[1,1024]{1,0:T(1,128)S(1)}, u32[]{:S(2)}, u32[]{:S(2)}) collective-permute-start(f32[1,1024]{1,0:T(1,128)S(1)} %get-tuple-element.71.refs_2_.refs_1_), channel_id=1, source_target_pairs={{0,6},{1,7},{2,4},{3,5},{4,2},{5,3},{6,0},{7,1},{8,14},{9,15},{10,... | collective-permute-start | bytes 12296 | tf_op jit(solution)/shard_map/ppermute | solution.py:397
  41.6 5.2 %collective-permute-start.13 = (f32[1,1024]{1,0:T(1,128)S(1)}, f32[1,1024]{1,0:T(1,128)S(1)}, u32[]{:S(2)}, u32[]{:S(2)}) collective-permute-start(f32[1,1024]{1,0:T(1,128)S(1)} %get-tuple-element.71.refs_2_.refs_1_), channel_id=1, source_target_pairs={{0,4},{1,5},{2,6},{3,7},{4,0},{5,1},{6,2},{7,3},{8,12},{9,13},{10,... | collective-permute-start | bytes 12296 | tf_op jit(solution)/shard_map/ppermute | solution.py:397
  41.6 5.2 %collective-permute-start.12 = (f32[1,1024]{1,0:T(1,128)S(1)}, f32[1,1024]{1,0:T(1,128)S(1)}, u32[]{:S(2)}, u32[]{:S(2)}) collective-permute-start(f32[1,1024]{1,0:T(1,128)S(1)} %get-tuple-element.71.refs_2_.refs_1_), channel_id=1, source_target_pairs={{0,2},{1,3},{2,0},{3,1},{4,6},{5,7},{6,4},{7,5},{8,10},{9,11},{10,... | collective-permute-start | bytes 12296 | tf_op jit(solution)/shard_map/ppermute | solution.py:397
  48.4 2.8 %collective-permute-start.15 = (f32[16,32,128]{2,1,0:T(8,128)S(1)}, f32[16,32,128]{2,1,0:T(8,128)S(1)}, u32[]{:S(2)}, u32[]{:S(2)}) collective-permute-start(f32[16,32,128]{2,1,0:T(8,128)S(1)} %get-tuple-element.93), channel_id=1, source_target_pairs={{0,8},{8,0},{16,24},{24,16},{1,9},{9,1},{17,25},{25,17},{2,10},{10... | collective-permute-start | bytes 786440 | tf_op jit(solution)/shard_map/ppermute | solution.py:397

commit v11 on v10

--- a/solution.py
+++ b/solution.py
@@ -332,7 +332,7 @@
     return (hi, lo), token
 
 
-def spread_body(n, t_first, t_count, parts, packs, count, u_ref, *refs):
+def spread_body(n, t_count, parts, packs, count, t_ref, u_ref, *refs):
     p = n // LANES
     w = u_ref[...] * total_of(refs[:parts])
     pack_refs = refs[parts : parts + packs]
@@ -349,21 +349,22 @@
             [jnp.concatenate([pair_refs[2 * k + part][t + q] for k in range(count)], 0) for q in range(2)], 1
         )
 
-    for t in range(t_first, t_first + t_count, 2):
+    for step in range(0, t_count, 2):
+        t = t_ref[0] + step
         two = jnp.dot(both, take(0, t), preferred_element_type=f32)
         out = two[:SEG] + two[SEG:] + jnp.dot(whi, take(1, t), preferred_element_type=f32)
-        o_ref[t - t_first] = out[:, :LANES]
-        o_ref[t - t_first + 1] = out[:, LANES:]
+        o_ref[step] = out[:, :LANES]
+        o_ref[step + 1] = out[:, LANES:]
 
 
 def spread_call(n, u, partials, packs, pairs, t_first, t_count, after):
     refs = [ref for pair in pairs for ref in pair]
-    args = [u, *partials, *packs, *refs]
+    args = [jnp.full((1,), t_first, jnp.int32), u, *partials, *packs, *refs]
     return pl.pallas_call(
         lambda *refs: spread_body(
-            n, t_first, t_count, len(partials), len(packs), len(pairs), *refs[: len(args)], *refs[-2:]
+            n, t_count, len(partials), len(packs), len(pairs), *refs[: len(args)], *refs[-2:]
         ),
-        in_specs=[VMEM] * len(args) + [ANY] * len(after),
+        in_specs=[pl.BlockSpec(memory_space=pltpu.SMEM)] + [VMEM] * (len(args) - 1) + [ANY] * len(after),
         out_specs=[VMEM] * 2,
         out_shape=[pltpu.VMEM((t_count, SEG, LANES), f32), pltpu.VMEM((1, n), f32)],
         compiler_params=PARAMS,
@@ -457,13 +458,13 @@
             after = tables(source, first, units, *after)
         return after
 
-    after = tables(0, ahead, 2, *tables(0, 0, ahead, filt))
+    after = tables(0, ahead, 1, *tables(0, 0, ahead, filt))
     rpacks = [over_y(gate(own[0], *xpacks, *ypacks, *after))]
     kernel, partial = gibbs_call(n, m, xpacks, ypacks, penalty, after)
     row_sums = pltpu.VMEM((1, len(xpacks) * n), f32)
     col_sums = pltpu.VMEM((1, len(ypacks) * m), f32)
     lines = along_z(partial)
-    after = tables(0, ahead + 2, 2, partial)
+    after = tables(0, ahead + 1, 3, partial)
     fills = [[(0, 1), (1, 3)], [(4, 1), (5, 3)]]
     for iteration in range(ITERS):
         cohort_scale, column = half_step(

time: 52.1 us -> 51.3 us (0.985)
  waiting for transfers between devices: 0.77 us -> 0.04 us
    ppermute x16, waiting for transfers between devices: 0.77 us -> 0.04 us  [move(): lax.ppermute(x, axis, [(b * pair + r, away(b) * pair + (r ^ flip)) for b...]
    pallas_call x9 -> x10, Pallas kernels: 18.7 us -> 19.1 us  [table_call(): pl.pallas_call(lambda *refs: table_body(n, first, count, *refs[:2], *refs...]
  transfers between devices with their start and end apart: 16 -> 16, of which waited for: 1 -> 0; matrix products, arithmetic and copies ran while one was open for 0% -> 0% of each run, Pallas kernels for 50% -> 51%
where the time goes in v11:
time: 51.3 us; the launch traced here: 51.1 us
  Pallas kernels  29.9 us (58%)
  starting transfers between devices  20.3 us (40%)
  between operations  0.86 us (2%)
    ppermute x16, starting transfers between devices, move(): lax.ppermute(x, axis, [(b * pair + r, away(b) * pair + (r ^ flip)) for b...  20.3 us
    pallas_call x10, Pallas kernels, table_call(): pl.pallas_call(lambda *refs: table_body(n, first, count, *refs[:2], *refs...  19.1 us
    pallas_call x2, Pallas kernels, spread_call(): pl.pallas_call(lambda *refs: spread_body(n, t_count, len(partials), len(p...  3.53 us
    pallas_call x4, Pallas kernels, half_step(): pl.pallas_call(lambda *refs: body(size, len(partials), len(packs), *refs[...  2.56 us
    pallas_call x2, Pallas kernels, hbm_call(): pl.pallas_call(body, in_specs=[HBM] * len(args), out_specs=[VMEM] * len(o...  2.27 us
    pallas_call x1, Pallas kernels, gibbs_call(): pl.pallas_call(lambda *refs: gibbs_body(n, m, len(xpacks), len(ypacks), *...  1.78 us
  transfers between devices with their start and end apart: 16, of which 0 were waited for; matrix products, arithmetic and copies ran while one was open for 0% of the time, Pallas kernels for 51%

profile of v11, /device:TPU:1, one launch (start us, length us, event | category | flops | bytes accessed | tf_op | source)
XLA Modules:
  0.0 51.1 jit_solution(17357096592060424524)
XLA Ops:
  0.6 0.0 copy-start
  0.6 1.1 %packs.1 = (f32[524,128]{1,0:T(8,128)S(1)}, f32[520,128]{1,0:T(8,128)S(1)}) custom-call(bf16[512,128]{1,0:T(8,128)(2,1)} %x_hbm.1, bf16[512,128]{1,0:T(8,128)(2,1)} %y_hbm.1, s32[4,128]{1,0:T(4,128)} %bitcast.7, s32[4,128]{1,0:T(4,128)} %bitcast.8, f32[4,128]{1,0:T(4,128)} %bitcast.9, s32[4,128]{1,0:T(4,128)} %bitcast.10, f32[4,128]{1,0:T(4,128)} %bitcast.11), custom_call_target="tpu_custom_call" | custom-call | tf_op jit(solution)/shard_map/packs/pallas_call | solution.py:148
  1.7 2.1 %collective-permute-start = (f32[524,128]{1,0:T(8,128)S(1)}, f32[524,128]{1,0:T(8,128)S(1)}, u32[]{:S(2)}, u32[]{:S(2)}) collective-permute-start(f32[524,128]{1,0:T(8,128)S(1)} %get-tuple-element.54.refs_0_.refs_4_.refs_6_), channel_id=1, source_target_pairs={{0,16},{8,24},{16,0},{24,8},{1,17},{9,25},{17,1},{25,9},{2,18},{10... | collective-permute-start | bytes 804872 | tf_op jit(solution)/shard_map/ppermute | solution.py:398
  3.9 1.2 %collective-permute-start.1 = (f32[520,128]{1,0:T(8,128)S(1)}, f32[520,128]{1,0:T(8,128)S(1)}, u32[]{:S(2)}, u32[]{:S(2)}) collective-permute-start(f32[520,128]{1,0:T(8,128)S(1)} %get-tuple-element.55.refs_2_), channel_id=1, source_target_pairs={{0,1},{1,0},{2,3},{3,2},{4,5},{5,4},{6,7},{7,6},{8,9},{9,8},{10,11... | collective-permute-start | bytes 798728 | tf_op jit(solution)/shard_map/ppermute | solution.py:398
  5.1 1.2 %records.1 = (f32[768,128]{1,0:T(8,128)S(1)}, f32[768,128]{1,0:T(8,128)S(1)}, f32[32,128]{1,0:T(8,128)S(1)}) custom-call(f32[4,32,128]{2,1,0:T(8,128)} %constant.6.clone.f_hbm, s32[512,128]{1,0:T(8,128)} %m_hbm.1, s32[512,128]{1,0:T(8,128)} %d_hbm.1, f32[512,128]{1,0:T(8,128)} %a_hbm.1), custom_call_target="tpu_custom_call" | custom-call | tf_op jit(solution)/shard_map/records/pallas_call | solution.py:148
  6.3 4.7 %tables.10 = (bf16[32,256,128]{2,1,0:T(8,128)(2,1)S(1)}, bf16[32,256,128]{2,1,0:T(8,128)(2,1)S(1)}, f32[8,128]{1,0:T(8,128)S(1)}) custom-call(f32[32,128]{1,0:T(8,128)S(1)} %get-tuple-element.56.refs_0_.refs_2_, f32[768,128]{1,0:T(8,128)S(1)} %get-tuple-element.66.refs_1_, f32[32,128]{1,0:T(8,128)S(1)} %get-tuple-element.56.refs_0_.refs_2_), custom_call_target="tpu_custom_call" | custom-call | flops 536870912 | bytes 15360000 | tf_op jit(solution)/shard_map/tables/pallas_call | solution.py:321
  10.9 1.3 %tables.11 = (bf16[32,64,128]{2,1,0:T(8,128)(2,1)S(1)}, bf16[32,64,128]{2,1,0:T(8,128)(2,1)S(1)}, f32[8,128]{1,0:T(8,128)S(1)}) custom-call(f32[32,128]{1,0:T(8,128)S(1)} %get-tuple-element.56.refs_0_.refs_2_, f32[768,128]{1,0:T(8,128)S(1)} %get-tuple-element.73.refs_1_, f32[8,128]{1,0:T(8,128)S(1)} %get-tuple-element.59.refs_2_), custom_call_target="tpu_custom_call" | custom-call | flops 134217728 | bytes 3840000 | tf_op jit(solution)/shard_map/tables/pallas_call | solution.py:321
  12.2 0.0 collective-permute-done.1.refs_3_
  12.2 0.0 collective-permute-done.refs_1_.refs_5_.refs_7_
  12.2 0.3 collective-permute-start.6
  12.5 0.0 copy-done
  12.5 1.8 %gibbs.1 = (f32[1024,1024]{1,0:T(8,128)S(1)}, f32[1,1024]{1,0:T(1,128)S(1)}) custom-call(f32[524,128]{1,0:T(8,128)S(1)} %get-tuple-element.54.refs_0_.refs_4_.refs_6_, f32[524,128]{1,0:T(8,128)S(1)} %collective-permute-done.refs_1_.refs_5_.refs_7_, f32[520,128]{1,0:T(8,128)S(1)} %get-tuple-element.55.refs_2_, f32[520,128]{1,0:T(8,128)S(1)} %collective-permute-done.1.refs_3_, ...), custom_call_target="tpu_custom_call" | custom-call | flops 268435456 | bytes 4194304 | tf_op jit(solution)/shard_map/gibbs/pallas_call | solution.py:231
  14.3 3.4 %collective-permute-start.4 = (f32[1,1024]{1,0:T(1,128)S(1)}, f32[1,1024]{1,0:T(1,128)S(1)}, u32[]{:S(2)}, u32[]{:S(2)}) collective-permute-start(f32[1,1024]{1,0:T(1,128)S(1)} %get-tuple-element.61.refs_2_.refs_0_), channel_id=1, source_target_pairs={{0,6},{1,7},{2,4},{3,5},{4,2},{5,3},{6,0},{7,1},{8,14},{9,15},{10,... | collective-permute-start | bytes 12296 | tf_op jit(solution)/shard_map/ppermute | solution.py:398
  17.7 0.0 collective-permute-start.3
  17.7 0.4 collective-permute-start.2
  18.1 2.2 %tables.12 = (bf16[32,128,128]{2,1,0:T(8,128)(2,1)S(1)}, bf16[32,128,128]{2,1,0:T(8,128)(2,1)S(1)}, f32[8,128]{1,0:T(8,128)S(1)}) custom-call(f32[32,128]{1,0:T(8,128)S(1)} %get-tuple-element.56.refs_0_.refs_2_, f32[768,128]{1,0:T(8,128)S(1)} %get-tuple-element.73.refs_1_, f32[1,1024]{1,0:T(1,128)S(1)} %get-tuple-element.61.refs_2_.refs_0_), custom_call_target="tpu_custom_call" | custom-call | flops 268435456 | bytes 7680000 | tf_op jit(solution)/shard_map/tables/pallas_call | solution.py:321
  20.3 1.2 %tables.13 = (bf16[32,64,128]{2,1,0:T(8,128)(2,1)S(1)}, bf16[32,64,128]{2,1,0:T(8,128)(2,1)S(1)}, f32[8,128]{1,0:T(8,128)S(1)}) custom-call(f32[32,128]{1,0:T(8,128)S(1)} %get-tuple-element.56.refs_0_.refs_2_, f32[768,128]{1,0:T(8,128)S(1)} %get-tuple-element.73.refs_1_, f32[8,128]{1,0:T(8,128)S(1)} %get-tuple-element.63.refs_2_), custom_call_target="tpu_custom_call" | custom-call | flops 134217728 | bytes 3840000 | tf_op jit(solution)/shard_map/tables/pallas_call | solution.py:321
  21.5 0.0 collective-permute-done.4.refs_3_
  21.5 0.0 collective-permute-done.3.refs_2_
  21.6 0.0 collective-permute-done.2.refs_1_
  21.6 1.0 %cols.2 = (f32[1,1024]{1,0:T(1,128)}, f32[1,1024]{1,0:T(1,128)S(1)}) custom-call(f32[1,1024]{1,0:T(1,128)S(1)} %get-tuple-element.61.refs_2_.refs_0_, f32[1,1024]{1,0:T(1,128)S(1)} %collective-permute-done.2.refs_1_, f32[1,1024]{1,0:T(1,128)S(1)} %collective-permute-done.3.refs_2_, f32[1,1024]{1,0:T(1,128)S(1)} %collective-permute-done.4.refs_3_, ...), custom_call_target="tpu_custom_call" | custom-call | tf_op jit(solution)/shard_map/cols/pallas_call | solution.py:273
  22.5 1.2 %collective-permute-start.11 = (f32[768,128]{1,0:T(8,128)S(1)}, f32[768,128]{1,0:T(8,128)S(1)}, u32[]{:S(2)}, u32[]{:S(2)}) collective-permute-start(f32[768,128]{1,0:T(8,128)S(1)} %get-tuple-element.73.refs_1_), channel_id=1, source_target_pairs={{0,16},{8,24},{16,0},{24,8},{1,17},{9,25},{17,1},{25,9},{2,18},{10... | collective-permute-start | bytes 1179656 | tf_op jit(solution)/shard_map/ppermute | solution.py:398
  23.8 2.7 %collective-permute-start.5 = (f32[1,1024]{1,0:T(1,128)S(1)}, f32[1,1024]{1,0:T(1,128)S(1)}, u32[]{:S(2)}, u32[]{:S(2)}) collective-permute-start(f32[1,1024]{1,0:T(1,128)S(1)} %get-tuple-element.65.refs_2_.refs_0_), channel_id=1, source_target_pairs={{0,8},{8,0},{16,24},{24,16},{1,9},{9,1},{17,25},{25,17},{2,10},{10... | collective-permute-start | bytes 12296 | tf_op jit(solution)/shard_map/ppermute | solution.py:398
  26.5 0.0 collective-permute-done.6.refs_1_
  26.5 1.2 %tables.14 = (bf16[32,64,128]{2,1,0:T(8,128)(2,1)S(1)}, bf16[32,64,128]{2,1,0:T(8,128)(2,1)S(1)}, f32[8,128]{1,0:T(8,128)S(1)}) custom-call(f32[32,128]{1,0:T(8,128)S(1)} %get-tuple-element.56.refs_0_.refs_2_, f32[768,128]{1,0:T(8,128)S(1)} %collective-permute-done.6.refs_1_, f32[1,1024]{1,0:T(1,128)S(1)} %get-tuple-element.65.refs_2_.refs_0_), custom_call_target="tpu_custom_call" | custom-call | flops 134217728 | bytes 3840000 | tf_op jit(solution)/shard_map/tables/pallas_call | solution.py:321
  27.7 0.0 collective-permute-done.5.refs_1_
  27.8 0.9 %rows.2 = (f32[1,512]{1,0:T(1,128)}, f32[1,1024]{1,0:T(1,128)S(1)}) custom-call(f32[1,1024]{1,0:T(1,128)S(1)} %get-tuple-element.65.refs_2_.refs_0_, f32[1,1024]{1,0:T(1,128)S(1)} %collective-permute-done.5.refs_1_, f32[520,128]{1,0:T(8,128)S(1)} %get-tuple-element.55.refs_2_, f32[520,128]{1,0:T(8,128)S(1)} %collective-permute-done.1.refs_3_, ...), custom_call_target="tpu_custom_call" | custom-call | tf_op jit(solution)/shard_map/rows/pallas_call | solution.py:273
  28.6 3.1 %collective-permute-start.9 = (f32[1,1024]{1,0:T(1,128)S(1)}, f32[1,1024]{1,0:T(1,128)S(1)}, u32[]{:S(2)}, u32[]{:S(2)}) collective-permute-start(f32[1,1024]{1,0:T(1,128)S(1)} %get-tuple-element.68.refs_2_.refs_0_), channel_id=1, source_target_pairs={{0,6},{1,7},{2,4},{3,5},{4,2},{5,3},{6,0},{7,1},{8,14},{9,15},{10,... | collective-permute-start | bytes 12296 | tf_op jit(solution)/shard_map/ppermute | solution.py:398
  31.7 0.0 collective-permute-start.8
  31.7 0.5 collective-permute-start.7
  32.2 2.2 %tables.15 = (bf16[32,128,128]{2,1,0:T(8,128)(2,1)S(1)}, bf16[32,128,128]{2,1,0:T(8,128)(2,1)S(1)}, f32[8,128]{1,0:T(8,128)S(1)}) custom-call(f32[32,128]{1,0:T(8,128)S(1)} %get-tuple-element.56.refs_0_.refs_2_, f32[768,128]{1,0:T(8,128)S(1)} %collective-permute-done.6.refs_1_, f32[1,1024]{1,0:T(1,128)S(1)} %get-tuple-element.68.refs_2_.refs_0_), custom_call_target="tpu_custom_call" | custom-call | flops 268435456 | bytes 7680000 | tf_op jit(solution)/shard_map/tables/pallas_call | solution.py:321
  34.4 1.3 %tables.16 = (bf16[32,64,128]{2,1,0:T(8,128)(2,1)S(1)}, bf16[32,64,128]{2,1,0:T(8,128)(2,1)S(1)}, f32[8,128]{1,0:T(8,128)S(1)}) custom-call(f32[32,128]{1,0:T(8,128)S(1)} %get-tuple-element.56.refs_0_.refs_2_, f32[768,128]{1,0:T(8,128)S(1)} %collective-permute-done.6.refs_1_, f32[8,128]{1,0:T(8,128)S(1)} %get-tuple-element.69.refs_2_), custom_call_target="tpu_custom_call" | custom-call | flops 134217728 | bytes 3840000 | tf_op jit(solution)/shard_map/tables/pallas_call | solution.py:321
  35.7 0.0 collective-permute-done.9.refs_3_
  35.7 0.0 collective-permute-done.8.refs_2_
  35.7 0.0 collective-permute-done.7.refs_1_
  35.7 0.4 cols.3
  36.1 0.9 %collective-permute-start.10 = (f32[1,1024]{1,0:T(1,128)S(1)}, f32[1,1024]{1,0:T(1,128)S(1)}, u32[]{:S(2)}, u32[]{:S(2)}) collective-permute-start(f32[1,1024]{1,0:T(1,128)S(1)} %get-tuple-element.72.refs_2_.refs_0_), channel_id=1, source_target_pairs={{0,8},{8,0},{16,24},{24,16},{1,9},{9,1},{17,25},{25,17},{2,10},{10... | collective-permute-start | bytes 12296 | tf_op jit(solution)/shard_map/ppermute | solution.py:398
  37.0 0.0 collective-permute-done.11.refs_1_
  37.0 1.5 %tables.17 = (bf16[32,64,128]{2,1,0:T(8,128)(2,1)S(1)}, bf16[32,64,128]{2,1,0:T(8,128)(2,1)S(1)}, f32[8,128]{1,0:T(8,128)S(1)}) custom-call(f32[32,128]{1,0:T(8,128)S(1)} %get-tuple-element.56.refs_0_.refs_2_, f32[768,128]{1,0:T(8,128)S(1)} %collective-permute-done.11.refs_1_, f32[1,1024]{1,0:T(1,128)S(1)} %get-tuple-element.72.refs_2_.refs_0_), custom_call_target="tpu_custom_call" | custom-call | flops 134217728 | bytes 3840000 | tf_op jit(solution)/shard_map/tables/pallas_call | solution.py:321
  38.5 0.0 collective-permute-done.10.refs_1_
  38.5 0.4 rows.3
  38.8 3.2 %collective-permute-start.14 = (f32[1,1024]{1,0:T(1,128)S(1)}, f32[1,1024]{1,0:T(1,128)S(1)}, u32[]{:S(2)}, u32[]{:S(2)}) collective-permute-start(f32[1,1024]{1,0:T(1,128)S(1)} %get-tuple-element.75.refs_2_), channel_id=1, source_target_pairs={{0,6},{1,7},{2,4},{3,5},{4,2},{5,3},{6,0},{7,1},{8,14},{9,15},{10,... | collective-permute-start | bytes 12296 | tf_op jit(solution)/shard_map/ppermute | solution.py:398
  42.0 0.0 collective-permute-start.13
  42.0 0.5 collective-permute-start.12
  42.5 2.2 %tables.18 = (bf16[32,128,128]{2,1,0:T(8,128)(2,1)S(1)}, bf16[32,128,128]{2,1,0:T(8,128)(2,1)S(1)}, f32[8,128]{1,0:T(8,128)S(1)}) custom-call(f32[32,128]{1,0:T(8,128)S(1)} %get-tuple-element.56.refs_0_.refs_2_, f32[768,128]{1,0:T(8,128)S(1)} %collective-permute-done.11.refs_1_, f32[1,1024]{1,0:T(1,128)S(1)} %get-tuple-element.75.refs_2_), custom_call_target="tpu_custom_call" | custom-call | flops 268435456 | bytes 7680000 | tf_op jit(solution)/shard_map/tables/pallas_call | solution.py:321
  44.7 1.3 %tables.19 = (bf16[32,64,128]{2,1,0:T(8,128)(2,1)S(1)}, bf16[32,64,128]{2,1,0:T(8,128)(2,1)S(1)}, f32[8,128]{1,0:T(8,128)S(1)}) custom-call(f32[32,128]{1,0:T(8,128)S(1)} %get-tuple-element.56.refs_0_.refs_2_, f32[768,128]{1,0:T(8,128)S(1)} %collective-permute-done.11.refs_1_, f32[8,128]{1,0:T(8,128)S(1)} %get-tuple-element.94.refs_2_), custom_call_target="tpu_custom_call" | custom-call | flops 134217728 | bytes 3840000 | tf_op jit(solution)/shard_map/tables/pallas_call | solution.py:321
  45.9 0.0 collective-permute-done.14.refs_5_
  46.0 0.0 collective-permute-done.13.refs_4_
  46.0 0.0 collective-permute-done.12.refs_3_
  46.0 1.6 %spread.3 = (f32[16,32,128]{2,1,0:T(8,128)S(1)}, f32[1,512]{1,0:T(1,128)S(1)}) custom-call(s32[1]{0:T(128)} %constant.2.clone.1.refs_0_, f32[1,1024]{1,0:T(1,128)S(1)} %get-tuple-element.71.refs_1_, f32[1,1024]{1,0:T(1,128)S(1)} %get-tuple-element.75.refs_2_, f32[1,1024]{1,0:T(1,128)S(1)} %collective-permute-done.12.refs_3_, ...), custom_call_target="tpu_custom_call" | custom-call | tf_op jit(solution)/shard_map/spread/pallas_call | solution.py:363
  47.5 0.9 %collective-permute-start.15 = (f32[16,32,128]{2,1,0:T(8,128)S(1)}, f32[16,32,128]{2,1,0:T(8,128)S(1)}, u32[]{:S(2)}, u32[]{:S(2)}) collective-permute-start(f32[16,32,128]{2,1,0:T(8,128)S(1)} %get-tuple-element.99), channel_id=1, source_target_pairs={{0,8},{8,0},{16,24},{24,16},{1,9},{9,1},{17,25},{25,17},{2,10},{10... | collective-permute-start | bytes 786440 | tf_op jit(solution)/shard_map/ppermute | solution.py:398
  48.4 2.0 %spread.2 = (f32[16,32,128]{2,1,0:T(8,128)S(1)}, f32[1,512]{1,0:T(1,128)}) custom-call(s32[1]{0:T(128)} %constant.1.clone.1.refs_0_, f32[1,1024]{1,0:T(1,128)S(1)} %get-tuple-element.71.refs_1_, f32[1,1024]{1,0:T(1,128)S(1)} %get-tuple-element.75.refs_2_, f32[1,1024]{1,0:T(1,128)S(1)} %collective-permute-done.12.refs_3_, ...), custom_call_target="tpu_custom_call" | custom-call | tf_op jit(solution)/shard_map/spread/pallas_call | solution.py:363
  50.4 0.0 collective-permute-done.15.b_ref
  50.4 0.8 %last.1 = (f32[16,32,128]{2,1,0:T(8,128)}, f32[1,512]{1,0:T(1,128)}, f32[1,512]{1,0:T(1,128)}) custom-call(f32[16,32,128]{2,1,0:T(8,128)S(1)} %get-tuple-element.98.a_ref, f32[16,32,128]{2,1,0:T(8,128)S(1)} %collective-permute-done.15.b_ref, f32[1,512]{1,0:T(1,128)S(1)} %get-tuple-element.100.w_ref, f32[1,512]{1,0:T(1,128)S(1)} %get-tuple-element.101.v_ref), custom_call_target="tpu_custom_call" | custom-call | tf_op jit(solution)/shard_map/last/pallas_call | solution.py:382
Async XLA Ops:
  0.6 11.9 %copy-start = (f32[32,32]{1,0:T(8,128)S(1)}, f32[32,32]{1,0:T(8,128)}, u32[]{:S(2)}) copy-start(f32[32,32]{1,0:T(8,128)} %refs_4_.1) | copy-start | bytes 12292
  1.7 10.5 %collective-permute-start = (f32[524,128]{1,0:T(8,128)S(1)}, f32[524,128]{1,0:T(8,128)S(1)}, u32[]{:S(2)}, u32[]{:S(2)}) collective-permute-start(f32[524,128]{1,0:T(8,128)S(1)} %get-tuple-element.54.refs_0_.refs_4_.refs_6_), channel_id=1, source_target_pairs={{0,16},{8,24},{16,0},{24,8},{1,17},{9,25},{17,1},{25,9},{2,18},{10... | collective-permute-start | bytes 804872 | tf_op jit(solution)/shard_map/ppermute | solution.py:398
  3.9 8.4 %collective-permute-start.1 = (f32[520,128]{1,0:T(8,128)S(1)}, f32[520,128]{1,0:T(8,128)S(1)}, u32[]{:S(2)}, u32[]{:S(2)}) collective-permute-start(f32[520,128]{1,0:T(8,128)S(1)} %get-tuple-element.55.refs_2_), channel_id=1, source_target_pairs={{0,1},{1,0},{2,3},{3,2},{4,5},{5,4},{6,7},{7,6},{8,9},{9,8},{10,11... | collective-permute-start | bytes 798728 | tf_op jit(solution)/shard_map/ppermute | solution.py:398
  12.2 14.2 %collective-permute-start.6 = (f32[768,128]{1,0:T(8,128)S(1)}, f32[768,128]{1,0:T(8,128)S(1)}, u32[]{:S(2)}, u32[]{:S(2)}) collective-permute-start(f32[768,128]{1,0:T(8,128)S(1)} %get-tuple-element.66.refs_1_), channel_id=1, source_target_pairs={{0,16},{8,24},{16,0},{24,8},{1,17},{9,25},{17,1},{25,9},{2,18},{10... | collective-permute-start | bytes 1179656 | tf_op jit(solution)/shard_map/ppermute | solution.py:398
  14.3 7.2 %collective-permute-start.4 = (f32[1,1024]{1,0:T(1,128)S(1)}, f32[1,1024]{1,0:T(1,128)S(1)}, u32[]{:S(2)}, u32[]{:S(2)}) collective-permute-start(f32[1,1024]{1,0:T(1,128)S(1)} %get-tuple-element.61.refs_2_.refs_0_), channel_id=1, source_target_pairs={{0,6},{1,7},{2,4},{3,5},{4,2},{5,3},{6,0},{7,1},{8,14},{9,15},{10,... | collective-permute-start | bytes 12296 | tf_op jit(solution)/shard_map/ppermute | solution.py:398
  17.7 3.8 %collective-permute-start.3 = (f32[1,1024]{1,0:T(1,128)S(1)}, f32[1,1024]{1,0:T(1,128)S(1)}, u32[]{:S(2)}, u32[]{:S(2)}) collective-permute-start(f32[1,1024]{1,0:T(1,128)S(1)} %get-tuple-element.61.refs_2_.refs_0_), channel_id=1, source_target_pairs={{0,4},{1,5},{2,6},{3,7},{4,0},{5,1},{6,2},{7,3},{8,12},{9,13},{10,... | collective-permute-start | bytes 12296 | tf_op jit(solution)/shard_map/ppermute | solution.py:398
  17.7 3.8 %collective-permute-start.2 = (f32[1,1024]{1,0:T(1,128)S(1)}, f32[1,1024]{1,0:T(1,128)S(1)}, u32[]{:S(2)}, u32[]{:S(2)}) collective-permute-start(f32[1,1024]{1,0:T(1,128)S(1)} %get-tuple-element.61.refs_2_.refs_0_), channel_id=1, source_target_pairs={{0,2},{1,3},{2,0},{3,1},{4,6},{5,7},{6,4},{7,5},{8,10},{9,11},{10,... | collective-permute-start | bytes 12296 | tf_op jit(solution)/shard_map/ppermute | solution.py:398
  22.5 14.5 %collective-permute-start.11 = (f32[768,128]{1,0:T(8,128)S(1)}, f32[768,128]{1,0:T(8,128)S(1)}, u32[]{:S(2)}, u32[]{:S(2)}) collective-permute-start(f32[768,128]{1,0:T(8,128)S(1)} %get-tuple-element.73.refs_1_), channel_id=1, source_target_pairs={{0,16},{8,24},{16,0},{24,8},{1,17},{9,25},{17,1},{25,9},{2,18},{10... | collective-permute-start | bytes 1179656 | tf_op jit(solution)/shard_map/ppermute | solution.py:398
  23.8 4.0 %collective-permute-start.5 = (f32[1,1024]{1,0:T(1,128)S(1)}, f32[1,1024]{1,0:T(1,128)S(1)}, u32[]{:S(2)}, u32[]{:S(2)}) collective-permute-start(f32[1,1024]{1,0:T(1,128)S(1)} %get-tuple-element.65.refs_2_.refs_0_), channel_id=1, source_target_pairs={{0,8},{8,0},{16,24},{24,16},{1,9},{9,1},{17,25},{25,17},{2,10},{10... | collective-permute-start | bytes 12296 | tf_op jit(solution)/shard_map/ppermute | solution.py:398
  28.6 7.1 %collective-permute-start.9 = (f32[1,1024]{1,0:T(1,128)S(1)}, f32[1,1024]{1,0:T(1,128)S(1)}, u32[]{:S(2)}, u32[]{:S(2)}) collective-permute-start(f32[1,1024]{1,0:T(1,128)S(1)} %get-tuple-element.68.refs_2_.refs_0_), channel_id=1, source_target_pairs={{0,6},{1,7},{2,4},{3,5},{4,2},{5,3},{6,0},{7,1},{8,14},{9,15},{10,... | collective-permute-start | bytes 12296 | tf_op jit(solution)/shard_map/ppermute | solution.py:398
  31.7 4.0 %collective-permute-start.8 = (f32[1,1024]{1,0:T(1,128)S(1)}, f32[1,1024]{1,0:T(1,128)S(1)}, u32[]{:S(2)}, u32[]{:S(2)}) collective-permute-start(f32[1,1024]{1,0:T(1,128)S(1)} %get-tuple-element.68.refs_2_.refs_0_), channel_id=1, source_target_pairs={{0,4},{1,5},{2,6},{3,7},{4,0},{5,1},{6,2},{7,3},{8,12},{9,13},{10,... | collective-permute-start | bytes 12296 | tf_op jit(solution)/shard_map/ppermute | solution.py:398
  31.7 4.0 %collective-permute-start.7 = (f32[1,1024]{1,0:T(1,128)S(1)}, f32[1,1024]{1,0:T(1,128)S(1)}, u32[]{:S(2)}, u32[]{:S(2)}) collective-permute-start(f32[1,1024]{1,0:T(1,128)S(1)} %get-tuple-element.68.refs_2_.refs_0_), channel_id=1, source_target_pairs={{0,2},{1,3},{2,0},{3,1},{4,6},{5,7},{6,4},{7,5},{8,10},{9,11},{10,... | collective-permute-start | bytes 12296 | tf_op jit(solution)/shard_map/ppermute | solution.py:398
  36.1 2.4 %collective-permute-start.10 = (f32[1,1024]{1,0:T(1,128)S(1)}, f32[1,1024]{1,0:T(1,128)S(1)}, u32[]{:S(2)}, u32[]{:S(2)}) collective-permute-start(f32[1,1024]{1,0:T(1,128)S(1)} %get-tuple-element.72.refs_2_.refs_0_), channel_id=1, source_target_pairs={{0,8},{8,0},{16,24},{24,16},{1,9},{9,1},{17,25},{25,17},{2,10},{10... | collective-permute-start | bytes 12296 | tf_op jit(solution)/shard_map/ppermute | solution.py:398
  38.8 7.1 %collective-permute-start.14 = (f32[1,1024]{1,0:T(1,128)S(1)}, f32[1,1024]{1,0:T(1,128)S(1)}, u32[]{:S(2)}, u32[]{:S(2)}) collective-permute-start(f32[1,1024]{1,0:T(1,128)S(1)} %get-tuple-element.75.refs_2_), channel_id=1, source_target_pairs={{0,6},{1,7},{2,4},{3,5},{4,2},{5,3},{6,0},{7,1},{8,14},{9,15},{10,... | collective-permute-start | bytes 12296 | tf_op jit(solution)/shard_map/ppermute | solution.py:398
  42.0 4.0 %collective-permute-start.13 = (f32[1,1024]{1,0:T(1,128)S(1)}, f32[1,1024]{1,0:T(1,128)S(1)}, u32[]{:S(2)}, u32[]{:S(2)}) collective-permute-start(f32[1,1024]{1,0:T(1,128)S(1)} %get-tuple-element.75.refs_2_), channel_id=1, source_target_pairs={{0,4},{1,5},{2,6},{3,7},{4,0},{5,1},{6,2},{7,3},{8,12},{9,13},{10,... | collective-permute-start | bytes 12296 | tf_op jit(solution)/shard_map/ppermute | solution.py:398
  42.0 4.0 %collective-permute-start.12 = (f32[1,1024]{1,0:T(1,128)S(1)}, f32[1,1024]{1,0:T(1,128)S(1)}, u32[]{:S(2)}, u32[]{:S(2)}) collective-permute-start(f32[1,1024]{1,0:T(1,128)S(1)} %get-tuple-element.75.refs_2_), channel_id=1, source_target_pairs={{0,2},{1,3},{2,0},{3,1},{4,6},{5,7},{6,4},{7,5},{8,10},{9,11},{10,... | collective-permute-start | bytes 12296 | tf_op jit(solution)/shard_map/ppermute | solution.py:398
  47.5 2.9 %collective-permute-start.15 = (f32[16,32,128]{2,1,0:T(8,128)S(1)}, f32[16,32,128]{2,1,0:T(8,128)S(1)}, u32[]{:S(2)}, u32[]{:S(2)}) collective-permute-start(f32[16,32,128]{2,1,0:T(8,128)S(1)} %get-tuple-element.99), channel_id=1, source_target_pairs={{0,8},{8,0},{16,24},{24,16},{1,9},{9,1},{17,25},{25,17},{2,10},{10... | collective-permute-start | bytes 786440 | tf_op jit(solution)/shard_map/ppermute | solution.py:398

commit v12 on v11

--- a/solution.py
+++ b/solution.py
@@ -15,6 +15,7 @@
 DAYS = 64
 LANES = 128
 UNROLL = 128
+WHOLE = 192
 
 half_span = 11
 
@@ -286,7 +287,7 @@
     merch_rows = lax.broadcasted_iota(jnp.int32, (MERCH_DEV, LANES), 0).astype(f32).astype(bf16)
     merch_cols = lax.broadcasted_iota(jnp.int32, (LANES, MERCH_DEV), 1).astype(f32).astype(bf16)
     one, zero = jnp.ones((MERCH_DEV, LANES), bf16), jnp.zeros((MERCH_DEV, LANES), bf16)
-    size = math.gcd(count, UNROLL)
+    size = count if count <= WHOLE else math.gcd(count, UNROLL)
 
     def group(step, carry):
         start = pl.multiple_of(step * size, size)
@@ -443,15 +444,12 @@
     pairs = {}
 
     def tables(source, first, units, *after):
-        for size in (units & ~1, units & 1):
-            if size:
-                late = int(first >= ahead)
-                pack = own[late] if source == 0 else rpacks[late][source - 1]
-                pairs[source, first], token = table_call(
-                    filt, pack, pack.shape[0] // 3, (first - late * ahead) * unit, size * unit, after
-                )
-                after, first = [token], first + size
-        return after
+        late = int(first >= ahead)
+        pack = own[late] if source == 0 else rpacks[late][source - 1]
+        pairs[source, first], token = table_call(
+            filt, pack, pack.shape[0] // 3, (first - late * ahead) * unit, units * unit, after
+        )
+        return [token]
 
     def others(first, units, *after):
         for source in range(1, n_y):

time: 51.3 us -> 50.6 us (0.986)
  Pallas kernels: 29.9 us -> 29 us
    pallas_call x10 -> x7, Pallas kernels: 19.1 us -> 18.1 us  [table_call(): pl.pallas_call(lambda *refs: table_body(n, first, count, *refs[:2], *refs...]
  transfers between devices with their start and end apart: 16 -> 16, of which waited for: 0 -> 0; matrix products, arithmetic and copies ran while one was open for 0% -> 0% of each run, Pallas kernels for 51% -> 50%
where the time goes in v12:
time: 50.6 us; the launch traced here: 50.4 us
  Pallas kernels  29 us (57%)
  starting transfers between devices  20.6 us (41%)
  between operations  0.83 us (2%)
    ppermute x16, starting transfers between devices, move(): lax.ppermute(x, axis, [(b * pair + r, away(b) * pair + (r ^ flip)) for b...  20.6 us
    pallas_call x7, Pallas kernels, table_call(): pl.pallas_call(lambda *refs: table_body(n, first, count, *refs[:2], *refs...  18.1 us
    pallas_call x2, Pallas kernels, spread_call(): pl.pallas_call(lambda *refs: spread_body(n, t_count, len(partials), len(p...  3.54 us
    pallas_call x4, Pallas kernels, half_step(): pl.pallas_call(lambda *refs: body(size, len(partials), len(packs), *refs[...  2.56 us
    pallas_call x2, Pallas kernels, hbm_call(): pl.pallas_call(body, in_specs=[HBM] * len(args), out_specs=[VMEM] * len(o...  2.26 us
    pallas_call x1, Pallas kernels, gibbs_call(): pl.pallas_call(lambda *refs: gibbs_body(n, m, len(xpacks), len(ypacks), *...  1.78 us
  transfers between devices with their start and end apart: 16, of which 0 were waited for; matrix products, arithmetic and copies ran while one was open for 0% of the time, Pallas kernels for 50%

profile of v12, /device:TPU:1, one launch (start us, length us, event | category | flops | bytes accessed | tf_op | source)
XLA Modules:
  0.0 50.4 jit_solution(2451475079915611305)
XLA Ops:
  0.6 1.1 %packs.1 = (f32[524,128]{1,0:T(8,128)S(1)}, f32[520,128]{1,0:T(8,128)S(1)}) custom-call(bf16[512,128]{1,0:T(8,128)(2,1)} %x_hbm.1, bf16[512,128]{1,0:T(8,128)(2,1)} %y_hbm.1, s32[4,128]{1,0:T(4,128)} %bitcast.7, s32[4,128]{1,0:T(4,128)} %bitcast.8, f32[4,128]{1,0:T(4,128)} %bitcast.9, s32[4,128]{1,0:T(4,128)} %bitcast.10, f32[4,128]{1,0:T(4,128)} %bitcast.11), custom_call_target="tpu_custom_call" | custom-call | tf_op jit(solution)/shard_map/packs/pallas_call | solution.py:149
  1.7 2.1 %collective-permute-start = (f32[524,128]{1,0:T(8,128)S(1)}, f32[524,128]{1,0:T(8,128)S(1)}, u32[]{:S(2)}, u32[]{:S(2)}) collective-permute-start(f32[524,128]{1,0:T(8,128)S(1)} %get-tuple-element.45.refs_0_.refs_4_.refs_6_), channel_id=1, source_target_pairs={{0,16},{8,24},{16,0},{24,8},{1,17},{9,25},{17,1},{25,9},{2,18},{10... | collective-permute-start | bytes 804872 | tf_op jit(solution)/shard_map/ppermute | solution.py:399
  3.9 0.0 copy-start
  3.9 1.2 %collective-permute-start.1 = (f32[520,128]{1,0:T(8,128)S(1)}, f32[520,128]{1,0:T(8,128)S(1)}, u32[]{:S(2)}, u32[]{:S(2)}) collective-permute-start(f32[520,128]{1,0:T(8,128)S(1)} %get-tuple-element.46.refs_2_), channel_id=1, source_target_pairs={{0,1},{1,0},{2,3},{3,2},{4,5},{5,4},{6,7},{7,6},{8,9},{9,8},{10,11... | collective-permute-start | bytes 798728 | tf_op jit(solution)/shard_map/ppermute | solution.py:399
  5.1 1.2 %records.1 = (f32[768,128]{1,0:T(8,128)S(1)}, f32[768,128]{1,0:T(8,128)S(1)}, f32[32,128]{1,0:T(8,128)S(1)}) custom-call(f32[4,32,128]{2,1,0:T(8,128)} %constant.6.clone.f_hbm, s32[512,128]{1,0:T(8,128)} %m_hbm.1, s32[512,128]{1,0:T(8,128)} %d_hbm.1, f32[512,128]{1,0:T(8,128)} %a_hbm.1), custom_call_target="tpu_custom_call" | custom-call | tf_op jit(solution)/shard_map/records/pallas_call | solution.py:149
  6.3 4.7 %tables.7 = (bf16[32,256,128]{2,1,0:T(8,128)(2,1)S(1)}, bf16[32,256,128]{2,1,0:T(8,128)(2,1)S(1)}, f32[8,128]{1,0:T(8,128)S(1)}) custom-call(f32[32,128]{1,0:T(8,128)S(1)} %get-tuple-element.47.refs_0_.refs_2_, f32[768,128]{1,0:T(8,128)S(1)} %get-tuple-element.56.refs_1_, f32[32,128]{1,0:T(8,128)S(1)} %get-tuple-element.47.refs_0_.refs_2_), custom_call_target="tpu_custom_call" | custom-call | flops 536870912 | bytes 15360000 | tf_op jit(solution)/shard_map/tables/pallas_call | solution.py:322
  10.9 1.2 %tables.8 = (bf16[32,64,128]{2,1,0:T(8,128)(2,1)S(1)}, bf16[32,64,128]{2,1,0:T(8,128)(2,1)S(1)}, f32[8,128]{1,0:T(8,128)S(1)}) custom-call(f32[32,128]{1,0:T(8,128)S(1)} %get-tuple-element.47.refs_0_.refs_2_, f32[768,128]{1,0:T(8,128)S(1)} %get-tuple-element.62.refs_1_, f32[8,128]{1,0:T(8,128)S(1)} %get-tuple-element.50.refs_2_), custom_call_target="tpu_custom_call" | custom-call | flops 134217728 | bytes 3840000 | tf_op jit(solution)/shard_map/tables/pallas_call | solution.py:322
  12.2 0.0 collective-permute-done.1.refs_3_
  12.2 0.0 collective-permute-done.refs_1_.refs_5_.refs_7_
  12.2 0.3 collective-permute-start.6
  12.5 0.0 copy-done
  12.5 1.8 %gibbs.1 = (f32[1024,1024]{1,0:T(8,128)S(1)}, f32[1,1024]{1,0:T(1,128)S(1)}) custom-call(f32[524,128]{1,0:T(8,128)S(1)} %get-tuple-element.45.refs_0_.refs_4_.refs_6_, f32[524,128]{1,0:T(8,128)S(1)} %collective-permute-done.refs_1_.refs_5_.refs_7_, f32[520,128]{1,0:T(8,128)S(1)} %get-tuple-element.46.refs_2_, f32[520,128]{1,0:T(8,128)S(1)} %collective-permute-done.1.refs_3_, ...), custom_call_target="tpu_custom_call" | custom-call | flops 268435456 | bytes 4194304 | tf_op jit(solution)/shard_map/gibbs/pallas_call | solution.py:232
  14.3 3.4 %collective-permute-start.4 = (f32[1,1024]{1,0:T(1,128)S(1)}, f32[1,1024]{1,0:T(1,128)S(1)}, u32[]{:S(2)}, u32[]{:S(2)}) collective-permute-start(f32[1,1024]{1,0:T(1,128)S(1)} %get-tuple-element.52.refs_2_.refs_0_), channel_id=1, source_target_pairs={{0,6},{1,7},{2,4},{3,5},{4,2},{5,3},{6,0},{7,1},{8,14},{9,15},{10,... | collective-permute-start | bytes 12296 | tf_op jit(solution)/shard_map/ppermute | solution.py:399
  17.7 0.0 collective-permute-start.3
  17.7 0.4 collective-permute-start.2
  18.0 3.2 %tables.9 = (bf16[32,192,128]{2,1,0:T(8,128)(2,1)S(1)}, bf16[32,192,128]{2,1,0:T(8,128)(2,1)S(1)}, f32[8,128]{1,0:T(8,128)S(1)}) custom-call(f32[32,128]{1,0:T(8,128)S(1)} %get-tuple-element.47.refs_0_.refs_2_, f32[768,128]{1,0:T(8,128)S(1)} %get-tuple-element.62.refs_1_, f32[1,1024]{1,0:T(1,128)S(1)} %get-tuple-element.52.refs_2_.refs_0_), custom_call_target="tpu_custom_call" | custom-call | flops 402653184 | bytes 11520000 | tf_op jit(solution)/shard_map/tables/pallas_call | solution.py:322
  21.2 0.0 collective-permute-done.4.refs_3_
  21.2 0.0 collective-permute-done.3.refs_2_
  21.2 0.0 collective-permute-done.2.refs_1_
  21.2 1.0 %cols.2 = (f32[1,1024]{1,0:T(1,128)}, f32[1,1024]{1,0:T(1,128)S(1)}) custom-call(f32[1,1024]{1,0:T(1,128)S(1)} %get-tuple-element.52.refs_2_.refs_0_, f32[1,1024]{1,0:T(1,128)S(1)} %collective-permute-done.2.refs_1_, f32[1,1024]{1,0:T(1,128)S(1)} %collective-permute-done.3.refs_2_, f32[1,1024]{1,0:T(1,128)S(1)} %collective-permute-done.4.refs_3_, ...), custom_call_target="tpu_custom_call" | custom-call | tf_op jit(solution)/shard_map/cols/pallas_call | solution.py:274
  22.2 1.2 %collective-permute-start.11 = (f32[768,128]{1,0:T(8,128)S(1)}, f32[768,128]{1,0:T(8,128)S(1)}, u32[]{:S(2)}, u32[]{:S(2)}) collective-permute-start(f32[768,128]{1,0:T(8,128)S(1)} %get-tuple-element.62.refs_1_), channel_id=1, source_target_pairs={{0,16},{8,24},{16,0},{24,8},{1,17},{9,25},{17,1},{25,9},{2,18},{10... | collective-permute-start | bytes 1179656 | tf_op jit(solution)/shard_map/ppermute | solution.py:399
  23.4 3.0 %collective-permute-start.5 = (f32[1,1024]{1,0:T(1,128)S(1)}, f32[1,1024]{1,0:T(1,128)S(1)}, u32[]{:S(2)}, u32[]{:S(2)}) collective-permute-start(f32[1,1024]{1,0:T(1,128)S(1)} %get-tuple-element.55.refs_2_.refs_0_), channel_id=1, source_target_pairs={{0,8},{8,0},{16,24},{24,16},{1,9},{9,1},{17,25},{25,17},{2,10},{10... | collective-permute-start | bytes 12296 | tf_op jit(solution)/shard_map/ppermute | solution.py:399
  26.4 0.0 collective-permute-done.6.refs_1_
  26.4 1.2 %tables.10 = (bf16[32,64,128]{2,1,0:T(8,128)(2,1)S(1)}, bf16[32,64,128]{2,1,0:T(8,128)(2,1)S(1)}, f32[8,128]{1,0:T(8,128)S(1)}) custom-call(f32[32,128]{1,0:T(8,128)S(1)} %get-tuple-element.47.refs_0_.refs_2_, f32[768,128]{1,0:T(8,128)S(1)} %collective-permute-done.6.refs_1_, f32[1,1024]{1,0:T(1,128)S(1)} %get-tuple-element.55.refs_2_.refs_0_), custom_call_target="tpu_custom_call" | custom-call | flops 134217728 | bytes 3840000 | tf_op jit(solution)/shard_map/tables/pallas_call | solution.py:322
  27.7 0.0 collective-permute-done.5.refs_1_
  27.7 0.9 %rows.2 = (f32[1,512]{1,0:T(1,128)}, f32[1,1024]{1,0:T(1,128)S(1)}) custom-call(f32[1,1024]{1,0:T(1,128)S(1)} %get-tuple-element.55.refs_2_.refs_0_, f32[1,1024]{1,0:T(1,128)S(1)} %collective-permute-done.5.refs_1_, f32[520,128]{1,0:T(8,128)S(1)} %get-tuple-element.46.refs_2_, f32[520,128]{1,0:T(8,128)S(1)} %collective-permute-done.1.refs_3_, ...), custom_call_target="tpu_custom_call" | custom-call | tf_op jit(solution)/shard_map/rows/pallas_call | solution.py:274
  28.6 2.8 %collective-permute-start.9 = (f32[1,1024]{1,0:T(1,128)S(1)}, f32[1,1024]{1,0:T(1,128)S(1)}, u32[]{:S(2)}, u32[]{:S(2)}) collective-permute-start(f32[1,1024]{1,0:T(1,128)S(1)} %get-tuple-element.58.refs_2_.refs_0_), channel_id=1, source_target_pairs={{0,6},{1,7},{2,4},{3,5},{4,2},{5,3},{6,0},{7,1},{8,14},{9,15},{10,... | collective-permute-start | bytes 12296 | tf_op jit(solution)/shard_map/ppermute | solution.py:399
  31.4 0.0 collective-permute-start.8
  31.4 0.7 %collective-permute-start.7 = (f32[1,1024]{1,0:T(1,128)S(1)}, f32[1,1024]{1,0:T(1,128)S(1)}, u32[]{:S(2)}, u32[]{:S(2)}) collective-permute-start(f32[1,1024]{1,0:T(1,128)S(1)} %get-tuple-element.58.refs_2_.refs_0_), channel_id=1, source_target_pairs={{0,2},{1,3},{2,0},{3,1},{4,6},{5,7},{6,4},{7,5},{8,10},{9,11},{10,... | collective-permute-start | bytes 12296 | tf_op jit(solution)/shard_map/ppermute | solution.py:399
  32.1 3.2 %tables.11 = (bf16[32,192,128]{2,1,0:T(8,128)(2,1)S(1)}, bf16[32,192,128]{2,1,0:T(8,128)(2,1)S(1)}, f32[8,128]{1,0:T(8,128)S(1)}) custom-call(f32[32,128]{1,0:T(8,128)S(1)} %get-tuple-element.47.refs_0_.refs_2_, f32[768,128]{1,0:T(8,128)S(1)} %collective-permute-done.6.refs_1_, f32[1,1024]{1,0:T(1,128)S(1)} %get-tuple-element.58.refs_2_.refs_0_), custom_call_target="tpu_custom_call" | custom-call | flops 402653184 | bytes 11520000 | tf_op jit(solution)/shard_map/tables/pallas_call | solution.py:322
  35.3 0.0 collective-permute-done.9.refs_3_
  35.3 0.0 collective-permute-done.8.refs_2_
  35.3 0.0 collective-permute-done.7.refs_1_
  35.3 0.4 cols.3
  35.7 0.9 %collective-permute-start.10 = (f32[1,1024]{1,0:T(1,128)S(1)}, f32[1,1024]{1,0:T(1,128)S(1)}, u32[]{:S(2)}, u32[]{:S(2)}) collective-permute-start(f32[1,1024]{1,0:T(1,128)S(1)} %get-tuple-element.61.refs_2_.refs_0_), channel_id=1, source_target_pairs={{0,8},{8,0},{16,24},{24,16},{1,9},{9,1},{17,25},{25,17},{2,10},{10... | collective-permute-start | bytes 12296 | tf_op jit(solution)/shard_map/ppermute | solution.py:399
  36.6 0.0 collective-permute-done.11.refs_1_
  36.6 1.5 %tables.12 = (bf16[32,64,128]{2,1,0:T(8,128)(2,1)S(1)}, bf16[32,64,128]{2,1,0:T(8,128)(2,1)S(1)}, f32[8,128]{1,0:T(8,128)S(1)}) custom-call(f32[32,128]{1,0:T(8,128)S(1)} %get-tuple-element.47.refs_0_.refs_2_, f32[768,128]{1,0:T(8,128)S(1)} %collective-permute-done.11.refs_1_, f32[1,1024]{1,0:T(1,128)S(1)} %get-tuple-element.61.refs_2_.refs_0_), custom_call_target="tpu_custom_call" | custom-call | flops 134217728 | bytes 3840000 | tf_op jit(solution)/shard_map/tables/pallas_call | solution.py:322
  38.1 0.0 collective-permute-done.10.refs_1_
  38.1 0.4 rows.3
  38.5 2.9 %collective-permute-start.14 = (f32[1,1024]{1,0:T(1,128)S(1)}, f32[1,1024]{1,0:T(1,128)S(1)}, u32[]{:S(2)}, u32[]{:S(2)}) collective-permute-start(f32[1,1024]{1,0:T(1,128)S(1)} %get-tuple-element.64.refs_2_), channel_id=1, source_target_pairs={{0,6},{1,7},{2,4},{3,5},{4,2},{5,3},{6,0},{7,1},{8,14},{9,15},{10,... | collective-permute-start | bytes 12296 | tf_op jit(solution)/shard_map/ppermute | solution.py:399
  41.3 0.0 collective-permute-start.13
  41.3 0.7 %collective-permute-start.12 = (f32[1,1024]{1,0:T(1,128)S(1)}, f32[1,1024]{1,0:T(1,128)S(1)}, u32[]{:S(2)}, u32[]{:S(2)}) collective-permute-start(f32[1,1024]{1,0:T(1,128)S(1)} %get-tuple-element.64.refs_2_), channel_id=1, source_target_pairs={{0,2},{1,3},{2,0},{3,1},{4,6},{5,7},{6,4},{7,5},{8,10},{9,11},{10,... | collective-permute-start | bytes 12296 | tf_op jit(solution)/shard_map/ppermute | solution.py:399
  42.1 3.2 %tables.13 = (bf16[32,192,128]{2,1,0:T(8,128)(2,1)S(1)}, bf16[32,192,128]{2,1,0:T(8,128)(2,1)S(1)}, f32[8,128]{1,0:T(8,128)S(1)}) custom-call(f32[32,128]{1,0:T(8,128)S(1)} %get-tuple-element.47.refs_0_.refs_2_, f32[768,128]{1,0:T(8,128)S(1)} %collective-permute-done.11.refs_1_, f32[1,1024]{1,0:T(1,128)S(1)} %get-tuple-element.64.refs_2_), custom_call_target="tpu_custom_call" | custom-call | flops 402653184 | bytes 11520000 | tf_op jit(solution)/shard_map/tables/pallas_call | solution.py:322
  45.3 0.0 collective-permute-done.14.refs_5_
  45.3 0.0 collective-permute-done.13.refs_4_
  45.3 0.0 collective-permute-done.12.refs_3_
  45.3 1.6 %spread.3 = (f32[16,32,128]{2,1,0:T(8,128)S(1)}, f32[1,512]{1,0:T(1,128)S(1)}) custom-call(s32[1]{0:T(128)} %constant.2.clone.1.refs_0_, f32[1,1024]{1,0:T(1,128)S(1)} %get-tuple-element.60.refs_1_, f32[1,1024]{1,0:T(1,128)S(1)} %get-tuple-element.64.refs_2_, f32[1,1024]{1,0:T(1,128)S(1)} %collective-permute-done.12.refs_3_, ...), custom_call_target="tpu_custom_call" | custom-call | tf_op jit(solution)/shard_map/spread/pallas_call | solution.py:364
  46.8 0.9 %collective-permute-start.15 = (f32[16,32,128]{2,1,0:T(8,128)S(1)}, f32[16,32,128]{2,1,0:T(8,128)S(1)}, u32[]{:S(2)}, u32[]{:S(2)}) collective-permute-start(f32[16,32,128]{2,1,0:T(8,128)S(1)} %get-tuple-element.81), channel_id=1, source_target_pairs={{0,8},{8,0},{16,24},{24,16},{1,9},{9,1},{17,25},{25,17},{2,10},{10... | collective-permute-start | bytes 786440 | tf_op jit(solution)/shard_map/ppermute | solution.py:399
  47.7 2.0 %spread.2 = (f32[16,32,128]{2,1,0:T(8,128)S(1)}, f32[1,512]{1,0:T(1,128)}) custom-call(s32[1]{0:T(128)} %constant.1.clone.1.refs_0_, f32[1,1024]{1,0:T(1,128)S(1)} %get-tuple-element.60.refs_1_, f32[1,1024]{1,0:T(1,128)S(1)} %get-tuple-element.64.refs_2_, f32[1,1024]{1,0:T(1,128)S(1)} %collective-permute-done.12.refs_3_, ...), custom_call_target="tpu_custom_call" | custom-call | tf_op jit(solution)/shard_map/spread/pallas_call | solution.py:364
  49.7 0.0 collective-permute-done.15.b_ref
  49.7 0.7 %last.1 = (f32[16,32,128]{2,1,0:T(8,128)}, f32[1,512]{1,0:T(1,128)}, f32[1,512]{1,0:T(1,128)}) custom-call(f32[16,32,128]{2,1,0:T(8,128)S(1)} %get-tuple-element.80.a_ref, f32[16,32,128]{2,1,0:T(8,128)S(1)} %collective-permute-done.15.b_ref, f32[1,512]{1,0:T(1,128)S(1)} %get-tuple-element.82.w_ref, f32[1,512]{1,0:T(1,128)S(1)} %get-tuple-element.83.v_ref), custom_call_target="tpu_custom_call" | custom-call | tf_op jit(solution)/shard_map/last/pallas_call | solution.py:383
Async XLA Ops:
  1.7 10.5 %collective-permute-start = (f32[524,128]{1,0:T(8,128)S(1)}, f32[524,128]{1,0:T(8,128)S(1)}, u32[]{:S(2)}, u32[]{:S(2)}) collective-permute-start(f32[524,128]{1,0:T(8,128)S(1)} %get-tuple-element.45.refs_0_.refs_4_.refs_6_), channel_id=1, source_target_pairs={{0,16},{8,24},{16,0},{24,8},{1,17},{9,25},{17,1},{25,9},{2,18},{10... | collective-permute-start | bytes 804872 | tf_op jit(solution)/shard_map/ppermute | solution.py:399
  3.9 8.6 %copy-start = (f32[32,32]{1,0:T(8,128)S(1)}, f32[32,32]{1,0:T(8,128)}, u32[]{:S(2)}) copy-start(f32[32,32]{1,0:T(8,128)} %refs_4_.1) | copy-start | bytes 12292
  3.9 8.3 %collective-permute-start.1 = (f32[520,128]{1,0:T(8,128)S(1)}, f32[520,128]{1,0:T(8,128)S(1)}, u32[]{:S(2)}, u32[]{:S(2)}) collective-permute-start(f32[520,128]{1,0:T(8,128)S(1)} %get-tuple-element.46.refs_2_), channel_id=1, source_target_pairs={{0,1},{1,0},{2,3},{3,2},{4,5},{5,4},{6,7},{7,6},{8,9},{9,8},{10,11... | collective-permute-start | bytes 798728 | tf_op jit(solution)/shard_map/ppermute | solution.py:399
  12.2 14.3 %collective-permute-start.6 = (f32[768,128]{1,0:T(8,128)S(1)}, f32[768,128]{1,0:T(8,128)S(1)}, u32[]{:S(2)}, u32[]{:S(2)}) collective-permute-start(f32[768,128]{1,0:T(8,128)S(1)} %get-tuple-element.56.refs_1_), channel_id=1, source_target_pairs={{0,16},{8,24},{16,0},{24,8},{1,17},{9,25},{17,1},{25,9},{2,18},{10... | collective-permute-start | bytes 1179656 | tf_op jit(solution)/shard_map/ppermute | solution.py:399
  14.3 6.9 %collective-permute-start.4 = (f32[1,1024]{1,0:T(1,128)S(1)}, f32[1,1024]{1,0:T(1,128)S(1)}, u32[]{:S(2)}, u32[]{:S(2)}) collective-permute-start(f32[1,1024]{1,0:T(1,128)S(1)} %get-tuple-element.52.refs_2_.refs_0_), channel_id=1, source_target_pairs={{0,6},{1,7},{2,4},{3,5},{4,2},{5,3},{6,0},{7,1},{8,14},{9,15},{10,... | collective-permute-start | bytes 12296 | tf_op jit(solution)/shard_map/ppermute | solution.py:399
  17.7 3.5 %collective-permute-start.3 = (f32[1,1024]{1,0:T(1,128)S(1)}, f32[1,1024]{1,0:T(1,128)S(1)}, u32[]{:S(2)}, u32[]{:S(2)}) collective-permute-start(f32[1,1024]{1,0:T(1,128)S(1)} %get-tuple-element.52.refs_2_.refs_0_), channel_id=1, source_target_pairs={{0,4},{1,5},{2,6},{3,7},{4,0},{5,1},{6,2},{7,3},{8,12},{9,13},{10,... | collective-permute-start | bytes 12296 | tf_op jit(solution)/shard_map/ppermute | solution.py:399
  17.7 3.6 %collective-permute-start.2 = (f32[1,1024]{1,0:T(1,128)S(1)}, f32[1,1024]{1,0:T(1,128)S(1)}, u32[]{:S(2)}, u32[]{:S(2)}) collective-permute-start(f32[1,1024]{1,0:T(1,128)S(1)} %get-tuple-element.52.refs_2_.refs_0_), channel_id=1, source_target_pairs={{0,2},{1,3},{2,0},{3,1},{4,6},{5,7},{6,4},{7,5},{8,10},{9,11},{10,... | collective-permute-start | bytes 12296 | tf_op jit(solution)/shard_map/ppermute | solution.py:399
  22.2 14.4 %collective-permute-start.11 = (f32[768,128]{1,0:T(8,128)S(1)}, f32[768,128]{1,0:T(8,128)S(1)}, u32[]{:S(2)}, u32[]{:S(2)}) collective-permute-start(f32[768,128]{1,0:T(8,128)S(1)} %get-tuple-element.62.refs_1_), channel_id=1, source_target_pairs={{0,16},{8,24},{16,0},{24,8},{1,17},{9,25},{17,1},{25,9},{2,18},{10... | collective-permute-start | bytes 1179656 | tf_op jit(solution)/shard_map/ppermute | solution.py:399
  23.4 4.3 %collective-permute-start.5 = (f32[1,1024]{1,0:T(1,128)S(1)}, f32[1,1024]{1,0:T(1,128)S(1)}, u32[]{:S(2)}, u32[]{:S(2)}) collective-permute-start(f32[1,1024]{1,0:T(1,128)S(1)} %get-tuple-element.55.refs_2_.refs_0_), channel_id=1, source_target_pairs={{0,8},{8,0},{16,24},{24,16},{1,9},{9,1},{17,25},{25,17},{2,10},{10... | collective-permute-start | bytes 12296 | tf_op jit(solution)/shard_map/ppermute | solution.py:399
  28.6 6.7 %collective-permute-start.9 = (f32[1,1024]{1,0:T(1,128)S(1)}, f32[1,1024]{1,0:T(1,128)S(1)}, u32[]{:S(2)}, u32[]{:S(2)}) collective-permute-start(f32[1,1024]{1,0:T(1,128)S(1)} %get-tuple-element.58.refs_2_.refs_0_), channel_id=1, source_target_pairs={{0,6},{1,7},{2,4},{3,5},{4,2},{5,3},{6,0},{7,1},{8,14},{9,15},{10,... | collective-permute-start | bytes 12296 | tf_op jit(solution)/shard_map/ppermute | solution.py:399
  31.4 3.9 %collective-permute-start.8 = (f32[1,1024]{1,0:T(1,128)S(1)}, f32[1,1024]{1,0:T(1,128)S(1)}, u32[]{:S(2)}, u32[]{:S(2)}) collective-permute-start(f32[1,1024]{1,0:T(1,128)S(1)} %get-tuple-element.58.refs_2_.refs_0_), channel_id=1, source_target_pairs={{0,4},{1,5},{2,6},{3,7},{4,0},{5,1},{6,2},{7,3},{8,12},{9,13},{10,... | collective-permute-start | bytes 12296 | tf_op jit(solution)/shard_map/ppermute | solution.py:399
  31.4 3.9 %collective-permute-start.7 = (f32[1,1024]{1,0:T(1,128)S(1)}, f32[1,1024]{1,0:T(1,128)S(1)}, u32[]{:S(2)}, u32[]{:S(2)}) collective-permute-start(f32[1,1024]{1,0:T(1,128)S(1)} %get-tuple-element.58.refs_2_.refs_0_), channel_id=1, source_target_pairs={{0,2},{1,3},{2,0},{3,1},{4,6},{5,7},{6,4},{7,5},{8,10},{9,11},{10,... | collective-permute-start | bytes 12296 | tf_op jit(solution)/shard_map/ppermute | solution.py:399
  35.7 2.4 %collective-permute-start.10 = (f32[1,1024]{1,0:T(1,128)S(1)}, f32[1,1024]{1,0:T(1,128)S(1)}, u32[]{:S(2)}, u32[]{:S(2)}) collective-permute-start(f32[1,1024]{1,0:T(1,128)S(1)} %get-tuple-element.61.refs_2_.refs_0_), channel_id=1, source_target_pairs={{0,8},{8,0},{16,24},{24,16},{1,9},{9,1},{17,25},{25,17},{2,10},{10... | collective-permute-start | bytes 12296 | tf_op jit(solution)/shard_map/ppermute | solution.py:399
  38.5 6.8 %collective-permute-start.14 = (f32[1,1024]{1,0:T(1,128)S(1)}, f32[1,1024]{1,0:T(1,128)S(1)}, u32[]{:S(2)}, u32[]{:S(2)}) collective-permute-start(f32[1,1024]{1,0:T(1,128)S(1)} %get-tuple-element.64.refs_2_), channel_id=1, source_target_pairs={{0,6},{1,7},{2,4},{3,5},{4,2},{5,3},{6,0},{7,1},{8,14},{9,15},{10,... | collective-permute-start | bytes 12296 | tf_op jit(solution)/shard_map/ppermute | solution.py:399
  41.3 3.9 %collective-permute-start.13 = (f32[1,1024]{1,0:T(1,128)S(1)}, f32[1,1024]{1,0:T(1,128)S(1)}, u32[]{:S(2)}, u32[]{:S(2)}) collective-permute-start(f32[1,1024]{1,0:T(1,128)S(1)} %get-tuple-element.64.refs_2_), channel_id=1, source_target_pairs={{0,4},{1,5},{2,6},{3,7},{4,0},{5,1},{6,2},{7,3},{8,12},{9,13},{10,... | collective-permute-start | bytes 12296 | tf_op jit(solution)/shard_map/ppermute | solution.py:399
  41.3 4.0 %collective-permute-start.12 = (f32[1,1024]{1,0:T(1,128)S(1)}, f32[1,1024]{1,0:T(1,128)S(1)}, u32[]{:S(2)}, u32[]{:S(2)}) collective-permute-start(f32[1,1024]{1,0:T(1,128)S(1)} %get-tuple-element.64.refs_2_), channel_id=1, source_target_pairs={{0,2},{1,3},{2,0},{3,1},{4,6},{5,7},{6,4},{7,5},{8,10},{9,11},{10,... | collective-permute-start | bytes 12296 | tf_op jit(solution)/shard_map/ppermute | solution.py:399
  46.8 2.9 %collective-permute-start.15 = (f32[16,32,128]{2,1,0:T(8,128)S(1)}, f32[16,32,128]{2,1,0:T(8,128)S(1)}, u32[]{:S(2)}, u32[]{:S(2)}) collective-permute-start(f32[16,32,128]{2,1,0:T(8,128)S(1)} %get-tuple-element.81), channel_id=1, source_target_pairs={{0,8},{8,0},{16,24},{24,16},{1,9},{9,1},{17,25},{25,17},{2,10},{10... | collective-permute-start | bytes 786440 | tf_op jit(solution)/shard_map/ppermute | solution.py:399

commit v13 on v12

--- a/solution.py
+++ b/solution.py
@@ -15,7 +15,7 @@
 DAYS = 64
 LANES = 128
 UNROLL = 128
-WHOLE = 192
+WHOLE = 256
 
 half_span = 11
 

time: 50.6 us -> 50.1 us (level)
    pallas_call x7, Pallas kernels: 18.1 us -> 17.4 us  [table_call(): pl.pallas_call(lambda *refs: table_body(n, first, count, *refs[:2], *refs...]
where the time goes in v13:
time: 50.1 us; the launch traced here: 49.9 us
  Pallas kernels  28.5 us (57%)
  starting transfers between devices  20.6 us (41%)
  between operations  0.83 us (2%)
    ppermute x16, starting transfers between devices, move(): lax.ppermute(x, axis, [(b * pair + r, away(b) * pair + (r ^ flip)) for b...  20.6 us
    pallas_call x7, Pallas kernels, table_call(): pl.pallas_call(lambda *refs: table_body(n, first, count, *refs[:2], *refs...  17.4 us
    pallas_call x2, Pallas kernels, spread_call(): pl.pallas_call(lambda *refs: spread_body(n, t_count, len(partials), len(p...  3.54 us
    pallas_call x4, Pallas kernels, half_step(): pl.pallas_call(lambda *refs: body(size, len(partials), len(packs), *refs[...  2.74 us
    pallas_call x2, Pallas kernels, hbm_call(): pl.pallas_call(body, in_specs=[HBM] * len(args), out_specs=[VMEM] * len(o...  2.26 us
    pallas_call x1, Pallas kernels, gibbs_call(): pl.pallas_call(lambda *refs: gibbs_body(n, m, len(xpacks), len(ypacks), *...  1.79 us
  transfers between devices with their start and end apart: 16, of which 0 were waited for; matrix products, arithmetic and copies ran while one was open for 0% of the time, Pallas kernels for 50%

profile of v13, /device:TPU:1, one launch (start us, length us, event | category | flops | bytes accessed | tf_op | source)
XLA Modules:
  0.0 49.9 jit_solution(11409239125074604545)
XLA Ops:
  0.6 1.1 %packs.1 = (f32[524,128]{1,0:T(8,128)S(1)}, f32[520,128]{1,0:T(8,128)S(1)}) custom-call(bf16[512,128]{1,0:T(8,128)(2,1)} %x_hbm.1, bf16[512,128]{1,0:T(8,128)(2,1)} %y_hbm.1, s32[4,128]{1,0:T(4,128)} %bitcast.7, s32[4,128]{1,0:T(4,128)} %bitcast.8, f32[4,128]{1,0:T(4,128)} %bitcast.9, s32[4,128]{1,0:T(4,128)} %bitcast.10, f32[4,128]{1,0:T(4,128)} %bitcast.11), custom_call_target="tpu_custom_call" | custom-call | tf_op jit(solution)/shard_map/packs/pallas_call | solution.py:149
  1.7 2.1 %collective-permute-start = (f32[524,128]{1,0:T(8,128)S(1)}, f32[524,128]{1,0:T(8,128)S(1)}, u32[]{:S(2)}, u32[]{:S(2)}) collective-permute-start(f32[524,128]{1,0:T(8,128)S(1)} %get-tuple-element.45.refs_0_.refs_4_.refs_6_), channel_id=1, source_target_pairs={{0,16},{8,24},{16,0},{24,8},{1,17},{9,25},{17,1},{25,9},{2,18},{10... | collective-permute-start | bytes 804872 | tf_op jit(solution)/shard_map/ppermute | solution.py:399
  3.9 0.0 copy-start
  3.9 1.2 %collective-permute-start.1 = (f32[520,128]{1,0:T(8,128)S(1)}, f32[520,128]{1,0:T(8,128)S(1)}, u32[]{:S(2)}, u32[]{:S(2)}) collective-permute-start(f32[520,128]{1,0:T(8,128)S(1)} %get-tuple-element.46.refs_2_), channel_id=1, source_target_pairs={{0,1},{1,0},{2,3},{3,2},{4,5},{5,4},{6,7},{7,6},{8,9},{9,8},{10,11... | collective-permute-start | bytes 798728 | tf_op jit(solution)/shard_map/ppermute | solution.py:399
  5.1 1.2 %records.1 = (f32[768,128]{1,0:T(8,128)S(1)}, f32[768,128]{1,0:T(8,128)S(1)}, f32[32,128]{1,0:T(8,128)S(1)}) custom-call(f32[4,32,128]{2,1,0:T(8,128)} %constant.6.clone.f_hbm, s32[512,128]{1,0:T(8,128)} %m_hbm.1, s32[512,128]{1,0:T(8,128)} %d_hbm.1, f32[512,128]{1,0:T(8,128)} %a_hbm.1), custom_call_target="tpu_custom_call" | custom-call | tf_op jit(solution)/shard_map/records/pallas_call | solution.py:149
  6.3 4.2 %tables.7 = (bf16[32,256,128]{2,1,0:T(8,128)(2,1)S(1)}, bf16[32,256,128]{2,1,0:T(8,128)(2,1)S(1)}, f32[8,128]{1,0:T(8,128)S(1)}) custom-call(f32[32,128]{1,0:T(8,128)S(1)} %get-tuple-element.47.refs_0_.refs_2_, f32[768,128]{1,0:T(8,128)S(1)} %get-tuple-element.56.refs_1_, f32[32,128]{1,0:T(8,128)S(1)} %get-tuple-element.47.refs_0_.refs_2_), custom_call_target="tpu_custom_call" | custom-call | flops 536870912 | bytes 15360000 | tf_op jit(solution)/shard_map/tables/pallas_call | solution.py:322
  10.4 1.2 %tables.8 = (bf16[32,64,128]{2,1,0:T(8,128)(2,1)S(1)}, bf16[32,64,128]{2,1,0:T(8,128)(2,1)S(1)}, f32[8,128]{1,0:T(8,128)S(1)}) custom-call(f32[32,128]{1,0:T(8,128)S(1)} %get-tuple-element.47.refs_0_.refs_2_, f32[768,128]{1,0:T(8,128)S(1)} %get-tuple-element.62.refs_1_, f32[8,128]{1,0:T(8,128)S(1)} %get-tuple-element.50.refs_2_), custom_call_target="tpu_custom_call" | custom-call | flops 134217728 | bytes 3840000 | tf_op jit(solution)/shard_map/tables/pallas_call | solution.py:322
  11.7 0.0 collective-permute-done.1.refs_3_
  11.7 0.0 collective-permute-done.refs_1_.refs_5_.refs_7_
  11.7 0.3 collective-permute-start.6
  12.0 0.0 copy-done
  12.0 1.8 %gibbs.1 = (f32[1024,1024]{1,0:T(8,128)S(1)}, f32[1,1024]{1,0:T(1,128)S(1)}) custom-call(f32[524,128]{1,0:T(8,128)S(1)} %get-tuple-element.45.refs_0_.refs_4_.refs_6_, f32[524,128]{1,0:T(8,128)S(1)} %collective-permute-done.refs_1_.refs_5_.refs_7_, f32[520,128]{1,0:T(8,128)S(1)} %get-tuple-element.46.refs_2_, f32[520,128]{1,0:T(8,128)S(1)} %collective-permute-done.1.refs_3_, ...), custom_call_target="tpu_custom_call" | custom-call | flops 268435456 | bytes 4194304 | tf_op jit(solution)/shard_map/gibbs/pallas_call | solution.py:232
  13.8 3.4 %collective-permute-start.4 = (f32[1,1024]{1,0:T(1,128)S(1)}, f32[1,1024]{1,0:T(1,128)S(1)}, u32[]{:S(2)}, u32[]{:S(2)}) collective-permute-start(f32[1,1024]{1,0:T(1,128)S(1)} %get-tuple-element.52.refs_2_.refs_0_), channel_id=1, source_target_pairs={{0,6},{1,7},{2,4},{3,5},{4,2},{5,3},{6,0},{7,1},{8,14},{9,15},{10,... | collective-permute-start | bytes 12296 | tf_op jit(solution)/shard_map/ppermute | solution.py:399
  17.2 0.0 collective-permute-start.3
  17.2 0.4 collective-permute-start.2
  17.5 3.2 %tables.9 = (bf16[32,192,128]{2,1,0:T(8,128)(2,1)S(1)}, bf16[32,192,128]{2,1,0:T(8,128)(2,1)S(1)}, f32[8,128]{1,0:T(8,128)S(1)}) custom-call(f32[32,128]{1,0:T(8,128)S(1)} %get-tuple-element.47.refs_0_.refs_2_, f32[768,128]{1,0:T(8,128)S(1)} %get-tuple-element.62.refs_1_, f32[1,1024]{1,0:T(1,128)S(1)} %get-tuple-element.52.refs_2_.refs_0_), custom_call_target="tpu_custom_call" | custom-call | flops 402653184 | bytes 11520000 | tf_op jit(solution)/shard_map/tables/pallas_call | solution.py:322
  20.7 0.0 collective-permute-done.4.refs_3_
  20.7 0.0 collective-permute-done.3.refs_2_
  20.7 0.0 collective-permute-done.2.refs_1_
  20.7 1.0 %cols.2 = (f32[1,1024]{1,0:T(1,128)}, f32[1,1024]{1,0:T(1,128)S(1)}) custom-call(f32[1,1024]{1,0:T(1,128)S(1)} %get-tuple-element.52.refs_2_.refs_0_, f32[1,1024]{1,0:T(1,128)S(1)} %collective-permute-done.2.refs_1_, f32[1,1024]{1,0:T(1,128)S(1)} %collective-permute-done.3.refs_2_, f32[1,1024]{1,0:T(1,128)S(1)} %collective-permute-done.4.refs_3_, ...), custom_call_target="tpu_custom_call" | custom-call | tf_op jit(solution)/shard_map/cols/pallas_call | solution.py:274
  21.7 1.2 %collective-permute-start.11 = (f32[768,128]{1,0:T(8,128)S(1)}, f32[768,128]{1,0:T(8,128)S(1)}, u32[]{:S(2)}, u32[]{:S(2)}) collective-permute-start(f32[768,128]{1,0:T(8,128)S(1)} %get-tuple-element.62.refs_1_), channel_id=1, source_target_pairs={{0,16},{8,24},{16,0},{24,8},{1,17},{9,25},{17,1},{25,9},{2,18},{10... | collective-permute-start | bytes 1179656 | tf_op jit(solution)/shard_map/ppermute | solution.py:399
  22.9 3.0 %collective-permute-start.5 = (f32[1,1024]{1,0:T(1,128)S(1)}, f32[1,1024]{1,0:T(1,128)S(1)}, u32[]{:S(2)}, u32[]{:S(2)}) collective-permute-start(f32[1,1024]{1,0:T(1,128)S(1)} %get-tuple-element.55.refs_2_.refs_0_), channel_id=1, source_target_pairs={{0,8},{8,0},{16,24},{24,16},{1,9},{9,1},{17,25},{25,17},{2,10},{10... | collective-permute-start | bytes 12296 | tf_op jit(solution)/shard_map/ppermute | solution.py:399
  26.0 0.0 collective-permute-done.6.refs_1_
  26.0 1.2 %tables.10 = (bf16[32,64,128]{2,1,0:T(8,128)(2,1)S(1)}, bf16[32,64,128]{2,1,0:T(8,128)(2,1)S(1)}, f32[8,128]{1,0:T(8,128)S(1)}) custom-call(f32[32,128]{1,0:T(8,128)S(1)} %get-tuple-element.47.refs_0_.refs_2_, f32[768,128]{1,0:T(8,128)S(1)} %collective-permute-done.6.refs_1_, f32[1,1024]{1,0:T(1,128)S(1)} %get-tuple-element.55.refs_2_.refs_0_), custom_call_target="tpu_custom_call" | custom-call | flops 134217728 | bytes 3840000 | tf_op jit(solution)/shard_map/tables/pallas_call | solution.py:322
  27.2 0.0 collective-permute-done.5.refs_1_
  27.2 1.0 %rows.2 = (f32[1,512]{1,0:T(1,128)}, f32[1,1024]{1,0:T(1,128)S(1)}) custom-call(f32[1,1024]{1,0:T(1,128)S(1)} %get-tuple-element.55.refs_2_.refs_0_, f32[1,1024]{1,0:T(1,128)S(1)} %collective-permute-done.5.refs_1_, f32[520,128]{1,0:T(8,128)S(1)} %get-tuple-element.46.refs_2_, f32[520,128]{1,0:T(8,128)S(1)} %collective-permute-done.1.refs_3_, ...), custom_call_target="tpu_custom_call" | custom-call | tf_op jit(solution)/shard_map/rows/pallas_call | solution.py:274
  28.3 2.8 %collective-permute-start.9 = (f32[1,1024]{1,0:T(1,128)S(1)}, f32[1,1024]{1,0:T(1,128)S(1)}, u32[]{:S(2)}, u32[]{:S(2)}) collective-permute-start(f32[1,1024]{1,0:T(1,128)S(1)} %get-tuple-element.58.refs_2_.refs_0_), channel_id=1, source_target_pairs={{0,6},{1,7},{2,4},{3,5},{4,2},{5,3},{6,0},{7,1},{8,14},{9,15},{10,... | collective-permute-start | bytes 12296 | tf_op jit(solution)/shard_map/ppermute | solution.py:399
  31.1 0.0 collective-permute-start.8
  31.1 0.7 %collective-permute-start.7 = (f32[1,1024]{1,0:T(1,128)S(1)}, f32[1,1024]{1,0:T(1,128)S(1)}, u32[]{:S(2)}, u32[]{:S(2)}) collective-permute-start(f32[1,1024]{1,0:T(1,128)S(1)} %get-tuple-element.58.refs_2_.refs_0_), channel_id=1, source_target_pairs={{0,2},{1,3},{2,0},{3,1},{4,6},{5,7},{6,4},{7,5},{8,10},{9,11},{10,... | collective-permute-start | bytes 12296 | tf_op jit(solution)/shard_map/ppermute | solution.py:399
  31.8 3.2 %tables.11 = (bf16[32,192,128]{2,1,0:T(8,128)(2,1)S(1)}, bf16[32,192,128]{2,1,0:T(8,128)(2,1)S(1)}, f32[8,128]{1,0:T(8,128)S(1)}) custom-call(f32[32,128]{1,0:T(8,128)S(1)} %get-tuple-element.47.refs_0_.refs_2_, f32[768,128]{1,0:T(8,128)S(1)} %collective-permute-done.6.refs_1_, f32[1,1024]{1,0:T(1,128)S(1)} %get-tuple-element.58.refs_2_.refs_0_), custom_call_target="tpu_custom_call" | custom-call | flops 402653184 | bytes 11520000 | tf_op jit(solution)/shard_map/tables/pallas_call | solution.py:322
  35.0 0.0 collective-permute-done.9.refs_3_
  35.0 0.0 collective-permute-done.8.refs_2_
  35.0 0.0 collective-permute-done.7.refs_1_
  35.0 0.4 cols.3
  35.4 0.9 %collective-permute-start.10 = (f32[1,1024]{1,0:T(1,128)S(1)}, f32[1,1024]{1,0:T(1,128)S(1)}, u32[]{:S(2)}, u32[]{:S(2)}) collective-permute-start(f32[1,1024]{1,0:T(1,128)S(1)} %get-tuple-element.61.refs_2_.refs_0_), channel_id=1, source_target_pairs={{0,8},{8,0},{16,24},{24,16},{1,9},{9,1},{17,25},{25,17},{2,10},{10... | collective-permute-start | bytes 12296 | tf_op jit(solution)/shard_map/ppermute | solution.py:399
  36.3 0.0 collective-permute-done.11.refs_1_
  36.3 1.2 %tables.12 = (bf16[32,64,128]{2,1,0:T(8,128)(2,1)S(1)}, bf16[32,64,128]{2,1,0:T(8,128)(2,1)S(1)}, f32[8,128]{1,0:T(8,128)S(1)}) custom-call(f32[32,128]{1,0:T(8,128)S(1)} %get-tuple-element.47.refs_0_.refs_2_, f32[768,128]{1,0:T(8,128)S(1)} %collective-permute-done.11.refs_1_, f32[1,1024]{1,0:T(1,128)S(1)} %get-tuple-element.61.refs_2_.refs_0_), custom_call_target="tpu_custom_call" | custom-call | flops 134217728 | bytes 3840000 | tf_op jit(solution)/shard_map/tables/pallas_call | solution.py:322
  37.6 0.0 collective-permute-done.10.refs_1_
  37.6 0.4 rows.3
  37.9 2.9 %collective-permute-start.14 = (f32[1,1024]{1,0:T(1,128)S(1)}, f32[1,1024]{1,0:T(1,128)S(1)}, u32[]{:S(2)}, u32[]{:S(2)}) collective-permute-start(f32[1,1024]{1,0:T(1,128)S(1)} %get-tuple-element.64.refs_2_), channel_id=1, source_target_pairs={{0,6},{1,7},{2,4},{3,5},{4,2},{5,3},{6,0},{7,1},{8,14},{9,15},{10,... | collective-permute-start | bytes 12296 | tf_op jit(solution)/shard_map/ppermute | solution.py:399
  40.8 0.0 collective-permute-start.13
  40.8 0.7 %collective-permute-start.12 = (f32[1,1024]{1,0:T(1,128)S(1)}, f32[1,1024]{1,0:T(1,128)S(1)}, u32[]{:S(2)}, u32[]{:S(2)}) collective-permute-start(f32[1,1024]{1,0:T(1,128)S(1)} %get-tuple-element.64.refs_2_), channel_id=1, source_target_pairs={{0,2},{1,3},{2,0},{3,1},{4,6},{5,7},{6,4},{7,5},{8,10},{9,11},{10,... | collective-permute-start | bytes 12296 | tf_op jit(solution)/shard_map/ppermute | solution.py:399
  41.5 3.2 %tables.13 = (bf16[32,192,128]{2,1,0:T(8,128)(2,1)S(1)}, bf16[32,192,128]{2,1,0:T(8,128)(2,1)S(1)}, f32[8,128]{1,0:T(8,128)S(1)}) custom-call(f32[32,128]{1,0:T(8,128)S(1)} %get-tuple-element.47.refs_0_.refs_2_, f32[768,128]{1,0:T(8,128)S(1)} %collective-permute-done.11.refs_1_, f32[1,1024]{1,0:T(1,128)S(1)} %get-tuple-element.64.refs_2_), custom_call_target="tpu_custom_call" | custom-call | flops 402653184 | bytes 11520000 | tf_op jit(solution)/shard_map/tables/pallas_call | solution.py:322
  44.7 0.0 collective-permute-done.14.refs_5_
  44.7 0.0 collective-permute-done.13.refs_4_
  44.8 0.0 collective-permute-done.12.refs_3_
  44.8 1.6 %spread.3 = (f32[16,32,128]{2,1,0:T(8,128)S(1)}, f32[1,512]{1,0:T(1,128)S(1)}) custom-call(s32[1]{0:T(128)} %constant.2.clone.1.refs_0_, f32[1,1024]{1,0:T(1,128)S(1)} %get-tuple-element.60.refs_1_, f32[1,1024]{1,0:T(1,128)S(1)} %get-tuple-element.64.refs_2_, f32[1,1024]{1,0:T(1,128)S(1)} %collective-permute-done.12.refs_3_, ...), custom_call_target="tpu_custom_call" | custom-call | tf_op jit(solution)/shard_map/spread/pallas_call | solution.py:364
  46.3 0.9 %collective-permute-start.15 = (f32[16,32,128]{2,1,0:T(8,128)S(1)}, f32[16,32,128]{2,1,0:T(8,128)S(1)}, u32[]{:S(2)}, u32[]{:S(2)}) collective-permute-start(f32[16,32,128]{2,1,0:T(8,128)S(1)} %get-tuple-element.81), channel_id=1, source_target_pairs={{0,8},{8,0},{16,24},{24,16},{1,9},{9,1},{17,25},{25,17},{2,10},{10... | collective-permute-start | bytes 786440 | tf_op jit(solution)/shard_map/ppermute | solution.py:399
  47.2 2.0 %spread.2 = (f32[16,32,128]{2,1,0:T(8,128)S(1)}, f32[1,512]{1,0:T(1,128)}) custom-call(s32[1]{0:T(128)} %constant.1.clone.1.refs_0_, f32[1,1024]{1,0:T(1,128)S(1)} %get-tuple-element.60.refs_1_, f32[1,1024]{1,0:T(1,128)S(1)} %get-tuple-element.64.refs_2_, f32[1,1024]{1,0:T(1,128)S(1)} %collective-permute-done.12.refs_3_, ...), custom_call_target="tpu_custom_call" | custom-call | tf_op jit(solution)/shard_map/spread/pallas_call | solution.py:364
  49.2 0.0 collective-permute-done.15.b_ref
  49.2 0.7 %last.1 = (f32[16,32,128]{2,1,0:T(8,128)}, f32[1,512]{1,0:T(1,128)}, f32[1,512]{1,0:T(1,128)}) custom-call(f32[16,32,128]{2,1,0:T(8,128)S(1)} %get-tuple-element.80.a_ref, f32[16,32,128]{2,1,0:T(8,128)S(1)} %collective-permute-done.15.b_ref, f32[1,512]{1,0:T(1,128)S(1)} %get-tuple-element.82.w_ref, f32[1,512]{1,0:T(1,128)S(1)} %get-tuple-element.83.v_ref), custom_call_target="tpu_custom_call" | custom-call | tf_op jit(solution)/shard_map/last/pallas_call | solution.py:383
Async XLA Ops:
  1.7 10.0 %collective-permute-start = (f32[524,128]{1,0:T(8,128)S(1)}, f32[524,128]{1,0:T(8,128)S(1)}, u32[]{:S(2)}, u32[]{:S(2)}) collective-permute-start(f32[524,128]{1,0:T(8,128)S(1)} %get-tuple-element.45.refs_0_.refs_4_.refs_6_), channel_id=1, source_target_pairs={{0,16},{8,24},{16,0},{24,8},{1,17},{9,25},{17,1},{25,9},{2,18},{10... | collective-permute-start | bytes 804872 | tf_op jit(solution)/shard_map/ppermute | solution.py:399
  3.9 8.1 %copy-start = (f32[32,32]{1,0:T(8,128)S(1)}, f32[32,32]{1,0:T(8,128)}, u32[]{:S(2)}) copy-start(f32[32,32]{1,0:T(8,128)} %refs_4_.1) | copy-start | bytes 12292
  3.9 7.8 %collective-permute-start.1 = (f32[520,128]{1,0:T(8,128)S(1)}, f32[520,128]{1,0:T(8,128)S(1)}, u32[]{:S(2)}, u32[]{:S(2)}) collective-permute-start(f32[520,128]{1,0:T(8,128)S(1)} %get-tuple-element.46.refs_2_), channel_id=1, source_target_pairs={{0,1},{1,0},{2,3},{3,2},{4,5},{5,4},{6,7},{7,6},{8,9},{9,8},{10,11... | collective-permute-start | bytes 798728 | tf_op jit(solution)/shard_map/ppermute | solution.py:399
  11.7 14.3 %collective-permute-start.6 = (f32[768,128]{1,0:T(8,128)S(1)}, f32[768,128]{1,0:T(8,128)S(1)}, u32[]{:S(2)}, u32[]{:S(2)}) collective-permute-start(f32[768,128]{1,0:T(8,128)S(1)} %get-tuple-element.56.refs_1_), channel_id=1, source_target_pairs={{0,16},{8,24},{16,0},{24,8},{1,17},{9,25},{17,1},{25,9},{2,18},{10... | collective-permute-start | bytes 1179656 | tf_op jit(solution)/shard_map/ppermute | solution.py:399
  13.8 6.9 %collective-permute-start.4 = (f32[1,1024]{1,0:T(1,128)S(1)}, f32[1,1024]{1,0:T(1,128)S(1)}, u32[]{:S(2)}, u32[]{:S(2)}) collective-permute-start(f32[1,1024]{1,0:T(1,128)S(1)} %get-tuple-element.52.refs_2_.refs_0_), channel_id=1, source_target_pairs={{0,6},{1,7},{2,4},{3,5},{4,2},{5,3},{6,0},{7,1},{8,14},{9,15},{10,... | collective-permute-start | bytes 12296 | tf_op jit(solution)/shard_map/ppermute | solution.py:399
  17.2 3.5 %collective-permute-start.3 = (f32[1,1024]{1,0:T(1,128)S(1)}, f32[1,1024]{1,0:T(1,128)S(1)}, u32[]{:S(2)}, u32[]{:S(2)}) collective-permute-start(f32[1,1024]{1,0:T(1,128)S(1)} %get-tuple-element.52.refs_2_.refs_0_), channel_id=1, source_target_pairs={{0,4},{1,5},{2,6},{3,7},{4,0},{5,1},{6,2},{7,3},{8,12},{9,13},{10,... | collective-permute-start | bytes 12296 | tf_op jit(solution)/shard_map/ppermute | solution.py:399
  17.2 3.6 %collective-permute-start.2 = (f32[1,1024]{1,0:T(1,128)S(1)}, f32[1,1024]{1,0:T(1,128)S(1)}, u32[]{:S(2)}, u32[]{:S(2)}) collective-permute-start(f32[1,1024]{1,0:T(1,128)S(1)} %get-tuple-element.52.refs_2_.refs_0_), channel_id=1, source_target_pairs={{0,2},{1,3},{2,0},{3,1},{4,6},{5,7},{6,4},{7,5},{8,10},{9,11},{10,... | collective-permute-start | bytes 12296 | tf_op jit(solution)/shard_map/ppermute | solution.py:399
  21.7 14.6 %collective-permute-start.11 = (f32[768,128]{1,0:T(8,128)S(1)}, f32[768,128]{1,0:T(8,128)S(1)}, u32[]{:S(2)}, u32[]{:S(2)}) collective-permute-start(f32[768,128]{1,0:T(8,128)S(1)} %get-tuple-element.62.refs_1_), channel_id=1, source_target_pairs={{0,16},{8,24},{16,0},{24,8},{1,17},{9,25},{17,1},{25,9},{2,18},{10... | collective-permute-start | bytes 1179656 | tf_op jit(solution)/shard_map/ppermute | solution.py:399
  22.9 4.3 %collective-permute-start.5 = (f32[1,1024]{1,0:T(1,128)S(1)}, f32[1,1024]{1,0:T(1,128)S(1)}, u32[]{:S(2)}, u32[]{:S(2)}) collective-permute-start(f32[1,1024]{1,0:T(1,128)S(1)} %get-tuple-element.55.refs_2_.refs_0_), channel_id=1, source_target_pairs={{0,8},{8,0},{16,24},{24,16},{1,9},{9,1},{17,25},{25,17},{2,10},{10... | collective-permute-start | bytes 12296 | tf_op jit(solution)/shard_map/ppermute | solution.py:399
  28.3 6.7 %collective-permute-start.9 = (f32[1,1024]{1,0:T(1,128)S(1)}, f32[1,1024]{1,0:T(1,128)S(1)}, u32[]{:S(2)}, u32[]{:S(2)}) collective-permute-start(f32[1,1024]{1,0:T(1,128)S(1)} %get-tuple-element.58.refs_2_.refs_0_), channel_id=1, source_target_pairs={{0,6},{1,7},{2,4},{3,5},{4,2},{5,3},{6,0},{7,1},{8,14},{9,15},{10,... | collective-permute-start | bytes 12296 | tf_op jit(solution)/shard_map/ppermute | solution.py:399
  31.1 3.9 %collective-permute-start.8 = (f32[1,1024]{1,0:T(1,128)S(1)}, f32[1,1024]{1,0:T(1,128)S(1)}, u32[]{:S(2)}, u32[]{:S(2)}) collective-permute-start(f32[1,1024]{1,0:T(1,128)S(1)} %get-tuple-element.58.refs_2_.refs_0_), channel_id=1, source_target_pairs={{0,4},{1,5},{2,6},{3,7},{4,0},{5,1},{6,2},{7,3},{8,12},{9,13},{10,... | collective-permute-start | bytes 12296 | tf_op jit(solution)/shard_map/ppermute | solution.py:399
  31.1 3.9 %collective-permute-start.7 = (f32[1,1024]{1,0:T(1,128)S(1)}, f32[1,1024]{1,0:T(1,128)S(1)}, u32[]{:S(2)}, u32[]{:S(2)}) collective-permute-start(f32[1,1024]{1,0:T(1,128)S(1)} %get-tuple-element.58.refs_2_.refs_0_), channel_id=1, source_target_pairs={{0,2},{1,3},{2,0},{3,1},{4,6},{5,7},{6,4},{7,5},{8,10},{9,11},{10,... | collective-permute-start | bytes 12296 | tf_op jit(solution)/shard_map/ppermute | solution.py:399
  35.4 2.2 %collective-permute-start.10 = (f32[1,1024]{1,0:T(1,128)S(1)}, f32[1,1024]{1,0:T(1,128)S(1)}, u32[]{:S(2)}, u32[]{:S(2)}) collective-permute-start(f32[1,1024]{1,0:T(1,128)S(1)} %get-tuple-element.61.refs_2_.refs_0_), channel_id=1, source_target_pairs={{0,8},{8,0},{16,24},{24,16},{1,9},{9,1},{17,25},{25,17},{2,10},{10... | collective-permute-start | bytes 12296 | tf_op jit(solution)/shard_map/ppermute | solution.py:399
  37.9 6.8 %collective-permute-start.14 = (f32[1,1024]{1,0:T(1,128)S(1)}, f32[1,1024]{1,0:T(1,128)S(1)}, u32[]{:S(2)}, u32[]{:S(2)}) collective-permute-start(f32[1,1024]{1,0:T(1,128)S(1)} %get-tuple-element.64.refs_2_), channel_id=1, source_target_pairs={{0,6},{1,7},{2,4},{3,5},{4,2},{5,3},{6,0},{7,1},{8,14},{9,15},{10,... | collective-permute-start | bytes 12296 | tf_op jit(solution)/shard_map/ppermute | solution.py:399
  40.8 3.9 %collective-permute-start.13 = (f32[1,1024]{1,0:T(1,128)S(1)}, f32[1,1024]{1,0:T(1,128)S(1)}, u32[]{:S(2)}, u32[]{:S(2)}) collective-permute-start(f32[1,1024]{1,0:T(1,128)S(1)} %get-tuple-element.64.refs_2_), channel_id=1, source_target_pairs={{0,4},{1,5},{2,6},{3,7},{4,0},{5,1},{6,2},{7,3},{8,12},{9,13},{10,... | collective-permute-start | bytes 12296 | tf_op jit(solution)/shard_map/ppermute | solution.py:399
  40.8 3.9 %collective-permute-start.12 = (f32[1,1024]{1,0:T(1,128)S(1)}, f32[1,1024]{1,0:T(1,128)S(1)}, u32[]{:S(2)}, u32[]{:S(2)}) collective-permute-start(f32[1,1024]{1,0:T(1,128)S(1)} %get-tuple-element.64.refs_2_), channel_id=1, source_target_pairs={{0,2},{1,3},{2,0},{3,1},{4,6},{5,7},{6,4},{7,5},{8,10},{9,11},{10,... | collective-permute-start | bytes 12296 | tf_op jit(solution)/shard_map/ppermute | solution.py:399
  46.3 2.8 %collective-permute-start.15 = (f32[16,32,128]{2,1,0:T(8,128)S(1)}, f32[16,32,128]{2,1,0:T(8,128)S(1)}, u32[]{:S(2)}, u32[]{:S(2)}) collective-permute-start(f32[16,32,128]{2,1,0:T(8,128)S(1)} %get-tuple-element.81), channel_id=1, source_target_pairs={{0,8},{8,0},{16,24},{24,16},{1,9},{9,1},{17,25},{25,17},{2,10},{10... | collective-permute-start | bytes 786440 | tf_op jit(solution)/shard_map/ppermute | solution.py:399
